TPU v7x, 32 devices: a whole 2x2x4 slice. The times are simulated.
32 devices in a mesh: groups: 2 (over y), expert: 4 (over x, core), replica: 4 (over z).
Axes of the slice: x: 2, y: 2, z: 4, core: 2. Of those that a mesh axis runs over, the one named last changes fastest.
Arguments:
- tokens: bfloat16 [8192, 2048], P(('groups', 'expert', 'replica')), parts along dimension 0, may hold values from -6 to 6
- norm_gain: float32 [2048], replicated, may hold values from 0.1 to 1.9
- router: bfloat16 [2048, 16], replicated, may hold values from -0.125 to 0.125
- down_proj: bfloat16 [2048, 512], P(('expert', 'replica')), may hold values from -0.125 to 0.125
- up_proj: bfloat16 [2048, 512], P(('expert', 'replica')), may hold values from -0.25 to 0.25
- expert_gate: bfloat16 [16, 512, 768], P('expert'), may hold values from -0.25 to 0.25
- expert_up: bfloat16 [16, 512, 768], P('expert'), may hold values from -0.25 to 0.25
- expert_down: bfloat16 [16, 768, 512], P('expert'), may hold values from -0.21875 to 0.21875
- expert_ids: int32 [8192, 8], P(('groups', 'expert', 'replica')), parts along dimension 0, may hold values from 0 to 15, as said below
- slot_pos: int32 [8192, 8], P(('groups', 'expert', 'replica')), parts along dimension 0, may hold values from -1 to 127, as said below
- overflow_list: int32 [32, 4, 4, 4], P(('groups', 'expert', 'replica')), parts along dimension 0, may hold values from -1 to 2047, as said below
Outputs:
- mixed: bfloat16 [8192, 2048], P(('groups', 'expert', 'replica')), parts along dimension 0
There are 2 independent parts, one for each index of `groups`. A program takes and returns all parts, laid end to end along the dimension named above; an argument that names none is the same for every part. Nothing has to cross between parts.
Inputs may be any that keep to these rules, and one draw needn't show every extreme that they name: `expert_ids`: the 8 ids of a token are distinct. `slot_pos`: within the 256 rows of one device, the choices of one expert that have a slot hold distinct slots 0, 1, 2, ... in row order, so at most 128 from one device to one expert; in every draw some expert gets all 128 slots from every device. `overflow_list`: an entry is a choice index t' * 8 + k of the source device's own rows whose expert is (destination index of the expert axis) * 4 + (local expert) and whose slot_pos is -1; each choice is listed at most once. In every draw some expert is listed at every copy by every source device.
All inputs are finite; a program needn't handle non-finite values.
Results may differ from a plain program's by a relative error of at most 0.0088.
Values may be sent and summed in bfloat16 or wider, within the bound.
No kernel may reach another device: no remote copies, remote signals or barrier semaphores. Data moves between devices by JAX's collectives and lax.ppermute only.
A program may use at most 128 MiB of HBM per device.

v0:
```python
import functools

import jax
import jax.numpy as jnp
from jax import lax
from jax.experimental import pallas as pl
from jax.experimental.pallas import tpu as pltpu
from jax.sharding import PartitionSpec as P

epsilon = 1e-06
F32 = jnp.float32
BF16 = jnp.bfloat16

VM = pl.BlockSpec(memory_space=pltpu.VMEM)
SM = pl.BlockSpec(memory_space=pltpu.SMEM)
HB = pl.BlockSpec(memory_space=pltpu.HBM)


def swap(x, axis, bits):
    size = lax.axis_size(axis)
    return lax.ppermute(x, axis, [(i, i ^ bits) for i in range(size)])


def swap_pair(x, axes, move):
    sizes = [lax.axis_size(axis) for axis in axes]
    pairs = []
    for i in range(sizes[0]):
        for j in range(sizes[1]):
            p, q = move(i, j)
            pairs.append((i * sizes[1] + j, p * sizes[1] + q))
    return lax.ppermute(x, axes, pairs)


def kernel(body, out_shape, operands, specs, mib, flops=0, nbytes=0, scratch=(), out_specs=None):
    many = isinstance(out_shape, tuple)
    if out_specs is None:
        out_specs = (VM,) * len(out_shape) if many else VM
    return pl.pallas_call(
        body,
        out_shape=out_shape,
        in_specs=specs,
        out_specs=out_specs,
        scratch_shapes=list(scratch),
        compiler_params=pltpu.CompilerParams(vmem_limit_bytes=mib * 1024 * 1024),
        cost_estimate=pl.CostEstimate(flops=flops, bytes_accessed=nbytes, transcendentals=0),
    )(*operands)


def gate_kernel(top, wide, pos_ref, list_ref, tok_ref, gain_ref, router_ref, ids_ref, slot_ref,
                g_ref, u_ref, d_ref, keep_ref, send_ref, wt_ref, g0_ref, u0_ref, d0_ref,
                normed_ref, sem):
    copies = [
        pltpu.make_async_copy(src.at[pl.ds(0, 1)], dst, sem.at[i])
        for i, (src, dst) in enumerate(((g_ref, g0_ref), (u_ref, u0_ref), (d_ref, d0_ref)))
    ]
    for copy in copies:
        copy.start()
    values = tok_ref[...].astype(F32)
    scale = lax.rsqrt(jnp.mean(values * values, axis=-1, keepdims=True) + epsilon)
    normed = (values * scale * gain_ref[...]).astype(BF16)
    normed_ref[...] = normed
    core = pos_ref[0]
    for h in range(keep_ref.shape[1] // wide):
        mine = pl.multiple_of((2 * h + core) * wide, wide)
        other = pl.multiple_of((2 * h + 1 - core) * wide, wide)
        keep_ref[:, h * wide:(h + 1) * wide] = normed_ref[:, pl.ds(mine, wide)]
        send_ref[:, h * wide:(h + 1) * wide] = normed_ref[:, pl.ds(other, wide)]
    logits = lax.dot_general(router_ref[...], normed_ref[...], (((1,), (1,)), ((), ())),
                             preferred_element_type=F32)
    sig = jax.nn.sigmoid(logits)
    experts, rows = sig.shape
    sub = lax.broadcasted_iota(jnp.int32, (experts, rows), 0)
    lane = lax.broadcasted_iota(jnp.int32, (experts, rows), 1)
    total = jnp.zeros((experts, rows), F32)
    served = jnp.zeros((experts, rows), F32)
    for k in range(top):
        hit = sub == ids_ref[k:k + 1, :]
        total = total + jnp.where(hit, 1.0, 0.0)
        served = served + jnp.where(hit & (slot_ref[k:k + 1, :] >= 0), 1.0, 0.0)
    _, shards, copies_n, local = list_ref.shape

    def listed(i, served):
        shard, copy = i // copies_n, i % copies_n
        for m in range(local):
            entry = list_ref[0, shard, copy, m]
            owner = jnp.where(entry >= 0, entry, -top) // top
            served = served + jnp.where((lane == owner) & (sub == shard * local + m), 1.0, 0.0)
        return served

    served = lax.fori_loop(0, shards * copies_n, listed, served)
    denom = jnp.sum(total * sig, axis=0, keepdims=True)
    wt_ref[...] = jnp.where(served > 0.0, sig / denom, 0.0)
    for copy in copies:
        copy.wait()


def latent_kernel(chunks, wide, pos_ref, keep_ref, recv_ref, *refs):
    w_refs, (out_ref, x_ref, w_ref) = refs[:-3], refs[-3:]
    half, rep, group = pos_ref[1], pos_ref[2], pos_ref[4]
    rows = keep_ref.shape[0]
    depth = w_refs[0].shape[0]
    for i, ((a, b), chunk) in enumerate(zip(chunks, w_refs)):
        if b == "A":
            b = 2 + group
        elif b == "B":
            b = 3 - group
        at = pl.multiple_of((half ^ a) * wide + (rep ^ b) * depth, depth)
        x_ref[:rows, i * depth:(i + 1) * depth] = keep_ref[:, pl.ds(at, depth)]
        x_ref[rows:, i * depth:(i + 1) * depth] = recv_ref[:, pl.ds(at, depth)]
        w_ref[i * depth:(i + 1) * depth, :] = chunk[...]
    out_ref[...] = jnp.dot(x_ref[...], w_ref[...], preferred_element_type=F32)


def finish_kernel(mine_ref, recv_ref, own_ref, core_ref):
    rows = own_ref.shape[0]
    own_ref[...] = (mine_ref[:rows, :] + recv_ref[rows:, :]).astype(BF16)
    core_ref[...] = (mine_ref[rows:, :] + recv_ref[:rows, :]).astype(BF16)


def expert(x, weight, gate_w, up_w, down_w):
    gate = jnp.dot(x, gate_w, preferred_element_type=F32)
    upper = jnp.dot(x, up_w, preferred_element_type=F32)
    half = 0.5 * gate
    hidden = ((half + half * jnp.tanh(half)) * upper).astype(BF16)
    result = jnp.dot(hidden, down_w, preferred_element_type=F32).astype(BF16)
    return result.astype(F32) * weight


def columns(me, local, wt_ref):
    _, rows = wt_ref.shape
    wt = wt_ref[...]
    sub = lax.broadcasted_iota(jnp.int32, wt.shape, 0)
    picked = [jnp.sum(jnp.where(sub == me * local + j, wt, 0.0), axis=0, keepdims=True)
              for j in range(local)]
    pad = jnp.zeros((-local % 8, rows), F32)
    return jnp.concatenate(picked + [pad], axis=0).T


def near_kernel(local, pos_ref, x0_ref, x1_ref, w0_ref, w1_ref, g0_ref, u0_ref, d0_ref,
                g_ref, u_ref, d_ref, o0_ref, o1_ref, gv_ref, uv_ref, dv_ref, acc_ref, sem):
    copies = {}
    for j in range(1, local):
        for i, (src, dst) in enumerate(((g_ref, gv_ref), (u_ref, uv_ref), (d_ref, dv_ref))):
            copies[j, i] = pltpu.make_async_copy(src.at[pl.ds(j, 1)], dst.at[pl.ds(j - 1, 1)],
                                                 sem.at[i, j - 1])
            copies[j, i].start()
    rows = x0_ref.shape[0]
    cols = [columns(pos_ref[3], local, w) for w in (w0_ref, w1_ref)]
    for j in range(local):
        if j == 0:
            weights = g0_ref[0], u0_ref[0], d0_ref[0]
        else:
            for i in range(3):
                copies[j, i].wait()
            weights = gv_ref[j - 1], uv_ref[j - 1], dv_ref[j - 1]
        for i, x_ref in enumerate((x0_ref, x1_ref)):
            part = expert(x_ref[...], cols[i][:, j:j + 1], *weights)
            span = slice(i * rows, (i + 1) * rows)
            acc_ref[span, :] = part if j == 0 else acc_ref[span, :] + part
    o0_ref[...] = acc_ref[:rows, :].astype(BF16)
    o1_ref[...] = acc_ref[rows:, :].astype(BF16)


def far_kernel(local, pos_ref, x_ref, w_ref, g0_ref, u0_ref, d0_ref, gv_ref, uv_ref, dv_ref,
               o_ref, acc_ref):
    cols = columns(pos_ref[3], local, w_ref)
    for j in range(local):
        if j == 0:
            weights = g0_ref[0], u0_ref[0], d0_ref[0]
        else:
            weights = gv_ref[j - 1], uv_ref[j - 1], dv_ref[j - 1]
        part = expert(x_ref[...], cols[:, j:j + 1], *weights)
        acc_ref[...] = part if j == 0 else acc_ref[...] + part
    o_ref[...] = acc_ref[...].astype(BF16)


def add_kernel(a_ref, b_ref, o_ref):
    o_ref[...] = (a_ref[...].astype(F32) + b_ref[...].astype(F32)).astype(BF16)


def join_kernel(*refs):
    depth = refs[0].shape[0]
    for i, x_ref in enumerate(refs[:-1]):
        refs[-1][i * depth:(i + 1) * depth, :] = x_ref[...]


def final_kernel(n_sum, chunks, copies, depth, pos_ref, *refs):
    out_ref = refs[-1]
    half, rep, core = pos_ref[1], pos_ref[2], pos_ref[0]
    total = refs[0][...].astype(F32)
    for s_ref in refs[1:n_sum]:
        total = total + s_ref[...].astype(F32)
    merged = total.astype(BF16)
    for (c, b), w_ref in zip(chunks, refs[n_sum:-1]):
        block = lax.dot_general(merged, w_ref[...], (((1,), (1,)), ((), ())),
                                preferred_element_type=F32).astype(BF16)
        for a in range(w_ref.shape[0] // depth):
            e = 2 * (half ^ a) + (core ^ c)
            at = pl.multiple_of((e * copies + (rep ^ b)) * depth, depth)
            out_ref[:, pl.ds(at, depth)] = block[:, a * depth:(a + 1) * depth]


def shape(dims, dtype=BF16):
    return jax.ShapeDtypeStruct(dims, dtype)


def on_device(tokens, norm_gain, router, down_proj, up_proj, expert_gate, expert_up, expert_down,
              expert_ids, slot_pos, overflow_list):
    rows, width = tokens.shape
    top = expert_ids.shape[1]
    local, _, ff = expert_gate.shape
    depth, latent = down_proj.shape
    groups = lax.axis_size("groups")
    shards = lax.axis_size("expert")
    copies = lax.axis_size("replica")
    chips = shards // 2
    wide = copies * depth
    spread = copies
    if depth % 128:
        down_proj = lax.all_gather(down_proj, "replica", axis=0, tiled=True)
        up_proj = lax.all_gather(up_proj, "replica", axis=0, tiled=True)
        depth, spread = wide, 1
    experts = shards * local
    g = lax.axis_index("groups")
    e = lax.axis_index("expert")
    r = lax.axis_index("replica")
    pos = jnp.stack([e % 2, e // 2, r if spread > 1 else 0 * r, e, g]).astype(jnp.int32)

    down = {(0, 0): down_proj}
    if spread == groups + 2 and groups == 2:
        near_z = swap(down_proj, "replica", 1)
        far_z = swap_pair(down_proj, ("groups", "replica"), lambda i, j: (i, j ^ (2 + i)))
        down[(0, 1)] = near_z
        down[(0, "A")] = far_z
        for a in range(1, chips):
            down[(a, 0)] = swap(down_proj, "expert", 2 * a)
        ups_x = [swap(up_proj, "expert", 2 * a) for a in range(1, chips)]
        for a in range(1, chips):
            down[(a, 1)] = swap(near_z, "expert", 2 * a)
            down[(a, "B")] = swap_pair(far_z, ("groups", "expert"),
                                       lambda i, j: (i ^ 1, j ^ (2 * a)))
            down[(a, "A")] = swap(far_z, "expert", 2 * a)
        down[(0, "B")] = swap(far_z, "groups", 1)
    else:
        for b in range(1, spread):
            down[(0, b)] = swap(down_proj, "replica", b)
        for b in range(spread):
            for a in range(1, chips):
                down[(a, b)] = swap(down[(0, b)], "expert", 2 * a)
        ups_x = [swap(up_proj, "expert", 2 * a) for a in range(1, chips)]

    one = [shape((1,) + w.shape[1:]) for w in (expert_gate, expert_up, expert_down)]
    rest = [shape((local - 1,) + w.shape[1:]) for w in (expert_gate, expert_up, expert_down)]
    keep, send, wt, *first = kernel(
        functools.partial(gate_kernel, top, wide),
        (shape((rows, width // 2)), shape((rows, width // 2)), shape((experts, rows), F32), *one),
        (pos, overflow_list, tokens, norm_gain.reshape(1, width), router.T, expert_ids.T,
         slot_pos.T, expert_gate, expert_up, expert_down),
        [SM, SM] + [VM] * 5 + [HB] * 3, 20, 4 * rows * width * experts, 4 * rows * width,
        [pltpu.VMEM((rows, width), BF16), pltpu.SemaphoreType.DMA((3,))])
    recv = swap(send, "expert", 1)
    wt_core = swap(wt, "expert", 1)

    order = list(down)
    partial = kernel(
        functools.partial(latent_kernel, order, wide), shape((2 * rows, latent), F32),
        (pos, keep, recv, *[down[k] for k in order]), [SM] + [VM] * (2 + len(order)), 14,
        2 * rows * width * latent, 2 * width * latent,
        [pltpu.VMEM((2 * rows, width // 2), BF16), pltpu.VMEM((width // 2, latent), BF16)])
    partial_core = swap(partial, "expert", 1)
    lat_own, lat_core = kernel(
        finish_kernel, (shape((rows, latent)),) * 2, (partial, partial_core), [VM, VM], 6,
        2 * rows * latent, 12 * rows * latent)

    far = []
    for a in range(1, chips):
        x0 = swap(lat_own, "expert", 2 * a)
        w0 = swap(wt, "expert", 2 * a)
        far.append((x0, w0, swap(x0, "expert", 1), swap(w0, "expert", 1)))
    work = 6 * rows * local * latent * ff
    near0, near1, *kept = kernel(
        functools.partial(near_kernel, local),
        (shape((rows, latent)), shape((rows, latent)), *rest),
        (pos, lat_own, lat_core, wt, wt_core, *first, expert_gate, expert_up, expert_down),
        [SM] + [VM] * 7 + [HB] * 3, 28, 2 * work, 6 * local * latent * ff,
        [pltpu.VMEM((2 * rows, latent), F32), pltpu.SemaphoreType.DMA((3, local - 1))])

    def run_far(x, w):
        return kernel(functools.partial(far_kernel, local), shape((rows, latent)),
                      (pos, x, w, *first, *kept), [SM] + [VM] * 8, 20, work, 6 * local * latent * ff,
                      [pltpu.VMEM((rows, latent), F32)])

    sums = [near0, swap(near1, "expert", 1)]
    for a in range(1, chips):
        x0, w0, x1, w1 = far[a - 1]
        o0 = run_far(x0, w0)
        o1 = run_far(x1, w1)
        back = swap(o1, "expert", 1)
        s = kernel(add_kernel, shape((rows, latent)), (o0, back), [VM, VM], 4,
                   rows * latent, 6 * rows * latent)
        sums.append(swap(s, "expert", 2 * a))

    pair = kernel(join_kernel, shape((chips * depth, latent)), (up_proj, *ups_x),
                  [VM] * chips, 4, 0, 4 * chips * depth * latent)
    ups = {(0, 0): pair}
    for b in range(1, spread):
        ups[(0, b)] = swap(pair, "replica", b)
    for b in range(spread):
        ups[(1, b)] = swap(ups[(0, b)], "expert", 1)
    order = sorted(ups)
    return kernel(
        functools.partial(final_kernel, len(sums), order, spread, depth),
        shape((rows, width)), (pos, *sums, *[ups[k] for k in order]),
        [SM] + [VM] * (len(sums) + len(order)), 14, 2 * rows * width * latent, 2 * width * latent)


def solution(mesh):
    placed = (
        P(("groups", "expert", "replica"), None),
        P(),
        P(),
        P(("expert", "replica"), None),
        P(("expert", "replica"), None),
        P("expert", None, None),
        P("expert", None, None),
        P("expert", None, None),
        P(("groups", "expert", "replica"), None),
        P(("groups", "expert", "replica"), None),
        P(("groups", "expert", "replica"), None, None, None),
    )

    return jax.shard_map(
        on_device,
        mesh=mesh,
        in_specs=placed,
        out_specs=P(("groups", "expert", "replica"), None),
        check_vma=False,
    )
```

profile of v0, /device:TPU:8, one launch (start us, length us, event | category | flops | bytes accessed | tf_op | source)
XLA Modules:
  0.0 89.9 jit_solution(17929253375493580634)
XLA Ops:
  0.0 0.1 stack.23.pos_ref
  0.1 1.9 %copy-done = bf16[4,512,768]{2,1,0:T(8,128)(2,1)S(1)} copy-done((bf16[4,512,768]{2,1,0:T(8,128)(2,1)S(1)}, bf16[4,512,768]{2,1,0:T(8,128)(2,1)}, u32[]{:S(2)}) %copy-start) | copy-done | bytes 3145752
  2.0 1.9 %copy-done.2 = bf16[4,512,768]{2,1,0:T(8,128)(2,1)S(1)} copy-done((bf16[4,512,768]{2,1,0:T(8,128)(2,1)S(1)}, bf16[4,512,768]{2,1,0:T(8,128)(2,1)}, u32[]{:S(2)}) %copy-start.2) | copy-done | bytes 3145752
  3.9 1.9 %copy-done.4 = bf16[4,768,512]{2,1,0:T(8,128)(2,1)S(1)} copy-done((bf16[4,768,512]{2,1,0:T(8,128)(2,1)S(1)}, bf16[4,768,512]{2,1,0:T(8,128)(2,1)}, u32[]{:S(2)}) %copy-start.4) | copy-done | bytes 3145752
  5.8 1.2 %copy-done.6 = bf16[256,2048]{1,0:T(8,128)(2,1)S(1)} copy-done((bf16[256,2048]{1,0:T(8,128)(2,1)S(1)}, bf16[256,2048]{1,0:T(8,128)(2,1)}, u32[]{:S(2)}) %copy-start.6) | copy-done | bytes 1048600
  7.0 0.8 copy-done.9
  7.8 0.7 copy-done.10
  8.5 0.7 copy-done.11
  9.2 0.7 copy-done.12
  9.9 0.7 copy-done.13
  10.6 2.4 %shard_map.109 = (bf16[256,1024]{1,0:T(8,128)(2,1)S(1)}, bf16[256,1024]{1,0:T(8,128)(2,1)S(1)}, f32[16,256]{1,0:T(8,128)S(1)}, bf16[1,512,768]{2,1,0:T(8,128)(2,...) custom-call(s32[5]{0:T(128)S(1)} %stack.23.pos_ref, s32[1,4,4,4]{3,2,1,0:T(4,128)S(1)} %copy-done.10, ...), custom_call_target="tpu_custom_call" | custom-call | flops 33554432 | bytes 2097152 | tf_op jit(solution)/shard_map/pallas_call | solution.py:38
  13.1 0.1 collective-permute-start
  13.2 0.1 collective-permute-start.1
  13.2 3.0 %collective-permute-start.2 = (bf16[128,512]{1,0:T(8,128)(2,1)S(1)}, bf16[128,512]{1,0:T(8,128)(2,1)S(1)}, u32[]{:S(2)}, u32[]{:S(2)}) collective-permute-start(bf16[128,512]{1,0:T(8,128)(2,1)S(1)} %copy-done.8), channel_id=1, source_target_pairs={{0,2},{1,3},{2,0},{3,1},{16,19},{17,18},{18,17},{19,16},{4,6},{5,7... | collective-permute-start | bytes 393224 | tf_op jit(solution)/shard_map/ppermute | solution.py:31
  16.3 1.5 %collective-permute-start.3 = (bf16[128,512]{1,0:T(8,128)(2,1)S(1)}, bf16[128,512]{1,0:T(8,128)(2,1)S(1)}, u32[]{:S(2)}, u32[]{:S(2)}) collective-permute-start(bf16[128,512]{1,0:T(8,128)(2,1)S(1)} %copy-done.8), channel_id=1, source_target_pairs={{0,8},{4,12},{8,0},{12,4},{1,9},{5,13},{9,1},{13,5},{2,10},{6,14},... | collective-permute-start | bytes 393224 | tf_op jit(solution)/shard_map/ppermute | solution.py:21
  17.8 1.8 %collective-permute-done.1.refs_1_ = bf16[128,512]{1,0:T(8,128)(2,1)S(1)} collective-permute-done((bf16[128,512]{1,0:T(8,128)(2,1)S(1)}, bf16[128,512]{1,0:T(8,128)(2,1)S(1)}, u32[]{:S(2)}, u32[]{:S(2)}) %collective-permute-start.1) | collective-permute-done | bytes 131104 | tf_op jit(solution)/shard_map/ppermute | solution.py:21
  19.6 1.5 %collective-permute-start.4 = (bf16[128,512]{1,0:T(8,128)(2,1)S(1)}, bf16[128,512]{1,0:T(8,128)(2,1)S(1)}, u32[]{:S(2)}, u32[]{:S(2)}) collective-permute-start(bf16[128,512]{1,0:T(8,128)(2,1)S(1)} %collective-permute-done.1.refs_1_), channel_id=1, source_target_pairs={{0,8},{4,12},{8,0},{12,4},{1,9},{5,13},{9,1},{13,5},{2,10},{6,14},... | collective-permute-start | bytes 393224 | tf_op jit(solution)/shard_map/ppermute | solution.py:21
  21.1 1.9 %collective-permute-done.2.refs_2_ = bf16[128,512]{1,0:T(8,128)(2,1)S(1)} collective-permute-done((bf16[128,512]{1,0:T(8,128)(2,1)S(1)}, bf16[128,512]{1,0:T(8,128)(2,1)S(1)}, u32[]{:S(2)}, u32[]{:S(2)}) %collective-permute-start.2) | collective-permute-done | bytes 131104 | tf_op jit(solution)/shard_map/ppermute | solution.py:31
  23.0 2.5 %collective-permute-start.5 = (bf16[128,512]{1,0:T(8,128)(2,1)S(1)}, bf16[128,512]{1,0:T(8,128)(2,1)S(1)}, u32[]{:S(2)}, u32[]{:S(2)}) collective-permute-start(bf16[128,512]{1,0:T(8,128)(2,1)S(1)} %collective-permute-done.2.refs_2_), channel_id=1, source_target_pairs={{0,24},{4,28},{8,16},{12,20},{16,8},{20,12},{24,0},{28,4},{1,25},{... | collective-permute-start | bytes 393224 | tf_op jit(solution)/shard_map/ppermute | solution.py:31
  25.4 0.5 collective-permute-start.6
  26.0 0.5 collective-permute-start.7
  26.5 3.7 %collective-permute-done.5.refs_5_ = bf16[128,512]{1,0:T(8,128)(2,1)S(1)} collective-permute-done((bf16[128,512]{1,0:T(8,128)(2,1)S(1)}, bf16[128,512]{1,0:T(8,128)(2,1)S(1)}, u32[]{:S(2)}, u32[]{:S(2)}) %collective-permute-start.5) | collective-permute-done | bytes 131104 | tf_op jit(solution)/shard_map/ppermute | solution.py:31
  30.2 0.4 collective-permute-done.6.refs_6_
  30.6 1.0 %collective-permute-done.7.refs_7_ = bf16[128,512]{1,0:T(8,128)(2,1)S(1)} collective-permute-done((bf16[128,512]{1,0:T(8,128)(2,1)S(1)}, bf16[128,512]{1,0:T(8,128)(2,1)S(1)}, u32[]{:S(2)}, u32[]{:S(2)}) %collective-permute-start.7) | collective-permute-done | bytes 131104 | tf_op jit(solution)/shard_map/ppermute | solution.py:21
  31.6 1.3 %shard_map.110.mine_ref = f32[512,512]{1,0:T(8,128)S(1)} custom-call(s32[5]{0:T(128)S(1)} %stack.23.pos_ref, bf16[256,1024]{1,0:T(8,128)(2,1)S(1)} %get-tuple-element.18.keep_ref, bf16[256,1024]{1,0:T(8,128)(2,1)S(1)} %collective-permute-done.recv_ref, bf16[128,512]{1,0:T(8,128)(2,1)S(1)} %copy-done.8, bf16[128,512]{1,0:T(8,128)(2,1)S(1)} %collective-permute-done.1.refs_1_, ...), custom_call_target="tpu_custom_call" | custom-call | flops 536870912 | bytes 2097152 | tf_op jit(solution)/shard_map/pallas_call | solution.py:38
  32.9 0.1 collective-permute-start.8
  33.0 2.6 %collective-permute-done.8.recv_ref = f32[512,512]{1,0:T(8,128)S(1)} collective-permute-done((f32[512,512]{1,0:T(8,128)S(1)}, f32[512,512]{1,0:T(8,128)S(1)}, u32[]{:S(2)}, u32[]{:S(2)}) %collective-permute-start.8) | collective-permute-done | bytes 1048608 | tf_op jit(solution)/shard_map/ppermute | solution.py:21
  35.7 0.1 shard_map.111
  35.7 1.6 %collective-permute-start.11 = (bf16[256,512]{1,0:T(8,128)(2,1)S(1)}, bf16[256,512]{1,0:T(8,128)(2,1)S(1)}, u32[]{:S(2)}, u32[]{:S(2)}) collective-permute-start(bf16[256,512]{1,0:T(8,128)(2,1)S(1)} %get-tuple-element.20.x0_ref), channel_id=1, source_target_pairs={{0,8},{4,12},{8,0},{12,4},{1,9},{5,13},{9,1},{13,5},{2,10},{6,14},... | collective-permute-start | bytes 786440 | tf_op jit(solution)/shard_map/ppermute | solution.py:21
  37.3 0.5 collective-permute-start.17
  37.8 1.5 %collective-permute-start.12 = (f32[16,256]{1,0:T(8,128)S(1)}, f32[16,256]{1,0:T(8,128)S(1)}, u32[]{:S(2)}, u32[]{:S(2)}) collective-permute-start(f32[16,256]{1,0:T(8,128)S(1)} %get-tuple-element.22.w0_ref), channel_id=1, source_target_pairs={{0,8},{4,12},{8,0},{12,4},{1,9},{5,13},{9,1},{13,5},{2,10},{6,14},... | collective-permute-start | bytes 49160 | tf_op jit(solution)/shard_map/ppermute | solution.py:21
  39.4 8.0 %collective-permute-done.12.w_ref = f32[16,256]{1,0:T(8,128)S(1)} collective-permute-done((f32[16,256]{1,0:T(8,128)S(1)}, f32[16,256]{1,0:T(8,128)S(1)}, u32[]{:S(2)}, u32[]{:S(2)}) %collective-permute-start.12) | collective-permute-done | bytes 16416 | tf_op jit(solution)/shard_map/ppermute | solution.py:21
  47.4 1.6 %collective-permute-start.18 = (bf16[256,512]{1,0:T(8,128)(2,1)S(1)}, bf16[256,512]{1,0:T(8,128)(2,1)S(1)}, u32[]{:S(2)}, u32[]{:S(2)}) collective-permute-start(bf16[256,512]{1,0:T(8,128)(2,1)S(1)} %shard_map.116.refs_3_), channel_id=1, source_target_pairs={{0,1},{1,0},{2,3},{3,2},{4,5},{5,4},{6,7},{7,6},{8,9},{9,8},{10,11... | collective-permute-start | bytes 786440 | tf_op jit(solution)/shard_map/ppermute | solution.py:21
  49.0 1.9 %collective-permute-start.19 = (bf16[256,512]{1,0:T(8,128)(2,1)S(1)}, bf16[256,512]{1,0:T(8,128)(2,1)S(1)}, u32[]{:S(2)}, u32[]{:S(2)}) collective-permute-start(bf16[256,512]{1,0:T(8,128)(2,1)S(1)} %shard_map.116.refs_3_), channel_id=1, source_target_pairs={{0,2},{1,3},{2,0},{3,1},{4,6},{5,7},{6,4},{7,5},{8,10},{9,11},{10,... | collective-permute-start | bytes 786440 | tf_op jit(solution)/shard_map/ppermute | solution.py:21
  50.9 0.5 collective-permute-start.20
  51.4 7.4 %shard_map.112 = (bf16[256,512]{1,0:T(8,128)(2,1)S(1)}, bf16[256,512]{1,0:T(8,128)(2,1)S(1)}, bf16[3,512,768]{2,1,0:T(8,128)(2,1)S(1)}, bf16[3,512,768]{2,1,0:T(8,128)(2,1)S(1)}, bf16[3,768,512]{2,1,0:T(8,128)(2,1)S(1)}) custom-call(s32[5]{0:T(128)S(1)} %stack.23.pos_ref, bf16[256,512]{1,0:T(8,128)(2,1)S(1)} %get-tuple-element.20.x0_ref, ...), custom_call_target="tpu_custom_call" | custom-call | flops 4831838208 | bytes 9437184 | tf_op jit(solution)/shard_map/pallas_call | solution.py:38
  58.8 3.5 %shard_map.114 = bf16[256,512]{1,0:T(8,128)(2,1)S(1)} custom-call(s32[5]{0:T(128)S(1)} %stack.23.pos_ref, bf16[256,512]{1,0:T(8,128)(2,1)S(1)} %collective-permute-done.13.x_ref, f32[16,256]{1,0:T(8,128)S(1)} %collective-permute-done.14.w_ref, bf16[1,512,768]{2,1,0:T(8,128)(2,1)S(1)} %get-tuple-element.23.g0_ref, ...), custom_call_target="tpu_custom_call" | custom-call | flops 2415919104 | bytes 9437184 | tf_op jit(solution)/shard_map/pallas_call | solution.py:38
  62.3 0.6 collective-permute-start.15
  62.9 0.1 collective-permute-start.21
  62.9 0.4 collective-permute-start.22
  63.4 5.5 %collective-permute-done.19.refs_5_ = bf16[256,512]{1,0:T(8,128)(2,1)S(1)} collective-permute-done((bf16[256,512]{1,0:T(8,128)(2,1)S(1)}, bf16[256,512]{1,0:T(8,128)(2,1)S(1)}, u32[]{:S(2)}, u32[]{:S(2)}) %collective-permute-start.19) | collective-permute-done | bytes 262176 | tf_op jit(solution)/shard_map/ppermute | solution.py:21
  68.8 6.1 %collective-permute-done.20.refs_6_ = bf16[256,512]{1,0:T(8,128)(2,1)S(1)} collective-permute-done((bf16[256,512]{1,0:T(8,128)(2,1)S(1)}, bf16[256,512]{1,0:T(8,128)(2,1)S(1)}, u32[]{:S(2)}, u32[]{:S(2)}) %collective-permute-start.20) | collective-permute-done | bytes 262176 | tf_op jit(solution)/shard_map/ppermute | solution.py:21
  74.9 3.5 %shard_map.113.a_ref = bf16[256,512]{1,0:T(8,128)(2,1)S(1)} custom-call(s32[5]{0:T(128)S(1)} %stack.23.pos_ref, bf16[256,512]{1,0:T(8,128)(2,1)S(1)} %collective-permute-done.11.x_ref, f32[16,256]{1,0:T(8,128)S(1)} %collective-permute-done.12.w_ref, bf16[1,512,768]{2,1,0:T(8,128)(2,1)S(1)} %get-tuple-element.23.g0_ref, ...), custom_call_target="tpu_custom_call" | custom-call | flops 2415919104 | bytes 9437184 | tf_op jit(solution)/shard_map/pallas_call | solution.py:38
  78.5 0.6 collective-permute-start.10
  79.1 1.0 %collective-permute-start.16 = (bf16[256,512]{1,0:T(8,128)(2,1)S(1)}, bf16[256,512]{1,0:T(8,128)(2,1)S(1)}, u32[]{:S(2)}, u32[]{:S(2)}) collective-permute-start(bf16[256,512]{1,0:T(8,128)(2,1)S(1)} %shard_map.115), channel_id=1, source_target_pairs={{0,8},{4,12},{8,0},{12,4},{1,9},{5,13},{9,1},{13,5},{2,10},{6,14},... | collective-permute-start | bytes 786440 | tf_op jit(solution)/shard_map/ppermute | solution.py:21
  80.1 0.1 collective-permute-done.10.refs_1_
  80.2 7.2 %collective-permute-done.16.refs_2_ = bf16[256,512]{1,0:T(8,128)(2,1)S(1)} collective-permute-done((bf16[256,512]{1,0:T(8,128)(2,1)S(1)}, bf16[256,512]{1,0:T(8,128)(2,1)S(1)}, u32[]{:S(2)}, u32[]{:S(2)}) %collective-permute-start.16) | collective-permute-done | bytes 262176 | tf_op jit(solution)/shard_map/ppermute | solution.py:21
  87.4 2.5 %shard_map.117 = bf16[256,2048]{1,0:T(8,128)(2,1)} custom-call(s32[5]{0:T(128)S(1)} %stack.23.pos_ref, bf16[256,512]{1,0:T(8,128)(2,1)S(1)} %get-tuple-element.26.refs_0_, bf16[256,512]{1,0:T(8,128)(2,1)S(1)} %collective-permute-done.10.refs_1_, bf16[256,512]{1,0:T(8,128)(2,1)S(1)} %collective-permute-done.16.refs_2_, ...), custom_call_target="tpu_custom_call" | custom-call | flops 536870912 | bytes 2097152 | tf_op jit(solution)/shard_map/pallas_call | solution.py:38
  (40 shorter events, 0.2 us)
Async XLA Ops:
  0.1 1.9 %copy-start = (bf16[4,512,768]{2,1,0:T(8,128)(2,1)S(1)}, bf16[4,512,768]{2,1,0:T(8,128)(2,1)}, u32[]{:S(2)}) copy-start(bf16[4,512,768]{2,1,0:T(8,128)(2,1)} %g_ref.3) | copy-start | bytes 9437188
  2.0 1.9 %copy-start.2 = (bf16[4,512,768]{2,1,0:T(8,128)(2,1)S(1)}, bf16[4,512,768]{2,1,0:T(8,128)(2,1)}, u32[]{:S(2)}) copy-start(bf16[4,512,768]{2,1,0:T(8,128)(2,1)} %u_ref.3) | copy-start | bytes 9437188
  3.9 1.9 %copy-start.4 = (bf16[4,768,512]{2,1,0:T(8,128)(2,1)S(1)}, bf16[4,768,512]{2,1,0:T(8,128)(2,1)}, u32[]{:S(2)}) copy-start(bf16[4,768,512]{2,1,0:T(8,128)(2,1)} %d_ref.3) | copy-start | bytes 9437188
  5.8 1.2 %copy-start.6 = (bf16[256,2048]{1,0:T(8,128)(2,1)S(1)}, bf16[256,2048]{1,0:T(8,128)(2,1)}, u32[]{:S(2)}) copy-start(bf16[256,2048]{1,0:T(8,128)(2,1)} %tok_ref.1) | copy-start | bytes 3145732
  7.0 0.8 copy-start.9
  7.8 0.7 copy-start.10
  8.5 0.7 copy-start.11
  9.2 0.7 copy-start.12
  9.9 0.7 copy-start.13
  10.6 2.6 %copy-start.8 = (bf16[128,512]{1,0:T(8,128)(2,1)S(1)}, bf16[128,512]{1,0:T(8,128)(2,1)}, u32[]{:S(2)}) copy-start(bf16[128,512]{1,0:T(8,128)(2,1)} %refs_0_.2) | copy-start | bytes 393220
  10.6 40.7 %copy-start.3 = (bf16[4,512,768]{2,1,0:T(8,128)(2,1)S(1)}, bf16[4,512,768]{2,1,0:T(8,128)(2,1)}, u32[]{:S(2)}) copy-start(bf16[4,512,768]{2,1,0:T(8,128)(2,1)} %u_ref.3) | copy-start | bytes 9437188
  10.6 40.7 %copy-start.5 = (bf16[4,768,512]{2,1,0:T(8,128)(2,1)S(1)}, bf16[4,768,512]{2,1,0:T(8,128)(2,1)}, u32[]{:S(2)}) copy-start(bf16[4,768,512]{2,1,0:T(8,128)(2,1)} %d_ref.3) | copy-start | bytes 9437188
  13.1 24.3 %copy-start.7 = (bf16[128,512]{1,0:T(8,128)(2,1)S(1)}, bf16[128,512]{1,0:T(8,128)(2,1)}, u32[]{:S(2)}) copy-start(bf16[128,512]{1,0:T(8,128)(2,1)} %refs_0_.3) | copy-start | bytes 393220
  13.1 38.3 %copy-start.1 = (bf16[4,512,768]{2,1,0:T(8,128)(2,1)S(1)}, bf16[4,512,768]{2,1,0:T(8,128)(2,1)}, u32[]{:S(2)}) copy-start(bf16[4,512,768]{2,1,0:T(8,128)(2,1)} %g_ref.3) | copy-start | bytes 9437188
  13.1 18.5 %collective-permute-start = (bf16[256,1024]{1,0:T(8,128)(2,1)S(1)}, bf16[256,1024]{1,0:T(8,128)(2,1)S(1)}, u32[]{:S(2)}, u32[]{:S(2)}) collective-permute-start(bf16[256,1024]{1,0:T(8,128)(2,1)S(1)} %get-tuple-element.19), channel_id=1, source_target_pairs={{0,4},{4,0},{8,12},{12,8},{1,5},{5,1},{9,13},{13,9},{2,6},{6,2},{1... | collective-permute-start | bytes 1572872 | tf_op jit(solution)/shard_map/ppermute | solution.py:21
  13.2 6.4 %collective-permute-start.1 = (bf16[128,512]{1,0:T(8,128)(2,1)S(1)}, bf16[128,512]{1,0:T(8,128)(2,1)S(1)}, u32[]{:S(2)}, u32[]{:S(2)}) collective-permute-start(bf16[128,512]{1,0:T(8,128)(2,1)S(1)} %copy-done.8), channel_id=1, source_target_pairs={{0,1},{1,0},{2,3},{3,2},{4,5},{5,4},{6,7},{7,6},{8,9},{9,8},{10,11... | collective-permute-start | bytes 393224 | tf_op jit(solution)/shard_map/ppermute | solution.py:21
  13.2 9.7 %collective-permute-start.2 = (bf16[128,512]{1,0:T(8,128)(2,1)S(1)}, bf16[128,512]{1,0:T(8,128)(2,1)S(1)}, u32[]{:S(2)}, u32[]{:S(2)}) collective-permute-start(bf16[128,512]{1,0:T(8,128)(2,1)S(1)} %copy-done.8), channel_id=1, source_target_pairs={{0,2},{1,3},{2,0},{3,1},{16,19},{17,18},{18,17},{19,16},{4,6},{5,7... | collective-permute-start | bytes 393224 | tf_op jit(solution)/shard_map/ppermute | solution.py:31
  16.3 9.7 %collective-permute-start.3 = (bf16[128,512]{1,0:T(8,128)(2,1)S(1)}, bf16[128,512]{1,0:T(8,128)(2,1)S(1)}, u32[]{:S(2)}, u32[]{:S(2)}) collective-permute-start(bf16[128,512]{1,0:T(8,128)(2,1)S(1)} %copy-done.8), channel_id=1, source_target_pairs={{0,8},{4,12},{8,0},{12,4},{1,9},{5,13},{9,1},{13,5},{2,10},{6,14},... | collective-permute-start | bytes 393224 | tf_op jit(solution)/shard_map/ppermute | solution.py:21
  19.6 6.9 %collective-permute-start.4 = (bf16[128,512]{1,0:T(8,128)(2,1)S(1)}, bf16[128,512]{1,0:T(8,128)(2,1)S(1)}, u32[]{:S(2)}, u32[]{:S(2)}) collective-permute-start(bf16[128,512]{1,0:T(8,128)(2,1)S(1)} %collective-permute-done.1.refs_1_), channel_id=1, source_target_pairs={{0,8},{4,12},{8,0},{12,4},{1,9},{5,13},{9,1},{13,5},{2,10},{6,14},... | collective-permute-start | bytes 393224 | tf_op jit(solution)/shard_map/ppermute | solution.py:21
  23.0 7.2 %collective-permute-start.5 = (bf16[128,512]{1,0:T(8,128)(2,1)S(1)}, bf16[128,512]{1,0:T(8,128)(2,1)S(1)}, u32[]{:S(2)}, u32[]{:S(2)}) collective-permute-start(bf16[128,512]{1,0:T(8,128)(2,1)S(1)} %collective-permute-done.2.refs_2_), channel_id=1, source_target_pairs={{0,24},{4,28},{8,16},{12,20},{16,8},{20,12},{24,0},{28,4},{1,25},{... | collective-permute-start | bytes 393224 | tf_op jit(solution)/shard_map/ppermute | solution.py:31
  25.4 5.2 %collective-permute-start.6 = (bf16[128,512]{1,0:T(8,128)(2,1)S(1)}, bf16[128,512]{1,0:T(8,128)(2,1)S(1)}, u32[]{:S(2)}, u32[]{:S(2)}) collective-permute-start(bf16[128,512]{1,0:T(8,128)(2,1)S(1)} %collective-permute-done.2.refs_2_), channel_id=1, source_target_pairs={{0,8},{4,12},{8,0},{12,4},{1,9},{5,13},{9,1},{13,5},{2,10},{6,14},... | collective-permute-start | bytes 393224 | tf_op jit(solution)/shard_map/ppermute | solution.py:21
  26.0 5.6 %collective-permute-start.7 = (bf16[128,512]{1,0:T(8,128)(2,1)S(1)}, bf16[128,512]{1,0:T(8,128)(2,1)S(1)}, u32[]{:S(2)}, u32[]{:S(2)}) collective-permute-start(bf16[128,512]{1,0:T(8,128)(2,1)S(1)} %collective-permute-done.2.refs_2_), channel_id=1, source_target_pairs={{0,16},{16,0},{1,17},{17,1},{2,18},{18,2},{3,19},{19,3},{4,20},{20... | collective-permute-start | bytes 393224 | tf_op jit(solution)/shard_map/ppermute | solution.py:21
  32.9 2.7 %collective-permute-start.8 = (f32[512,512]{1,0:T(8,128)S(1)}, f32[512,512]{1,0:T(8,128)S(1)}, u32[]{:S(2)}, u32[]{:S(2)}) collective-permute-start(f32[512,512]{1,0:T(8,128)S(1)} %shard_map.110.mine_ref), channel_id=1, source_target_pairs={{0,4},{4,0},{8,12},{12,8},{1,5},{5,1},{9,13},{13,9},{2,6},{6,2},{1... | collective-permute-start | bytes 3145736 | tf_op jit(solution)/shard_map/ppermute | solution.py:21
  35.7 15.6 %collective-permute-start.11 = (bf16[256,512]{1,0:T(8,128)(2,1)S(1)}, bf16[256,512]{1,0:T(8,128)(2,1)S(1)}, u32[]{:S(2)}, u32[]{:S(2)}) collective-permute-start(bf16[256,512]{1,0:T(8,128)(2,1)S(1)} %get-tuple-element.20.x0_ref), channel_id=1, source_target_pairs={{0,8},{4,12},{8,0},{12,4},{1,9},{5,13},{9,1},{13,5},{2,10},{6,14},... | collective-permute-start | bytes 786440 | tf_op jit(solution)/shard_map/ppermute | solution.py:21
  37.3 10.0 %collective-permute-start.17 = (bf16[128,512]{1,0:T(8,128)(2,1)S(1)}, bf16[128,512]{1,0:T(8,128)(2,1)S(1)}, u32[]{:S(2)}, u32[]{:S(2)}) collective-permute-start(bf16[128,512]{1,0:T(8,128)(2,1)S(1)} %copy-done.7), channel_id=1, source_target_pairs={{0,8},{4,12},{8,0},{12,4},{1,9},{5,13},{9,1},{13,5},{2,10},{6,14},... | collective-permute-start | bytes 393224 | tf_op jit(solution)/shard_map/ppermute | solution.py:21
  37.8 9.5 %collective-permute-start.12 = (f32[16,256]{1,0:T(8,128)S(1)}, f32[16,256]{1,0:T(8,128)S(1)}, u32[]{:S(2)}, u32[]{:S(2)}) collective-permute-start(f32[16,256]{1,0:T(8,128)S(1)} %get-tuple-element.22.w0_ref), channel_id=1, source_target_pairs={{0,8},{4,12},{8,0},{12,4},{1,9},{5,13},{9,1},{13,5},{2,10},{6,14},... | collective-permute-start | bytes 49160 | tf_op jit(solution)/shard_map/ppermute | solution.py:21
  39.4 11.5 %collective-permute-start.9 = (f32[16,256]{1,0:T(8,128)S(1)}, f32[16,256]{1,0:T(8,128)S(1)}, u32[]{:S(2)}, u32[]{:S(2)}) collective-permute-start(f32[16,256]{1,0:T(8,128)S(1)} %get-tuple-element.22.w0_ref), channel_id=1, source_target_pairs={{0,4},{4,0},{8,12},{12,8},{1,5},{5,1},{9,13},{13,9},{2,6},{6,2},{1... | collective-permute-start | bytes 49160 | tf_op jit(solution)/shard_map/ppermute | solution.py:21
  47.3 11.4 %collective-permute-start.14 = (f32[16,256]{1,0:T(8,128)S(1)}, f32[16,256]{1,0:T(8,128)S(1)}, u32[]{:S(2)}, u32[]{:S(2)}) collective-permute-start(f32[16,256]{1,0:T(8,128)S(1)} %collective-permute-done.12.w_ref), channel_id=1, source_target_pairs={{0,4},{4,0},{8,12},{12,8},{1,5},{5,1},{9,13},{13,9},{2,6},{6,2},{1... | collective-permute-start | bytes 49160 | tf_op jit(solution)/shard_map/ppermute | solution.py:21
  47.4 15.6 %collective-permute-start.18 = (bf16[256,512]{1,0:T(8,128)(2,1)S(1)}, bf16[256,512]{1,0:T(8,128)(2,1)S(1)}, u32[]{:S(2)}, u32[]{:S(2)}) collective-permute-start(bf16[256,512]{1,0:T(8,128)(2,1)S(1)} %shard_map.116.refs_3_), channel_id=1, source_target_pairs={{0,1},{1,0},{2,3},{3,2},{4,5},{5,4},{6,7},{7,6},{8,9},{9,8},{10,11... | collective-permute-start | bytes 786440 | tf_op jit(solution)/shard_map/ppermute | solution.py:21
  49.0 19.8 %collective-permute-start.19 = (bf16[256,512]{1,0:T(8,128)(2,1)S(1)}, bf16[256,512]{1,0:T(8,128)(2,1)S(1)}, u32[]{:S(2)}, u32[]{:S(2)}) collective-permute-start(bf16[256,512]{1,0:T(8,128)(2,1)S(1)} %shard_map.116.refs_3_), channel_id=1, source_target_pairs={{0,2},{1,3},{2,0},{3,1},{4,6},{5,7},{6,4},{7,5},{8,10},{9,11},{10,... | collective-permute-start | bytes 786440 | tf_op jit(solution)/shard_map/ppermute | solution.py:21
  50.9 24.1 %collective-permute-start.20 = (bf16[256,512]{1,0:T(8,128)(2,1)S(1)}, bf16[256,512]{1,0:T(8,128)(2,1)S(1)}, u32[]{:S(2)}, u32[]{:S(2)}) collective-permute-start(bf16[256,512]{1,0:T(8,128)(2,1)S(1)} %shard_map.116.refs_3_), channel_id=1, source_target_pairs={{0,3},{1,2},{2,1},{3,0},{4,7},{5,6},{6,5},{7,4},{8,11},{9,10},{10,... | collective-permute-start | bytes 786440 | tf_op jit(solution)/shard_map/ppermute | solution.py:21
  51.4 7.4 %collective-permute-start.13 = (bf16[256,512]{1,0:T(8,128)(2,1)S(1)}, bf16[256,512]{1,0:T(8,128)(2,1)S(1)}, u32[]{:S(2)}, u32[]{:S(2)}) collective-permute-start(bf16[256,512]{1,0:T(8,128)(2,1)S(1)} %collective-permute-done.11.x_ref), channel_id=1, source_target_pairs={{0,4},{4,0},{8,12},{12,8},{1,5},{5,1},{9,13},{13,9},{2,6},{6,2},{1... | collective-permute-start | bytes 786440 | tf_op jit(solution)/shard_map/ppermute | solution.py:21
  62.3 16.2 %collective-permute-start.15 = (bf16[256,512]{1,0:T(8,128)(2,1)S(1)}, bf16[256,512]{1,0:T(8,128)(2,1)S(1)}, u32[]{:S(2)}, u32[]{:S(2)}) collective-permute-start(bf16[256,512]{1,0:T(8,128)(2,1)S(1)} %shard_map.114), channel_id=1, source_target_pairs={{0,4},{4,0},{8,12},{12,8},{1,5},{5,1},{9,13},{13,9},{2,6},{6,2},{1... | collective-permute-start | bytes 786440 | tf_op jit(solution)/shard_map/ppermute | solution.py:21
  62.9 16.2 %collective-permute-start.21 = (bf16[256,512]{1,0:T(8,128)(2,1)S(1)}, bf16[256,512]{1,0:T(8,128)(2,1)S(1)}, u32[]{:S(2)}, u32[]{:S(2)}) collective-permute-start(bf16[256,512]{1,0:T(8,128)(2,1)S(1)} %shard_map.116.refs_3_), channel_id=1, source_target_pairs={{0,4},{4,0},{8,12},{12,8},{1,5},{5,1},{9,13},{13,9},{2,6},{6,2},{1... | collective-permute-start | bytes 786440 | tf_op jit(solution)/shard_map/ppermute | solution.py:21
  62.9 17.1 %collective-permute-start.22 = (bf16[256,512]{1,0:T(8,128)(2,1)S(1)}, bf16[256,512]{1,0:T(8,128)(2,1)S(1)}, u32[]{:S(2)}, u32[]{:S(2)}) collective-permute-start(bf16[256,512]{1,0:T(8,128)(2,1)S(1)} %collective-permute-done.18.refs_4_), channel_id=1, source_target_pairs={{0,4},{4,0},{8,12},{12,8},{1,5},{5,1},{9,13},{13,9},{2,6},{6,2},{1... | collective-permute-start | bytes 786440 | tf_op jit(solution)/shard_map/ppermute | solution.py:21
  68.8 11.3 %collective-permute-start.23 = (bf16[256,512]{1,0:T(8,128)(2,1)S(1)}, bf16[256,512]{1,0:T(8,128)(2,1)S(1)}, u32[]{:S(2)}, u32[]{:S(2)}) collective-permute-start(bf16[256,512]{1,0:T(8,128)(2,1)S(1)} %collective-permute-done.19.refs_5_), channel_id=1, source_target_pairs={{0,4},{4,0},{8,12},{12,8},{1,5},{5,1},{9,13},{13,9},{2,6},{6,2},{1... | collective-permute-start | bytes 786440 | tf_op jit(solution)/shard_map/ppermute | solution.py:21
  74.9 5.2 %collective-permute-start.24 = (bf16[256,512]{1,0:T(8,128)(2,1)S(1)}, bf16[256,512]{1,0:T(8,128)(2,1)S(1)}, u32[]{:S(2)}, u32[]{:S(2)}) collective-permute-start(bf16[256,512]{1,0:T(8,128)(2,1)S(1)} %collective-permute-done.20.refs_6_), channel_id=1, source_target_pairs={{0,4},{4,0},{8,12},{12,8},{1,5},{5,1},{9,13},{13,9},{2,6},{6,2},{1... | collective-permute-start | bytes 786440 | tf_op jit(solution)/shard_map/ppermute | solution.py:21
  78.5 1.7 %collective-permute-start.10 = (bf16[256,512]{1,0:T(8,128)(2,1)S(1)}, bf16[256,512]{1,0:T(8,128)(2,1)S(1)}, u32[]{:S(2)}, u32[]{:S(2)}) collective-permute-start(bf16[256,512]{1,0:T(8,128)(2,1)S(1)} %get-tuple-element.27), channel_id=1, source_target_pairs={{0,4},{4,0},{8,12},{12,8},{1,5},{5,1},{9,13},{13,9},{2,6},{6,2},{1... | collective-permute-start | bytes 786440 | tf_op jit(solution)/shard_map/ppermute | solution.py:21
  79.1 8.3 %collective-permute-start.16 = (bf16[256,512]{1,0:T(8,128)(2,1)S(1)}, bf16[256,512]{1,0:T(8,128)(2,1)S(1)}, u32[]{:S(2)}, u32[]{:S(2)}) collective-permute-start(bf16[256,512]{1,0:T(8,128)(2,1)S(1)} %shard_map.115), channel_id=1, source_target_pairs={{0,8},{4,12},{8,0},{12,4},{1,9},{5,13},{9,1},{13,5},{2,10},{6,14},... | collective-permute-start | bytes 786440 | tf_op jit(solution)/shard_map/ppermute | solution.py:21
where the time goes:
time: 90.4 us; the launch traced here: 89.9 us
  waiting for transfers between devices  38.4 us (42%)
  Pallas kernels  20.8 us (23%)
  starting transfers between devices  19.9 us (22%)
  local copies, waits for them, and re-layouts  10.6 us (12%)
    ppermute x23, waiting for transfers between devices, swap(): return lax.ppermute(x, axis, [(i, i ^ bits) for i in range(size)])  32.7 us
    pallas_call x9, Pallas kernels, kernel(): pl.pallas_call(body, out_shape=out_shape, in_specs=specs, out_specs=out_s...  20.8 us
    ppermute x23, starting transfers between devices, swap(): return lax.ppermute(x, axis, [(i, i ^ bits) for i in range(size)])  14.4 us
    unnamed x28, local copies, waits for them, and re-layouts  10.5 us
    ppermute x2, waiting for transfers between devices, swap_pair(): return lax.ppermute(x, axes, pairs)  5.65 us
    ppermute x2, starting transfers between devices, swap_pair(): return lax.ppermute(x, axes, pairs)  5.49 us
  transfers between devices with their start and end apart: 25, of which 11 were waited for; matrix products, arithmetic and copies ran while one was open for 0% of the time, Pallas kernels for 16%

commit v1 on v0

v1 whole, which is shorter than its diff:
```python
import functools

import jax
import jax.numpy as jnp
from jax import lax
from jax.experimental import pallas as pl
from jax.experimental.pallas import tpu as pltpu
from jax.sharding import PartitionSpec as P

epsilon = 1e-06
F32 = jnp.float32
BF16 = jnp.bfloat16

VM = pl.BlockSpec(memory_space=pltpu.VMEM)
SM = pl.BlockSpec(memory_space=pltpu.SMEM)
AN = pl.BlockSpec(memory_space=pl.ANY)


def in_hbm(x):
    return pltpu.with_memory_space_constraint(x, pltpu.HBM)


def swap(x, axis, bits):
    size = lax.axis_size(axis)
    return lax.ppermute(x, axis, [(i, i ^ bits) for i in range(size)])


def swap_pair(x, axes, move):
    sizes = [lax.axis_size(axis) for axis in axes]
    pairs = []
    for i in range(sizes[0]):
        for j in range(sizes[1]):
            p, q = move(i, j)
            pairs.append((i * sizes[1] + j, p * sizes[1] + q))
    return lax.ppermute(x, axes, pairs)


def kernel(body, out_shape, operands, specs, mib, flops=0, nbytes=0, scratch=(), out_specs=None):
    many = isinstance(out_shape, tuple)
    if out_specs is None:
        out_specs = (VM,) * len(out_shape) if many else VM
    return pl.pallas_call(
        body,
        out_shape=out_shape,
        in_specs=specs,
        out_specs=out_specs,
        scratch_shapes=list(scratch),
        compiler_params=pltpu.CompilerParams(vmem_limit_bytes=mib * 1024 * 1024),
        cost_estimate=pl.CostEstimate(flops=flops, bytes_accessed=nbytes, transcendentals=0),
    )(*operands)


def gate_kernel(top, wide, pos_ref, list_ref, tok_hbm, gain_hbm, router_hbm, ids_hbm, slot_hbm,
                keep_ref, send_ref, wt_ref, normed_ref, tok_ref, gain_ref, router_ref, ids_ref,
                slot_ref, sem):
    pairs = ((tok_hbm, tok_ref), (gain_hbm, gain_ref), (router_hbm, router_ref),
             (ids_hbm, ids_ref), (slot_hbm, slot_ref))
    copies = [pltpu.make_async_copy(src, dst, sem.at[i]) for i, (src, dst) in enumerate(pairs)]
    for copy in copies:
        copy.start()
    for copy in copies:
        copy.wait()
    values = tok_ref[...].astype(F32)
    scale = lax.rsqrt(jnp.mean(values * values, axis=-1, keepdims=True) + epsilon)
    normed = (values * scale * gain_ref[...]).astype(BF16)
    normed_ref[...] = normed
    core = pos_ref[0]
    for h in range(keep_ref.shape[1] // wide):
        mine = pl.multiple_of((2 * h + core) * wide, wide)
        other = pl.multiple_of((2 * h + 1 - core) * wide, wide)
        keep_ref[:, h * wide:(h + 1) * wide] = normed_ref[:, pl.ds(mine, wide)]
        send_ref[:, h * wide:(h + 1) * wide] = normed_ref[:, pl.ds(other, wide)]
    logits = lax.dot_general(router_ref[...], normed_ref[...], (((1,), (1,)), ((), ())),
                             preferred_element_type=F32)
    sig = jax.nn.sigmoid(logits)
    experts, rows = sig.shape
    sub = lax.broadcasted_iota(jnp.int32, (experts, rows), 0)
    lane = lax.broadcasted_iota(jnp.int32, (experts, rows), 1)
    total = jnp.zeros((experts, rows), F32)
    served = jnp.zeros((experts, rows), F32)
    for k in range(top):
        hit = sub == ids_ref[k:k + 1, :]
        total = total + jnp.where(hit, 1.0, 0.0)
        served = served + jnp.where(hit & (slot_ref[k:k + 1, :] >= 0), 1.0, 0.0)
    _, shards, copies_n, local = list_ref.shape

    def listed(i, served):
        shard, copy = i // copies_n, i % copies_n
        for m in range(local):
            entry = list_ref[0, shard, copy, m]
            owner = jnp.where(entry >= 0, entry, -top) // top
            served = served + jnp.where((lane == owner) & (sub == shard * local + m), 1.0, 0.0)
        return served

    served = lax.fori_loop(0, shards * copies_n, listed, served)
    denom = jnp.sum(total * sig, axis=0, keepdims=True)
    wt_ref[...] = jnp.where(served > 0.0, sig / denom, 0.0)


def latent_kernel(chunks, wide, pos_ref, keep_ref, recv_ref, wt_ref, *refs):
    w_refs, (out_ref, x_ref, w_ref, sem) = refs[:-4], refs[-4:]
    half, rep, group = pos_ref[1], pos_ref[2], pos_ref[4]
    rows = keep_ref.shape[0]
    depth = w_refs[0].shape[0]
    load = pltpu.make_async_copy(w_refs[0], w_ref.at[pl.ds(0, depth)], sem)
    load.start()
    for i, ((a, b), chunk) in enumerate(zip(chunks, w_refs)):
        if b == "A":
            b = 2 + group
        elif b == "B":
            b = 3 - group
        at = pl.multiple_of((half ^ a) * wide + (rep ^ b) * depth, depth)
        x_ref[:rows, i * depth:(i + 1) * depth] = keep_ref[:, pl.ds(at, depth)]
        x_ref[rows:, i * depth:(i + 1) * depth] = recv_ref[:, pl.ds(at, depth)]
        if i:
            w_ref[i * depth:(i + 1) * depth, :] = chunk[...]
    load.wait()
    out_ref[:2 * rows, :] = jnp.dot(x_ref[...], w_ref[...], preferred_element_type=F32)
    out_ref[2 * rows:, :rows] = wt_ref[...]
    out_ref[2 * rows:, rows:] = jnp.zeros_like(out_ref[2 * rows:, rows:])


def finish_kernel(mine_ref, recv_ref, own_ref, core_ref):
    rows = (own_ref.shape[1]) // 2
    own_ref[:rows, :] = (mine_ref[:rows, :] + recv_ref[rows:2 * rows, :]).astype(BF16)
    core_ref[:rows, :] = (mine_ref[rows:2 * rows, :] + recv_ref[:rows, :]).astype(BF16)
    for src, dst in ((mine_ref, own_ref), (recv_ref, core_ref)):
        wt = src[2 * rows:, :rows]
        lead = wt.astype(BF16)
        dst[rows:, :rows] = lead
        dst[rows:, rows:] = (wt - lead.astype(F32)).astype(BF16)


def expert(x, weight, gate_w, up_w, down_w):
    gate = jnp.dot(x, gate_w, preferred_element_type=F32)
    upper = jnp.dot(x, up_w, preferred_element_type=F32)
    half = 0.5 * gate
    hidden = ((half + half * jnp.tanh(half)) * upper).astype(BF16)
    result = jnp.dot(hidden, down_w, preferred_element_type=F32).astype(BF16)
    return result.astype(F32) * weight


def columns(me, local, pay_ref, at, size):
    rows = pay_ref.shape[1] // 2
    wt = (pay_ref[rows:, at:at + size].astype(F32)
          + pay_ref[rows:, rows + at:rows + at + size].astype(F32))
    sub = lax.broadcasted_iota(jnp.int32, wt.shape, 0)
    picked = [jnp.sum(jnp.where(sub == me * local + j, wt, 0.0), axis=0, keepdims=True)
              for j in range(local)]
    pad = jnp.zeros((-local % 8, size), F32)
    return jnp.concatenate(picked + [pad], axis=0).T


def near_kernel(local, held, pos_ref, x0_ref, x1_ref, g_ref, u_ref, d_hbm, o0_ref, o1_ref, d_ref,
                acc_ref, sem):
    loads = [pltpu.make_async_copy(d_hbm.at[pl.ds(j, 1)], d_ref.at[pl.ds(j, 1)], sem.at[j])
             for j in range(local)]
    for load in loads:
        load.start()
    rows = o0_ref.shape[0]
    cols = [columns(pos_ref[3], local, p, 0, rows) for p in (x0_ref, x1_ref)]
    for j in range(local):
        loads[j].wait()
        weights = g_ref[j], u_ref[j], d_ref[j]
        part = expert(x1_ref[:rows, :], cols[1][:, j:j + 1], *weights)
        acc_ref[...] = part if j == 0 else acc_ref[...] + part
        if j < local - held:
            part = expert(x0_ref[:rows, :], cols[0][:, j:j + 1], *weights)
            o0_ref[...] = part if j == 0 else o0_ref[...] + part
    o1_ref[...] = acc_ref[...].astype(BF16)


def rest_kernel(local, held, pos_ref, x_ref, a_ref, g_ref, u_ref, d_ref, o_ref):
    rows = o_ref.shape[0]
    cols = columns(pos_ref[3], local, x_ref, 0, rows)
    o_ref[...] = a_ref[...]
    for j in range(local - held, local):
        o_ref[...] += expert(x_ref[:rows, :], cols[:, j:j + 1], g_ref[j], u_ref[j], d_ref[j])


def far_kernel(local, at, pos_ref, x0_ref, x1_ref, g_ref, u_ref, d_ref, o0_ref, o1_ref, x_ref, acc_ref):
    size = o0_ref.shape[0]
    x_ref[:size, :] = x0_ref[at:at + size, :]
    x_ref[size:, :] = x1_ref[at:at + size, :]
    cols = jnp.concatenate([columns(pos_ref[3], local, p, at, size) for p in (x0_ref, x1_ref)], axis=0)
    for j in range(local):
        part = expert(x_ref[...], cols[:, j:j + 1], g_ref[j], u_ref[j], d_ref[j])
        acc_ref[...] = part if j == 0 else acc_ref[...] + part
    o0_ref[...] = acc_ref[:size, :].astype(BF16)
    o1_ref[...] = acc_ref[size:, :].astype(BF16)


def add_kernel(a_ref, b_ref, o_ref):
    o_ref[...] = (a_ref[...].astype(F32) + b_ref[...].astype(F32)).astype(BF16)


def join_kernel(own_ref, *refs):
    x_refs, (out_ref, held_ref, sem) = refs[:-3], refs[-3:]
    depth = own_ref.shape[0]
    load = pltpu.make_async_copy(own_ref, held_ref, sem)
    load.start()
    for i, x_ref in enumerate(x_refs):
        out_ref[:, (i + 1) * depth:(i + 2) * depth] = x_ref[...].T
    load.wait()
    out_ref[:, :depth] = held_ref[...].T


def final_kernel(n_sum, parts, chunks, copies, depth, pos_ref, *refs):
    out_ref, block_ref, sem = refs[-3:]
    half, rep, core = pos_ref[1], pos_ref[2], pos_ref[0]
    total = refs[0][...].astype(F32)
    for s_ref in refs[1:n_sum]:
        total = total + s_ref[...].astype(F32)
    back = refs[n_sum:n_sum + parts]
    total = total + jnp.concatenate([s_ref[...].astype(F32) for s_ref in back], axis=0)
    merged = total.astype(BF16)
    outs = []
    for i, ((c, b), w_ref) in enumerate(zip(chunks, refs[n_sum + parts:-3])):
        block_ref[i] = jnp.dot(merged, w_ref[...], preferred_element_type=F32).astype(BF16)
        for a in range(w_ref.shape[1] // depth):
            e = 2 * (half ^ a) + (core ^ c)
            at = pl.multiple_of((e * copies + (rep ^ b)) * depth, depth)
            outs.append(pltpu.make_async_copy(block_ref.at[i, :, pl.ds(a * depth, depth)],
                                              out_ref.at[:, pl.ds(at, depth)], sem.at[i, a]))
            outs[-1].start()
    for out in outs:
        out.wait()


def shape(dims, dtype=BF16):
    return jax.ShapeDtypeStruct(dims, dtype)


def on_device(tokens, norm_gain, router, down_proj, up_proj, expert_gate, expert_up, expert_down,
              expert_ids, slot_pos, overflow_list):
    rows, width = tokens.shape
    top = expert_ids.shape[1]
    local, _, ff = expert_gate.shape
    depth, latent = down_proj.shape
    groups = lax.axis_size("groups")
    shards = lax.axis_size("expert")
    copies = lax.axis_size("replica")
    chips = shards // 2
    wide = copies * depth
    spread = copies
    if depth % 128:
        down_proj = lax.all_gather(down_proj, "replica", axis=0, tiled=True)
        up_proj = lax.all_gather(up_proj, "replica", axis=0, tiled=True)
        depth, spread = wide, 1
    experts = shards * local
    g = lax.axis_index("groups")
    e = lax.axis_index("expert")
    r = lax.axis_index("replica")
    pos = jnp.stack([e % 2, e // 2, r if spread > 1 else 0 * r, e, g]).astype(jnp.int32)

    down = {(0, 0): down_proj}
    if spread == groups + 2 and groups == 2:
        near_z = swap(down_proj, "replica", 1)
        far_z = swap_pair(down_proj, ("groups", "replica"), lambda i, j: (i, j ^ (2 + i)))
        down[(0, 1)] = near_z
        down[(0, "A")] = far_z
        for a in range(1, chips):
            down[(a, 0)] = swap(down_proj, "expert", 2 * a)
        ups_x = [swap(up_proj, "expert", 2 * a) for a in range(1, chips)]
        for a in range(1, chips):
            down[(a, 1)] = swap(near_z, "expert", 2 * a)
            down[(a, "B")] = swap_pair(far_z, ("groups", "expert"),
                                       lambda i, j: (i ^ 1, j ^ (2 * a)))
            down[(a, "A")] = swap(far_z, "expert", 2 * a)
        down[(0, "B")] = swap(far_z, "groups", 1)
    else:
        for b in range(1, spread):
            down[(0, b)] = swap(down_proj, "replica", b)
        for b in range(spread):
            for a in range(1, chips):
                down[(a, b)] = swap(down[(0, b)], "expert", 2 * a)
        ups_x = [swap(up_proj, "expert", 2 * a) for a in range(1, chips)]

    keep, send, wt = kernel(
        functools.partial(gate_kernel, top, wide),
        (shape((rows, width // 2)), shape((rows, width // 2)), shape((experts, rows), F32)),
        (pos, overflow_list, *map(in_hbm, (
            tokens, norm_gain.reshape(1, width), router.T, expert_ids.T, slot_pos.T))),
        [SM, SM] + [AN] * 5, 20, 4 * rows * width * experts, 4 * rows * width,
        [pltpu.VMEM((rows, width), BF16), pltpu.VMEM((rows, width), BF16), pltpu.VMEM((1, width), F32),
         pltpu.VMEM((experts, width), BF16), pltpu.VMEM((top, rows), jnp.int32),
         pltpu.VMEM((top, rows), jnp.int32), pltpu.SemaphoreType.DMA((5,))])
    recv = swap(send, "expert", 1)

    order = list(down)
    partial = kernel(
        functools.partial(latent_kernel, order, wide), shape((2 * rows + experts, latent), F32),
        (pos, keep, recv, wt, in_hbm(down_proj), *[down[k] for k in order[1:]]),
        [SM] + [VM] * 3 + [AN] + [VM] * (len(order) - 1), 14, 2 * rows * width * latent, 2 * width * latent,
        [pltpu.VMEM((2 * rows, width // 2), BF16), pltpu.VMEM((width // 2, latent), BF16),
         pltpu.SemaphoreType.DMA])
    partial_core = swap(partial, "expert", 1)
    own, core = kernel(
        finish_kernel, (shape((rows + experts, latent)),) * 2, (partial, partial_core), [VM, VM],
        6, 2 * rows * latent, 12 * rows * latent)

    work = 6 * rows * latent * ff
    load = 6 * latent * ff
    held = 1
    far = []
    for a in range(1, chips):
        x0 = swap(own, "expert", 2 * a)
        far.append((x0, swap(x0, "expert", 1)))
    near0, near1, kept = kernel(
        functools.partial(near_kernel, local, held),
        (shape((rows, latent), F32), shape((rows, latent)), shape(expert_down.shape)),
        (pos, own, core, expert_gate, expert_up, in_hbm(expert_down)), [SM] + [VM] * 4 + [AN], 20,
        (2 * local - held) * work, local * load,
        [pltpu.VMEM((rows, latent), F32), pltpu.SemaphoreType.DMA((local,))])
    weights = (expert_gate, expert_up, kept)
    near0 = kernel(
        functools.partial(rest_kernel, local, held), shape((rows, latent), F32),
        (pos, own, near0, *weights), [SM] + [VM] * 5, 20, held * work, held * load)
    sums = [near0, swap(near1, "expert", 1)]
    parts = 2
    size = rows // parts
    back = []
    for a in range(1, chips):
        back.append([])
        for h in range(parts):
            o0, o1 = kernel(
                functools.partial(far_kernel, local, h * size), (shape((size, latent)),) * 2,
                (pos, *far[a - 1], *weights), [SM] + [VM] * 5, 20, local * work, local * load,
                [pltpu.VMEM((2 * size, latent), BF16), pltpu.VMEM((2 * size, latent), F32)])
            other = swap(o1, "expert", 1)
            s = kernel(add_kernel, shape((size, latent)), (o0, other), [VM, VM], 4,
                       size * latent, 6 * size * latent)
            back[-1].append(swap(s, "expert", 2 * a))
    for more in back[1:]:
        sums.append(jnp.concatenate(more, axis=0))

    pair = kernel(join_kernel, shape((latent, chips * depth)), (in_hbm(up_proj), *ups_x),
                  [AN] + [VM] * (chips - 1), 4, 0, 4 * chips * depth * latent,
                  [pltpu.VMEM((depth, latent), BF16), pltpu.SemaphoreType.DMA])
    ups = {(0, 0): pair}
    for b in range(1, spread):
        ups[(0, b)] = swap(pair, "replica", b)
    for b in range(spread):
        ups[(1, b)] = swap(ups[(0, b)], "expert", 1)
    order = sorted(ups)
    return kernel(
        functools.partial(final_kernel, len(sums), parts, order, spread, depth),
        shape((rows, width)), (pos, *sums, *back[0], *[ups[k] for k in order]),
        [SM] + [VM] * (len(sums) + parts + len(order)), 14, 2 * rows * width * latent, 2 * width * latent,
        [pltpu.VMEM((len(order), rows, chips * depth), BF16), pltpu.SemaphoreType.DMA((len(order), chips))],
        AN)


def solution(mesh):
    placed = (
        P(("groups", "expert", "replica"), None),
        P(),
        P(),
        P(("expert", "replica"), None),
        P(("expert", "replica"), None),
        P("expert", None, None),
        P("expert", None, None),
        P("expert", None, None),
        P(("groups", "expert", "replica"), None),
        P(("groups", "expert", "replica"), None),
        P(("groups", "expert", "replica"), None, None, None),
    )

    return jax.shard_map(
        on_device,
        mesh=mesh,
        in_specs=placed,
        out_specs=P(("groups", "expert", "replica"), None),
        check_vma=False,
    )
```

time: 90.4 us -> 79.1 us (0.87)
  local copies, waits for them, and re-layouts: 10.6 us -> 0.79 us
  waiting for transfers between devices: 38.4 us -> 33.5 us
  Pallas kernels: 20.8 us -> 24.9 us
    unnamed x28 -> x8, local copies, waits for them, and re-layouts: 10.5 us -> 0.71 us
    ppermute x23 -> x22, waiting for transfers between devices: 32.7 us -> 27.8 us  [swap(): return lax.ppermute(x, axis, [(i, i ^ bits) for i in range(size)])]
    pallas_call x9 -> x11, Pallas kernels: 20.8 us -> 24.9 us  [kernel(): pl.pallas_call(body, out_shape=out_shape, in_specs=specs, out_specs=out_s...]
    ppermute x23 -> x22, starting transfers between devices: 14.4 us -> 14.1 us  [swap(): return lax.ppermute(x, axis, [(i, i ^ bits) for i in range(size)])]
  transfers between devices with their start and end apart: 25 -> 24, of which waited for: 11 -> 11; matrix products, arithmetic and copies ran while one was open for 0% -> 0% of each run, Pallas kernels for 16% -> 21%
where the time goes in v1:
time: 79.1 us; the launch traced here: 78.9 us
  waiting for transfers between devices  33.5 us (42%)
  Pallas kernels  24.9 us (31%)
  starting transfers between devices  19.6 us (25%)
    ppermute x22, waiting for transfers between devices, swap(): return lax.ppermute(x, axis, [(i, i ^ bits) for i in range(size)])  27.8 us
    pallas_call x11, Pallas kernels, kernel(): pl.pallas_call(body, out_shape=out_shape, in_specs=specs, out_specs=out_s...  24.9 us
    ppermute x22, starting transfers between devices, swap(): return lax.ppermute(x, axis, [(i, i ^ bits) for i in range(size)])  14.1 us
    ppermute x2, waiting for transfers between devices, swap_pair(): return lax.ppermute(x, axes, pairs)  5.64 us
    ppermute x2, starting transfers between devices, swap_pair(): return lax.ppermute(x, axes, pairs)  5.52 us
  transfers between devices with their start and end apart: 24, of which 11 were waited for; matrix products, arithmetic and copies ran while one was open for 0% of the time, Pallas kernels for 21%

profile of v1, /device:TPU:8, one launch (start us, length us, event | category | flops | bytes accessed | tf_op | source)
XLA Modules:
  0.0 78.9 jit_solution(1307738483401975754)
XLA Ops:
  0.0 0.1 stack.23.pos_ref
  0.1 0.7 copy-done.2
  0.8 3.9 %shard_map.109 = (bf16[256,1024]{1,0:T(8,128)(2,1)S(1)}, bf16[256,1024]{1,0:T(8,128)(2,1)S(1)}, f32[16,256]{1,0:T(8,128)S(1)}) custom-call(s32[5]{0:T(128)S(1)} %stack.23.pos_ref, s32[1,4,4,4]{3,2,1,0:T(4,128)S(1)} %copy-done.2, bf16[256,2048]{1,0:T(8,128)(2,1)} %tok_hbm.1, f32[1,2048]{1,0:T(1,128)} %bitcast.10, bf16[16,2048]{1,0:T(8,128)(2,1)} %bitcast.9, ...), custom_call_target="tpu_custom_call" | custom-call | flops 33554432 | bytes 2097152 | tf_op jit(solution)/shard_map/pallas_call | solution.py:42
  4.7 0.0 copy-start
  4.7 0.1 collective-permute-start
  4.8 0.1 collective-permute-start.1
  4.9 3.0 %collective-permute-start.2 = (bf16[128,512]{1,0:T(8,128)(2,1)}, bf16[128,512]{1,0:T(8,128)(2,1)S(1)}, u32[]{:S(2)}, u32[]{:S(2)}) collective-permute-start(bf16[128,512]{1,0:T(8,128)(2,1)} %refs_0_.1), channel_id=1, source_target_pairs={{0,2},{1,3},{2,0},{3,1},{16,19},{17,18},{18,17},{19,16},{4,6},{5,7... | collective-permute-start | bytes 393224 | tf_op jit(solution)/shard_map/ppermute | solution.py:35
  7.9 1.5 %collective-permute-start.3 = (bf16[128,512]{1,0:T(8,128)(2,1)}, bf16[128,512]{1,0:T(8,128)(2,1)S(1)}, u32[]{:S(2)}, u32[]{:S(2)}) collective-permute-start(bf16[128,512]{1,0:T(8,128)(2,1)} %refs_0_.1), channel_id=1, source_target_pairs={{0,8},{4,12},{8,0},{12,4},{1,9},{5,13},{9,1},{13,5},{2,10},{6,14},... | collective-permute-start | bytes 393224 | tf_op jit(solution)/shard_map/ppermute | solution.py:25
  9.4 2.0 %collective-permute-done.1.refs_1_ = bf16[128,512]{1,0:T(8,128)(2,1)S(1)} collective-permute-done((bf16[128,512]{1,0:T(8,128)(2,1)}, bf16[128,512]{1,0:T(8,128)(2,1)S(1)}, u32[]{:S(2)}, u32[]{:S(2)}) %collective-permute-start.1) | collective-permute-done | bytes 131104 | tf_op jit(solution)/shard_map/ppermute | solution.py:25
  11.4 1.5 %collective-permute-start.4 = (bf16[128,512]{1,0:T(8,128)(2,1)S(1)}, bf16[128,512]{1,0:T(8,128)(2,1)S(1)}, u32[]{:S(2)}, u32[]{:S(2)}) collective-permute-start(bf16[128,512]{1,0:T(8,128)(2,1)S(1)} %collective-permute-done.1.refs_1_), channel_id=1, source_target_pairs={{0,8},{4,12},{8,0},{12,4},{1,9},{5,13},{9,1},{13,5},{2,10},{6,14},... | collective-permute-start | bytes 393224 | tf_op jit(solution)/shard_map/ppermute | solution.py:25
  12.9 1.9 %collective-permute-done.2.refs_2_ = bf16[128,512]{1,0:T(8,128)(2,1)S(1)} collective-permute-done((bf16[128,512]{1,0:T(8,128)(2,1)}, bf16[128,512]{1,0:T(8,128)(2,1)S(1)}, u32[]{:S(2)}, u32[]{:S(2)}) %collective-permute-start.2) | collective-permute-done | bytes 131104 | tf_op jit(solution)/shard_map/ppermute | solution.py:35
  14.8 2.5 %collective-permute-start.5 = (bf16[128,512]{1,0:T(8,128)(2,1)S(1)}, bf16[128,512]{1,0:T(8,128)(2,1)S(1)}, u32[]{:S(2)}, u32[]{:S(2)}) collective-permute-start(bf16[128,512]{1,0:T(8,128)(2,1)S(1)} %collective-permute-done.2.refs_2_), channel_id=1, source_target_pairs={{0,24},{4,28},{8,16},{12,20},{16,8},{20,12},{24,0},{28,4},{1,25},{... | collective-permute-start | bytes 393224 | tf_op jit(solution)/shard_map/ppermute | solution.py:35
  17.3 0.5 collective-permute-start.6
  17.9 0.0 collective-permute-done.3.refs_3_
  17.9 0.5 collective-permute-start.7
  18.3 3.7 %collective-permute-done.5.refs_5_ = bf16[128,512]{1,0:T(8,128)(2,1)S(1)} collective-permute-done((bf16[128,512]{1,0:T(8,128)(2,1)S(1)}, bf16[128,512]{1,0:T(8,128)(2,1)S(1)}, u32[]{:S(2)}, u32[]{:S(2)}) %collective-permute-start.5) | collective-permute-done | bytes 131104 | tf_op jit(solution)/shard_map/ppermute | solution.py:35
  22.1 0.5 collective-permute-done.6.refs_6_
  22.6 0.9 %collective-permute-done.7.refs_7_ = bf16[128,512]{1,0:T(8,128)(2,1)S(1)} collective-permute-done((bf16[128,512]{1,0:T(8,128)(2,1)S(1)}, bf16[128,512]{1,0:T(8,128)(2,1)S(1)}, u32[]{:S(2)}, u32[]{:S(2)}) %collective-permute-start.7) | collective-permute-done | bytes 131104 | tf_op jit(solution)/shard_map/ppermute | solution.py:25
  23.5 2.2 %shard_map.110.mine_ref = f32[528,512]{1,0:T(8,128)S(1)} custom-call(s32[5]{0:T(128)S(1)} %stack.23.pos_ref, bf16[256,1024]{1,0:T(8,128)(2,1)S(1)} %get-tuple-element.17.keep_ref, bf16[256,1024]{1,0:T(8,128)(2,1)S(1)} %collective-permute-done.recv_ref, f32[16,256]{1,0:T(8,128)S(1)} %get-tuple-element.19.wt_ref, bf16[128,512]{1,0:T(8,128)(2,1)} %refs_0_.1, ...), custom_call_target="tpu_custom_call" | custom-call | flops 536870912 | bytes 2097152 | tf_op jit(solution)/shard_map/pallas_call | solution.py:42
  25.6 0.1 collective-permute-start.8
  25.7 2.7 %collective-permute-done.8.recv_ref = f32[528,512]{1,0:T(8,128)S(1)} collective-permute-done((f32[528,512]{1,0:T(8,128)S(1)}, f32[528,512]{1,0:T(8,128)S(1)}, u32[]{:S(2)}, u32[]{:S(2)}) %collective-permute-start.8) | collective-permute-done | bytes 1081376 | tf_op jit(solution)/shard_map/ppermute | solution.py:25
  28.4 0.1 shard_map.111
  28.5 1.6 %collective-permute-start.10 = (bf16[272,512]{1,0:T(8,128)(2,1)S(1)}, bf16[272,512]{1,0:T(8,128)(2,1)S(1)}, u32[]{:S(2)}, u32[]{:S(2)}) collective-permute-start(bf16[272,512]{1,0:T(8,128)(2,1)S(1)} %get-tuple-element.20.x0_ref.x_ref), channel_id=1, source_target_pairs={{0,8},{4,12},{8,0},{12,4},{1,9},{5,13},{9,1},{13,5},{2,10},{6,14},... | collective-permute-start | bytes 835592 | tf_op jit(solution)/shard_map/ppermute | solution.py:25
  30.1 0.5 collective-permute-start.16
  30.6 9.5 %collective-permute-done.16.refs_0_ = bf16[128,512]{1,0:T(8,128)(2,1)S(1)} collective-permute-done((bf16[128,512]{1,0:T(8,128)(2,1)S(1)}, bf16[128,512]{1,0:T(8,128)(2,1)S(1)}, u32[]{:S(2)}, u32[]{:S(2)}) %collective-permute-start.16) | collective-permute-done | bytes 131104 | tf_op jit(solution)/shard_map/ppermute | solution.py:25
  40.1 1.0 %shard_map.118.refs_4_ = bf16[512,256]{1,0:T(8,128)(2,1)S(1)} custom-call(bf16[128,512]{1,0:T(8,128)(2,1)} %own_ref.1, bf16[128,512]{1,0:T(8,128)(2,1)S(1)} %collective-permute-done.16.refs_0_), custom_call_target="tpu_custom_call" | custom-call | bytes 524288 | tf_op jit(solution)/shard_map/pallas_call | solution.py:42
  41.1 1.7 %collective-permute-start.17 = (bf16[512,256]{1,0:T(8,128)(2,1)S(1)}, bf16[512,256]{1,0:T(8,128)(2,1)S(1)}, u32[]{:S(2)}, u32[]{:S(2)}) collective-permute-start(bf16[512,256]{1,0:T(8,128)(2,1)S(1)} %shard_map.118.refs_4_), channel_id=1, source_target_pairs={{0,1},{1,0},{2,3},{3,2},{4,5},{5,4},{6,7},{7,6},{8,9},{9,8},{10,11... | collective-permute-start | bytes 786440 | tf_op jit(solution)/shard_map/ppermute | solution.py:25
  42.8 1.8 %collective-permute-start.18 = (bf16[512,256]{1,0:T(8,128)(2,1)S(1)}, bf16[512,256]{1,0:T(8,128)(2,1)S(1)}, u32[]{:S(2)}, u32[]{:S(2)}) collective-permute-start(bf16[512,256]{1,0:T(8,128)(2,1)S(1)} %shard_map.118.refs_4_), channel_id=1, source_target_pairs={{0,2},{1,3},{2,0},{3,1},{4,6},{5,7},{6,4},{7,5},{8,10},{9,11},{10,... | collective-permute-start | bytes 786440 | tf_op jit(solution)/shard_map/ppermute | solution.py:25
  44.6 0.5 collective-permute-start.19
  45.1 0.0 collective-permute-done.10.x0_ref
  45.1 0.0 collective-permute-start.11
  45.1 7.2 %shard_map.112 = (f32[256,512]{1,0:T(8,128)S(1)}, bf16[256,512]{1,0:T(8,128)(2,1)S(1)}, bf16[4,768,512]{2,1,0:T(8,128)(2,1)S(1)}) custom-call(s32[5]{0:T(128)S(1)} %stack.23.pos_ref, bf16[272,512]{1,0:T(8,128)(2,1)S(1)} %get-tuple-element.20.x0_ref.x_ref, bf16[272,512]{1,0:T(8,128)(2,1)S(1)} %get-tuple-element.21.x1_ref, bf16[4,512,768]{2,1,0:T(8,128)(2,1)S(1)} %copy-done, ...), custom_call_target="tpu_custom_call" | custom-call | flops 4227858432 | bytes 9437184 | tf_op jit(solution)/shard_map/pallas_call | solution.py:42
  52.3 3.5 %shard_map.114 = (bf16[128,512]{1,0:T(8,128)(2,1)S(1)}, bf16[128,512]{1,0:T(8,128)(2,1)S(1)}) custom-call(s32[5]{0:T(128)S(1)} %stack.23.pos_ref, bf16[272,512]{1,0:T(8,128)(2,1)S(1)} %collective-permute-done.10.x0_ref, bf16[272,512]{1,0:T(8,128)(2,1)S(1)} %collective-permute-done.11.x1_ref, bf16[4,512,768]{2,1,0:T(8,128)(2,1)S(1)} %copy-done, ...), custom_call_target="tpu_custom_call" | custom-call | flops 2415919104 | bytes 9437184 | tf_op jit(solution)/shard_map/pallas_call | solution.py:42
  55.8 0.6 collective-permute-start.12
  56.4 3.5 %shard_map.116 = (bf16[128,512]{1,0:T(8,128)(2,1)S(1)}, bf16[128,512]{1,0:T(8,128)(2,1)S(1)}) custom-call(s32[5]{0:T(128)S(1)} %stack.23.pos_ref, bf16[272,512]{1,0:T(8,128)(2,1)S(1)} %collective-permute-done.10.x0_ref, bf16[272,512]{1,0:T(8,128)(2,1)S(1)} %collective-permute-done.11.x1_ref, bf16[4,512,768]{2,1,0:T(8,128)(2,1)S(1)} %copy-done, ...), custom_call_target="tpu_custom_call" | custom-call | flops 2415919104 | bytes 9437184 | tf_op jit(solution)/shard_map/pallas_call | solution.py:42
  59.9 0.1 collective-permute-start.14
  60.0 0.5 collective-permute-start.20
  60.4 2.1 %collective-permute-done.18.refs_6_ = bf16[512,256]{1,0:T(8,128)(2,1)S(1)} collective-permute-done((bf16[512,256]{1,0:T(8,128)(2,1)S(1)}, bf16[512,256]{1,0:T(8,128)(2,1)S(1)}, u32[]{:S(2)}, u32[]{:S(2)}) %collective-permute-start.18) | collective-permute-done | bytes 262176 | tf_op jit(solution)/shard_map/ppermute | solution.py:25
  62.5 4.9 %collective-permute-done.19.refs_7_ = bf16[512,256]{1,0:T(8,128)(2,1)S(1)} collective-permute-done((bf16[512,256]{1,0:T(8,128)(2,1)S(1)}, bf16[512,256]{1,0:T(8,128)(2,1)S(1)}, u32[]{:S(2)}, u32[]{:S(2)}) %collective-permute-start.19) | collective-permute-done | bytes 262176 | tf_op jit(solution)/shard_map/ppermute | solution.py:25
  67.5 0.5 collective-permute-start.23
  68.0 0.1 collective-permute-start.9
  68.1 0.0 collective-permute-done.20.refs_8_
  68.1 1.0 %collective-permute-start.13 = (bf16[128,512]{1,0:T(8,128)(2,1)S(1)}, bf16[128,512]{1,0:T(8,128)(2,1)S(1)}, u32[]{:S(2)}, u32[]{:S(2)}) collective-permute-start(bf16[128,512]{1,0:T(8,128)(2,1)S(1)} %shard_map.115), channel_id=1, source_target_pairs={{0,8},{4,12},{8,0},{12,4},{1,9},{5,13},{9,1},{13,5},{2,10},{6,14},... | collective-permute-start | bytes 393224 | tf_op jit(solution)/shard_map/ppermute | solution.py:25
  69.1 1.1 %collective-permute-start.15 = (bf16[128,512]{1,0:T(8,128)(2,1)S(1)}, bf16[128,512]{1,0:T(8,128)(2,1)S(1)}, u32[]{:S(2)}, u32[]{:S(2)}) collective-permute-start(bf16[128,512]{1,0:T(8,128)(2,1)S(1)} %shard_map.117), channel_id=1, source_target_pairs={{0,8},{4,12},{8,0},{12,4},{1,9},{5,13},{9,1},{13,5},{2,10},{6,14},... | collective-permute-start | bytes 393224 | tf_op jit(solution)/shard_map/ppermute | solution.py:25
  70.2 1.4 %shard_map.113.refs_0_ = f32[256,512]{1,0:T(8,128)S(1)} custom-call(s32[5]{0:T(128)S(1)} %stack.23.pos_ref, bf16[272,512]{1,0:T(8,128)(2,1)S(1)} %get-tuple-element.20.x0_ref.x_ref, f32[256,512]{1,0:T(8,128)S(1)} %get-tuple-element.22.a_ref, bf16[4,512,768]{2,1,0:T(8,128)(2,1)S(1)} %copy-done, bf16[4,512,768]{2,1,0:T(8,128)(2,1)S(1)} %copy-done.1, ...), custom_call_target="tpu_custom_call" | custom-call | flops 603979776 | bytes 2359296 | tf_op jit(solution)/shard_map/pallas_call | solution.py:42
  71.7 2.9 %collective-permute-done.13.refs_2_ = bf16[128,512]{1,0:T(8,128)(2,1)S(1)} collective-permute-done((bf16[128,512]{1,0:T(8,128)(2,1)S(1)}, bf16[128,512]{1,0:T(8,128)(2,1)S(1)}, u32[]{:S(2)}, u32[]{:S(2)}) %collective-permute-start.13) | collective-permute-done | bytes 131104 | tf_op jit(solution)/shard_map/ppermute | solution.py:25
  74.6 2.3 %collective-permute-done.15.refs_3_ = bf16[128,512]{1,0:T(8,128)(2,1)S(1)} collective-permute-done((bf16[128,512]{1,0:T(8,128)(2,1)S(1)}, bf16[128,512]{1,0:T(8,128)(2,1)S(1)}, u32[]{:S(2)}, u32[]{:S(2)}) %collective-permute-start.15) | collective-permute-done | bytes 131104 | tf_op jit(solution)/shard_map/ppermute | solution.py:25
  76.8 2.1 %shard_map.119 = bf16[256,2048]{1,0:T(8,128)(2,1)} custom-call(s32[5]{0:T(128)S(1)} %stack.23.pos_ref, f32[256,512]{1,0:T(8,128)S(1)} %shard_map.113.refs_0_, bf16[256,512]{1,0:T(8,128)(2,1)S(1)} %collective-permute-done.9.refs_1_, bf16[128,512]{1,0:T(8,128)(2,1)S(1)} %collective-permute-done.13.refs_2_, ...), custom_call_target="tpu_custom_call" | custom-call | flops 536870912 | bytes 2097152 | tf_op jit(solution)/shard_map/pallas_call | solution.py:42
  (20 shorter events, 0.1 us)
Async XLA Ops:
  0.1 0.7 copy-start.2
  0.8 29.3 %copy-start.3 = (bf16[128,512]{1,0:T(8,128)(2,1)S(1)}, bf16[128,512]{1,0:T(8,128)(2,1)}, u32[]{:S(2)}) copy-start(bf16[128,512]{1,0:T(8,128)(2,1)} %own_ref.1) | copy-start | bytes 393220
  0.8 44.3 %copy-start.1 = (bf16[4,512,768]{2,1,0:T(8,128)(2,1)S(1)}, bf16[4,512,768]{2,1,0:T(8,128)(2,1)}, u32[]{:S(2)}) copy-start(bf16[4,512,768]{2,1,0:T(8,128)(2,1)} %u_ref.7) | copy-start | bytes 9437188
  4.7 40.4 %copy-start = (bf16[4,512,768]{2,1,0:T(8,128)(2,1)S(1)}, bf16[4,512,768]{2,1,0:T(8,128)(2,1)}, u32[]{:S(2)}) copy-start(bf16[4,512,768]{2,1,0:T(8,128)(2,1)} %g_ref.7) | copy-start | bytes 9437188
  4.7 18.7 %collective-permute-start = (bf16[256,1024]{1,0:T(8,128)(2,1)S(1)}, bf16[256,1024]{1,0:T(8,128)(2,1)S(1)}, u32[]{:S(2)}, u32[]{:S(2)}) collective-permute-start(bf16[256,1024]{1,0:T(8,128)(2,1)S(1)} %get-tuple-element.18), channel_id=1, source_target_pairs={{0,4},{4,0},{8,12},{12,8},{1,5},{5,1},{9,13},{13,9},{2,6},{6,2},{1... | collective-permute-start | bytes 1572872 | tf_op jit(solution)/shard_map/ppermute | solution.py:25
  4.8 6.6 %collective-permute-start.1 = (bf16[128,512]{1,0:T(8,128)(2,1)}, bf16[128,512]{1,0:T(8,128)(2,1)S(1)}, u32[]{:S(2)}, u32[]{:S(2)}) collective-permute-start(bf16[128,512]{1,0:T(8,128)(2,1)} %refs_0_.1), channel_id=1, source_target_pairs={{0,1},{1,0},{2,3},{3,2},{4,5},{5,4},{6,7},{7,6},{8,9},{9,8},{10,11... | collective-permute-start | bytes 393224 | tf_op jit(solution)/shard_map/ppermute | solution.py:25
  4.9 10.0 %collective-permute-start.2 = (bf16[128,512]{1,0:T(8,128)(2,1)}, bf16[128,512]{1,0:T(8,128)(2,1)S(1)}, u32[]{:S(2)}, u32[]{:S(2)}) collective-permute-start(bf16[128,512]{1,0:T(8,128)(2,1)} %refs_0_.1), channel_id=1, source_target_pairs={{0,2},{1,3},{2,0},{3,1},{16,19},{17,18},{18,17},{19,16},{4,6},{5,7... | collective-permute-start | bytes 393224 | tf_op jit(solution)/shard_map/ppermute | solution.py:35
  7.9 10.0 %collective-permute-start.3 = (bf16[128,512]{1,0:T(8,128)(2,1)}, bf16[128,512]{1,0:T(8,128)(2,1)S(1)}, u32[]{:S(2)}, u32[]{:S(2)}) collective-permute-start(bf16[128,512]{1,0:T(8,128)(2,1)} %refs_0_.1), channel_id=1, source_target_pairs={{0,8},{4,12},{8,0},{12,4},{1,9},{5,13},{9,1},{13,5},{2,10},{6,14},... | collective-permute-start | bytes 393224 | tf_op jit(solution)/shard_map/ppermute | solution.py:25
  11.4 6.9 %collective-permute-start.4 = (bf16[128,512]{1,0:T(8,128)(2,1)S(1)}, bf16[128,512]{1,0:T(8,128)(2,1)S(1)}, u32[]{:S(2)}, u32[]{:S(2)}) collective-permute-start(bf16[128,512]{1,0:T(8,128)(2,1)S(1)} %collective-permute-done.1.refs_1_), channel_id=1, source_target_pairs={{0,8},{4,12},{8,0},{12,4},{1,9},{5,13},{9,1},{13,5},{2,10},{6,14},... | collective-permute-start | bytes 393224 | tf_op jit(solution)/shard_map/ppermute | solution.py:25
  14.8 7.2 %collective-permute-start.5 = (bf16[128,512]{1,0:T(8,128)(2,1)S(1)}, bf16[128,512]{1,0:T(8,128)(2,1)S(1)}, u32[]{:S(2)}, u32[]{:S(2)}) collective-permute-start(bf16[128,512]{1,0:T(8,128)(2,1)S(1)} %collective-permute-done.2.refs_2_), channel_id=1, source_target_pairs={{0,24},{4,28},{8,16},{12,20},{16,8},{20,12},{24,0},{28,4},{1,25},{... | collective-permute-start | bytes 393224 | tf_op jit(solution)/shard_map/ppermute | solution.py:35
  17.3 5.2 %collective-permute-start.6 = (bf16[128,512]{1,0:T(8,128)(2,1)S(1)}, bf16[128,512]{1,0:T(8,128)(2,1)S(1)}, u32[]{:S(2)}, u32[]{:S(2)}) collective-permute-start(bf16[128,512]{1,0:T(8,128)(2,1)S(1)} %collective-permute-done.2.refs_2_), channel_id=1, source_target_pairs={{0,8},{4,12},{8,0},{12,4},{1,9},{5,13},{9,1},{13,5},{2,10},{6,14},... | collective-permute-start | bytes 393224 | tf_op jit(solution)/shard_map/ppermute | solution.py:25
  17.9 5.6 %collective-permute-start.7 = (bf16[128,512]{1,0:T(8,128)(2,1)S(1)}, bf16[128,512]{1,0:T(8,128)(2,1)S(1)}, u32[]{:S(2)}, u32[]{:S(2)}) collective-permute-start(bf16[128,512]{1,0:T(8,128)(2,1)S(1)} %collective-permute-done.2.refs_2_), channel_id=1, source_target_pairs={{0,16},{16,0},{1,17},{17,1},{2,18},{18,2},{3,19},{19,3},{4,20},{20... | collective-permute-start | bytes 393224 | tf_op jit(solution)/shard_map/ppermute | solution.py:25
  25.6 2.8 %collective-permute-start.8 = (f32[528,512]{1,0:T(8,128)S(1)}, f32[528,512]{1,0:T(8,128)S(1)}, u32[]{:S(2)}, u32[]{:S(2)}) collective-permute-start(f32[528,512]{1,0:T(8,128)S(1)} %shard_map.110.mine_ref), channel_id=1, source_target_pairs={{0,4},{4,0},{8,12},{12,8},{1,5},{5,1},{9,13},{13,9},{2,6},{6,2},{1... | collective-permute-start | bytes 3244040 | tf_op jit(solution)/shard_map/ppermute | solution.py:25
  28.5 16.6 %collective-permute-start.10 = (bf16[272,512]{1,0:T(8,128)(2,1)S(1)}, bf16[272,512]{1,0:T(8,128)(2,1)S(1)}, u32[]{:S(2)}, u32[]{:S(2)}) collective-permute-start(bf16[272,512]{1,0:T(8,128)(2,1)S(1)} %get-tuple-element.20.x0_ref.x_ref), channel_id=1, source_target_pairs={{0,8},{4,12},{8,0},{12,4},{1,9},{5,13},{9,1},{13,5},{2,10},{6,14},... | collective-permute-start | bytes 835592 | tf_op jit(solution)/shard_map/ppermute | solution.py:25
  30.1 10.0 %collective-permute-start.16 = (bf16[128,512]{1,0:T(8,128)(2,1)S(1)}, bf16[128,512]{1,0:T(8,128)(2,1)S(1)}, u32[]{:S(2)}, u32[]{:S(2)}) collective-permute-start(bf16[128,512]{1,0:T(8,128)(2,1)S(1)} %copy-done.3), channel_id=1, source_target_pairs={{0,8},{4,12},{8,0},{12,4},{1,9},{5,13},{9,1},{13,5},{2,10},{6,14},... | collective-permute-start | bytes 393224 | tf_op jit(solution)/shard_map/ppermute | solution.py:25
  41.1 18.8 %collective-permute-start.17 = (bf16[512,256]{1,0:T(8,128)(2,1)S(1)}, bf16[512,256]{1,0:T(8,128)(2,1)S(1)}, u32[]{:S(2)}, u32[]{:S(2)}) collective-permute-start(bf16[512,256]{1,0:T(8,128)(2,1)S(1)} %shard_map.118.refs_4_), channel_id=1, source_target_pairs={{0,1},{1,0},{2,3},{3,2},{4,5},{5,4},{6,7},{7,6},{8,9},{9,8},{10,11... | collective-permute-start | bytes 786440 | tf_op jit(solution)/shard_map/ppermute | solution.py:25
  42.8 19.8 %collective-permute-start.18 = (bf16[512,256]{1,0:T(8,128)(2,1)S(1)}, bf16[512,256]{1,0:T(8,128)(2,1)S(1)}, u32[]{:S(2)}, u32[]{:S(2)}) collective-permute-start(bf16[512,256]{1,0:T(8,128)(2,1)S(1)} %shard_map.118.refs_4_), channel_id=1, source_target_pairs={{0,2},{1,3},{2,0},{3,1},{4,6},{5,7},{6,4},{7,5},{8,10},{9,11},{10,... | collective-permute-start | bytes 786440 | tf_op jit(solution)/shard_map/ppermute | solution.py:25
  44.6 22.9 %collective-permute-start.19 = (bf16[512,256]{1,0:T(8,128)(2,1)S(1)}, bf16[512,256]{1,0:T(8,128)(2,1)S(1)}, u32[]{:S(2)}, u32[]{:S(2)}) collective-permute-start(bf16[512,256]{1,0:T(8,128)(2,1)S(1)} %shard_map.118.refs_4_), channel_id=1, source_target_pairs={{0,3},{1,2},{2,1},{3,0},{4,7},{5,6},{6,5},{7,4},{8,11},{9,10},{10,... | collective-permute-start | bytes 786440 | tf_op jit(solution)/shard_map/ppermute | solution.py:25
  45.1 7.2 %collective-permute-start.11 = (bf16[272,512]{1,0:T(8,128)(2,1)S(1)}, bf16[272,512]{1,0:T(8,128)(2,1)S(1)}, u32[]{:S(2)}, u32[]{:S(2)}) collective-permute-start(bf16[272,512]{1,0:T(8,128)(2,1)S(1)} %collective-permute-done.10.x0_ref), channel_id=1, source_target_pairs={{0,4},{4,0},{8,12},{12,8},{1,5},{5,1},{9,13},{13,9},{2,6},{6,2},{1... | collective-permute-start | bytes 835592 | tf_op jit(solution)/shard_map/ppermute | solution.py:25
  55.8 11.7 %collective-permute-start.12 = (bf16[128,512]{1,0:T(8,128)(2,1)S(1)}, bf16[128,512]{1,0:T(8,128)(2,1)S(1)}, u32[]{:S(2)}, u32[]{:S(2)}) collective-permute-start(bf16[128,512]{1,0:T(8,128)(2,1)S(1)} %get-tuple-element.26), channel_id=1, source_target_pairs={{0,4},{4,0},{8,12},{12,8},{1,5},{5,1},{9,13},{13,9},{2,6},{6,2},{1... | collective-permute-start | bytes 393224 | tf_op jit(solution)/shard_map/ppermute | solution.py:25
  59.9 8.1 %collective-permute-start.14 = (bf16[128,512]{1,0:T(8,128)(2,1)S(1)}, bf16[128,512]{1,0:T(8,128)(2,1)S(1)}, u32[]{:S(2)}, u32[]{:S(2)}) collective-permute-start(bf16[128,512]{1,0:T(8,128)(2,1)S(1)} %get-tuple-element.28), channel_id=1, source_target_pairs={{0,4},{4,0},{8,12},{12,8},{1,5},{5,1},{9,13},{13,9},{2,6},{6,2},{1... | collective-permute-start | bytes 393224 | tf_op jit(solution)/shard_map/ppermute | solution.py:25
  60.0 8.2 %collective-permute-start.20 = (bf16[512,256]{1,0:T(8,128)(2,1)S(1)}, bf16[512,256]{1,0:T(8,128)(2,1)S(1)}, u32[]{:S(2)}, u32[]{:S(2)}) collective-permute-start(bf16[512,256]{1,0:T(8,128)(2,1)S(1)} %shard_map.118.refs_4_), channel_id=1, source_target_pairs={{0,4},{4,0},{8,12},{12,8},{1,5},{5,1},{9,13},{13,9},{2,6},{6,2},{1... | collective-permute-start | bytes 786440 | tf_op jit(solution)/shard_map/ppermute | solution.py:25
  62.5 6.6 %collective-permute-start.21 = (bf16[512,256]{1,0:T(8,128)(2,1)S(1)}, bf16[512,256]{1,0:T(8,128)(2,1)S(1)}, u32[]{:S(2)}, u32[]{:S(2)}) collective-permute-start(bf16[512,256]{1,0:T(8,128)(2,1)S(1)} %collective-permute-done.17.refs_5_), channel_id=1, source_target_pairs={{0,4},{4,0},{8,12},{12,8},{1,5},{5,1},{9,13},{13,9},{2,6},{6,2},{1... | collective-permute-start | bytes 786440 | tf_op jit(solution)/shard_map/ppermute | solution.py:25
  67.5 4.2 %collective-permute-start.22 = (bf16[512,256]{1,0:T(8,128)(2,1)S(1)}, bf16[512,256]{1,0:T(8,128)(2,1)S(1)}, u32[]{:S(2)}, u32[]{:S(2)}) collective-permute-start(bf16[512,256]{1,0:T(8,128)(2,1)S(1)} %collective-permute-done.18.refs_6_), channel_id=1, source_target_pairs={{0,4},{4,0},{8,12},{12,8},{1,5},{5,1},{9,13},{13,9},{2,6},{6,2},{1... | collective-permute-start | bytes 786440 | tf_op jit(solution)/shard_map/ppermute | solution.py:25
  67.5 4.2 %collective-permute-start.23 = (bf16[512,256]{1,0:T(8,128)(2,1)S(1)}, bf16[512,256]{1,0:T(8,128)(2,1)S(1)}, u32[]{:S(2)}, u32[]{:S(2)}) collective-permute-start(bf16[512,256]{1,0:T(8,128)(2,1)S(1)} %collective-permute-done.19.refs_7_), channel_id=1, source_target_pairs={{0,4},{4,0},{8,12},{12,8},{1,5},{5,1},{9,13},{13,9},{2,6},{6,2},{1... | collective-permute-start | bytes 786440 | tf_op jit(solution)/shard_map/ppermute | solution.py:25
  68.0 3.7 %collective-permute-start.9 = (bf16[256,512]{1,0:T(8,128)(2,1)S(1)}, bf16[256,512]{1,0:T(8,128)(2,1)S(1)}, u32[]{:S(2)}, u32[]{:S(2)}) collective-permute-start(bf16[256,512]{1,0:T(8,128)(2,1)S(1)} %get-tuple-element.24), channel_id=1, source_target_pairs={{0,4},{4,0},{8,12},{12,8},{1,5},{5,1},{9,13},{13,9},{2,6},{6,2},{1... | collective-permute-start | bytes 786440 | tf_op jit(solution)/shard_map/ppermute | solution.py:25
  68.1 6.4 %collective-permute-start.13 = (bf16[128,512]{1,0:T(8,128)(2,1)S(1)}, bf16[128,512]{1,0:T(8,128)(2,1)S(1)}, u32[]{:S(2)}, u32[]{:S(2)}) collective-permute-start(bf16[128,512]{1,0:T(8,128)(2,1)S(1)} %shard_map.115), channel_id=1, source_target_pairs={{0,8},{4,12},{8,0},{12,4},{1,9},{5,13},{9,1},{13,5},{2,10},{6,14},... | collective-permute-start | bytes 393224 | tf_op jit(solution)/shard_map/ppermute | solution.py:25
  69.1 7.8 %collective-permute-start.15 = (bf16[128,512]{1,0:T(8,128)(2,1)S(1)}, bf16[128,512]{1,0:T(8,128)(2,1)S(1)}, u32[]{:S(2)}, u32[]{:S(2)}) collective-permute-start(bf16[128,512]{1,0:T(8,128)(2,1)S(1)} %shard_map.117), channel_id=1, source_target_pairs={{0,8},{4,12},{8,0},{12,4},{1,9},{5,13},{9,1},{13,5},{2,10},{6,14},... | collective-permute-start | bytes 393224 | tf_op jit(solution)/shard_map/ppermute | solution.py:25

commit v2 on v1

v2 whole, which is shorter than its diff:
```python
import functools

import jax
import jax.numpy as jnp
from jax import lax
from jax.experimental import pallas as pl
from jax.experimental.pallas import tpu as pltpu
from jax.sharding import PartitionSpec as P

epsilon = 1e-06
F32 = jnp.float32
BF16 = jnp.bfloat16

VM = pl.BlockSpec(memory_space=pltpu.VMEM)
SM = pl.BlockSpec(memory_space=pltpu.SMEM)
AN = pl.BlockSpec(memory_space=pl.ANY)


def in_hbm(x):
    return pltpu.with_memory_space_constraint(x, pltpu.HBM)


def swap(x, axis, bits):
    size = lax.axis_size(axis)
    return lax.ppermute(x, axis, [(i, i ^ bits) for i in range(size)])


def swap_pair(x, axes, move):
    sizes = [lax.axis_size(axis) for axis in axes]
    pairs = []
    for i in range(sizes[0]):
        for j in range(sizes[1]):
            p, q = move(i, j)
            pairs.append((i * sizes[1] + j, p * sizes[1] + q))
    return lax.ppermute(x, axes, pairs)


def kernel(body, out_shape, operands, specs, mib, flops=0, nbytes=0, scratch=(), out_specs=None,
           aliases={}):
    many = isinstance(out_shape, tuple)
    if out_specs is None:
        out_specs = (VM,) * len(out_shape) if many else VM
    return pl.pallas_call(
        body,
        out_shape=out_shape,
        in_specs=specs,
        out_specs=out_specs,
        scratch_shapes=list(scratch),
        input_output_aliases=aliases,
        compiler_params=pltpu.CompilerParams(vmem_limit_bytes=mib * 1024 * 1024),
        cost_estimate=pl.CostEstimate(flops=flops, bytes_accessed=nbytes, transcendentals=0),
    )(*operands)


def norm_kernel(wide, pos_ref, tok_hbm, gain_hbm, keep_ref, send_ref, normed_ref, tok_ref, gain_ref, sem):
    pairs = ((tok_hbm, tok_ref), (gain_hbm, gain_ref))
    copies = [pltpu.make_async_copy(src, dst, sem.at[i]) for i, (src, dst) in enumerate(pairs)]
    for copy in copies:
        copy.start()
    for copy in copies:
        copy.wait()
    values = tok_ref[...].astype(F32)
    scale = lax.rsqrt(jnp.mean(values * values, axis=-1, keepdims=True) + epsilon)
    normed_ref[...] = (values * scale * gain_ref[...]).astype(BF16)
    core = pos_ref[0]
    for h in range(keep_ref.shape[1] // wide):
        mine = pl.multiple_of((2 * h + core) * wide, wide)
        other = pl.multiple_of((2 * h + 1 - core) * wide, wide)
        keep_ref[:, h * wide:(h + 1) * wide] = normed_ref[:, pl.ds(mine, wide)]
        send_ref[:, h * wide:(h + 1) * wide] = normed_ref[:, pl.ds(other, wide)]


def gate_kernel(top, normed_ref, list_hbm, router_hbm, ids_hbm, slot_hbm, down_hbm, up_hbm, last_hbm,
                wt_ref, down_ref, up_ref, last_ref, list_ref, router_ref, ids_ref, slot_ref, sem):
    pairs = ((router_hbm, router_ref), (ids_hbm, ids_ref), (slot_hbm, slot_ref), (list_hbm, list_ref),
             (up_hbm, up_ref), (down_hbm, down_ref), (last_hbm, last_ref))
    copies = [pltpu.make_async_copy(src, dst, sem.at[i]) for i, (src, dst) in enumerate(pairs)]
    for copy in copies:
        copy.start()
    for copy in copies[:4]:
        copy.wait()
    logits = lax.dot_general(router_ref[...], normed_ref[...], (((1,), (1,)), ((), ())),
                             preferred_element_type=F32)
    sig = jax.nn.sigmoid(logits)
    experts, rows = sig.shape
    sub = lax.broadcasted_iota(jnp.int32, (experts, rows), 0)
    lane = lax.broadcasted_iota(jnp.int32, (experts, rows), 1)
    total = jnp.zeros((experts, rows), F32)
    served = jnp.zeros((experts, rows), F32)
    for k in range(top):
        hit = sub == ids_ref[k:k + 1, :]
        total = total + jnp.where(hit, 1.0, 0.0)
        served = served + jnp.where(hit & (slot_ref[k:k + 1, :] >= 0), 1.0, 0.0)
    _, shards, copies_n, local = list_ref.shape

    def listed(i, served):
        shard, copy = i // copies_n, i % copies_n
        for m in range(local):
            entry = list_ref[0, shard, copy, m]
            owner = jnp.where(entry >= 0, entry, -top) // top
            served = served + jnp.where((lane == owner) & (sub == shard * local + m), 1.0, 0.0)
        return served

    served = lax.fori_loop(0, shards * copies_n, listed, served)
    denom = jnp.sum(total * sig, axis=0, keepdims=True)
    wt_ref[...] = jnp.where(served > 0.0, sig / denom, 0.0)
    for copy in copies[4:]:
        copy.wait()


def partial_sum(chunks, wide, pos_ref, keep_ref, recv_ref, w_refs, x_ref, w_ref):
    half, rep, group = pos_ref[1], pos_ref[2], pos_ref[4]
    rows = keep_ref.shape[0]
    depth = w_refs[0].shape[0]
    for i, ((a, b), chunk) in enumerate(zip(chunks, w_refs)):
        if b == "A":
            b = 2 + group
        elif b == "B":
            b = 3 - group
        at = pl.multiple_of((half ^ a) * wide + (rep ^ b) * depth, depth)
        x_ref[:rows, i * depth:(i + 1) * depth] = keep_ref[:, pl.ds(at, depth)]
        x_ref[rows:, i * depth:(i + 1) * depth] = recv_ref[:, pl.ds(at, depth)]
        w_ref[i * depth:(i + 1) * depth, :] = chunk[...]
    return jnp.dot(x_ref[...], w_ref[...], preferred_element_type=F32)


def early_kernel(chunks, wide, pos_ref, keep_ref, recv_ref, *refs):
    w_refs, (out_ref, x_ref, w_ref) = refs[:-3], refs[-3:]
    out_ref[...] = partial_sum(chunks, wide, pos_ref, keep_ref, recv_ref, w_refs, x_ref, w_ref)


def late_kernel(chunks, wide, pos_ref, keep_ref, recv_ref, sum_ref, wt_ref, *refs):
    w_refs, (out_ref, x_ref, w_ref) = refs[:-3], refs[-3:]
    rows = keep_ref.shape[0]
    out_ref[2 * rows:, :rows] = wt_ref[...]
    out_ref[2 * rows:, rows:] = jnp.zeros_like(out_ref[2 * rows:, rows:])
    out_ref[:2 * rows, :] = sum_ref[...] + partial_sum(
        chunks, wide, pos_ref, keep_ref, recv_ref, w_refs, x_ref, w_ref)


def finish_kernel(mine_ref, recv_ref, own_ref, core_ref):
    rows = (own_ref.shape[1]) // 2
    own_ref[:rows, :] = (mine_ref[:rows, :] + recv_ref[rows:2 * rows, :]).astype(BF16)
    core_ref[:rows, :] = (mine_ref[rows:2 * rows, :] + recv_ref[:rows, :]).astype(BF16)
    for src, dst in ((mine_ref, own_ref), (recv_ref, core_ref)):
        wt = src[2 * rows:, :rows]
        lead = wt.astype(BF16)
        dst[rows:, :rows] = lead
        dst[rows:, rows:] = (wt - lead.astype(F32)).astype(BF16)


def expert(x, weight, gate_w, up_w, down_w):
    gate = jnp.dot(x, gate_w, preferred_element_type=F32)
    upper = jnp.dot(x, up_w, preferred_element_type=F32)
    half = 0.5 * gate
    hidden = ((half + half * jnp.tanh(half)) * upper).astype(BF16)
    result = jnp.dot(hidden, down_w, preferred_element_type=F32).astype(BF16)
    return result.astype(F32) * weight


def columns(me, local, pay_ref, at, size):
    rows = pay_ref.shape[1] // 2
    wt = (pay_ref[rows:, at:at + size].astype(F32)
          + pay_ref[rows:, rows + at:rows + at + size].astype(F32))
    sub = lax.broadcasted_iota(jnp.int32, wt.shape, 0)
    picked = [jnp.sum(jnp.where(sub == me * local + j, wt, 0.0), axis=0, keepdims=True)
              for j in range(local)]
    pad = jnp.zeros((-local % 8, size), F32)
    return jnp.concatenate(picked + [pad], axis=0).T


def near_kernel(local, pos_ref, x0_ref, x1_ref, g_ref, u_ref, d_ref, o0_ref, o1_ref, acc_ref):
    rows = o0_ref.shape[0]
    cols = [columns(pos_ref[3], local, p, 0, rows) for p in (x0_ref, x1_ref)]
    for j in range(local):
        for x_ref, sum_ref, col in ((x0_ref, o0_ref, cols[0]), (x1_ref, acc_ref, cols[1])):
            part = expert(x_ref[:rows, :], col[:, j:j + 1], g_ref[j], u_ref[j], d_ref[j])
            sum_ref[...] = part if j == 0 else sum_ref[...] + part
    o1_ref[...] = acc_ref[...].astype(BF16)


def far_open_kernel(local, at, span, pos_ref, x0_ref, x1_ref, g_ref, u_ref, d_ref, x_ref, col_ref, acc_ref):
    size = x_ref.shape[0] // 2
    x_ref[:size, :] = x0_ref[at:at + size, :]
    x_ref[size:, :] = x1_ref[at:at + size, :]
    cols = jnp.concatenate([columns(pos_ref[3], local, p, at, size) for p in (x0_ref, x1_ref)], axis=0)
    col_ref[...] = cols
    for j in span:
        part = expert(x_ref[...], cols[:, j:j + 1], g_ref[j], u_ref[j], d_ref[j])
        acc_ref[...] = part if j == 0 else acc_ref[...] + part


def far_close_kernel(span, x_ref, col_ref, sum_ref, g_ref, u_ref, d_ref, o0_ref, o1_ref, acc_ref):
    size = o0_ref.shape[0]
    for j in span:
        part = expert(x_ref[...], col_ref[:, j:j + 1], g_ref[j], u_ref[j], d_ref[j])
        acc_ref[...] = (sum_ref if j == span[0] else acc_ref)[...] + part
    o0_ref[...] = acc_ref[:size, :].astype(BF16)
    o1_ref[...] = acc_ref[size:, :].astype(BF16)


def far_kernel(local, at, pos_ref, x0_ref, x1_ref, g_ref, u_ref, d_ref, o0_ref, o1_ref, x_ref, col_ref,
               acc_ref):
    size = o0_ref.shape[0]
    far_open_kernel(local, at, range(local), pos_ref, x0_ref, x1_ref, g_ref, u_ref, d_ref, x_ref, col_ref,
                    acc_ref)
    o0_ref[...] = acc_ref[:size, :].astype(BF16)
    o1_ref[...] = acc_ref[size:, :].astype(BF16)


def add_kernel(a_ref, b_ref, o_ref):
    o_ref[...] = (a_ref[...].astype(F32) + b_ref[...].astype(F32)).astype(BF16)


def join_kernel(*refs):
    depth = refs[0].shape[0]
    for i, x_ref in enumerate(refs[:-1]):
        refs[-1][:, i * depth:(i + 1) * depth] = x_ref[...].T


def final_kernel(n_back, at, chunks, copies, depth, pos_ref, near_ref, core_ref, *refs):
    out_ref, block_ref, sem = refs[-3:]
    half, rep, core = pos_ref[1], pos_ref[2], pos_ref[0]
    size = block_ref.shape[1]
    total = near_ref[at:at + size, :] + core_ref[at:at + size, :].astype(F32)
    for s_ref in refs[:n_back]:
        total = total + s_ref[...].astype(F32)
    merged = total.astype(BF16)
    outs = []
    for i, ((c, b), w_ref) in enumerate(zip(chunks, refs[n_back:])):
        block_ref[i] = jnp.dot(merged, w_ref[...], preferred_element_type=F32).astype(BF16)
        for a in range(w_ref.shape[1] // depth):
            e = 2 * (half ^ a) + (core ^ c)
            to = pl.multiple_of((e * copies + (rep ^ b)) * depth, depth)
            outs.append(pltpu.make_async_copy(block_ref.at[i, :, pl.ds(a * depth, depth)],
                                              out_ref.at[pl.ds(at, size), pl.ds(to, depth)], sem.at[i, a]))
            outs[-1].start()
    for out in outs:
        out.wait()


def shape(dims, dtype=BF16):
    return jax.ShapeDtypeStruct(dims, dtype)


def on_device(tokens, norm_gain, router, down_proj, up_proj, expert_gate, expert_up, expert_down,
              expert_ids, slot_pos, overflow_list):
    rows, width = tokens.shape
    top = expert_ids.shape[1]
    local, _, ff = expert_gate.shape
    depth, latent = down_proj.shape
    groups = lax.axis_size("groups")
    shards = lax.axis_size("expert")
    copies = lax.axis_size("replica")
    chips = shards // 2
    wide = copies * depth
    spread = copies
    if depth % 128:
        down_proj = lax.all_gather(down_proj, "replica", axis=0, tiled=True)
        up_proj = lax.all_gather(up_proj, "replica", axis=0, tiled=True)
        depth, spread = wide, 1
    experts = shards * local
    g = lax.axis_index("groups")
    e = lax.axis_index("expert")
    r = lax.axis_index("replica")
    pos = jnp.stack([e % 2, e // 2, r if spread > 1 else 0 * r, e, g]).astype(jnp.int32)

    down = {(0, 0): down_proj}
    if spread == groups + 2 and groups == 2:
        near_z = swap(down_proj, "replica", 1)
        far_z = swap_pair(down_proj, ("groups", "replica"), lambda i, j: (i, j ^ (2 + i)))
        down[(0, 1)] = near_z
        down[(0, "A")] = far_z
        for a in range(1, chips):
            down[(a, 0)] = swap(down_proj, "expert", 2 * a)
        ups_x = [swap(up_proj, "expert", 2 * a) for a in range(1, chips)]
        for a in range(1, chips):
            down[(a, 1)] = swap(near_z, "expert", 2 * a)
            down[(a, "B")] = swap_pair(far_z, ("groups", "expert"),
                                       lambda i, j: (i ^ 1, j ^ (2 * a)))
            down[(a, "A")] = swap(far_z, "expert", 2 * a)
        down[(0, "B")] = swap(far_z, "groups", 1)
    else:
        for b in range(1, spread):
            down[(0, b)] = swap(down_proj, "replica", b)
        for b in range(spread):
            for a in range(1, chips):
                down[(a, b)] = swap(down[(0, b)], "expert", 2 * a)
        ups_x = [swap(up_proj, "expert", 2 * a) for a in range(1, chips)]

    keep, send, normed = kernel(
        functools.partial(norm_kernel, wide),
        (shape((rows, width // 2)), shape((rows, width // 2)), shape((rows, width))),
        (pos, in_hbm(tokens), in_hbm(norm_gain.reshape(1, width))), [SM] + [AN] * 2, 16,
        8 * rows * width, 4 * rows * width,
        [pltpu.VMEM((rows, width), BF16), pltpu.VMEM((1, width), F32), pltpu.SemaphoreType.DMA((2,))])
    recv = swap(send, "expert", 1)
    wt, own_down, own_up, last = kernel(
        functools.partial(gate_kernel, top),
        (shape((experts, rows), F32), shape(down_proj.shape), shape(up_proj.shape), shape(expert_down.shape)),
        (normed, *map(in_hbm, (overflow_list, router.T, expert_ids.T, slot_pos.T, down_proj, up_proj,
                               expert_down))),
        [VM] + [AN] * 7, 14, 4 * rows * width * experts, 4 * rows * width,
        [pltpu.SMEM(overflow_list.shape, jnp.int32), pltpu.VMEM((experts, width), BF16),
         pltpu.VMEM((top, rows), jnp.int32), pltpu.VMEM((top, rows), jnp.int32),
         pltpu.SemaphoreType.DMA((7,))])
    down[(0, 0)] = own_down
    weights = (expert_gate, expert_up, last)

    late = [k for k in down if (k[1] == "A" and k[0]) or k[1] == "B"] or list(down)[-1:]
    early = [k for k in down if k not in late]

    def scratch(n):
        return [pltpu.VMEM((2 * rows, n * depth), BF16), pltpu.VMEM((n * depth, latent), BF16)]

    opened = kernel(
        functools.partial(early_kernel, early, wide), shape((2 * rows, latent), F32),
        (pos, keep, recv, *[down[k] for k in early]), [SM] + [VM] * (2 + len(early)), 12,
        4 * rows * len(early) * depth * latent, 2 * len(early) * depth * latent, scratch(len(early)))
    partial = kernel(
        functools.partial(late_kernel, late, wide), shape((2 * rows + experts, latent), F32),
        (pos, keep, recv, opened, wt, *[down[k] for k in late]), [SM] + [VM] * (4 + len(late)), 12,
        4 * rows * len(late) * depth * latent, 2 * len(late) * depth * latent, scratch(len(late)))
    partial_core = swap(partial, "expert", 1)
    own, core = kernel(
        finish_kernel, (shape((rows + experts, latent)),) * 2, (partial, partial_core), [VM, VM],
        6, 2 * rows * latent, 12 * rows * latent)

    work = 6 * rows * latent * ff
    load = 6 * latent * ff
    far = []
    for a in range(1, chips):
        x0 = swap(own, "expert", 2 * a)
        far.append((x0, swap(x0, "expert", 1)))
    near0, near1 = kernel(
        functools.partial(near_kernel, local), (shape((rows, latent), F32), shape((rows, latent))),
        (pos, own, core, *weights), [SM] + [VM] * 5, 20, 2 * local * work, local * load,
        [pltpu.VMEM((rows, latent), F32)])
    near1 = swap(near1, "expert", 1)
    parts = 2
    size = rows // parts
    cut = local // 2
    back = [[], []]
    for a in range(1, chips):
        x = shape((2 * size, latent))
        col = shape((2 * size, local + -local % 8), F32)
        acc = shape((2 * size, latent), F32)
        out = (shape((size, latent)),) * 2
        o0, o1 = kernel(
            functools.partial(far_kernel, local, 0), out, (pos, *far[a - 1], *weights),
            [SM] + [VM] * 5, 20, local * work, local * load,
            [pltpu.VMEM(v.shape, v.dtype) for v in (x, col, acc)])
        results = [(o0, swap(o1, "expert", 1))]
        held = kernel(
            functools.partial(far_open_kernel, local, size, range(cut)), (x, col, acc),
            (pos, *far[a - 1], *weights), [SM] + [VM] * 5, 20, cut * work, cut * load)
        o0, o1 = kernel(
            functools.partial(far_close_kernel, range(cut, local)), out, (*held, *weights),
            [VM] * 6, 20, (local - cut) * work, (local - cut) * load, [pltpu.VMEM(acc.shape, F32)])
        results.append((o0, swap(o1, "expert", 1)))
        for h, pair in enumerate(results):
            s = kernel(add_kernel, shape((size, latent)), pair, [VM, VM], 4,
                       size * latent, 6 * size * latent)
            back[h].append(swap(s, "expert", 2 * a))

    pair = kernel(join_kernel, shape((latent, chips * depth)), (own_up, *ups_x),
                  [VM] * chips, 4, 0, 4 * chips * depth * latent)
    ups = {(0, 0): pair}
    for b in range(1, spread):
        ups[(0, b)] = swap(pair, "replica", b)
    for b in range(spread):
        ups[(1, b)] = swap(ups[(0, b)], "expert", 1)
    order = sorted(ups)
    result = None
    for h in range(parts):
        operands = (pos, near0, near1, *back[h], *[ups[k] for k in order])
        result = kernel(
            functools.partial(final_kernel, len(back[h]), h * size, order, spread, depth),
            shape((rows, width)), operands + ((result,) if h else ()),
            [SM] + [VM] * (len(operands) - 1) + [AN] * h, 10, 2 * size * width * latent, 2 * width * latent,
            [pltpu.VMEM((len(order), size, chips * depth), BF16),
             pltpu.SemaphoreType.DMA((len(order), chips))],
            AN, {len(operands): 0} if h else {})
    return result


def solution(mesh):
    placed = (
        P(("groups", "expert", "replica"), None),
        P(),
        P(),
        P(("expert", "replica"), None),
        P(("expert", "replica"), None),
        P("expert", None, None),
        P("expert", None, None),
        P("expert", None, None),
        P(("groups", "expert", "replica"), None),
        P(("groups", "expert", "replica"), None),
        P(("groups", "expert", "replica"), None, None, None),
    )

    return jax.shard_map(
        on_device,
        mesh=mesh,
        in_specs=placed,
        out_specs=P(("groups", "expert", "replica"), None),
        check_vma=False,
    )
```

time: 79.1 us -> 81.3 us (1.028)
  the two profiles are of different devices: /device:TPU:8 before, /device:TPU:0 now
where the time goes in v2:
time: 81.3 us; the launch traced here: 79.8 us
  waiting for transfers between devices  31.8 us (39%)
  starting transfers between devices  24 us (30%)
  Pallas kernels  23.8 us (29%)
    ppermute x22, waiting for transfers between devices, swap(): return lax.ppermute(x, axis, [(i, i ^ bits) for i in range(size)])  30.7 us
    pallas_call x14, Pallas kernels, kernel(): pl.pallas_call(body, out_shape=out_shape, in_specs=specs, out_specs=out_s...  23.8 us
    ppermute x22, starting transfers between devices, swap(): return lax.ppermute(x, axis, [(i, i ^ bits) for i in range(size)])  19.1 us
    ppermute x2, starting transfers between devices, swap_pair(): return lax.ppermute(x, axes, pairs)  4.9 us
  transfers between devices with their start and end apart: 24, of which 12 were waited for; matrix products, arithmetic and copies ran while one was open for 0% of the time, Pallas kernels for 24%

profile of v2, /device:TPU:0, one launch (start us, length us, event | category | flops | bytes accessed | tf_op | source)
XLA Modules:
  0.0 79.8 jit_solution(16649525928035867825)
XLA Ops:
  0.0 0.1 stack.23.pos_ref
  0.1 2.3 %shard_map.109 = (bf16[256,1024]{1,0:T(8,128)(2,1)S(1)}, bf16[256,1024]{1,0:T(8,128)(2,1)S(1)}, bf16[256,2048]{1,0:T(8,128)(2,1)S(1)}) custom-call(s32[5]{0:T(128)S(1)} %stack.23.pos_ref, bf16[256,2048]{1,0:T(8,128)(2,1)} %tok_hbm.1, f32[1,2048]{1,0:T(1,128)} %bitcast.10), custom_call_target="tpu_custom_call" | custom-call | flops 4194304 | bytes 2097152 | tf_op jit(solution)/shard_map/pallas_call | solution.py:43
  2.4 0.6 collective-permute-start
  2.9 2.6 %collective-permute-start.1 = (bf16[128,512]{1,0:T(8,128)(2,1)}, bf16[128,512]{1,0:T(8,128)(2,1)S(1)}, u32[]{:S(2)}, u32[]{:S(2)}) collective-permute-start(bf16[128,512]{1,0:T(8,128)(2,1)} %down_hbm.1), channel_id=1, source_target_pairs={{0,1},{1,0},{2,3},{3,2},{4,5},{5,4},{6,7},{7,6},{8,9},{9,8},{10,11... | collective-permute-start | bytes 393224 | tf_op jit(solution)/shard_map/ppermute | solution.py:25
  5.6 2.6 %collective-permute-start.2 = (bf16[128,512]{1,0:T(8,128)(2,1)}, bf16[128,512]{1,0:T(8,128)(2,1)S(1)}, u32[]{:S(2)}, u32[]{:S(2)}) collective-permute-start(bf16[128,512]{1,0:T(8,128)(2,1)} %down_hbm.1), channel_id=1, source_target_pairs={{0,2},{1,3},{2,0},{3,1},{16,19},{17,18},{18,17},{19,16},{4,6},{5,7... | collective-permute-start | bytes 393224 | tf_op jit(solution)/shard_map/ppermute | solution.py:35
  8.1 1.5 %collective-permute-start.3 = (bf16[128,512]{1,0:T(8,128)(2,1)}, bf16[128,512]{1,0:T(8,128)(2,1)S(1)}, u32[]{:S(2)}, u32[]{:S(2)}) collective-permute-start(bf16[128,512]{1,0:T(8,128)(2,1)} %down_hbm.1), channel_id=1, source_target_pairs={{0,8},{4,12},{8,0},{12,4},{1,9},{5,13},{9,1},{13,5},{2,10},{6,14},... | collective-permute-start | bytes 393224 | tf_op jit(solution)/shard_map/ppermute | solution.py:25
  9.6 2.6 %collective-permute-done.1.refs_1_ = bf16[128,512]{1,0:T(8,128)(2,1)S(1)} collective-permute-done((bf16[128,512]{1,0:T(8,128)(2,1)}, bf16[128,512]{1,0:T(8,128)(2,1)S(1)}, u32[]{:S(2)}, u32[]{:S(2)}) %collective-permute-start.1) | collective-permute-done | bytes 131104 | tf_op jit(solution)/shard_map/ppermute | solution.py:25
  12.3 1.8 %collective-permute-start.4 = (bf16[128,512]{1,0:T(8,128)(2,1)S(1)}, bf16[128,512]{1,0:T(8,128)(2,1)S(1)}, u32[]{:S(2)}, u32[]{:S(2)}) collective-permute-start(bf16[128,512]{1,0:T(8,128)(2,1)S(1)} %collective-permute-done.1.refs_1_), channel_id=1, source_target_pairs={{0,8},{4,12},{8,0},{12,4},{1,9},{5,13},{9,1},{13,5},{2,10},{6,14},... | collective-permute-start | bytes 393224 | tf_op jit(solution)/shard_map/ppermute | solution.py:25
  14.1 1.0 %collective-permute-done.2.refs_2_ = bf16[128,512]{1,0:T(8,128)(2,1)S(1)} collective-permute-done((bf16[128,512]{1,0:T(8,128)(2,1)}, bf16[128,512]{1,0:T(8,128)(2,1)S(1)}, u32[]{:S(2)}, u32[]{:S(2)}) %collective-permute-start.2) | collective-permute-done | bytes 131104 | tf_op jit(solution)/shard_map/ppermute | solution.py:35
  15.1 2.3 %collective-permute-start.5 = (bf16[128,512]{1,0:T(8,128)(2,1)S(1)}, bf16[128,512]{1,0:T(8,128)(2,1)S(1)}, u32[]{:S(2)}, u32[]{:S(2)}) collective-permute-start(bf16[128,512]{1,0:T(8,128)(2,1)S(1)} %collective-permute-done.2.refs_2_), channel_id=1, source_target_pairs={{0,24},{4,28},{8,16},{12,20},{16,8},{20,12},{24,0},{28,4},{1,25},{... | collective-permute-start | bytes 393224 | tf_op jit(solution)/shard_map/ppermute | solution.py:35
  17.4 0.5 collective-permute-start.6
  17.9 0.6 collective-permute-start.7
  18.6 2.2 %shard_map.110 = (f32[16,256]{1,0:T(8,128)S(1)}, bf16[128,512]{1,0:T(8,128)(2,1)S(1)}, bf16[128,512]{1,0:T(8,128)(2,1)S(1)}, bf16[4,768,512]{2,1,0:T(8,128)(2,1)S(1)}) custom-call(bf16[256,2048]{1,0:T(8,128)(2,1)S(1)} %get-tuple-element.25.normed_ref, s32[1,4,4,4]{3,2,1,0:T(4,128)} %list_hbm.1, bf16[16,2048]{1,0:T(8,128)(2,1)} %bitcast.9, ...), custom_call_target="tpu_custom_call" | custom-call | flops 33554432 | bytes 2097152 | tf_op jit(solution)/shard_map/pallas_call | solution.py:43
  20.8 0.0 copy-start.2
  20.8 1.2 %shard_map.111.sum_ref = f32[512,512]{1,0:T(8,128)S(1)} custom-call(s32[5]{0:T(128)S(1)} %stack.23.pos_ref, bf16[256,1024]{1,0:T(8,128)(2,1)S(1)} %get-tuple-element.23.keep_ref, bf16[256,1024]{1,0:T(8,128)(2,1)S(1)} %collective-permute-done.recv_ref, bf16[128,512]{1,0:T(8,128)(2,1)S(1)} %get-tuple-element.26.refs_0_, ...), custom_call_target="tpu_custom_call" | custom-call | flops 335544320 | bytes 655360 | tf_op jit(solution)/shard_map/pallas_call | solution.py:43
  22.0 0.0 copy-start
  22.0 0.1 collective-permute-done.5.refs_0_
  22.1 1.6 %collective-permute-done.6.refs_1_ = bf16[128,512]{1,0:T(8,128)(2,1)S(1)} collective-permute-done((bf16[128,512]{1,0:T(8,128)(2,1)S(1)}, bf16[128,512]{1,0:T(8,128)(2,1)S(1)}, u32[]{:S(2)}, u32[]{:S(2)}) %collective-permute-start.6) | collective-permute-done | bytes 131104 | tf_op jit(solution)/shard_map/ppermute | solution.py:25
  23.6 0.1 collective-permute-done.7.refs_2_
  23.7 1.0 %shard_map.112.mine_ref = f32[528,512]{1,0:T(8,128)S(1)} custom-call(s32[5]{0:T(128)S(1)} %stack.23.pos_ref, bf16[256,1024]{1,0:T(8,128)(2,1)S(1)} %get-tuple-element.23.keep_ref, bf16[256,1024]{1,0:T(8,128)(2,1)S(1)} %collective-permute-done.recv_ref, f32[512,512]{1,0:T(8,128)S(1)} %shard_map.111.sum_ref, f32[16,256]{1,0:T(8,128)S(1)} %get-tuple-element.27.wt_ref, ...), custom_call_target="tpu_custom_call" | custom-call | flops 201326592 | bytes 393216 | tf_op jit(solution)/shard_map/pallas_call | solution.py:43
  24.7 0.1 collective-permute-start.8
  24.8 1.6 %collective-permute-start.14 = (bf16[128,512]{1,0:T(8,128)(2,1)S(1)}, bf16[128,512]{1,0:T(8,128)(2,1)S(1)}, u32[]{:S(2)}, u32[]{:S(2)}) collective-permute-start(bf16[128,512]{1,0:T(8,128)(2,1)S(1)} %copy-done.2), channel_id=1, source_target_pairs={{0,8},{4,12},{8,0},{12,4},{1,9},{5,13},{9,1},{13,5},{2,10},{6,14},... | collective-permute-start | bytes 393224 | tf_op jit(solution)/shard_map/ppermute | solution.py:25
  26.4 1.1 %collective-permute-done.8.recv_ref = f32[528,512]{1,0:T(8,128)S(1)} collective-permute-done((f32[528,512]{1,0:T(8,128)S(1)}, f32[528,512]{1,0:T(8,128)S(1)}, u32[]{:S(2)}, u32[]{:S(2)}) %collective-permute-start.8) | collective-permute-done | bytes 1081376 | tf_op jit(solution)/shard_map/ppermute | solution.py:25
  27.5 0.1 shard_map.113
  27.6 1.6 %collective-permute-start.10 = (bf16[272,512]{1,0:T(8,128)(2,1)S(1)}, bf16[272,512]{1,0:T(8,128)(2,1)S(1)}, u32[]{:S(2)}, u32[]{:S(2)}) collective-permute-start(bf16[272,512]{1,0:T(8,128)(2,1)S(1)} %get-tuple-element.28.x0_ref), channel_id=1, source_target_pairs={{0,8},{4,12},{8,0},{12,4},{1,9},{5,13},{9,1},{13,5},{2,10},{6,14},... | collective-permute-start | bytes 835592 | tf_op jit(solution)/shard_map/ppermute | solution.py:25
  29.2 1.9 %collective-permute-done.14.refs_1_ = bf16[128,512]{1,0:T(8,128)(2,1)S(1)} collective-permute-done((bf16[128,512]{1,0:T(8,128)(2,1)S(1)}, bf16[128,512]{1,0:T(8,128)(2,1)S(1)}, u32[]{:S(2)}, u32[]{:S(2)}) %collective-permute-start.14) | collective-permute-done | bytes 131104 | tf_op jit(solution)/shard_map/ppermute | solution.py:25
  31.0 0.1 shard_map.118.refs_1_
  31.1 0.5 collective-permute-start.15
  31.6 3.3 %collective-permute-start.16 = (bf16[512,256]{1,0:T(8,128)(2,1)S(1)}, bf16[512,256]{1,0:T(8,128)(2,1)S(1)}, u32[]{:S(2)}, u32[]{:S(2)}) collective-permute-start(bf16[512,256]{1,0:T(8,128)(2,1)S(1)} %shard_map.118.refs_1_), channel_id=1, source_target_pairs={{0,2},{1,3},{2,0},{3,1},{4,6},{5,7},{6,4},{7,5},{8,10},{9,11},{10,... | collective-permute-start | bytes 786440 | tf_op jit(solution)/shard_map/ppermute | solution.py:25
  35.0 0.6 collective-permute-start.17
  35.6 7.8 %collective-permute-done.15.refs_2_ = bf16[512,256]{1,0:T(8,128)(2,1)S(1)} collective-permute-done((bf16[512,256]{1,0:T(8,128)(2,1)S(1)}, bf16[512,256]{1,0:T(8,128)(2,1)S(1)}, u32[]{:S(2)}, u32[]{:S(2)}) %collective-permute-start.15) | collective-permute-done | bytes 262176 | tf_op jit(solution)/shard_map/ppermute | solution.py:25
  43.4 10.0 %collective-permute-done.16.refs_3_ = bf16[512,256]{1,0:T(8,128)(2,1)S(1)} collective-permute-done((bf16[512,256]{1,0:T(8,128)(2,1)S(1)}, bf16[512,256]{1,0:T(8,128)(2,1)S(1)}, u32[]{:S(2)}, u32[]{:S(2)}) %collective-permute-start.16) | collective-permute-done | bytes 262176 | tf_op jit(solution)/shard_map/ppermute | solution.py:25
  53.4 0.5 collective-permute-start.21
  53.9 0.1 collective-permute-start.11
  54.0 6.2 %shard_map.114 = (f32[256,512]{1,0:T(8,128)S(1)}, bf16[256,512]{1,0:T(8,128)(2,1)S(1)}) custom-call(s32[5]{0:T(128)S(1)} %stack.23.pos_ref, bf16[272,512]{1,0:T(8,128)(2,1)S(1)} %get-tuple-element.28.x0_ref, bf16[272,512]{1,0:T(8,128)(2,1)S(1)} %get-tuple-element.29.x1_ref, bf16[4,512,768]{2,1,0:T(8,128)(2,1)S(1)} %copy-done, ...), custom_call_target="tpu_custom_call" | custom-call | flops 4831838208 | bytes 9437184 | tf_op jit(solution)/shard_map/pallas_call | solution.py:43
  60.2 3.5 %shard_map.119 = (bf16[128,512]{1,0:T(8,128)(2,1)S(1)}, bf16[128,512]{1,0:T(8,128)(2,1)S(1)}) custom-call(s32[5]{0:T(128)S(1)} %stack.23.pos_ref, bf16[272,512]{1,0:T(8,128)(2,1)S(1)} %collective-permute-done.10.x0_ref, bf16[272,512]{1,0:T(8,128)(2,1)S(1)} %collective-permute-done.11.x1_ref, bf16[4,512,768]{2,1,0:T(8,128)(2,1)S(1)} %copy-done, ...), custom_call_target="tpu_custom_call" | custom-call | flops 2415919104 | bytes 9437184 | tf_op jit(solution)/shard_map/pallas_call | solution.py:43
  63.7 0.5 collective-permute-start.22
  64.2 2.1 %shard_map.115 = (bf16[256,512]{1,0:T(8,128)(2,1)S(1)}, f32[256,8]{1,0:T(8,128)S(1)}, f32[256,512]{1,0:T(8,128)S(1)}) custom-call(s32[5]{0:T(128)S(1)} %stack.23.pos_ref, bf16[272,512]{1,0:T(8,128)(2,1)S(1)} %collective-permute-done.10.x0_ref, bf16[272,512]{1,0:T(8,128)(2,1)S(1)} %collective-permute-done.11.x1_ref, bf16[4,512,768]{2,1,0:T(8,128)(2,1)S(1)} %copy-done, ...), custom_call_target="tpu_custom_call" | custom-call | flops 1207959552 | bytes 4718592 | tf_op jit(solution)/shard_map/pallas_call | solution.py:43
  66.3 1.6 %shard_map.116 = (bf16[128,512]{1,0:T(8,128)(2,1)S(1)}, bf16[128,512]{1,0:T(8,128)(2,1)S(1)}) custom-call(bf16[256,512]{1,0:T(8,128)(2,1)S(1)} %get-tuple-element.33.x_ref, f32[256,8]{1,0:T(8,128)S(1)} %get-tuple-element.34.col_ref, f32[256,512]{1,0:T(8,128)S(1)} %get-tuple-element.35.sum_ref, bf16[4,512,768]{2,1,0:T(8,128)(2,1)S(1)} %copy-done, ...), custom_call_target="tpu_custom_call" | custom-call | flops 1207959552 | bytes 4718592 | tf_op jit(solution)/shard_map/pallas_call | solution.py:43
  67.9 0.1 collective-permute-start.9
  68.1 0.4 collective-permute-start.12
  68.5 1.2 %collective-permute-done.12.b_ref = bf16[128,512]{1,0:T(8,128)(2,1)S(1)} collective-permute-done((bf16[128,512]{1,0:T(8,128)(2,1)S(1)}, bf16[128,512]{1,0:T(8,128)(2,1)S(1)}, u32[]{:S(2)}, u32[]{:S(2)}) %collective-permute-start.12) | collective-permute-done | bytes 131104 | tf_op jit(solution)/shard_map/ppermute | solution.py:25
  69.7 1.1 %collective-permute-start.23 = (bf16[128,512]{1,0:T(8,128)(2,1)S(1)}, bf16[128,512]{1,0:T(8,128)(2,1)S(1)}, u32[]{:S(2)}, u32[]{:S(2)}) collective-permute-start(bf16[128,512]{1,0:T(8,128)(2,1)S(1)} %shard_map.120), channel_id=1, source_target_pairs={{0,8},{4,12},{8,0},{12,4},{1,9},{5,13},{9,1},{13,5},{2,10},{6,14},... | collective-permute-start | bytes 393224 | tf_op jit(solution)/shard_map/ppermute | solution.py:25
  70.8 1.0 %collective-permute-start.13 = (bf16[128,512]{1,0:T(8,128)(2,1)S(1)}, bf16[128,512]{1,0:T(8,128)(2,1)S(1)}, u32[]{:S(2)}, u32[]{:S(2)}) collective-permute-start(bf16[128,512]{1,0:T(8,128)(2,1)S(1)} %shard_map.117), channel_id=1, source_target_pairs={{0,8},{4,12},{8,0},{12,4},{1,9},{5,13},{9,1},{13,5},{2,10},{6,14},... | collective-permute-start | bytes 393224 | tf_op jit(solution)/shard_map/ppermute | solution.py:25
  71.9 4.2 %collective-permute-done.23.refs_0_ = bf16[128,512]{1,0:T(8,128)(2,1)S(1)} collective-permute-done((bf16[128,512]{1,0:T(8,128)(2,1)S(1)}, bf16[128,512]{1,0:T(8,128)(2,1)S(1)}, u32[]{:S(2)}, u32[]{:S(2)}) %collective-permute-start.23) | collective-permute-done | bytes 131104 | tf_op jit(solution)/shard_map/ppermute | solution.py:25
  76.1 1.8 %shard_map.121.refs_9_ = bf16[256,2048]{1,0:T(8,128)(2,1)} custom-call(s32[5]{0:T(128)S(1)} %stack.23.pos_ref, f32[256,512]{1,0:T(8,128)S(1)} %get-tuple-element.31.near_ref, bf16[256,512]{1,0:T(8,128)(2,1)S(1)} %collective-permute-done.9.core_ref, bf16[128,512]{1,0:T(8,128)(2,1)S(1)} %collective-permute-done.23.refs_0_, ...), custom_call_target="tpu_custom_call" | custom-call | flops 268435456 | bytes 2097152 | tf_op jit(solution)/shard_map/pallas_call | solution.py:43
  77.9 0.2 collective-permute-done.13.refs_0_
  78.1 1.8 %shard_map.122 = bf16[256,2048]{1,0:T(8,128)(2,1)} custom-call(s32[5]{0:T(128)S(1)} %stack.23.pos_ref, f32[256,512]{1,0:T(8,128)S(1)} %get-tuple-element.31.near_ref, bf16[256,512]{1,0:T(8,128)(2,1)S(1)} %collective-permute-done.9.core_ref, bf16[128,512]{1,0:T(8,128)(2,1)S(1)} %collective-permute-done.13.refs_0_, ...), custom_call_target="tpu_custom_call", output_to_operand_aliasing={{}: (12, {})} | custom-call | flops 268435456 | bytes 2097152 | tf_op jit(solution)/shard_map/pallas_call | solution.py:43
  (21 shorter events, 0.1 us)
Async XLA Ops:
  2.4 18.4 %collective-permute-start = (bf16[256,1024]{1,0:T(8,128)(2,1)S(1)}, bf16[256,1024]{1,0:T(8,128)(2,1)S(1)}, u32[]{:S(2)}, u32[]{:S(2)}) collective-permute-start(bf16[256,1024]{1,0:T(8,128)(2,1)S(1)} %get-tuple-element.24), channel_id=1, source_target_pairs={{0,4},{4,0},{8,12},{12,8},{1,5},{5,1},{9,13},{13,9},{2,6},{6,2},{1... | collective-permute-start | bytes 1572872 | tf_op jit(solution)/shard_map/ppermute | solution.py:25
  2.9 9.4 %collective-permute-start.1 = (bf16[128,512]{1,0:T(8,128)(2,1)}, bf16[128,512]{1,0:T(8,128)(2,1)S(1)}, u32[]{:S(2)}, u32[]{:S(2)}) collective-permute-start(bf16[128,512]{1,0:T(8,128)(2,1)} %down_hbm.1), channel_id=1, source_target_pairs={{0,1},{1,0},{2,3},{3,2},{4,5},{5,4},{6,7},{7,6},{8,9},{9,8},{10,11... | collective-permute-start | bytes 393224 | tf_op jit(solution)/shard_map/ppermute | solution.py:25
  5.6 9.5 %collective-permute-start.2 = (bf16[128,512]{1,0:T(8,128)(2,1)}, bf16[128,512]{1,0:T(8,128)(2,1)S(1)}, u32[]{:S(2)}, u32[]{:S(2)}) collective-permute-start(bf16[128,512]{1,0:T(8,128)(2,1)} %down_hbm.1), channel_id=1, source_target_pairs={{0,2},{1,3},{2,0},{3,1},{16,19},{17,18},{18,17},{19,16},{4,6},{5,7... | collective-permute-start | bytes 393224 | tf_op jit(solution)/shard_map/ppermute | solution.py:35
  8.1 9.8 %collective-permute-start.3 = (bf16[128,512]{1,0:T(8,128)(2,1)}, bf16[128,512]{1,0:T(8,128)(2,1)S(1)}, u32[]{:S(2)}, u32[]{:S(2)}) collective-permute-start(bf16[128,512]{1,0:T(8,128)(2,1)} %down_hbm.1), channel_id=1, source_target_pairs={{0,8},{4,12},{8,0},{12,4},{1,9},{5,13},{9,1},{13,5},{2,10},{6,14},... | collective-permute-start | bytes 393224 | tf_op jit(solution)/shard_map/ppermute | solution.py:25
  12.3 8.5 %collective-permute-start.4 = (bf16[128,512]{1,0:T(8,128)(2,1)S(1)}, bf16[128,512]{1,0:T(8,128)(2,1)S(1)}, u32[]{:S(2)}, u32[]{:S(2)}) collective-permute-start(bf16[128,512]{1,0:T(8,128)(2,1)S(1)} %collective-permute-done.1.refs_1_), channel_id=1, source_target_pairs={{0,8},{4,12},{8,0},{12,4},{1,9},{5,13},{9,1},{13,5},{2,10},{6,14},... | collective-permute-start | bytes 393224 | tf_op jit(solution)/shard_map/ppermute | solution.py:25
  15.1 7.0 %collective-permute-start.5 = (bf16[128,512]{1,0:T(8,128)(2,1)S(1)}, bf16[128,512]{1,0:T(8,128)(2,1)S(1)}, u32[]{:S(2)}, u32[]{:S(2)}) collective-permute-start(bf16[128,512]{1,0:T(8,128)(2,1)S(1)} %collective-permute-done.2.refs_2_), channel_id=1, source_target_pairs={{0,24},{4,28},{8,16},{12,20},{16,8},{20,12},{24,0},{28,4},{1,25},{... | collective-permute-start | bytes 393224 | tf_op jit(solution)/shard_map/ppermute | solution.py:35
  17.4 6.2 %collective-permute-start.6 = (bf16[128,512]{1,0:T(8,128)(2,1)S(1)}, bf16[128,512]{1,0:T(8,128)(2,1)S(1)}, u32[]{:S(2)}, u32[]{:S(2)}) collective-permute-start(bf16[128,512]{1,0:T(8,128)(2,1)S(1)} %collective-permute-done.2.refs_2_), channel_id=1, source_target_pairs={{0,8},{4,12},{8,0},{12,4},{1,9},{5,13},{9,1},{13,5},{2,10},{6,14},... | collective-permute-start | bytes 393224 | tf_op jit(solution)/shard_map/ppermute | solution.py:25
  17.9 5.8 %collective-permute-start.7 = (bf16[128,512]{1,0:T(8,128)(2,1)S(1)}, bf16[128,512]{1,0:T(8,128)(2,1)S(1)}, u32[]{:S(2)}, u32[]{:S(2)}) collective-permute-start(bf16[128,512]{1,0:T(8,128)(2,1)S(1)} %collective-permute-done.2.refs_2_), channel_id=1, source_target_pairs={{0,16},{16,0},{1,17},{17,1},{2,18},{18,2},{3,19},{19,3},{4,20},{20... | collective-permute-start | bytes 393224 | tf_op jit(solution)/shard_map/ppermute | solution.py:25
  20.8 4.0 %copy-start.2 = (bf16[128,512]{1,0:T(8,128)(2,1)S(1)}, bf16[128,512]{1,0:T(8,128)(2,1)}, u32[]{:S(2)}) copy-start(bf16[128,512]{1,0:T(8,128)(2,1)} %up_hbm.1) | copy-start | bytes 393220
  20.8 33.2 %copy-start.1 = (bf16[4,512,768]{2,1,0:T(8,128)(2,1)S(1)}, bf16[4,512,768]{2,1,0:T(8,128)(2,1)}, u32[]{:S(2)}) copy-start(bf16[4,512,768]{2,1,0:T(8,128)(2,1)} %u_ref.7) | copy-start | bytes 9437188
  22.0 32.0 %copy-start = (bf16[4,512,768]{2,1,0:T(8,128)(2,1)S(1)}, bf16[4,512,768]{2,1,0:T(8,128)(2,1)}, u32[]{:S(2)}) copy-start(bf16[4,512,768]{2,1,0:T(8,128)(2,1)} %g_ref.7) | copy-start | bytes 9437188
  24.7 2.8 %collective-permute-start.8 = (f32[528,512]{1,0:T(8,128)S(1)}, f32[528,512]{1,0:T(8,128)S(1)}, u32[]{:S(2)}, u32[]{:S(2)}) collective-permute-start(f32[528,512]{1,0:T(8,128)S(1)} %shard_map.112.mine_ref), channel_id=1, source_target_pairs={{0,4},{4,0},{8,12},{12,8},{1,5},{5,1},{9,13},{13,9},{2,6},{6,2},{1... | collective-permute-start | bytes 3244040 | tf_op jit(solution)/shard_map/ppermute | solution.py:25
  24.8 6.2 %collective-permute-start.14 = (bf16[128,512]{1,0:T(8,128)(2,1)S(1)}, bf16[128,512]{1,0:T(8,128)(2,1)S(1)}, u32[]{:S(2)}, u32[]{:S(2)}) collective-permute-start(bf16[128,512]{1,0:T(8,128)(2,1)S(1)} %copy-done.2), channel_id=1, source_target_pairs={{0,8},{4,12},{8,0},{12,4},{1,9},{5,13},{9,1},{13,5},{2,10},{6,14},... | collective-permute-start | bytes 393224 | tf_op jit(solution)/shard_map/ppermute | solution.py:25
  27.6 26.3 %collective-permute-start.10 = (bf16[272,512]{1,0:T(8,128)(2,1)S(1)}, bf16[272,512]{1,0:T(8,128)(2,1)S(1)}, u32[]{:S(2)}, u32[]{:S(2)}) collective-permute-start(bf16[272,512]{1,0:T(8,128)(2,1)S(1)} %get-tuple-element.28.x0_ref), channel_id=1, source_target_pairs={{0,8},{4,12},{8,0},{12,4},{1,9},{5,13},{9,1},{13,5},{2,10},{6,14},... | collective-permute-start | bytes 835592 | tf_op jit(solution)/shard_map/ppermute | solution.py:25
  31.1 12.2 %collective-permute-start.15 = (bf16[512,256]{1,0:T(8,128)(2,1)S(1)}, bf16[512,256]{1,0:T(8,128)(2,1)S(1)}, u32[]{:S(2)}, u32[]{:S(2)}) collective-permute-start(bf16[512,256]{1,0:T(8,128)(2,1)S(1)} %shard_map.118.refs_1_), channel_id=1, source_target_pairs={{0,1},{1,0},{2,3},{3,2},{4,5},{5,4},{6,7},{7,6},{8,9},{9,8},{10,11... | collective-permute-start | bytes 786440 | tf_op jit(solution)/shard_map/ppermute | solution.py:25
  31.6 21.7 %collective-permute-start.16 = (bf16[512,256]{1,0:T(8,128)(2,1)S(1)}, bf16[512,256]{1,0:T(8,128)(2,1)S(1)}, u32[]{:S(2)}, u32[]{:S(2)}) collective-permute-start(bf16[512,256]{1,0:T(8,128)(2,1)S(1)} %shard_map.118.refs_1_), channel_id=1, source_target_pairs={{0,2},{1,3},{2,0},{3,1},{4,6},{5,7},{6,4},{7,5},{8,10},{9,11},{10,... | collective-permute-start | bytes 786440 | tf_op jit(solution)/shard_map/ppermute | solution.py:25
  35.0 18.4 %collective-permute-start.17 = (bf16[512,256]{1,0:T(8,128)(2,1)S(1)}, bf16[512,256]{1,0:T(8,128)(2,1)S(1)}, u32[]{:S(2)}, u32[]{:S(2)}) collective-permute-start(bf16[512,256]{1,0:T(8,128)(2,1)S(1)} %shard_map.118.refs_1_), channel_id=1, source_target_pairs={{0,3},{1,2},{2,1},{3,0},{4,7},{5,6},{6,5},{7,4},{8,11},{9,10},{10,... | collective-permute-start | bytes 786440 | tf_op jit(solution)/shard_map/ppermute | solution.py:25
  35.6 32.3 %collective-permute-start.18 = (bf16[512,256]{1,0:T(8,128)(2,1)S(1)}, bf16[512,256]{1,0:T(8,128)(2,1)S(1)}, u32[]{:S(2)}, u32[]{:S(2)}) collective-permute-start(bf16[512,256]{1,0:T(8,128)(2,1)S(1)} %shard_map.118.refs_1_), channel_id=1, source_target_pairs={{0,4},{4,0},{8,12},{12,8},{1,5},{5,1},{9,13},{13,9},{2,6},{6,2},{1... | collective-permute-start | bytes 786440 | tf_op jit(solution)/shard_map/ppermute | solution.py:25
  43.4 27.5 %collective-permute-start.19 = (bf16[512,256]{1,0:T(8,128)(2,1)S(1)}, bf16[512,256]{1,0:T(8,128)(2,1)S(1)}, u32[]{:S(2)}, u32[]{:S(2)}) collective-permute-start(bf16[512,256]{1,0:T(8,128)(2,1)S(1)} %collective-permute-done.15.refs_2_), channel_id=1, source_target_pairs={{0,4},{4,0},{8,12},{12,8},{1,5},{5,1},{9,13},{13,9},{2,6},{6,2},{1... | collective-permute-start | bytes 786440 | tf_op jit(solution)/shard_map/ppermute | solution.py:25
  53.4 18.5 %collective-permute-start.20 = (bf16[512,256]{1,0:T(8,128)(2,1)S(1)}, bf16[512,256]{1,0:T(8,128)(2,1)S(1)}, u32[]{:S(2)}, u32[]{:S(2)}) collective-permute-start(bf16[512,256]{1,0:T(8,128)(2,1)S(1)} %collective-permute-done.16.refs_3_), channel_id=1, source_target_pairs={{0,4},{4,0},{8,12},{12,8},{1,5},{5,1},{9,13},{13,9},{2,6},{6,2},{1... | collective-permute-start | bytes 786440 | tf_op jit(solution)/shard_map/ppermute | solution.py:25
  53.4 18.5 %collective-permute-start.21 = (bf16[512,256]{1,0:T(8,128)(2,1)S(1)}, bf16[512,256]{1,0:T(8,128)(2,1)S(1)}, u32[]{:S(2)}, u32[]{:S(2)}) collective-permute-start(bf16[512,256]{1,0:T(8,128)(2,1)S(1)} %collective-permute-done.17.refs_4_), channel_id=1, source_target_pairs={{0,4},{4,0},{8,12},{12,8},{1,5},{5,1},{9,13},{13,9},{2,6},{6,2},{1... | collective-permute-start | bytes 786440 | tf_op jit(solution)/shard_map/ppermute | solution.py:25
  53.9 6.3 %collective-permute-start.11 = (bf16[272,512]{1,0:T(8,128)(2,1)S(1)}, bf16[272,512]{1,0:T(8,128)(2,1)S(1)}, u32[]{:S(2)}, u32[]{:S(2)}) collective-permute-start(bf16[272,512]{1,0:T(8,128)(2,1)S(1)} %collective-permute-done.10.x0_ref), channel_id=1, source_target_pairs={{0,4},{4,0},{8,12},{12,8},{1,5},{5,1},{9,13},{13,9},{2,6},{6,2},{1... | collective-permute-start | bytes 835592 | tf_op jit(solution)/shard_map/ppermute | solution.py:25
  63.7 4.3 %collective-permute-start.22 = (bf16[128,512]{1,0:T(8,128)(2,1)S(1)}, bf16[128,512]{1,0:T(8,128)(2,1)S(1)}, u32[]{:S(2)}, u32[]{:S(2)}) collective-permute-start(bf16[128,512]{1,0:T(8,128)(2,1)S(1)} %get-tuple-element.40), channel_id=1, source_target_pairs={{0,4},{4,0},{8,12},{12,8},{1,5},{5,1},{9,13},{13,9},{2,6},{6,2},{1... | collective-permute-start | bytes 393224 | tf_op jit(solution)/shard_map/ppermute | solution.py:25
  67.9 3.9 %collective-permute-start.9 = (bf16[256,512]{1,0:T(8,128)(2,1)S(1)}, bf16[256,512]{1,0:T(8,128)(2,1)S(1)}, u32[]{:S(2)}, u32[]{:S(2)}) collective-permute-start(bf16[256,512]{1,0:T(8,128)(2,1)S(1)} %get-tuple-element.32), channel_id=1, source_target_pairs={{0,4},{4,0},{8,12},{12,8},{1,5},{5,1},{9,13},{13,9},{2,6},{6,2},{1... | collective-permute-start | bytes 786440 | tf_op jit(solution)/shard_map/ppermute | solution.py:25
  68.1 1.6 %collective-permute-start.12 = (bf16[128,512]{1,0:T(8,128)(2,1)S(1)}, bf16[128,512]{1,0:T(8,128)(2,1)S(1)}, u32[]{:S(2)}, u32[]{:S(2)}) collective-permute-start(bf16[128,512]{1,0:T(8,128)(2,1)S(1)} %get-tuple-element.37), channel_id=1, source_target_pairs={{0,4},{4,0},{8,12},{12,8},{1,5},{5,1},{9,13},{13,9},{2,6},{6,2},{1... | collective-permute-start | bytes 393224 | tf_op jit(solution)/shard_map/ppermute | solution.py:25
  69.7 6.4 %collective-permute-start.23 = (bf16[128,512]{1,0:T(8,128)(2,1)S(1)}, bf16[128,512]{1,0:T(8,128)(2,1)S(1)}, u32[]{:S(2)}, u32[]{:S(2)}) collective-permute-start(bf16[128,512]{1,0:T(8,128)(2,1)S(1)} %shard_map.120), channel_id=1, source_target_pairs={{0,8},{4,12},{8,0},{12,4},{1,9},{5,13},{9,1},{13,5},{2,10},{6,14},... | collective-permute-start | bytes 393224 | tf_op jit(solution)/shard_map/ppermute | solution.py:25
  70.8 7.2 %collective-permute-start.13 = (bf16[128,512]{1,0:T(8,128)(2,1)S(1)}, bf16[128,512]{1,0:T(8,128)(2,1)S(1)}, u32[]{:S(2)}, u32[]{:S(2)}) collective-permute-start(bf16[128,512]{1,0:T(8,128)(2,1)S(1)} %shard_map.117), channel_id=1, source_target_pairs={{0,8},{4,12},{8,0},{12,4},{1,9},{5,13},{9,1},{13,5},{2,10},{6,14},... | collective-permute-start | bytes 393224 | tf_op jit(solution)/shard_map/ppermute | solution.py:25

commit v3 on v2

--- a/solution.py
+++ b/solution.py
@@ -52,7 +52,7 @@
     )(*operands)
 
 
-def norm_kernel(wide, pos_ref, tok_hbm, gain_hbm, keep_ref, send_ref, normed_ref, tok_ref, gain_ref, sem):
+def norm_kernel(pos_ref, tok_hbm, gain_hbm, normed_ref, tok_ref, gain_ref, sem):
     pairs = ((tok_hbm, tok_ref), (gain_hbm, gain_ref))
     copies = [pltpu.make_async_copy(src, dst, sem.at[i]) for i, (src, dst) in enumerate(pairs)]
     for copy in copies:
@@ -62,12 +62,6 @@
     values = tok_ref[...].astype(F32)
     scale = lax.rsqrt(jnp.mean(values * values, axis=-1, keepdims=True) + epsilon)
     normed_ref[...] = (values * scale * gain_ref[...]).astype(BF16)
-    core = pos_ref[0]
-    for h in range(keep_ref.shape[1] // wide):
-        mine = pl.multiple_of((2 * h + core) * wide, wide)
-        other = pl.multiple_of((2 * h + 1 - core) * wide, wide)
-        keep_ref[:, h * wide:(h + 1) * wide] = normed_ref[:, pl.ds(mine, wide)]
-        send_ref[:, h * wide:(h + 1) * wide] = normed_ref[:, pl.ds(other, wide)]
 
 
 def gate_kernel(top, normed_ref, list_hbm, router_hbm, ids_hbm, slot_hbm, down_hbm, up_hbm, last_hbm,
@@ -108,45 +102,45 @@
         copy.wait()
 
 
-def partial_sum(chunks, wide, pos_ref, keep_ref, recv_ref, w_refs, x_ref, w_ref):
-    half, rep, group = pos_ref[1], pos_ref[2], pos_ref[4]
-    rows = keep_ref.shape[0]
-    depth = w_refs[0].shape[0]
-    for i, ((a, b), chunk) in enumerate(zip(chunks, w_refs)):
+def pile_kernel(*refs):
+    depth = refs[0].shape[0]
+    for i, x_ref in enumerate(refs[:-1]):
+        refs[-1][i * depth:(i + 1) * depth, :] = x_ref[...]
+
+
+def pick(chunks, other, depth, copies, pos_ref, normed_ref, x_ref):
+    core, half, rep, group = pos_ref[0], pos_ref[1], pos_ref[2], pos_ref[4]
+    for i, (a, b) in enumerate(chunks):
         if b == "A":
             b = 2 + group
         elif b == "B":
             b = 3 - group
-        at = pl.multiple_of((half ^ a) * wide + (rep ^ b) * depth, depth)
-        x_ref[:rows, i * depth:(i + 1) * depth] = keep_ref[:, pl.ds(at, depth)]
-        x_ref[rows:, i * depth:(i + 1) * depth] = recv_ref[:, pl.ds(at, depth)]
+        at = ((2 * (half ^ a) + (core ^ other)) * copies + (rep ^ b)) * depth
+        x_ref[:, i * depth:(i + 1) * depth] = normed_ref[:, pl.ds(pl.multiple_of(at, depth), depth)]
+
+
+def early_kernel(chunks, depth, copies, pos_ref, normed_ref, w0_ref, w1_ref, out_ref, x_ref):
+    pick(chunks, 0, depth, copies, pos_ref, normed_ref, x_ref.at[0])
+    pick(chunks, 1, depth, copies, pos_ref, normed_ref, x_ref.at[1])
+    out_ref[...] = (jnp.dot(x_ref[0], w0_ref[...], preferred_element_type=F32)
+                    + jnp.dot(x_ref[1], w1_ref[...], preferred_element_type=F32))
+
+
+def late_kernel(chunks, copies, pos_ref, normed_ref, sum_ref, wt_ref, *refs):
+    w_refs, (out_ref, x_ref, w_ref) = refs[:-3], refs[-3:]
+    n = len(chunks)
+    rows = normed_ref.shape[0]
+    depth = w_refs[0].shape[0]
+    for c in range(2):
+        pick(chunks, c, depth, copies, pos_ref, normed_ref, x_ref.at[:, c * n * depth:(c + 1) * n * depth])
+    for i, chunk in enumerate(w_refs):
         w_ref[i * depth:(i + 1) * depth, :] = chunk[...]
-    return jnp.dot(x_ref[...], w_ref[...], preferred_element_type=F32)
-
-
-def early_kernel(chunks, wide, pos_ref, keep_ref, recv_ref, *refs):
-    w_refs, (out_ref, x_ref, w_ref) = refs[:-3], refs[-3:]
-    out_ref[...] = partial_sum(chunks, wide, pos_ref, keep_ref, recv_ref, w_refs, x_ref, w_ref)
-
-
-def late_kernel(chunks, wide, pos_ref, keep_ref, recv_ref, sum_ref, wt_ref, *refs):
-    w_refs, (out_ref, x_ref, w_ref) = refs[:-3], refs[-3:]
-    rows = keep_ref.shape[0]
-    out_ref[2 * rows:, :rows] = wt_ref[...]
-    out_ref[2 * rows:, rows:] = jnp.zeros_like(out_ref[2 * rows:, rows:])
-    out_ref[:2 * rows, :] = sum_ref[...] + partial_sum(
-        chunks, wide, pos_ref, keep_ref, recv_ref, w_refs, x_ref, w_ref)
-
-
-def finish_kernel(mine_ref, recv_ref, own_ref, core_ref):
-    rows = (own_ref.shape[1]) // 2
-    own_ref[:rows, :] = (mine_ref[:rows, :] + recv_ref[rows:2 * rows, :]).astype(BF16)
-    core_ref[:rows, :] = (mine_ref[rows:2 * rows, :] + recv_ref[:rows, :]).astype(BF16)
-    for src, dst in ((mine_ref, own_ref), (recv_ref, core_ref)):
-        wt = src[2 * rows:, :rows]
-        lead = wt.astype(BF16)
-        dst[rows:, :rows] = lead
-        dst[rows:, rows:] = (wt - lead.astype(F32)).astype(BF16)
+    out_ref[:rows, :] = (sum_ref[...] + jnp.dot(x_ref[...], w_ref[...],
+                                                preferred_element_type=F32)).astype(BF16)
+    wt = wt_ref[...]
+    lead = wt.astype(BF16)
+    out_ref[rows:, :rows] = lead
+    out_ref[rows:, rows:] = (wt - lead.astype(F32)).astype(BF16)
 
 
 def expert(x, weight, gate_w, up_w, down_w):
@@ -219,24 +213,22 @@
 
 
 def final_kernel(n_back, at, chunks, copies, depth, pos_ref, near_ref, core_ref, *refs):
-    out_ref, block_ref, sem = refs[-3:]
+    out_ref, rows_ref, sem = refs[-3:]
     half, rep, core = pos_ref[1], pos_ref[2], pos_ref[0]
-    size = block_ref.shape[1]
+    size = rows_ref.shape[0]
     total = near_ref[at:at + size, :] + core_ref[at:at + size, :].astype(F32)
     for s_ref in refs[:n_back]:
         total = total + s_ref[...].astype(F32)
     merged = total.astype(BF16)
-    outs = []
-    for i, ((c, b), w_ref) in enumerate(zip(chunks, refs[n_back:])):
-        block_ref[i] = jnp.dot(merged, w_ref[...], preferred_element_type=F32).astype(BF16)
+    for (c, b), w_ref in zip(chunks, refs[n_back:]):
+        block = jnp.dot(merged, w_ref[...], preferred_element_type=F32).astype(BF16)
         for a in range(w_ref.shape[1] // depth):
             e = 2 * (half ^ a) + (core ^ c)
             to = pl.multiple_of((e * copies + (rep ^ b)) * depth, depth)
-            outs.append(pltpu.make_async_copy(block_ref.at[i, :, pl.ds(a * depth, depth)],
-                                              out_ref.at[pl.ds(at, size), pl.ds(to, depth)], sem.at[i, a]))
-            outs[-1].start()
-    for out in outs:
-        out.wait()
+            rows_ref[:, pl.ds(to, depth)] = block[:, a * depth:(a + 1) * depth]
+    out = pltpu.make_async_copy(rows_ref, out_ref.at[pl.ds(at, size), :], sem)
+    out.start()
+    out.wait()
 
 
 def shape(dims, dtype=BF16):
@@ -288,13 +280,10 @@
                 down[(a, b)] = swap(down[(0, b)], "expert", 2 * a)
         ups_x = [swap(up_proj, "expert", 2 * a) for a in range(1, chips)]
 
-    keep, send, normed = kernel(
-        functools.partial(norm_kernel, wide),
-        (shape((rows, width // 2)), shape((rows, width // 2)), shape((rows, width))),
-        (pos, in_hbm(tokens), in_hbm(norm_gain.reshape(1, width))), [SM] + [AN] * 2, 16,
-        8 * rows * width, 4 * rows * width,
+    normed = kernel(
+        norm_kernel, shape((rows, width)), (pos, in_hbm(tokens), in_hbm(norm_gain.reshape(1, width))),
+        [SM] + [AN] * 2, 16, 8 * rows * width, 4 * rows * width,
         [pltpu.VMEM((rows, width), BF16), pltpu.VMEM((1, width), F32), pltpu.SemaphoreType.DMA((2,))])
-    recv = swap(send, "expert", 1)
     wt, own_down, own_up, last = kernel(
         functools.partial(gate_kernel, top),
         (shape((experts, rows), F32), shape(down_proj.shape), shape(up_proj.shape), shape(expert_down.shape)),
@@ -310,21 +299,22 @@
     late = [k for k in down if (k[1] == "A" and k[0]) or k[1] == "B"] or list(down)[-1:]
     early = [k for k in down if k not in late]
 
-    def scratch(n):
-        return [pltpu.VMEM((2 * rows, n * depth), BF16), pltpu.VMEM((n * depth, latent), BF16)]
-
+    n = len(early)
+    stacked = kernel(pile_kernel, shape((n * depth, latent)), [down[k] for k in early], [VM] * n,
+                     6, 0, 4 * n * depth * latent)
+    stacked_core = swap(stacked, "expert", 1)
+    late_core = [swap(down[k], "expert", 1) for k in late]
     opened = kernel(
-        functools.partial(early_kernel, early, wide), shape((2 * rows, latent), F32),
-        (pos, keep, recv, *[down[k] for k in early]), [SM] + [VM] * (2 + len(early)), 12,
-        4 * rows * len(early) * depth * latent, 2 * len(early) * depth * latent, scratch(len(early)))
-    partial = kernel(
-        functools.partial(late_kernel, late, wide), shape((2 * rows + experts, latent), F32),
-        (pos, keep, recv, opened, wt, *[down[k] for k in late]), [SM] + [VM] * (4 + len(late)), 12,
-        4 * rows * len(late) * depth * latent, 2 * len(late) * depth * latent, scratch(len(late)))
-    partial_core = swap(partial, "expert", 1)
-    own, core = kernel(
-        finish_kernel, (shape((rows + experts, latent)),) * 2, (partial, partial_core), [VM, VM],
-        6, 2 * rows * latent, 12 * rows * latent)
+        functools.partial(early_kernel, early, depth, spread), shape((rows, latent), F32),
+        (pos, normed, stacked, stacked_core), [SM] + [VM] * 3, 10, 4 * rows * n * depth * latent,
+        4 * n * depth * latent, [pltpu.VMEM((2, rows, n * depth), BF16)])
+    n = len(late)
+    own = kernel(
+        functools.partial(late_kernel, late, spread), shape((rows + experts, latent)),
+        (pos, normed, opened, wt, *[down[k] for k in late], *late_core), [SM] + [VM] * (3 + 2 * n), 10,
+        4 * rows * n * depth * latent, 4 * n * depth * latent,
+        [pltpu.VMEM((rows, 2 * n * depth), BF16), pltpu.VMEM((2 * n * depth, latent), BF16)])
+    core = swap(own, "expert", 1)
 
     work = 6 * rows * latent * ff
     load = 6 * latent * ff
@@ -378,8 +368,7 @@
             functools.partial(final_kernel, len(back[h]), h * size, order, spread, depth),
             shape((rows, width)), operands + ((result,) if h else ()),
             [SM] + [VM] * (len(operands) - 1) + [AN] * h, 10, 2 * size * width * latent, 2 * width * latent,
-            [pltpu.VMEM((len(order), size, chips * depth), BF16),
-             pltpu.SemaphoreType.DMA((len(order), chips))],
+            [pltpu.VMEM((size, width), BF16), pltpu.SemaphoreType.DMA],
             AN, {len(operands): 0} if h else {})
     return result
 

time: 81.3 us -> 82.7 us (1.017)
  waiting for transfers between devices: 31.8 us -> 33.3 us
    ppermute x2, waiting for transfers between devices: 1.12 us -> 3.83 us  [swap_pair(): return lax.ppermute(x, axes, pairs)]
    ppermute x2, starting transfers between devices: 4.9 us -> 3.38 us  [swap_pair(): return lax.ppermute(x, axes, pairs)]
    ppermute x22 -> x25, starting transfers between devices: 19.1 us -> 20.5 us  [swap(): return lax.ppermute(x, axis, [(i, i ^ bits) for i in range(size)])]
    ppermute x22 -> x25, waiting for transfers between devices: 30.7 us -> 29.5 us  [swap(): return lax.ppermute(x, axis, [(i, i ^ bits) for i in range(size)])]
  transfers between devices with their start and end apart: 24 -> 27, of which waited for: 12 -> 10; matrix products, arithmetic and copies ran while one was open for 0% -> 0% of each run, Pallas kernels for 24% -> 27%
where the time goes in v3:
time: 82.7 us; the launch traced here: 81.2 us
  waiting for transfers between devices  33.3 us (40%)
  starting transfers between devices  23.8 us (29%)
  Pallas kernels  23.7 us (29%)
    ppermute x25, waiting for transfers between devices, swap(): return lax.ppermute(x, axis, [(i, i ^ bits) for i in range(size)])  29.5 us
    pallas_call x14, Pallas kernels, kernel(): pl.pallas_call(body, out_shape=out_shape, in_specs=specs, out_specs=out_s...  23.7 us
    ppermute x25, starting transfers between devices, swap(): return lax.ppermute(x, axis, [(i, i ^ bits) for i in range(size)])  20.5 us
    ppermute x2, waiting for transfers between devices, swap_pair(): return lax.ppermute(x, axes, pairs)  3.83 us
    ppermute x2, starting transfers between devices, swap_pair(): return lax.ppermute(x, axes, pairs)  3.38 us
  transfers between devices with their start and end apart: 27, of which 10 were waited for; matrix products, arithmetic and copies ran while one was open for 0% of the time, Pallas kernels for 27%

profile of v3, /device:TPU:0, one launch (start us, length us, event | category | flops | bytes accessed | tf_op | source)
XLA Modules:
  0.0 81.2 jit_solution(14602297487040485058)
XLA Ops:
  0.0 3.1 %collective-permute-start = (bf16[128,512]{1,0:T(8,128)(2,1)}, bf16[128,512]{1,0:T(8,128)(2,1)S(1)}, u32[]{:S(2)}, u32[]{:S(2)}) collective-permute-start(bf16[128,512]{1,0:T(8,128)(2,1)} %down_hbm.1), channel_id=1, source_target_pairs={{0,1},{1,0},{2,3},{3,2},{4,5},{5,4},{6,7},{7,6},{8,9},{9,8},{10,11... | collective-permute-start | bytes 393224 | tf_op jit(solution)/shard_map/ppermute | solution.py:25
  3.1 2.6 %collective-permute-start.1 = (bf16[128,512]{1,0:T(8,128)(2,1)}, bf16[128,512]{1,0:T(8,128)(2,1)S(1)}, u32[]{:S(2)}, u32[]{:S(2)}) collective-permute-start(bf16[128,512]{1,0:T(8,128)(2,1)} %down_hbm.1), channel_id=1, source_target_pairs={{0,2},{1,3},{2,0},{3,1},{16,19},{17,18},{18,17},{19,16},{4,6},{5,7... | collective-permute-start | bytes 393224 | tf_op jit(solution)/shard_map/ppermute | solution.py:35
  5.6 1.5 %collective-permute-start.2 = (bf16[128,512]{1,0:T(8,128)(2,1)}, bf16[128,512]{1,0:T(8,128)(2,1)S(1)}, u32[]{:S(2)}, u32[]{:S(2)}) collective-permute-start(bf16[128,512]{1,0:T(8,128)(2,1)} %down_hbm.1), channel_id=1, source_target_pairs={{0,8},{4,12},{8,0},{12,4},{1,9},{5,13},{9,1},{13,5},{2,10},{6,14},... | collective-permute-start | bytes 393224 | tf_op jit(solution)/shard_map/ppermute | solution.py:25
  7.1 1.4 %collective-permute-done.refs_1_ = bf16[128,512]{1,0:T(8,128)(2,1)S(1)} collective-permute-done((bf16[128,512]{1,0:T(8,128)(2,1)}, bf16[128,512]{1,0:T(8,128)(2,1)S(1)}, u32[]{:S(2)}, u32[]{:S(2)}) %collective-permute-start) | collective-permute-done | bytes 131104 | tf_op jit(solution)/shard_map/ppermute | solution.py:25
  8.6 1.8 %collective-permute-start.3 = (bf16[128,512]{1,0:T(8,128)(2,1)S(1)}, bf16[128,512]{1,0:T(8,128)(2,1)S(1)}, u32[]{:S(2)}, u32[]{:S(2)}) collective-permute-start(bf16[128,512]{1,0:T(8,128)(2,1)S(1)} %collective-permute-done.refs_1_), channel_id=1, source_target_pairs={{0,8},{4,12},{8,0},{12,4},{1,9},{5,13},{9,1},{13,5},{2,10},{6,14},... | collective-permute-start | bytes 393224 | tf_op jit(solution)/shard_map/ppermute | solution.py:25
  10.4 0.1 stack.23.pos_ref
  10.5 2.2 %shard_map.109.normed_ref = bf16[256,2048]{1,0:T(8,128)(2,1)S(1)} custom-call(s32[5]{0:T(128)S(1)} %stack.23.pos_ref, bf16[256,2048]{1,0:T(8,128)(2,1)} %tok_hbm.1, f32[1,2048]{1,0:T(1,128)} %bitcast.10), custom_call_target="tpu_custom_call" | custom-call | flops 4194304 | bytes 2097152 | tf_op jit(solution)/shard_map/pallas_call | solution.py:43
  12.7 0.0 copy-start.2
  12.7 2.2 %shard_map.110 = (f32[16,256]{1,0:T(8,128)S(1)}, bf16[128,512]{1,0:T(8,128)(2,1)S(1)}, bf16[128,512]{1,0:T(8,128)(2,1)S(1)}, bf16[4,768,512]{2,1,0:T(8,128)(2,1)S(1)}) custom-call(bf16[256,2048]{1,0:T(8,128)(2,1)S(1)} %shard_map.109.normed_ref, s32[1,4,4,4]{3,2,1,0:T(4,128)} %list_hbm.1, bf16[16,2048]{1,0:T(8,128)(2,1)} %bitcast.9, s32[8,256]{1,0:T(8,128)} %bitcast.11, ...), custom_call_target="tpu_custom_call" | custom-call | flops 33554432 | bytes 2097152 | tf_op jit(solution)/shard_map/pallas_call | solution.py:43
  14.9 0.0 collective-permute-done.1.refs_2_
  14.9 0.0 copy-start.1
  15.0 0.0 copy-start
  15.0 0.1 collective-permute-start.4
  15.1 0.8 collective-permute-start.5
  15.9 0.5 collective-permute-start.6
  16.4 2.2 %collective-permute-start.7 = (bf16[128,512]{1,0:T(8,128)(2,1)S(1)}, bf16[128,512]{1,0:T(8,128)(2,1)S(1)}, u32[]{:S(2)}, u32[]{:S(2)}) collective-permute-start(bf16[128,512]{1,0:T(8,128)(2,1)S(1)} %collective-permute-done.1.refs_2_), channel_id=1, source_target_pairs={{0,16},{16,0},{1,17},{17,1},{2,18},{18,2},{3,19},{19,3},{4,20},{20... | collective-permute-start | bytes 393224 | tf_op jit(solution)/shard_map/ppermute | solution.py:25
  18.6 3.8 %collective-permute-done.5.refs_0_ = bf16[128,512]{1,0:T(8,128)(2,1)S(1)} collective-permute-done((bf16[128,512]{1,0:T(8,128)(2,1)S(1)}, bf16[128,512]{1,0:T(8,128)(2,1)S(1)}, u32[]{:S(2)}, u32[]{:S(2)}) %collective-permute-start.5) | collective-permute-done | bytes 131104 | tf_op jit(solution)/shard_map/ppermute | solution.py:35
  22.5 0.6 collective-permute-done.6.refs_1_
  23.0 1.7 %collective-permute-done.7.refs_2_ = bf16[128,512]{1,0:T(8,128)(2,1)S(1)} collective-permute-done((bf16[128,512]{1,0:T(8,128)(2,1)S(1)}, bf16[128,512]{1,0:T(8,128)(2,1)S(1)}, u32[]{:S(2)}, u32[]{:S(2)}) %collective-permute-start.7) | collective-permute-done | bytes 131104 | tf_op jit(solution)/shard_map/ppermute | solution.py:25
  24.7 0.0 collective-permute-start.10
  24.7 0.4 collective-permute-start.17
  25.1 1.2 %shard_map.112.sum_ref = f32[256,512]{1,0:T(8,128)S(1)} custom-call(s32[5]{0:T(128)S(1)} %stack.23.pos_ref, bf16[256,2048]{1,0:T(8,128)(2,1)S(1)} %shard_map.109.normed_ref, bf16[640,512]{1,0:T(8,128)(2,1)S(1)} %shard_map.111.w0_ref, bf16[640,512]{1,0:T(8,128)(2,1)S(1)} %collective-permute-done.4.w1_ref), custom_call_target="tpu_custom_call" | custom-call | flops 335544320 | bytes 1310720 | tf_op jit(solution)/shard_map/pallas_call | solution.py:43
  26.3 0.9 %shard_map.113.x0_ref = bf16[272,512]{1,0:T(8,128)(2,1)S(1)} custom-call(s32[5]{0:T(128)S(1)} %stack.23.pos_ref, bf16[256,2048]{1,0:T(8,128)(2,1)S(1)} %shard_map.109.normed_ref, f32[256,512]{1,0:T(8,128)S(1)} %shard_map.112.sum_ref, f32[16,256]{1,0:T(8,128)S(1)} %get-tuple-element.19.wt_ref, bf16[128,512]{1,0:T(8,128)(2,1)S(1)} %collective-permute-done.5.refs_0_, ...), custom_call_target="tpu_custom_call" | custom-call | flops 201326592 | bytes 786432 | tf_op jit(solution)/shard_map/pallas_call | solution.py:43
  27.3 0.3 collective-permute-start.11
  27.6 1.6 %collective-permute-start.13 = (bf16[272,512]{1,0:T(8,128)(2,1)S(1)}, bf16[272,512]{1,0:T(8,128)(2,1)S(1)}, u32[]{:S(2)}, u32[]{:S(2)}) collective-permute-start(bf16[272,512]{1,0:T(8,128)(2,1)S(1)} %shard_map.113.x0_ref), channel_id=1, source_target_pairs={{0,8},{4,12},{8,0},{12,4},{1,9},{5,13},{9,1},{13,5},{2,10},{6,14},... | collective-permute-start | bytes 835592 | tf_op jit(solution)/shard_map/ppermute | solution.py:25
  29.2 1.6 %collective-permute-done.17.refs_1_ = bf16[128,512]{1,0:T(8,128)(2,1)S(1)} collective-permute-done((bf16[128,512]{1,0:T(8,128)(2,1)S(1)}, bf16[128,512]{1,0:T(8,128)(2,1)S(1)}, u32[]{:S(2)}, u32[]{:S(2)}) %collective-permute-start.17) | collective-permute-done | bytes 131104 | tf_op jit(solution)/shard_map/ppermute | solution.py:25
  30.8 0.1 shard_map.118.refs_1_
  30.9 0.3 collective-permute-start.18
  31.2 4.8 %collective-permute-start.19 = (bf16[512,256]{1,0:T(8,128)(2,1)S(1)}, bf16[512,256]{1,0:T(8,128)(2,1)S(1)}, u32[]{:S(2)}, u32[]{:S(2)}) collective-permute-start(bf16[512,256]{1,0:T(8,128)(2,1)S(1)} %shard_map.118.refs_1_), channel_id=1, source_target_pairs={{0,2},{1,3},{2,0},{3,1},{4,6},{5,7},{6,4},{7,5},{8,10},{9,11},{10,... | collective-permute-start | bytes 786440 | tf_op jit(solution)/shard_map/ppermute | solution.py:25
  36.0 7.3 %collective-permute-done.18.refs_2_ = bf16[512,256]{1,0:T(8,128)(2,1)S(1)} collective-permute-done((bf16[512,256]{1,0:T(8,128)(2,1)S(1)}, bf16[512,256]{1,0:T(8,128)(2,1)S(1)}, u32[]{:S(2)}, u32[]{:S(2)}) %collective-permute-start.18) | collective-permute-done | bytes 262176 | tf_op jit(solution)/shard_map/ppermute | solution.py:25
  43.3 11.1 %collective-permute-done.19.refs_3_ = bf16[512,256]{1,0:T(8,128)(2,1)S(1)} collective-permute-done((bf16[512,256]{1,0:T(8,128)(2,1)S(1)}, bf16[512,256]{1,0:T(8,128)(2,1)S(1)}, u32[]{:S(2)}, u32[]{:S(2)}) %collective-permute-start.19) | collective-permute-done | bytes 262176 | tf_op jit(solution)/shard_map/ppermute | solution.py:25
  54.4 0.5 collective-permute-start.23
  54.9 0.1 collective-permute-start.24
  54.9 0.4 collective-permute-start.14
  55.4 6.2 %shard_map.114 = (f32[256,512]{1,0:T(8,128)S(1)}, bf16[256,512]{1,0:T(8,128)(2,1)S(1)}) custom-call(s32[5]{0:T(128)S(1)} %stack.23.pos_ref, bf16[272,512]{1,0:T(8,128)(2,1)S(1)} %shard_map.113.x0_ref, bf16[272,512]{1,0:T(8,128)(2,1)S(1)} %collective-permute-done.11.x1_ref, bf16[4,512,768]{2,1,0:T(8,128)(2,1)S(1)} %copy-done, ...), custom_call_target="tpu_custom_call" | custom-call | flops 4831838208 | bytes 9437184 | tf_op jit(solution)/shard_map/pallas_call | solution.py:43
  61.6 3.5 %shard_map.119 = (bf16[128,512]{1,0:T(8,128)(2,1)S(1)}, bf16[128,512]{1,0:T(8,128)(2,1)S(1)}) custom-call(s32[5]{0:T(128)S(1)} %stack.23.pos_ref, bf16[272,512]{1,0:T(8,128)(2,1)S(1)} %collective-permute-done.13.x0_ref, bf16[272,512]{1,0:T(8,128)(2,1)S(1)} %collective-permute-done.14.x1_ref, bf16[4,512,768]{2,1,0:T(8,128)(2,1)S(1)} %copy-done, ...), custom_call_target="tpu_custom_call" | custom-call | flops 2415919104 | bytes 9437184 | tf_op jit(solution)/shard_map/pallas_call | solution.py:43
  65.1 0.1 collective-permute-start.25
  65.3 2.1 %shard_map.115 = (bf16[256,512]{1,0:T(8,128)(2,1)S(1)}, f32[256,8]{1,0:T(8,128)S(1)}, f32[256,512]{1,0:T(8,128)S(1)}) custom-call(s32[5]{0:T(128)S(1)} %stack.23.pos_ref, bf16[272,512]{1,0:T(8,128)(2,1)S(1)} %collective-permute-done.13.x0_ref, bf16[272,512]{1,0:T(8,128)(2,1)S(1)} %collective-permute-done.14.x1_ref, bf16[4,512,768]{2,1,0:T(8,128)(2,1)S(1)} %copy-done, ...), custom_call_target="tpu_custom_call" | custom-call | flops 1207959552 | bytes 4718592 | tf_op jit(solution)/shard_map/pallas_call | solution.py:43
  67.4 1.6 %shard_map.116 = (bf16[128,512]{1,0:T(8,128)(2,1)S(1)}, bf16[128,512]{1,0:T(8,128)(2,1)S(1)}) custom-call(bf16[256,512]{1,0:T(8,128)(2,1)S(1)} %get-tuple-element.23.x_ref, f32[256,8]{1,0:T(8,128)S(1)} %get-tuple-element.24.col_ref, f32[256,512]{1,0:T(8,128)S(1)} %get-tuple-element.25.sum_ref, bf16[4,512,768]{2,1,0:T(8,128)(2,1)S(1)} %copy-done, ...), custom_call_target="tpu_custom_call" | custom-call | flops 1207959552 | bytes 4718592 | tf_op jit(solution)/shard_map/pallas_call | solution.py:43
  69.0 0.5 collective-permute-start.12
  69.5 0.1 collective-permute-start.15
  69.6 1.2 %collective-permute-done.15.b_ref = bf16[128,512]{1,0:T(8,128)(2,1)S(1)} collective-permute-done((bf16[128,512]{1,0:T(8,128)(2,1)S(1)}, bf16[128,512]{1,0:T(8,128)(2,1)S(1)}, u32[]{:S(2)}, u32[]{:S(2)}) %collective-permute-start.15) | collective-permute-done | bytes 131104 | tf_op jit(solution)/shard_map/ppermute | solution.py:25
  70.8 0.5 collective-permute-start.26
  71.4 1.6 %collective-permute-start.16 = (bf16[128,512]{1,0:T(8,128)(2,1)S(1)}, bf16[128,512]{1,0:T(8,128)(2,1)S(1)}, u32[]{:S(2)}, u32[]{:S(2)}) collective-permute-start(bf16[128,512]{1,0:T(8,128)(2,1)S(1)} %shard_map.117), channel_id=1, source_target_pairs={{0,8},{4,12},{8,0},{12,4},{1,9},{5,13},{9,1},{13,5},{2,10},{6,14},... | collective-permute-start | bytes 393224 | tf_op jit(solution)/shard_map/ppermute | solution.py:25
  73.0 4.2 %collective-permute-done.26.refs_0_ = bf16[128,512]{1,0:T(8,128)(2,1)S(1)} collective-permute-done((bf16[128,512]{1,0:T(8,128)(2,1)S(1)}, bf16[128,512]{1,0:T(8,128)(2,1)S(1)}, u32[]{:S(2)}, u32[]{:S(2)}) %collective-permute-start.26) | collective-permute-done | bytes 131104 | tf_op jit(solution)/shard_map/ppermute | solution.py:25
  77.2 1.8 %shard_map.121.refs_9_ = bf16[256,2048]{1,0:T(8,128)(2,1)} custom-call(s32[5]{0:T(128)S(1)} %stack.23.pos_ref, f32[256,512]{1,0:T(8,128)S(1)} %get-tuple-element.21.near_ref, bf16[256,512]{1,0:T(8,128)(2,1)S(1)} %collective-permute-done.12.core_ref, bf16[128,512]{1,0:T(8,128)(2,1)S(1)} %collective-permute-done.26.refs_0_, ...), custom_call_target="tpu_custom_call" | custom-call | flops 268435456 | bytes 2097152 | tf_op jit(solution)/shard_map/pallas_call | solution.py:43
  79.0 0.4 collective-permute-done.16.refs_0_
  79.4 1.8 %shard_map.122 = bf16[256,2048]{1,0:T(8,128)(2,1)} custom-call(s32[5]{0:T(128)S(1)} %stack.23.pos_ref, f32[256,512]{1,0:T(8,128)S(1)} %get-tuple-element.21.near_ref, bf16[256,512]{1,0:T(8,128)(2,1)S(1)} %collective-permute-done.12.core_ref, bf16[128,512]{1,0:T(8,128)(2,1)S(1)} %collective-permute-done.16.refs_0_, ...), custom_call_target="tpu_custom_call", output_to_operand_aliasing={{}: (12, {})} | custom-call | flops 268435456 | bytes 2097152 | tf_op jit(solution)/shard_map/pallas_call | solution.py:43
  (27 shorter events, 0.2 us)
Async XLA Ops:
  0.0 8.6 %collective-permute-start = (bf16[128,512]{1,0:T(8,128)(2,1)}, bf16[128,512]{1,0:T(8,128)(2,1)S(1)}, u32[]{:S(2)}, u32[]{:S(2)}) collective-permute-start(bf16[128,512]{1,0:T(8,128)(2,1)} %down_hbm.1), channel_id=1, source_target_pairs={{0,1},{1,0},{2,3},{3,2},{4,5},{5,4},{6,7},{7,6},{8,9},{9,8},{10,11... | collective-permute-start | bytes 393224 | tf_op jit(solution)/shard_map/ppermute | solution.py:25
  3.1 11.8 %collective-permute-start.1 = (bf16[128,512]{1,0:T(8,128)(2,1)}, bf16[128,512]{1,0:T(8,128)(2,1)S(1)}, u32[]{:S(2)}, u32[]{:S(2)}) collective-permute-start(bf16[128,512]{1,0:T(8,128)(2,1)} %down_hbm.1), channel_id=1, source_target_pairs={{0,2},{1,3},{2,0},{3,1},{16,19},{17,18},{18,17},{19,16},{4,6},{5,7... | collective-permute-start | bytes 393224 | tf_op jit(solution)/shard_map/ppermute | solution.py:35
  5.6 9.3 %collective-permute-start.2 = (bf16[128,512]{1,0:T(8,128)(2,1)}, bf16[128,512]{1,0:T(8,128)(2,1)S(1)}, u32[]{:S(2)}, u32[]{:S(2)}) collective-permute-start(bf16[128,512]{1,0:T(8,128)(2,1)} %down_hbm.1), channel_id=1, source_target_pairs={{0,8},{4,12},{8,0},{12,4},{1,9},{5,13},{9,1},{13,5},{2,10},{6,14},... | collective-permute-start | bytes 393224 | tf_op jit(solution)/shard_map/ppermute | solution.py:25
  8.6 6.3 %collective-permute-start.3 = (bf16[128,512]{1,0:T(8,128)(2,1)S(1)}, bf16[128,512]{1,0:T(8,128)(2,1)S(1)}, u32[]{:S(2)}, u32[]{:S(2)}) collective-permute-start(bf16[128,512]{1,0:T(8,128)(2,1)S(1)} %collective-permute-done.refs_1_), channel_id=1, source_target_pairs={{0,8},{4,12},{8,0},{12,4},{1,9},{5,13},{9,1},{13,5},{2,10},{6,14},... | collective-permute-start | bytes 393224 | tf_op jit(solution)/shard_map/ppermute | solution.py:25
  12.7 12.0 %copy-start.2 = (bf16[128,512]{1,0:T(8,128)(2,1)S(1)}, bf16[128,512]{1,0:T(8,128)(2,1)}, u32[]{:S(2)}) copy-start(bf16[128,512]{1,0:T(8,128)(2,1)} %up_hbm.1) | copy-start | bytes 393220
  14.9 40.5 %copy-start.1 = (bf16[4,512,768]{2,1,0:T(8,128)(2,1)S(1)}, bf16[4,512,768]{2,1,0:T(8,128)(2,1)}, u32[]{:S(2)}) copy-start(bf16[4,512,768]{2,1,0:T(8,128)(2,1)} %u_ref.7) | copy-start | bytes 9437188
  15.0 40.4 %copy-start = (bf16[4,512,768]{2,1,0:T(8,128)(2,1)S(1)}, bf16[4,512,768]{2,1,0:T(8,128)(2,1)}, u32[]{:S(2)}) copy-start(bf16[4,512,768]{2,1,0:T(8,128)(2,1)} %g_ref.7) | copy-start | bytes 9437188
  15.0 10.1 %collective-permute-start.4 = (bf16[640,512]{1,0:T(8,128)(2,1)S(1)}, bf16[640,512]{1,0:T(8,128)(2,1)S(1)}, u32[]{:S(2)}, u32[]{:S(2)}) collective-permute-start(bf16[640,512]{1,0:T(8,128)(2,1)S(1)} %shard_map.111.w0_ref), channel_id=1, source_target_pairs={{0,4},{4,0},{8,12},{12,8},{1,5},{5,1},{9,13},{13,9},{2,6},{6,2},{1... | collective-permute-start | bytes 1966088 | tf_op jit(solution)/shard_map/ppermute | solution.py:25
  15.1 7.4 %collective-permute-start.5 = (bf16[128,512]{1,0:T(8,128)(2,1)S(1)}, bf16[128,512]{1,0:T(8,128)(2,1)S(1)}, u32[]{:S(2)}, u32[]{:S(2)}) collective-permute-start(bf16[128,512]{1,0:T(8,128)(2,1)S(1)} %collective-permute-done.1.refs_2_), channel_id=1, source_target_pairs={{0,24},{4,28},{8,16},{12,20},{16,8},{20,12},{24,0},{28,4},{1,25},{... | collective-permute-start | bytes 393224 | tf_op jit(solution)/shard_map/ppermute | solution.py:35
  15.9 7.2 %collective-permute-start.6 = (bf16[128,512]{1,0:T(8,128)(2,1)S(1)}, bf16[128,512]{1,0:T(8,128)(2,1)S(1)}, u32[]{:S(2)}, u32[]{:S(2)}) collective-permute-start(bf16[128,512]{1,0:T(8,128)(2,1)S(1)} %collective-permute-done.1.refs_2_), channel_id=1, source_target_pairs={{0,8},{4,12},{8,0},{12,4},{1,9},{5,13},{9,1},{13,5},{2,10},{6,14},... | collective-permute-start | bytes 393224 | tf_op jit(solution)/shard_map/ppermute | solution.py:25
  16.4 8.3 %collective-permute-start.7 = (bf16[128,512]{1,0:T(8,128)(2,1)S(1)}, bf16[128,512]{1,0:T(8,128)(2,1)S(1)}, u32[]{:S(2)}, u32[]{:S(2)}) collective-permute-start(bf16[128,512]{1,0:T(8,128)(2,1)S(1)} %collective-permute-done.1.refs_2_), channel_id=1, source_target_pairs={{0,16},{16,0},{1,17},{17,1},{2,18},{18,2},{3,19},{19,3},{4,20},{20... | collective-permute-start | bytes 393224 | tf_op jit(solution)/shard_map/ppermute | solution.py:25
  22.5 3.8 %collective-permute-start.8 = (bf16[128,512]{1,0:T(8,128)(2,1)S(1)}, bf16[128,512]{1,0:T(8,128)(2,1)S(1)}, u32[]{:S(2)}, u32[]{:S(2)}) collective-permute-start(bf16[128,512]{1,0:T(8,128)(2,1)S(1)} %collective-permute-done.5.refs_0_), channel_id=1, source_target_pairs={{0,4},{4,0},{8,12},{12,8},{1,5},{5,1},{9,13},{13,9},{2,6},{6,2},{1... | collective-permute-start | bytes 393224 | tf_op jit(solution)/shard_map/ppermute | solution.py:25
  23.0 3.3 %collective-permute-start.9 = (bf16[128,512]{1,0:T(8,128)(2,1)S(1)}, bf16[128,512]{1,0:T(8,128)(2,1)S(1)}, u32[]{:S(2)}, u32[]{:S(2)}) collective-permute-start(bf16[128,512]{1,0:T(8,128)(2,1)S(1)} %collective-permute-done.6.refs_1_), channel_id=1, source_target_pairs={{0,4},{4,0},{8,12},{12,8},{1,5},{5,1},{9,13},{13,9},{2,6},{6,2},{1... | collective-permute-start | bytes 393224 | tf_op jit(solution)/shard_map/ppermute | solution.py:25
  24.7 1.6 %collective-permute-start.10 = (bf16[128,512]{1,0:T(8,128)(2,1)S(1)}, bf16[128,512]{1,0:T(8,128)(2,1)S(1)}, u32[]{:S(2)}, u32[]{:S(2)}) collective-permute-start(bf16[128,512]{1,0:T(8,128)(2,1)S(1)} %collective-permute-done.7.refs_2_), channel_id=1, source_target_pairs={{0,4},{4,0},{8,12},{12,8},{1,5},{5,1},{9,13},{13,9},{2,6},{6,2},{1... | collective-permute-start | bytes 393224 | tf_op jit(solution)/shard_map/ppermute | solution.py:25
  24.7 6.0 %collective-permute-start.17 = (bf16[128,512]{1,0:T(8,128)(2,1)S(1)}, bf16[128,512]{1,0:T(8,128)(2,1)S(1)}, u32[]{:S(2)}, u32[]{:S(2)}) collective-permute-start(bf16[128,512]{1,0:T(8,128)(2,1)S(1)} %copy-done.2), channel_id=1, source_target_pairs={{0,8},{4,12},{8,0},{12,4},{1,9},{5,13},{9,1},{13,5},{2,10},{6,14},... | collective-permute-start | bytes 393224 | tf_op jit(solution)/shard_map/ppermute | solution.py:25
  27.3 27.6 %collective-permute-start.11 = (bf16[272,512]{1,0:T(8,128)(2,1)S(1)}, bf16[272,512]{1,0:T(8,128)(2,1)S(1)}, u32[]{:S(2)}, u32[]{:S(2)}) collective-permute-start(bf16[272,512]{1,0:T(8,128)(2,1)S(1)} %shard_map.113.x0_ref), channel_id=1, source_target_pairs={{0,4},{4,0},{8,12},{12,8},{1,5},{5,1},{9,13},{13,9},{2,6},{6,2},{1... | collective-permute-start | bytes 835592 | tf_op jit(solution)/shard_map/ppermute | solution.py:25
  27.6 27.4 %collective-permute-start.13 = (bf16[272,512]{1,0:T(8,128)(2,1)S(1)}, bf16[272,512]{1,0:T(8,128)(2,1)S(1)}, u32[]{:S(2)}, u32[]{:S(2)}) collective-permute-start(bf16[272,512]{1,0:T(8,128)(2,1)S(1)} %shard_map.113.x0_ref), channel_id=1, source_target_pairs={{0,8},{4,12},{8,0},{12,4},{1,9},{5,13},{9,1},{13,5},{2,10},{6,14},... | collective-permute-start | bytes 835592 | tf_op jit(solution)/shard_map/ppermute | solution.py:25
  30.9 12.4 %collective-permute-start.18 = (bf16[512,256]{1,0:T(8,128)(2,1)S(1)}, bf16[512,256]{1,0:T(8,128)(2,1)S(1)}, u32[]{:S(2)}, u32[]{:S(2)}) collective-permute-start(bf16[512,256]{1,0:T(8,128)(2,1)S(1)} %shard_map.118.refs_1_), channel_id=1, source_target_pairs={{0,1},{1,0},{2,3},{3,2},{4,5},{5,4},{6,7},{7,6},{8,9},{9,8},{10,11... | collective-permute-start | bytes 786440 | tf_op jit(solution)/shard_map/ppermute | solution.py:25
  31.2 23.2 %collective-permute-start.19 = (bf16[512,256]{1,0:T(8,128)(2,1)S(1)}, bf16[512,256]{1,0:T(8,128)(2,1)S(1)}, u32[]{:S(2)}, u32[]{:S(2)}) collective-permute-start(bf16[512,256]{1,0:T(8,128)(2,1)S(1)} %shard_map.118.refs_1_), channel_id=1, source_target_pairs={{0,2},{1,3},{2,0},{3,1},{4,6},{5,7},{6,4},{7,5},{8,10},{9,11},{10,... | collective-permute-start | bytes 786440 | tf_op jit(solution)/shard_map/ppermute | solution.py:25
  36.0 18.4 %collective-permute-start.20 = (bf16[512,256]{1,0:T(8,128)(2,1)S(1)}, bf16[512,256]{1,0:T(8,128)(2,1)S(1)}, u32[]{:S(2)}, u32[]{:S(2)}) collective-permute-start(bf16[512,256]{1,0:T(8,128)(2,1)S(1)} %shard_map.118.refs_1_), channel_id=1, source_target_pairs={{0,3},{1,2},{2,1},{3,0},{4,7},{5,6},{6,5},{7,4},{8,11},{9,10},{10,... | collective-permute-start | bytes 786440 | tf_op jit(solution)/shard_map/ppermute | solution.py:25
  43.3 25.7 %collective-permute-start.21 = (bf16[512,256]{1,0:T(8,128)(2,1)S(1)}, bf16[512,256]{1,0:T(8,128)(2,1)S(1)}, u32[]{:S(2)}, u32[]{:S(2)}) collective-permute-start(bf16[512,256]{1,0:T(8,128)(2,1)S(1)} %shard_map.118.refs_1_), channel_id=1, source_target_pairs={{0,4},{4,0},{8,12},{12,8},{1,5},{5,1},{9,13},{13,9},{2,6},{6,2},{1... | collective-permute-start | bytes 786440 | tf_op jit(solution)/shard_map/ppermute | solution.py:25
  54.3 17.1 %collective-permute-start.22 = (bf16[512,256]{1,0:T(8,128)(2,1)S(1)}, bf16[512,256]{1,0:T(8,128)(2,1)S(1)}, u32[]{:S(2)}, u32[]{:S(2)}) collective-permute-start(bf16[512,256]{1,0:T(8,128)(2,1)S(1)} %collective-permute-done.18.refs_2_), channel_id=1, source_target_pairs={{0,4},{4,0},{8,12},{12,8},{1,5},{5,1},{9,13},{13,9},{2,6},{6,2},{1... | collective-permute-start | bytes 786440 | tf_op jit(solution)/shard_map/ppermute | solution.py:25
  54.4 18.6 %collective-permute-start.23 = (bf16[512,256]{1,0:T(8,128)(2,1)S(1)}, bf16[512,256]{1,0:T(8,128)(2,1)S(1)}, u32[]{:S(2)}, u32[]{:S(2)}) collective-permute-start(bf16[512,256]{1,0:T(8,128)(2,1)S(1)} %collective-permute-done.19.refs_3_), channel_id=1, source_target_pairs={{0,4},{4,0},{8,12},{12,8},{1,5},{5,1},{9,13},{13,9},{2,6},{6,2},{1... | collective-permute-start | bytes 786440 | tf_op jit(solution)/shard_map/ppermute | solution.py:25
  54.9 18.1 %collective-permute-start.24 = (bf16[512,256]{1,0:T(8,128)(2,1)S(1)}, bf16[512,256]{1,0:T(8,128)(2,1)S(1)}, u32[]{:S(2)}, u32[]{:S(2)}) collective-permute-start(bf16[512,256]{1,0:T(8,128)(2,1)S(1)} %collective-permute-done.20.refs_4_), channel_id=1, source_target_pairs={{0,4},{4,0},{8,12},{12,8},{1,5},{5,1},{9,13},{13,9},{2,6},{6,2},{1... | collective-permute-start | bytes 786440 | tf_op jit(solution)/shard_map/ppermute | solution.py:25
  54.9 6.7 %collective-permute-start.14 = (bf16[272,512]{1,0:T(8,128)(2,1)S(1)}, bf16[272,512]{1,0:T(8,128)(2,1)S(1)}, u32[]{:S(2)}, u32[]{:S(2)}) collective-permute-start(bf16[272,512]{1,0:T(8,128)(2,1)S(1)} %collective-permute-done.13.x0_ref), channel_id=1, source_target_pairs={{0,4},{4,0},{8,12},{12,8},{1,5},{5,1},{9,13},{13,9},{2,6},{6,2},{1... | collective-permute-start | bytes 835592 | tf_op jit(solution)/shard_map/ppermute | solution.py:25
  65.1 4.3 %collective-permute-start.25 = (bf16[128,512]{1,0:T(8,128)(2,1)S(1)}, bf16[128,512]{1,0:T(8,128)(2,1)S(1)}, u32[]{:S(2)}, u32[]{:S(2)}) collective-permute-start(bf16[128,512]{1,0:T(8,128)(2,1)S(1)} %get-tuple-element.30), channel_id=1, source_target_pairs={{0,4},{4,0},{8,12},{12,8},{1,5},{5,1},{9,13},{13,9},{2,6},{6,2},{1... | collective-permute-start | bytes 393224 | tf_op jit(solution)/shard_map/ppermute | solution.py:25
  69.0 4.0 %collective-permute-start.12 = (bf16[256,512]{1,0:T(8,128)(2,1)S(1)}, bf16[256,512]{1,0:T(8,128)(2,1)S(1)}, u32[]{:S(2)}, u32[]{:S(2)}) collective-permute-start(bf16[256,512]{1,0:T(8,128)(2,1)S(1)} %get-tuple-element.22), channel_id=1, source_target_pairs={{0,4},{4,0},{8,12},{12,8},{1,5},{5,1},{9,13},{13,9},{2,6},{6,2},{1... | collective-permute-start | bytes 786440 | tf_op jit(solution)/shard_map/ppermute | solution.py:25
  69.5 1.3 %collective-permute-start.15 = (bf16[128,512]{1,0:T(8,128)(2,1)S(1)}, bf16[128,512]{1,0:T(8,128)(2,1)S(1)}, u32[]{:S(2)}, u32[]{:S(2)}) collective-permute-start(bf16[128,512]{1,0:T(8,128)(2,1)S(1)} %get-tuple-element.27), channel_id=1, source_target_pairs={{0,4},{4,0},{8,12},{12,8},{1,5},{5,1},{9,13},{13,9},{2,6},{6,2},{1... | collective-permute-start | bytes 393224 | tf_op jit(solution)/shard_map/ppermute | solution.py:25
  70.8 6.4 %collective-permute-start.26 = (bf16[128,512]{1,0:T(8,128)(2,1)S(1)}, bf16[128,512]{1,0:T(8,128)(2,1)S(1)}, u32[]{:S(2)}, u32[]{:S(2)}) collective-permute-start(bf16[128,512]{1,0:T(8,128)(2,1)S(1)} %shard_map.120), channel_id=1, source_target_pairs={{0,8},{4,12},{8,0},{12,4},{1,9},{5,13},{9,1},{13,5},{2,10},{6,14},... | collective-permute-start | bytes 393224 | tf_op jit(solution)/shard_map/ppermute | solution.py:25
  71.4 8.0 %collective-permute-start.16 = (bf16[128,512]{1,0:T(8,128)(2,1)S(1)}, bf16[128,512]{1,0:T(8,128)(2,1)S(1)}, u32[]{:S(2)}, u32[]{:S(2)}) collective-permute-start(bf16[128,512]{1,0:T(8,128)(2,1)S(1)} %shard_map.117), channel_id=1, source_target_pairs={{0,8},{4,12},{8,0},{12,4},{1,9},{5,13},{9,1},{13,5},{2,10},{6,14},... | collective-permute-start | bytes 393224 | tf_op jit(solution)/shard_map/ppermute | solution.py:25

commit v4 on v3

--- a/solution.py
+++ b/solution.py
@@ -12,8 +12,13 @@
 BF16 = jnp.bfloat16
 
 VM = pl.BlockSpec(memory_space=pltpu.VMEM)
-SM = pl.BlockSpec(memory_space=pltpu.SMEM)
 AN = pl.BlockSpec(memory_space=pl.ANY)
+
+
+def here(copies):
+    e = lax.axis_index("expert")
+    rep = lax.axis_index("replica") if copies > 1 else 0
+    return lax.rem(e, 2), e // 2, rep, lax.axis_index("groups")
 
 
 def in_hbm(x):
@@ -52,7 +57,7 @@
     )(*operands)
 
 
-def norm_kernel(pos_ref, tok_hbm, gain_hbm, normed_ref, tok_ref, gain_ref, sem):
+def norm_kernel(tok_hbm, gain_hbm, normed_ref, tok_ref, gain_ref, sem):
     pairs = ((tok_hbm, tok_ref), (gain_hbm, gain_ref))
     copies = [pltpu.make_async_copy(src, dst, sem.at[i]) for i, (src, dst) in enumerate(pairs)]
     for copy in copies:
@@ -108,8 +113,8 @@
         refs[-1][i * depth:(i + 1) * depth, :] = x_ref[...]
 
 
-def pick(chunks, other, depth, copies, pos_ref, normed_ref, x_ref):
-    core, half, rep, group = pos_ref[0], pos_ref[1], pos_ref[2], pos_ref[4]
+def pick(chunks, other, depth, copies, normed_ref, x_ref):
+    core, half, rep, group = here(copies)
     for i, (a, b) in enumerate(chunks):
         if b == "A":
             b = 2 + group
@@ -119,20 +124,20 @@
         x_ref[:, i * depth:(i + 1) * depth] = normed_ref[:, pl.ds(pl.multiple_of(at, depth), depth)]
 
 
-def early_kernel(chunks, depth, copies, pos_ref, normed_ref, w0_ref, w1_ref, out_ref, x_ref):
-    pick(chunks, 0, depth, copies, pos_ref, normed_ref, x_ref.at[0])
-    pick(chunks, 1, depth, copies, pos_ref, normed_ref, x_ref.at[1])
+def early_kernel(chunks, depth, copies, normed_ref, w0_ref, w1_ref, out_ref, x_ref):
+    pick(chunks, 0, depth, copies, normed_ref, x_ref.at[0])
+    pick(chunks, 1, depth, copies, normed_ref, x_ref.at[1])
     out_ref[...] = (jnp.dot(x_ref[0], w0_ref[...], preferred_element_type=F32)
                     + jnp.dot(x_ref[1], w1_ref[...], preferred_element_type=F32))
 
 
-def late_kernel(chunks, copies, pos_ref, normed_ref, sum_ref, wt_ref, *refs):
+def late_kernel(chunks, copies, normed_ref, sum_ref, wt_ref, *refs):
     w_refs, (out_ref, x_ref, w_ref) = refs[:-3], refs[-3:]
     n = len(chunks)
     rows = normed_ref.shape[0]
     depth = w_refs[0].shape[0]
     for c in range(2):
-        pick(chunks, c, depth, copies, pos_ref, normed_ref, x_ref.at[:, c * n * depth:(c + 1) * n * depth])
+        pick(chunks, c, depth, copies, normed_ref, x_ref.at[:, c * n * depth:(c + 1) * n * depth])
     for i, chunk in enumerate(w_refs):
         w_ref[i * depth:(i + 1) * depth, :] = chunk[...]
     out_ref[:rows, :] = (sum_ref[...] + jnp.dot(x_ref[...], w_ref[...],
@@ -157,53 +162,33 @@
     wt = (pay_ref[rows:, at:at + size].astype(F32)
           + pay_ref[rows:, rows + at:rows + at + size].astype(F32))
     sub = lax.broadcasted_iota(jnp.int32, wt.shape, 0)
-    picked = [jnp.sum(jnp.where(sub == me * local + j, wt, 0.0), axis=0, keepdims=True)
-              for j in range(local)]
-    pad = jnp.zeros((-local % 8, size), F32)
-    return jnp.concatenate(picked + [pad], axis=0).T
-
-
-def near_kernel(local, pos_ref, x0_ref, x1_ref, g_ref, u_ref, d_ref, o0_ref, o1_ref, acc_ref):
-    rows = o0_ref.shape[0]
-    cols = [columns(pos_ref[3], local, p, 0, rows) for p in (x0_ref, x1_ref)]
-    for j in range(local):
-        for x_ref, sum_ref, col in ((x0_ref, o0_ref, cols[0]), (x1_ref, acc_ref, cols[1])):
-            part = expert(x_ref[:rows, :], col[:, j:j + 1], g_ref[j], u_ref[j], d_ref[j])
-            sum_ref[...] = part if j == 0 else sum_ref[...] + part
-    o1_ref[...] = acc_ref[...].astype(BF16)
-
-
-def far_open_kernel(local, at, span, pos_ref, x0_ref, x1_ref, g_ref, u_ref, d_ref, x_ref, col_ref, acc_ref):
-    size = x_ref.shape[0] // 2
-    x_ref[:size, :] = x0_ref[at:at + size, :]
-    x_ref[size:, :] = x1_ref[at:at + size, :]
-    cols = jnp.concatenate([columns(pos_ref[3], local, p, at, size) for p in (x0_ref, x1_ref)], axis=0)
-    col_ref[...] = cols
+    picked = [jnp.sum(jnp.where(sub == (me ^ c) * local + j, wt, 0.0), axis=0, keepdims=True)
+              for c in range(2) for j in range(local)]
+    pad = [jnp.zeros((-len(picked) % 8, size), F32)] if len(picked) % 8 else []
+    return jnp.concatenate(picked + pad, axis=0).T
+
+
+def run_experts(span, at, size, pay_ref, w_refs, out_ref, start_ref=None):
+    local = w_refs[0].shape[0]
+    cols = columns(lax.axis_index("expert"), local, pay_ref, at, size)
+    x = pay_ref[at:at + size, :]
     for j in span:
-        part = expert(x_ref[...], cols[:, j:j + 1], g_ref[j], u_ref[j], d_ref[j])
-        acc_ref[...] = part if j == 0 else acc_ref[...] + part
-
-
-def far_close_kernel(span, x_ref, col_ref, sum_ref, g_ref, u_ref, d_ref, o0_ref, o1_ref, acc_ref):
-    size = o0_ref.shape[0]
-    for j in span:
-        part = expert(x_ref[...], col_ref[:, j:j + 1], g_ref[j], u_ref[j], d_ref[j])
-        acc_ref[...] = (sum_ref if j == span[0] else acc_ref)[...] + part
-    o0_ref[...] = acc_ref[:size, :].astype(BF16)
-    o1_ref[...] = acc_ref[size:, :].astype(BF16)
-
-
-def far_kernel(local, at, pos_ref, x0_ref, x1_ref, g_ref, u_ref, d_ref, o0_ref, o1_ref, x_ref, col_ref,
-               acc_ref):
-    size = o0_ref.shape[0]
-    far_open_kernel(local, at, range(local), pos_ref, x0_ref, x1_ref, g_ref, u_ref, d_ref, x_ref, col_ref,
-                    acc_ref)
-    o0_ref[...] = acc_ref[:size, :].astype(BF16)
-    o1_ref[...] = acc_ref[size:, :].astype(BF16)
-
-
-def add_kernel(a_ref, b_ref, o_ref):
-    o_ref[...] = (a_ref[...].astype(F32) + b_ref[...].astype(F32)).astype(BF16)
+        refs = w_refs[:3] if j < local else w_refs[3:]
+        part = expert(x, cols[:, j:j + 1], *(ref[j % local] for ref in refs))
+        if j == span[0]:
+            out_ref[...] = part if start_ref is None else start_ref[at:at + size, :] + part
+        else:
+            out_ref[...] += part
+
+
+def near_kernel(span, pay_ref, *refs):
+    run_experts(span, 0, refs[-1].shape[0], pay_ref, refs[:6], refs[-1])
+
+
+def far_kernel(span, at, pay_ref, sum_ref, *refs):
+    out_ref, acc_ref = refs[-2:]
+    run_experts(span, at, out_ref.shape[0], pay_ref, refs[:6], acc_ref, sum_ref)
+    out_ref[...] = acc_ref[...].astype(BF16)
 
 
 def join_kernel(*refs):
@@ -212,11 +197,11 @@
         refs[-1][:, i * depth:(i + 1) * depth] = x_ref[...].T
 
 
-def final_kernel(n_back, at, chunks, copies, depth, pos_ref, near_ref, core_ref, *refs):
+def final_kernel(n_back, at, chunks, copies, depth, near_ref, *refs):
     out_ref, rows_ref, sem = refs[-3:]
-    half, rep, core = pos_ref[1], pos_ref[2], pos_ref[0]
+    core, half, rep, _ = here(copies)
     size = rows_ref.shape[0]
-    total = near_ref[at:at + size, :] + core_ref[at:at + size, :].astype(F32)
+    total = near_ref[at:at + size, :]
     for s_ref in refs[:n_back]:
         total = total + s_ref[...].astype(F32)
     merged = total.astype(BF16)
@@ -252,11 +237,6 @@
         up_proj = lax.all_gather(up_proj, "replica", axis=0, tiled=True)
         depth, spread = wide, 1
     experts = shards * local
-    g = lax.axis_index("groups")
-    e = lax.axis_index("expert")
-    r = lax.axis_index("replica")
-    pos = jnp.stack([e % 2, e // 2, r if spread > 1 else 0 * r, e, g]).astype(jnp.int32)
-
     down = {(0, 0): down_proj}
     if spread == groups + 2 and groups == 2:
         near_z = swap(down_proj, "replica", 1)
@@ -281,8 +261,8 @@
         ups_x = [swap(up_proj, "expert", 2 * a) for a in range(1, chips)]
 
     normed = kernel(
-        norm_kernel, shape((rows, width)), (pos, in_hbm(tokens), in_hbm(norm_gain.reshape(1, width))),
-        [SM] + [AN] * 2, 16, 8 * rows * width, 4 * rows * width,
+        norm_kernel, shape((rows, width)), (in_hbm(tokens), in_hbm(norm_gain.reshape(1, width))),
+        [AN] * 2, 16, 8 * rows * width, 4 * rows * width,
         [pltpu.VMEM((rows, width), BF16), pltpu.VMEM((1, width), F32), pltpu.SemaphoreType.DMA((2,))])
     wt, own_down, own_up, last = kernel(
         functools.partial(gate_kernel, top),
@@ -294,7 +274,8 @@
          pltpu.VMEM((top, rows), jnp.int32), pltpu.VMEM((top, rows), jnp.int32),
          pltpu.SemaphoreType.DMA((7,))])
     down[(0, 0)] = own_down
-    weights = (expert_gate, expert_up, last)
+    weights = (expert_gate, expert_up, last, *[
+        swap(w, "expert", 1) for w in (expert_gate, expert_up, expert_down)])
 
     late = [k for k in down if (k[1] == "A" and k[0]) or k[1] == "B"] or list(down)[-1:]
     early = [k for k in down if k not in late]
@@ -306,51 +287,36 @@
     late_core = [swap(down[k], "expert", 1) for k in late]
     opened = kernel(
         functools.partial(early_kernel, early, depth, spread), shape((rows, latent), F32),
-        (pos, normed, stacked, stacked_core), [SM] + [VM] * 3, 10, 4 * rows * n * depth * latent,
+        (normed, stacked, stacked_core), [VM] * 3, 10, 4 * rows * n * depth * latent,
         4 * n * depth * latent, [pltpu.VMEM((2, rows, n * depth), BF16)])
     n = len(late)
     own = kernel(
         functools.partial(late_kernel, late, spread), shape((rows + experts, latent)),
-        (pos, normed, opened, wt, *[down[k] for k in late], *late_core), [SM] + [VM] * (3 + 2 * n), 10,
+        (normed, opened, wt, *[down[k] for k in late], *late_core), [VM] * (3 + 2 * n), 10,
         4 * rows * n * depth * latent, 4 * n * depth * latent,
         [pltpu.VMEM((rows, 2 * n * depth), BF16), pltpu.VMEM((2 * n * depth, latent), BF16)])
-    core = swap(own, "expert", 1)
-
     work = 6 * rows * latent * ff
     load = 6 * latent * ff
-    far = []
-    for a in range(1, chips):
-        x0 = swap(own, "expert", 2 * a)
-        far.append((x0, swap(x0, "expert", 1)))
-    near0, near1 = kernel(
-        functools.partial(near_kernel, local), (shape((rows, latent), F32), shape((rows, latent))),
-        (pos, own, core, *weights), [SM] + [VM] * 5, 20, 2 * local * work, local * load,
-        [pltpu.VMEM((rows, latent), F32)])
-    near1 = swap(near1, "expert", 1)
+    count = 2 * local
+    cut = count - local // 2
+    far = [swap(own, "expert", 2 * a) for a in range(1, chips)]
+
+    def run(payload, span):
+        return kernel(
+            functools.partial(near_kernel, span), shape((rows, latent), F32), (payload, *weights),
+            [VM] * 7, 16, len(span) * work, len(span) * load)
+
+    near = run(own, range(count))
     parts = 2
     size = rows // parts
-    cut = local // 2
-    back = [[], []]
+    back = [[] for _ in range(parts)]
     for a in range(1, chips):
-        x = shape((2 * size, latent))
-        col = shape((2 * size, local + -local % 8), F32)
-        acc = shape((2 * size, latent), F32)
-        out = (shape((size, latent)),) * 2
-        o0, o1 = kernel(
-            functools.partial(far_kernel, local, 0), out, (pos, *far[a - 1], *weights),
-            [SM] + [VM] * 5, 20, local * work, local * load,
-            [pltpu.VMEM(v.shape, v.dtype) for v in (x, col, acc)])
-        results = [(o0, swap(o1, "expert", 1))]
-        held = kernel(
-            functools.partial(far_open_kernel, local, size, range(cut)), (x, col, acc),
-            (pos, *far[a - 1], *weights), [SM] + [VM] * 5, 20, cut * work, cut * load)
-        o0, o1 = kernel(
-            functools.partial(far_close_kernel, range(cut, local)), out, (*held, *weights),
-            [VM] * 6, 20, (local - cut) * work, (local - cut) * load, [pltpu.VMEM(acc.shape, F32)])
-        results.append((o0, swap(o1, "expert", 1)))
-        for h, pair in enumerate(results):
-            s = kernel(add_kernel, shape((size, latent)), pair, [VM, VM], 4,
-                       size * latent, 6 * size * latent)
+        opened = run(far[a - 1], range(cut))
+        for h in range(parts):
+            s = kernel(
+                functools.partial(far_kernel, range(cut, count), h * size),
+                shape((size, latent)), (far[a - 1], opened, *weights), [VM] * 8, 14,
+                (count - cut) * work // parts, (count - cut) * load, [pltpu.VMEM((size, latent), F32)])
             back[h].append(swap(s, "expert", 2 * a))
 
     pair = kernel(join_kernel, shape((latent, chips * depth)), (own_up, *ups_x),
@@ -363,11 +329,11 @@
     order = sorted(ups)
     result = None
     for h in range(parts):
-        operands = (pos, near0, near1, *back[h], *[ups[k] for k in order])
+        operands = (near, *back[h], *[ups[k] for k in order])
         result = kernel(
             functools.partial(final_kernel, len(back[h]), h * size, order, spread, depth),
             shape((rows, width)), operands + ((result,) if h else ()),
-            [SM] + [VM] * (len(operands) - 1) + [AN] * h, 10, 2 * size * width * latent, 2 * width * latent,
+            [VM] * len(operands) + [AN] * h, 10, 2 * size * width * latent, 2 * width * latent,
             [pltpu.VMEM((size, width), BF16), pltpu.SemaphoreType.DMA],
             AN, {len(operands): 0} if h else {})
     return result

time: 82.7 us -> 83.6 us (1.011)
  the two profiles are of different devices: /device:TPU:0 before, /device:TPU:12 now
where the time goes in v4:
time: 83.6 us; the launch traced here: 83.4 us
  waiting for transfers between devices  40.7 us (49%)
  starting transfers between devices  23.4 us (28%)
  Pallas kernels  19.1 us (23%)
    ppermute x23, waiting for transfers between devices, swap(): return lax.ppermute(x, axis, [(i, i ^ bits) for i in range(size)])  38.7 us
    pallas_call x12, Pallas kernels, kernel(): pl.pallas_call(body, out_shape=out_shape, in_specs=specs, out_specs=out_s...  19.1 us
    ppermute x23, starting transfers between devices, swap(): return lax.ppermute(x, axis, [(i, i ^ bits) for i in range(size)])  18.6 us
    ppermute x2, starting transfers between devices, swap_pair(): return lax.ppermute(x, axes, pairs)  4.79 us
    ppermute x2, waiting for transfers between devices, swap_pair(): return lax.ppermute(x, axes, pairs)  2.02 us
  transfers between devices with their start and end apart: 25, of which 12 were waited for; matrix products, arithmetic and copies ran while one was open for 0% of the time, Pallas kernels for 21%

profile of v4, /device:TPU:12, one launch (start us, length us, event | category | flops | bytes accessed | tf_op | source)
XLA Modules:
  0.0 83.4 jit_solution(11282852782157967544)
XLA Ops:
  0.0 0.5 collective-permute-start.12
  0.5 0.0 collective-permute-start.13
  0.5 0.4 collective-permute-start
  1.0 2.7 %collective-permute-start.1 = (bf16[128,512]{1,0:T(8,128)(2,1)}, bf16[128,512]{1,0:T(8,128)(2,1)S(1)}, u32[]{:S(2)}, u32[]{:S(2)}) collective-permute-start(bf16[128,512]{1,0:T(8,128)(2,1)} %down_hbm.1), channel_id=1, source_target_pairs={{0,2},{1,3},{2,0},{3,1},{16,19},{17,18},{18,17},{19,16},{4,6},{5,7... | collective-permute-start | bytes 393224 | tf_op jit(solution)/shard_map/ppermute | solution.py:40
  3.7 3.4 %collective-permute-done.refs_1_ = bf16[128,512]{1,0:T(8,128)(2,1)S(1)} collective-permute-done((bf16[128,512]{1,0:T(8,128)(2,1)}, bf16[128,512]{1,0:T(8,128)(2,1)S(1)}, u32[]{:S(2)}, u32[]{:S(2)}) %collective-permute-start) | collective-permute-done | bytes 131104 | tf_op jit(solution)/shard_map/ppermute | solution.py:30
  7.1 1.5 %collective-permute-start.2 = (bf16[128,512]{1,0:T(8,128)(2,1)}, bf16[128,512]{1,0:T(8,128)(2,1)S(1)}, u32[]{:S(2)}, u32[]{:S(2)}) collective-permute-start(bf16[128,512]{1,0:T(8,128)(2,1)} %down_hbm.1), channel_id=1, source_target_pairs={{0,8},{4,12},{8,0},{12,4},{1,9},{5,13},{9,1},{13,5},{2,10},{6,14},... | collective-permute-start | bytes 393224 | tf_op jit(solution)/shard_map/ppermute | solution.py:30
  8.6 2.0 %collective-permute-done.1.refs_2_ = bf16[128,512]{1,0:T(8,128)(2,1)S(1)} collective-permute-done((bf16[128,512]{1,0:T(8,128)(2,1)}, bf16[128,512]{1,0:T(8,128)(2,1)S(1)}, u32[]{:S(2)}, u32[]{:S(2)}) %collective-permute-start.1) | collective-permute-done | bytes 131104 | tf_op jit(solution)/shard_map/ppermute | solution.py:40
  10.6 1.5 %collective-permute-start.16 = (bf16[128,512]{1,0:T(8,128)(2,1)}, bf16[128,512]{1,0:T(8,128)(2,1)S(1)}, u32[]{:S(2)}, u32[]{:S(2)}) collective-permute-start(bf16[128,512]{1,0:T(8,128)(2,1)} %up_hbm.1), channel_id=1, source_target_pairs={{0,8},{4,12},{8,0},{12,4},{1,9},{5,13},{9,1},{13,5},{2,10},{6,14},... | collective-permute-start | bytes 393224 | tf_op jit(solution)/shard_map/ppermute | solution.py:30
  12.1 0.5 collective-permute-done.2.refs_3_
  12.6 1.5 %collective-permute-start.3 = (bf16[128,512]{1,0:T(8,128)(2,1)S(1)}, bf16[128,512]{1,0:T(8,128)(2,1)S(1)}, u32[]{:S(2)}, u32[]{:S(2)}) collective-permute-start(bf16[128,512]{1,0:T(8,128)(2,1)S(1)} %collective-permute-done.refs_1_), channel_id=1, source_target_pairs={{0,8},{4,12},{8,0},{12,4},{1,9},{5,13},{9,1},{13,5},{2,10},{6,14},... | collective-permute-start | bytes 393224 | tf_op jit(solution)/shard_map/ppermute | solution.py:30
  14.1 2.4 %collective-permute-done.16.refs_1_ = bf16[128,512]{1,0:T(8,128)(2,1)S(1)} collective-permute-done((bf16[128,512]{1,0:T(8,128)(2,1)}, bf16[128,512]{1,0:T(8,128)(2,1)S(1)}, u32[]{:S(2)}, u32[]{:S(2)}) %collective-permute-start.16) | collective-permute-done | bytes 131104 | tf_op jit(solution)/shard_map/ppermute | solution.py:30
  16.5 2.1 %collective-permute-start.5 = (bf16[128,512]{1,0:T(8,128)(2,1)S(1)}, bf16[128,512]{1,0:T(8,128)(2,1)S(1)}, u32[]{:S(2)}, u32[]{:S(2)}) collective-permute-start(bf16[128,512]{1,0:T(8,128)(2,1)S(1)} %collective-permute-done.1.refs_2_), channel_id=1, source_target_pairs={{0,24},{4,28},{8,16},{12,20},{16,8},{20,12},{24,0},{28,4},{1,25},{... | collective-permute-start | bytes 393224 | tf_op jit(solution)/shard_map/ppermute | solution.py:40
  18.6 0.2 collective-permute-done.3.refs_4_
  18.7 1.5 %collective-permute-start.6 = (bf16[128,512]{1,0:T(8,128)(2,1)S(1)}, bf16[128,512]{1,0:T(8,128)(2,1)S(1)}, u32[]{:S(2)}, u32[]{:S(2)}) collective-permute-start(bf16[128,512]{1,0:T(8,128)(2,1)S(1)} %collective-permute-done.1.refs_2_), channel_id=1, source_target_pairs={{0,8},{4,12},{8,0},{12,4},{1,9},{5,13},{9,1},{13,5},{2,10},{6,14},... | collective-permute-start | bytes 393224 | tf_op jit(solution)/shard_map/ppermute | solution.py:30
  20.2 1.6 %shard_map.109.normed_ref = bf16[256,2048]{1,0:T(8,128)(2,1)S(1)} custom-call(bf16[256,2048]{1,0:T(8,128)(2,1)} %tok_hbm.1, f32[1,2048]{1,0:T(1,128)} %bitcast.5), custom_call_target="tpu_custom_call" | custom-call | flops 4194304 | bytes 2097152 | tf_op jit(solution)/shard_map/pallas_call | solution.py:48
  21.9 2.2 %shard_map.110 = (f32[16,256]{1,0:T(8,128)S(1)}, bf16[128,512]{1,0:T(8,128)(2,1)S(1)}, bf16[128,512]{1,0:T(8,128)(2,1)S(1)}, bf16[4,768,512]{2,1,0:T(8,128)(2,1)S(1)}) custom-call(bf16[256,2048]{1,0:T(8,128)(2,1)S(1)} %shard_map.109.normed_ref, s32[1,4,4,4]{3,2,1,0:T(4,128)} %list_hbm.1, bf16[16,2048]{1,0:T(8,128)(2,1)} %bitcast.4, s32[8,256]{1,0:T(8,128)} %bitcast.6, ...), custom_call_target="tpu_custom_call" | custom-call | flops 33554432 | bytes 2097152 | tf_op jit(solution)/shard_map/pallas_call | solution.py:48
  24.1 0.0 copy-start.1
  24.1 0.0 copy-start
  24.1 0.0 collective-permute-done.5.refs_0_
  24.1 0.1 collective-permute-start.4
  24.2 0.0 collective-permute-done.6.refs_1_
  24.2 1.8 %collective-permute-start.7 = (bf16[128,512]{1,0:T(8,128)(2,1)S(1)}, bf16[128,512]{1,0:T(8,128)(2,1)S(1)}, u32[]{:S(2)}, u32[]{:S(2)}) collective-permute-start(bf16[128,512]{1,0:T(8,128)(2,1)S(1)} %collective-permute-done.1.refs_2_), channel_id=1, source_target_pairs={{0,16},{16,0},{1,17},{17,1},{2,18},{18,2},{3,19},{19,3},{4,20},{20... | collective-permute-start | bytes 393224 | tf_op jit(solution)/shard_map/ppermute | solution.py:30
  26.0 4.1 %collective-permute-done.7.refs_2_ = bf16[128,512]{1,0:T(8,128)(2,1)S(1)} collective-permute-done((bf16[128,512]{1,0:T(8,128)(2,1)S(1)}, bf16[128,512]{1,0:T(8,128)(2,1)S(1)}, u32[]{:S(2)}, u32[]{:S(2)}) %collective-permute-start.7) | collective-permute-done | bytes 131104 | tf_op jit(solution)/shard_map/ppermute | solution.py:30
  30.1 1.3 %collective-permute-done.8.refs_3_ = bf16[128,512]{1,0:T(8,128)(2,1)S(1)} collective-permute-done((bf16[128,512]{1,0:T(8,128)(2,1)S(1)}, bf16[128,512]{1,0:T(8,128)(2,1)S(1)}, u32[]{:S(2)}, u32[]{:S(2)}) %collective-permute-start.8) | collective-permute-done | bytes 131104 | tf_op jit(solution)/shard_map/ppermute | solution.py:30
  31.5 0.1 collective-permute-start.9
  31.6 1.2 %collective-permute-done.9.refs_4_ = bf16[128,512]{1,0:T(8,128)(2,1)S(1)} collective-permute-done((bf16[128,512]{1,0:T(8,128)(2,1)S(1)}, bf16[128,512]{1,0:T(8,128)(2,1)S(1)}, u32[]{:S(2)}, u32[]{:S(2)}) %collective-permute-start.9) | collective-permute-done | bytes 131104 | tf_op jit(solution)/shard_map/ppermute | solution.py:30
  32.8 0.1 collective-permute-start.10
  33.0 0.1 shard_map.117.refs_1_
  33.1 1.1 %collective-permute-done.10.refs_5_ = bf16[128,512]{1,0:T(8,128)(2,1)S(1)} collective-permute-done((bf16[128,512]{1,0:T(8,128)(2,1)S(1)}, bf16[128,512]{1,0:T(8,128)(2,1)S(1)}, u32[]{:S(2)}, u32[]{:S(2)}) %collective-permute-start.10) | collective-permute-done | bytes 131104 | tf_op jit(solution)/shard_map/ppermute | solution.py:30
  34.2 2.7 %collective-permute-start.17 = (bf16[512,256]{1,0:T(8,128)(2,1)S(1)}, bf16[512,256]{1,0:T(8,128)(2,1)S(1)}, u32[]{:S(2)}, u32[]{:S(2)}) collective-permute-start(bf16[512,256]{1,0:T(8,128)(2,1)S(1)} %shard_map.117.refs_1_), channel_id=1, source_target_pairs={{0,1},{1,0},{2,3},{3,2},{4,5},{5,4},{6,7},{7,6},{8,9},{9,8},{10,11... | collective-permute-start | bytes 786440 | tf_op jit(solution)/shard_map/ppermute | solution.py:30
  36.9 3.4 %collective-permute-start.18 = (bf16[512,256]{1,0:T(8,128)(2,1)S(1)}, bf16[512,256]{1,0:T(8,128)(2,1)S(1)}, u32[]{:S(2)}, u32[]{:S(2)}) collective-permute-start(bf16[512,256]{1,0:T(8,128)(2,1)S(1)} %shard_map.117.refs_1_), channel_id=1, source_target_pairs={{0,2},{1,3},{2,0},{3,1},{4,6},{5,7},{6,4},{7,5},{8,10},{9,11},{10,... | collective-permute-start | bytes 786440 | tf_op jit(solution)/shard_map/ppermute | solution.py:30
  40.3 0.6 shard_map.112.sum_ref
  40.9 0.4 shard_map.113.pay_ref
  41.3 6.8 %collective-permute-done.17.refs_2_ = bf16[512,256]{1,0:T(8,128)(2,1)S(1)} collective-permute-done((bf16[512,256]{1,0:T(8,128)(2,1)S(1)}, bf16[512,256]{1,0:T(8,128)(2,1)S(1)}, u32[]{:S(2)}, u32[]{:S(2)}) %collective-permute-start.17) | collective-permute-done | bytes 262176 | tf_op jit(solution)/shard_map/ppermute | solution.py:30
  48.2 0.2 collective-permute-start.14
  48.4 4.3 %collective-permute-done.18.refs_3_ = bf16[512,256]{1,0:T(8,128)(2,1)S(1)} collective-permute-done((bf16[512,256]{1,0:T(8,128)(2,1)S(1)}, bf16[512,256]{1,0:T(8,128)(2,1)S(1)}, u32[]{:S(2)}, u32[]{:S(2)}) %collective-permute-start.18) | collective-permute-done | bytes 262176 | tf_op jit(solution)/shard_map/ppermute | solution.py:30
  52.6 13.3 %collective-permute-done.19.refs_4_ = bf16[512,256]{1,0:T(8,128)(2,1)S(1)} collective-permute-done((bf16[512,256]{1,0:T(8,128)(2,1)S(1)}, bf16[512,256]{1,0:T(8,128)(2,1)S(1)}, u32[]{:S(2)}, u32[]{:S(2)}) %collective-permute-start.19) | collective-permute-done | bytes 262176 | tf_op jit(solution)/shard_map/ppermute | solution.py:30
  66.0 0.5 collective-permute-start.21
  66.5 0.1 collective-permute-start.22
  66.6 0.4 collective-permute-start.23
  67.0 4.1 %shard_map.115.sum_ref = f32[256,512]{1,0:T(8,128)S(1)} custom-call(bf16[272,512]{1,0:T(8,128)(2,1)S(1)} %collective-permute-done.14.pay_ref, bf16[4,512,768]{2,1,0:T(8,128)(2,1)S(1)} %copy-done, bf16[4,512,768]{2,1,0:T(8,128)(2,1)S(1)} %copy-done.1, bf16[4,768,512]{2,1,0:T(8,128)(2,1)S(1)} %get-tuple-element.11.refs_2_, ...), custom_call_target="tpu_custom_call" | custom-call | flops 3623878656 | bytes 14155776 | tf_op jit(solution)/shard_map/pallas_call | solution.py:48
  71.2 1.0 %shard_map.116 = bf16[128,512]{1,0:T(8,128)(2,1)S(1)} custom-call(bf16[272,512]{1,0:T(8,128)(2,1)S(1)} %collective-permute-done.14.pay_ref, f32[256,512]{1,0:T(8,128)S(1)} %shard_map.115.sum_ref, bf16[4,512,768]{2,1,0:T(8,128)(2,1)S(1)} %copy-done, bf16[4,512,768]{2,1,0:T(8,128)(2,1)S(1)} %copy-done.1, bf16[4,768,512]{2,1,0:T(8,128)(2,1)S(1)} %get-tuple-element.11.refs_2_, ...), custom_call_target="tpu_custom_call" | custom-call | flops 603979776 | bytes 4718592 | tf_op jit(solution)/shard_map/pallas_call | solution.py:48
  72.2 0.6 collective-permute-start.15
  72.8 1.0 %shard_map.118 = bf16[128,512]{1,0:T(8,128)(2,1)S(1)} custom-call(bf16[272,512]{1,0:T(8,128)(2,1)S(1)} %collective-permute-done.14.pay_ref, f32[256,512]{1,0:T(8,128)S(1)} %shard_map.115.sum_ref, bf16[4,512,768]{2,1,0:T(8,128)(2,1)S(1)} %copy-done, bf16[4,512,768]{2,1,0:T(8,128)(2,1)S(1)} %copy-done.1, bf16[4,768,512]{2,1,0:T(8,128)(2,1)S(1)} %get-tuple-element.11.refs_2_, ...), custom_call_target="tpu_custom_call" | custom-call | flops 603979776 | bytes 4718592 | tf_op jit(solution)/shard_map/pallas_call | solution.py:48
  73.8 1.5 %collective-permute-start.24 = (bf16[128,512]{1,0:T(8,128)(2,1)S(1)}, bf16[128,512]{1,0:T(8,128)(2,1)S(1)}, u32[]{:S(2)}, u32[]{:S(2)}) collective-permute-start(bf16[128,512]{1,0:T(8,128)(2,1)S(1)} %shard_map.118), channel_id=1, source_target_pairs={{0,8},{4,12},{8,0},{12,4},{1,9},{5,13},{9,1},{13,5},{2,10},{6,14},... | collective-permute-start | bytes 393224 | tf_op jit(solution)/shard_map/ppermute | solution.py:30
  75.3 5.4 %shard_map.114.near_ref = f32[256,512]{1,0:T(8,128)S(1)} custom-call(bf16[272,512]{1,0:T(8,128)(2,1)S(1)} %shard_map.113.pay_ref, bf16[4,512,768]{2,1,0:T(8,128)(2,1)S(1)} %copy-done, bf16[4,512,768]{2,1,0:T(8,128)(2,1)S(1)} %copy-done.1, bf16[4,768,512]{2,1,0:T(8,128)(2,1)S(1)} %get-tuple-element.11.refs_2_, ...), custom_call_target="tpu_custom_call" | custom-call | flops 4831838208 | bytes 18874368 | tf_op jit(solution)/shard_map/pallas_call | solution.py:48
  80.8 1.3 %shard_map.119.refs_9_ = bf16[256,2048]{1,0:T(8,128)(2,1)} custom-call(f32[256,512]{1,0:T(8,128)S(1)} %shard_map.114.near_ref, bf16[128,512]{1,0:T(8,128)(2,1)S(1)} %collective-permute-done.24.refs_0_, bf16[512,256]{1,0:T(8,128)(2,1)S(1)} %shard_map.117.refs_1_, bf16[512,256]{1,0:T(8,128)(2,1)S(1)} %collective-permute-done.17.refs_2_, ...), custom_call_target="tpu_custom_call" | custom-call | flops 268435456 | bytes 2097152 | tf_op jit(solution)/shard_map/pallas_call | solution.py:48
  82.1 1.3 %shard_map.120 = bf16[256,2048]{1,0:T(8,128)(2,1)} custom-call(f32[256,512]{1,0:T(8,128)S(1)} %shard_map.114.near_ref, bf16[128,512]{1,0:T(8,128)(2,1)S(1)} %collective-permute-done.15.refs_0_, bf16[512,256]{1,0:T(8,128)(2,1)S(1)} %shard_map.117.refs_1_, bf16[512,256]{1,0:T(8,128)(2,1)S(1)} %collective-permute-done.17.refs_2_, ...), custom_call_target="tpu_custom_call", output_to_operand_aliasing={{}: (10, {})} | custom-call | flops 268435456 | bytes 2097152 | tf_op jit(solution)/shard_map/pallas_call | solution.py:48
  (18 shorter events, 0.1 us)
Async XLA Ops:
  0.0 66.5 %collective-permute-start.11 = (bf16[4,512,768]{2,1,0:T(8,128)(2,1)}, bf16[4,512,768]{2,1,0:T(8,128)(2,1)S(1)}, u32[]{:S(2)}, u32[]{:S(2)}) collective-permute-start(bf16[4,512,768]{2,1,0:T(8,128)(2,1)} %refs_0_.7), channel_id=1, source_target_pairs={{0,4},{4,0},{8,12},{12,8},{1,5},{5,1},{9,13},{13,9},{2,6},{6,2},{1... | collective-permute-start | bytes 9437192 | tf_op jit(solution)/shard_map/ppermute | solution.py:30
  0.0 66.6 %collective-permute-start.12 = (bf16[4,512,768]{2,1,0:T(8,128)(2,1)}, bf16[4,512,768]{2,1,0:T(8,128)(2,1)S(1)}, u32[]{:S(2)}, u32[]{:S(2)}) collective-permute-start(bf16[4,512,768]{2,1,0:T(8,128)(2,1)} %refs_1_.7), channel_id=1, source_target_pairs={{0,4},{4,0},{8,12},{12,8},{1,5},{5,1},{9,13},{13,9},{2,6},{6,2},{1... | collective-permute-start | bytes 9437192 | tf_op jit(solution)/shard_map/ppermute | solution.py:30
  0.5 66.5 %collective-permute-start.13 = (bf16[4,768,512]{2,1,0:T(8,128)(2,1)}, bf16[4,768,512]{2,1,0:T(8,128)(2,1)S(1)}, u32[]{:S(2)}, u32[]{:S(2)}) collective-permute-start(bf16[4,768,512]{2,1,0:T(8,128)(2,1)} %last_hbm.1), channel_id=1, source_target_pairs={{0,4},{4,0},{8,12},{12,8},{1,5},{5,1},{9,13},{13,9},{2,6},{6,2},{1... | collective-permute-start | bytes 9437192 | tf_op jit(solution)/shard_map/ppermute | solution.py:30
  0.5 6.6 %collective-permute-start = (bf16[128,512]{1,0:T(8,128)(2,1)}, bf16[128,512]{1,0:T(8,128)(2,1)S(1)}, u32[]{:S(2)}, u32[]{:S(2)}) collective-permute-start(bf16[128,512]{1,0:T(8,128)(2,1)} %down_hbm.1), channel_id=1, source_target_pairs={{0,1},{1,0},{2,3},{3,2},{4,5},{5,4},{6,7},{7,6},{8,9},{9,8},{10,11... | collective-permute-start | bytes 393224 | tf_op jit(solution)/shard_map/ppermute | solution.py:30
  1.0 9.6 %collective-permute-start.1 = (bf16[128,512]{1,0:T(8,128)(2,1)}, bf16[128,512]{1,0:T(8,128)(2,1)S(1)}, u32[]{:S(2)}, u32[]{:S(2)}) collective-permute-start(bf16[128,512]{1,0:T(8,128)(2,1)} %down_hbm.1), channel_id=1, source_target_pairs={{0,2},{1,3},{2,0},{3,1},{16,19},{17,18},{18,17},{19,16},{4,6},{5,7... | collective-permute-start | bytes 393224 | tf_op jit(solution)/shard_map/ppermute | solution.py:40
  7.1 5.5 %collective-permute-start.2 = (bf16[128,512]{1,0:T(8,128)(2,1)}, bf16[128,512]{1,0:T(8,128)(2,1)S(1)}, u32[]{:S(2)}, u32[]{:S(2)}) collective-permute-start(bf16[128,512]{1,0:T(8,128)(2,1)} %down_hbm.1), channel_id=1, source_target_pairs={{0,8},{4,12},{8,0},{12,4},{1,9},{5,13},{9,1},{13,5},{2,10},{6,14},... | collective-permute-start | bytes 393224 | tf_op jit(solution)/shard_map/ppermute | solution.py:30
  10.6 5.9 %collective-permute-start.16 = (bf16[128,512]{1,0:T(8,128)(2,1)}, bf16[128,512]{1,0:T(8,128)(2,1)S(1)}, u32[]{:S(2)}, u32[]{:S(2)}) collective-permute-start(bf16[128,512]{1,0:T(8,128)(2,1)} %up_hbm.1), channel_id=1, source_target_pairs={{0,8},{4,12},{8,0},{12,4},{1,9},{5,13},{9,1},{13,5},{2,10},{6,14},... | collective-permute-start | bytes 393224 | tf_op jit(solution)/shard_map/ppermute | solution.py:30
  12.6 6.2 %collective-permute-start.3 = (bf16[128,512]{1,0:T(8,128)(2,1)S(1)}, bf16[128,512]{1,0:T(8,128)(2,1)S(1)}, u32[]{:S(2)}, u32[]{:S(2)}) collective-permute-start(bf16[128,512]{1,0:T(8,128)(2,1)S(1)} %collective-permute-done.refs_1_), channel_id=1, source_target_pairs={{0,8},{4,12},{8,0},{12,4},{1,9},{5,13},{9,1},{13,5},{2,10},{6,14},... | collective-permute-start | bytes 393224 | tf_op jit(solution)/shard_map/ppermute | solution.py:30
  16.5 7.6 %collective-permute-start.5 = (bf16[128,512]{1,0:T(8,128)(2,1)S(1)}, bf16[128,512]{1,0:T(8,128)(2,1)S(1)}, u32[]{:S(2)}, u32[]{:S(2)}) collective-permute-start(bf16[128,512]{1,0:T(8,128)(2,1)S(1)} %collective-permute-done.1.refs_2_), channel_id=1, source_target_pairs={{0,24},{4,28},{8,16},{12,20},{16,8},{20,12},{24,0},{28,4},{1,25},{... | collective-permute-start | bytes 393224 | tf_op jit(solution)/shard_map/ppermute | solution.py:40
  18.7 5.5 %collective-permute-start.6 = (bf16[128,512]{1,0:T(8,128)(2,1)S(1)}, bf16[128,512]{1,0:T(8,128)(2,1)S(1)}, u32[]{:S(2)}, u32[]{:S(2)}) collective-permute-start(bf16[128,512]{1,0:T(8,128)(2,1)S(1)} %collective-permute-done.1.refs_2_), channel_id=1, source_target_pairs={{0,8},{4,12},{8,0},{12,4},{1,9},{5,13},{9,1},{13,5},{2,10},{6,14},... | collective-permute-start | bytes 393224 | tf_op jit(solution)/shard_map/ppermute | solution.py:30
  24.1 43.0 %copy-start.1 = (bf16[4,512,768]{2,1,0:T(8,128)(2,1)S(1)}, bf16[4,512,768]{2,1,0:T(8,128)(2,1)}, u32[]{:S(2)}) copy-start(bf16[4,512,768]{2,1,0:T(8,128)(2,1)} %refs_1_.7) | copy-start | bytes 9437188
  24.1 42.9 %copy-start = (bf16[4,512,768]{2,1,0:T(8,128)(2,1)S(1)}, bf16[4,512,768]{2,1,0:T(8,128)(2,1)}, u32[]{:S(2)}) copy-start(bf16[4,512,768]{2,1,0:T(8,128)(2,1)} %refs_0_.7) | copy-start | bytes 9437188
  24.1 12.8 %collective-permute-start.4 = (bf16[640,512]{1,0:T(8,128)(2,1)S(1)}, bf16[640,512]{1,0:T(8,128)(2,1)S(1)}, u32[]{:S(2)}, u32[]{:S(2)}) collective-permute-start(bf16[640,512]{1,0:T(8,128)(2,1)S(1)} %shard_map.111.w0_ref), channel_id=1, source_target_pairs={{0,4},{4,0},{8,12},{12,8},{1,5},{5,1},{9,13},{13,9},{2,6},{6,2},{1... | collective-permute-start | bytes 1966088 | tf_op jit(solution)/shard_map/ppermute | solution.py:30
  24.2 5.9 %collective-permute-start.7 = (bf16[128,512]{1,0:T(8,128)(2,1)S(1)}, bf16[128,512]{1,0:T(8,128)(2,1)S(1)}, u32[]{:S(2)}, u32[]{:S(2)}) collective-permute-start(bf16[128,512]{1,0:T(8,128)(2,1)S(1)} %collective-permute-done.1.refs_2_), channel_id=1, source_target_pairs={{0,16},{16,0},{1,17},{17,1},{2,18},{18,2},{3,19},{19,3},{4,20},{20... | collective-permute-start | bytes 393224 | tf_op jit(solution)/shard_map/ppermute | solution.py:30
  30.1 1.3 %collective-permute-start.8 = (bf16[128,512]{1,0:T(8,128)(2,1)S(1)}, bf16[128,512]{1,0:T(8,128)(2,1)S(1)}, u32[]{:S(2)}, u32[]{:S(2)}) collective-permute-start(bf16[128,512]{1,0:T(8,128)(2,1)S(1)} %collective-permute-done.5.refs_0_), channel_id=1, source_target_pairs={{0,4},{4,0},{8,12},{12,8},{1,5},{5,1},{9,13},{13,9},{2,6},{6,2},{1... | collective-permute-start | bytes 393224 | tf_op jit(solution)/shard_map/ppermute | solution.py:30
  31.5 1.3 %collective-permute-start.9 = (bf16[128,512]{1,0:T(8,128)(2,1)S(1)}, bf16[128,512]{1,0:T(8,128)(2,1)S(1)}, u32[]{:S(2)}, u32[]{:S(2)}) collective-permute-start(bf16[128,512]{1,0:T(8,128)(2,1)S(1)} %collective-permute-done.6.refs_1_), channel_id=1, source_target_pairs={{0,4},{4,0},{8,12},{12,8},{1,5},{5,1},{9,13},{13,9},{2,6},{6,2},{1... | collective-permute-start | bytes 393224 | tf_op jit(solution)/shard_map/ppermute | solution.py:30
  32.8 1.3 %collective-permute-start.10 = (bf16[128,512]{1,0:T(8,128)(2,1)S(1)}, bf16[128,512]{1,0:T(8,128)(2,1)S(1)}, u32[]{:S(2)}, u32[]{:S(2)}) collective-permute-start(bf16[128,512]{1,0:T(8,128)(2,1)S(1)} %collective-permute-done.7.refs_2_), channel_id=1, source_target_pairs={{0,4},{4,0},{8,12},{12,8},{1,5},{5,1},{9,13},{13,9},{2,6},{6,2},{1... | collective-permute-start | bytes 393224 | tf_op jit(solution)/shard_map/ppermute | solution.py:30
  34.2 14.0 %collective-permute-start.17 = (bf16[512,256]{1,0:T(8,128)(2,1)S(1)}, bf16[512,256]{1,0:T(8,128)(2,1)S(1)}, u32[]{:S(2)}, u32[]{:S(2)}) collective-permute-start(bf16[512,256]{1,0:T(8,128)(2,1)S(1)} %shard_map.117.refs_1_), channel_id=1, source_target_pairs={{0,1},{1,0},{2,3},{3,2},{4,5},{5,4},{6,7},{7,6},{8,9},{9,8},{10,11... | collective-permute-start | bytes 786440 | tf_op jit(solution)/shard_map/ppermute | solution.py:30
  36.9 15.7 %collective-permute-start.18 = (bf16[512,256]{1,0:T(8,128)(2,1)S(1)}, bf16[512,256]{1,0:T(8,128)(2,1)S(1)}, u32[]{:S(2)}, u32[]{:S(2)}) collective-permute-start(bf16[512,256]{1,0:T(8,128)(2,1)S(1)} %shard_map.117.refs_1_), channel_id=1, source_target_pairs={{0,2},{1,3},{2,0},{3,1},{4,6},{5,7},{6,4},{7,5},{8,10},{9,11},{10,... | collective-permute-start | bytes 786440 | tf_op jit(solution)/shard_map/ppermute | solution.py:30
  48.2 17.8 %collective-permute-start.14 = (bf16[272,512]{1,0:T(8,128)(2,1)S(1)}, bf16[272,512]{1,0:T(8,128)(2,1)S(1)}, u32[]{:S(2)}, u32[]{:S(2)}) collective-permute-start(bf16[272,512]{1,0:T(8,128)(2,1)S(1)} %shard_map.113.pay_ref), channel_id=1, source_target_pairs={{0,8},{4,12},{8,0},{12,4},{1,9},{5,13},{9,1},{13,5},{2,10},{6,14},... | collective-permute-start | bytes 835592 | tf_op jit(solution)/shard_map/ppermute | solution.py:30
  52.6 13.3 %collective-permute-start.19 = (bf16[512,256]{1,0:T(8,128)(2,1)S(1)}, bf16[512,256]{1,0:T(8,128)(2,1)S(1)}, u32[]{:S(2)}, u32[]{:S(2)}) collective-permute-start(bf16[512,256]{1,0:T(8,128)(2,1)S(1)} %shard_map.117.refs_1_), channel_id=1, source_target_pairs={{0,3},{1,2},{2,1},{3,0},{4,7},{5,6},{6,5},{7,4},{8,11},{9,10},{10,... | collective-permute-start | bytes 786440 | tf_op jit(solution)/shard_map/ppermute | solution.py:30
  66.0 7.8 %collective-permute-start.20 = (bf16[512,256]{1,0:T(8,128)(2,1)S(1)}, bf16[512,256]{1,0:T(8,128)(2,1)S(1)}, u32[]{:S(2)}, u32[]{:S(2)}) collective-permute-start(bf16[512,256]{1,0:T(8,128)(2,1)S(1)} %shard_map.117.refs_1_), channel_id=1, source_target_pairs={{0,4},{4,0},{8,12},{12,8},{1,5},{5,1},{9,13},{13,9},{2,6},{6,2},{1... | collective-permute-start | bytes 786440 | tf_op jit(solution)/shard_map/ppermute | solution.py:30
  66.0 14.8 %collective-permute-start.21 = (bf16[512,256]{1,0:T(8,128)(2,1)S(1)}, bf16[512,256]{1,0:T(8,128)(2,1)S(1)}, u32[]{:S(2)}, u32[]{:S(2)}) collective-permute-start(bf16[512,256]{1,0:T(8,128)(2,1)S(1)} %collective-permute-done.17.refs_2_), channel_id=1, source_target_pairs={{0,4},{4,0},{8,12},{12,8},{1,5},{5,1},{9,13},{13,9},{2,6},{6,2},{1... | collective-permute-start | bytes 786440 | tf_op jit(solution)/shard_map/ppermute | solution.py:30
  66.5 14.3 %collective-permute-start.22 = (bf16[512,256]{1,0:T(8,128)(2,1)S(1)}, bf16[512,256]{1,0:T(8,128)(2,1)S(1)}, u32[]{:S(2)}, u32[]{:S(2)}) collective-permute-start(bf16[512,256]{1,0:T(8,128)(2,1)S(1)} %collective-permute-done.18.refs_3_), channel_id=1, source_target_pairs={{0,4},{4,0},{8,12},{12,8},{1,5},{5,1},{9,13},{13,9},{2,6},{6,2},{1... | collective-permute-start | bytes 786440 | tf_op jit(solution)/shard_map/ppermute | solution.py:30
  66.6 14.2 %collective-permute-start.23 = (bf16[512,256]{1,0:T(8,128)(2,1)S(1)}, bf16[512,256]{1,0:T(8,128)(2,1)S(1)}, u32[]{:S(2)}, u32[]{:S(2)}) collective-permute-start(bf16[512,256]{1,0:T(8,128)(2,1)S(1)} %collective-permute-done.19.refs_4_), channel_id=1, source_target_pairs={{0,4},{4,0},{8,12},{12,8},{1,5},{5,1},{9,13},{13,9},{2,6},{6,2},{1... | collective-permute-start | bytes 786440 | tf_op jit(solution)/shard_map/ppermute | solution.py:30
  72.2 9.9 %collective-permute-start.15 = (bf16[128,512]{1,0:T(8,128)(2,1)S(1)}, bf16[128,512]{1,0:T(8,128)(2,1)S(1)}, u32[]{:S(2)}, u32[]{:S(2)}) collective-permute-start(bf16[128,512]{1,0:T(8,128)(2,1)S(1)} %shard_map.116), channel_id=1, source_target_pairs={{0,8},{4,12},{8,0},{12,4},{1,9},{5,13},{9,1},{13,5},{2,10},{6,14},... | collective-permute-start | bytes 393224 | tf_op jit(solution)/shard_map/ppermute | solution.py:30
  73.8 7.0 %collective-permute-start.24 = (bf16[128,512]{1,0:T(8,128)(2,1)S(1)}, bf16[128,512]{1,0:T(8,128)(2,1)S(1)}, u32[]{:S(2)}, u32[]{:S(2)}) collective-permute-start(bf16[128,512]{1,0:T(8,128)(2,1)S(1)} %shard_map.118), channel_id=1, source_target_pairs={{0,8},{4,12},{8,0},{12,4},{1,9},{5,13},{9,1},{13,5},{2,10},{6,14},... | collective-permute-start | bytes 393224 | tf_op jit(solution)/shard_map/ppermute | solution.py:30

commit v5 on v4

--- a/solution.py
+++ b/solution.py
@@ -57,22 +57,24 @@
     )(*operands)
 
 
-def norm_kernel(tok_hbm, gain_hbm, normed_ref, tok_ref, gain_ref, sem):
-    pairs = ((tok_hbm, tok_ref), (gain_hbm, gain_ref))
+def norm_kernel(tok_hbm, gain_hbm, down_hbm, up_hbm, normed_ref, down_ref, up_ref, tok_ref, gain_ref, sem):
+    pairs = ((tok_hbm, tok_ref), (gain_hbm, gain_ref), (down_hbm, down_ref), (up_hbm, up_ref))
     copies = [pltpu.make_async_copy(src, dst, sem.at[i]) for i, (src, dst) in enumerate(pairs)]
     for copy in copies:
         copy.start()
-    for copy in copies:
+    for copy in copies[:2]:
         copy.wait()
     values = tok_ref[...].astype(F32)
     scale = lax.rsqrt(jnp.mean(values * values, axis=-1, keepdims=True) + epsilon)
     normed_ref[...] = (values * scale * gain_ref[...]).astype(BF16)
-
-
-def gate_kernel(top, normed_ref, list_hbm, router_hbm, ids_hbm, slot_hbm, down_hbm, up_hbm, last_hbm,
-                wt_ref, down_ref, up_ref, last_ref, list_ref, router_ref, ids_ref, slot_ref, sem):
+    for copy in copies[2:]:
+        copy.wait()
+
+
+def gate_kernel(top, normed_ref, list_hbm, router_hbm, ids_hbm, slot_hbm, last_hbm, wt_ref, last_ref,
+                list_ref, router_ref, ids_ref, slot_ref, sem):
     pairs = ((router_hbm, router_ref), (ids_hbm, ids_ref), (slot_hbm, slot_ref), (list_hbm, list_ref),
-             (up_hbm, up_ref), (down_hbm, down_ref), (last_hbm, last_ref))
+             (last_hbm, last_ref))
     copies = [pltpu.make_async_copy(src, dst, sem.at[i]) for i, (src, dst) in enumerate(pairs)]
     for copy in copies:
         copy.start()
@@ -116,10 +118,7 @@
 def pick(chunks, other, depth, copies, normed_ref, x_ref):
     core, half, rep, group = here(copies)
     for i, (a, b) in enumerate(chunks):
-        if b == "A":
-            b = 2 + group
-        elif b == "B":
-            b = 3 - group
+        b = {"A": 2 + group, "B": 3 - group}.get(b, b)
         at = ((2 * (half ^ a) + (core ^ other)) * copies + (rep ^ b)) * depth
         x_ref[:, i * depth:(i + 1) * depth] = normed_ref[:, pl.ds(pl.multiple_of(at, depth), depth)]
 
@@ -199,13 +198,14 @@
 
 def final_kernel(n_back, at, chunks, copies, depth, near_ref, *refs):
     out_ref, rows_ref, sem = refs[-3:]
-    core, half, rep, _ = here(copies)
+    core, half, rep, group = here(copies)
     size = rows_ref.shape[0]
     total = near_ref[at:at + size, :]
     for s_ref in refs[:n_back]:
         total = total + s_ref[...].astype(F32)
     merged = total.astype(BF16)
     for (c, b), w_ref in zip(chunks, refs[n_back:]):
+        b = {"A": 2 + group, "B": 3 - group}.get(b, b)
         block = jnp.dot(merged, w_ref[...], preferred_element_type=F32).astype(BF16)
         for a in range(w_ref.shape[1] // depth):
             e = 2 * (half ^ a) + (core ^ c)
@@ -238,6 +238,7 @@
         depth, spread = wide, 1
     experts = shards * local
     down = {(0, 0): down_proj}
+    far_z = None
     if spread == groups + 2 and groups == 2:
         near_z = swap(down_proj, "replica", 1)
         far_z = swap_pair(down_proj, ("groups", "replica"), lambda i, j: (i, j ^ (2 + i)))
@@ -260,19 +261,19 @@
                 down[(a, b)] = swap(down[(0, b)], "expert", 2 * a)
         ups_x = [swap(up_proj, "expert", 2 * a) for a in range(1, chips)]
 
-    normed = kernel(
-        norm_kernel, shape((rows, width)), (in_hbm(tokens), in_hbm(norm_gain.reshape(1, width))),
-        [AN] * 2, 16, 8 * rows * width, 4 * rows * width,
-        [pltpu.VMEM((rows, width), BF16), pltpu.VMEM((1, width), F32), pltpu.SemaphoreType.DMA((2,))])
-    wt, own_down, own_up, last = kernel(
+    normed, own_down, own_up = kernel(
+        norm_kernel, (shape((rows, width)), shape(down_proj.shape), shape(up_proj.shape)),
+        tuple(map(in_hbm, (tokens, norm_gain.reshape(1, width), down_proj, up_proj))),
+        [AN] * 4, 16, 8 * rows * width, 4 * rows * width,
+        [pltpu.VMEM((rows, width), BF16), pltpu.VMEM((1, width), F32), pltpu.SemaphoreType.DMA((4,))])
+    wt, last = kernel(
         functools.partial(gate_kernel, top),
-        (shape((experts, rows), F32), shape(down_proj.shape), shape(up_proj.shape), shape(expert_down.shape)),
-        (normed, *map(in_hbm, (overflow_list, router.T, expert_ids.T, slot_pos.T, down_proj, up_proj,
-                               expert_down))),
-        [VM] + [AN] * 7, 14, 4 * rows * width * experts, 4 * rows * width,
+        (shape((experts, rows), F32), shape(expert_down.shape)),
+        (normed, *map(in_hbm, (overflow_list, router.T, expert_ids.T, slot_pos.T, expert_down))),
+        [VM] + [AN] * 5, 14, 4 * rows * width * experts, 4 * rows * width,
         [pltpu.SMEM(overflow_list.shape, jnp.int32), pltpu.VMEM((experts, width), BF16),
          pltpu.VMEM((top, rows), jnp.int32), pltpu.VMEM((top, rows), jnp.int32),
-         pltpu.SemaphoreType.DMA((7,))])
+         pltpu.SemaphoreType.DMA((5,))])
     down[(0, 0)] = own_down
     weights = (expert_gate, expert_up, last, *[
         swap(w, "expert", 1) for w in (expert_gate, expert_up, expert_down)])
@@ -322,11 +323,16 @@
     pair = kernel(join_kernel, shape((latent, chips * depth)), (own_up, *ups_x),
                   [VM] * chips, 4, 0, 4 * chips * depth * latent)
     ups = {(0, 0): pair}
-    for b in range(1, spread):
-        ups[(0, b)] = swap(pair, "replica", b)
-    for b in range(spread):
+    if far_z is not None:
+        ups[(0, 1)] = swap(pair, "replica", 1)
+        ups[(0, "A")] = swap_pair(pair, ("groups", "replica"), lambda i, j: (i, j ^ (2 + i)))
+        ups[(0, "B")] = swap(ups[(0, "A")], "groups", 1)
+    else:
+        for b in range(1, spread):
+            ups[(0, b)] = swap(pair, "replica", b)
+    for _, b in list(ups):
         ups[(1, b)] = swap(ups[(0, b)], "expert", 1)
-    order = sorted(ups)
+    order = list(ups)
     result = None
     for h in range(parts):
         operands = (near, *back[h], *[ups[k] for k in order])

time: 83.6 us -> 78.8 us (0.943)
  the two profiles are of different devices: /device:TPU:12 before, /device:TPU:0 now
where the time goes in v5:
time: 78.8 us; the launch traced here: 78.6 us
  waiting for transfers between devices  32.5 us (41%)
  starting transfers between devices  26.8 us (34%)
  Pallas kernels  19.1 us (24%)
    ppermute x22, waiting for transfers between devices, swap(): return lax.ppermute(x, axis, [(i, i ^ bits) for i in range(size)])  31.1 us
    pallas_call x12, Pallas kernels, kernel(): pl.pallas_call(body, out_shape=out_shape, in_specs=specs, out_specs=out_s...  19.1 us
    ppermute x22, starting transfers between devices, swap(): return lax.ppermute(x, axis, [(i, i ^ bits) for i in range(size)])  18 us
    ppermute x3, starting transfers between devices, swap_pair(): return lax.ppermute(x, axes, pairs)  8.85 us
  transfers between devices with their start and end apart: 25, of which 13 were waited for; matrix products, arithmetic and copies ran while one was open for 0% of the time, Pallas kernels for 23%

profile of v5, /device:TPU:0, one launch (start us, length us, event | category | flops | bytes accessed | tf_op | source)
XLA Modules:
  0.0 78.6 jit_solution(8579854553410678962)
XLA Ops:
  0.0 0.5 collective-permute-start.11
  0.5 0.0 collective-permute-start.12
  0.5 0.5 collective-permute-start.13
  1.0 2.6 %collective-permute-start = (bf16[128,512]{1,0:T(8,128)(2,1)}, bf16[128,512]{1,0:T(8,128)(2,1)S(1)}, u32[]{:S(2)}, u32[]{:S(2)}) collective-permute-start(bf16[128,512]{1,0:T(8,128)(2,1)} %down_hbm.1), channel_id=1, source_target_pairs={{0,1},{1,0},{2,3},{3,2},{4,5},{5,4},{6,7},{7,6},{8,9},{9,8},{10,11... | collective-permute-start | bytes 393224 | tf_op jit(solution)/shard_map/ppermute | solution.py:30
  3.6 2.6 %collective-permute-start.1 = (bf16[128,512]{1,0:T(8,128)(2,1)}, bf16[128,512]{1,0:T(8,128)(2,1)S(1)}, u32[]{:S(2)}, u32[]{:S(2)}) collective-permute-start(bf16[128,512]{1,0:T(8,128)(2,1)} %down_hbm.1), channel_id=1, source_target_pairs={{0,2},{1,3},{2,0},{3,1},{16,19},{17,18},{18,17},{19,16},{4,6},{5,7... | collective-permute-start | bytes 393224 | tf_op jit(solution)/shard_map/ppermute | solution.py:40
  6.2 4.3 %collective-permute-done.refs_1_ = bf16[128,512]{1,0:T(8,128)(2,1)S(1)} collective-permute-done((bf16[128,512]{1,0:T(8,128)(2,1)}, bf16[128,512]{1,0:T(8,128)(2,1)S(1)}, u32[]{:S(2)}, u32[]{:S(2)}) %collective-permute-start) | collective-permute-done | bytes 131104 | tf_op jit(solution)/shard_map/ppermute | solution.py:30
  10.4 1.8 %collective-permute-start.2 = (bf16[128,512]{1,0:T(8,128)(2,1)}, bf16[128,512]{1,0:T(8,128)(2,1)S(1)}, u32[]{:S(2)}, u32[]{:S(2)}) collective-permute-start(bf16[128,512]{1,0:T(8,128)(2,1)} %down_hbm.1), channel_id=1, source_target_pairs={{0,8},{4,12},{8,0},{12,4},{1,9},{5,13},{9,1},{13,5},{2,10},{6,14},... | collective-permute-start | bytes 393224 | tf_op jit(solution)/shard_map/ppermute | solution.py:30
  12.3 0.9 %collective-permute-done.1.refs_2_ = bf16[128,512]{1,0:T(8,128)(2,1)S(1)} collective-permute-done((bf16[128,512]{1,0:T(8,128)(2,1)}, bf16[128,512]{1,0:T(8,128)(2,1)S(1)}, u32[]{:S(2)}, u32[]{:S(2)}) %collective-permute-start.1) | collective-permute-done | bytes 131104 | tf_op jit(solution)/shard_map/ppermute | solution.py:40
  13.2 1.5 %collective-permute-start.16 = (bf16[128,512]{1,0:T(8,128)(2,1)}, bf16[128,512]{1,0:T(8,128)(2,1)S(1)}, u32[]{:S(2)}, u32[]{:S(2)}) collective-permute-start(bf16[128,512]{1,0:T(8,128)(2,1)} %up_hbm.1), channel_id=1, source_target_pairs={{0,8},{4,12},{8,0},{12,4},{1,9},{5,13},{9,1},{13,5},{2,10},{6,14},... | collective-permute-start | bytes 393224 | tf_op jit(solution)/shard_map/ppermute | solution.py:30
  14.7 2.3 %collective-permute-done.2.refs_3_ = bf16[128,512]{1,0:T(8,128)(2,1)S(1)} collective-permute-done((bf16[128,512]{1,0:T(8,128)(2,1)}, bf16[128,512]{1,0:T(8,128)(2,1)S(1)}, u32[]{:S(2)}, u32[]{:S(2)}) %collective-permute-start.2) | collective-permute-done | bytes 131104 | tf_op jit(solution)/shard_map/ppermute | solution.py:30
  17.0 1.8 %collective-permute-start.3 = (bf16[128,512]{1,0:T(8,128)(2,1)S(1)}, bf16[128,512]{1,0:T(8,128)(2,1)S(1)}, u32[]{:S(2)}, u32[]{:S(2)}) collective-permute-start(bf16[128,512]{1,0:T(8,128)(2,1)S(1)} %collective-permute-done.refs_1_), channel_id=1, source_target_pairs={{0,8},{4,12},{8,0},{12,4},{1,9},{5,13},{9,1},{13,5},{2,10},{6,14},... | collective-permute-start | bytes 393224 | tf_op jit(solution)/shard_map/ppermute | solution.py:30
  18.9 1.0 %collective-permute-done.16.refs_1_ = bf16[128,512]{1,0:T(8,128)(2,1)S(1)} collective-permute-done((bf16[128,512]{1,0:T(8,128)(2,1)}, bf16[128,512]{1,0:T(8,128)(2,1)S(1)}, u32[]{:S(2)}, u32[]{:S(2)}) %collective-permute-start.16) | collective-permute-done | bytes 131104 | tf_op jit(solution)/shard_map/ppermute | solution.py:30
  19.8 2.2 %collective-permute-start.5 = (bf16[128,512]{1,0:T(8,128)(2,1)S(1)}, bf16[128,512]{1,0:T(8,128)(2,1)S(1)}, u32[]{:S(2)}, u32[]{:S(2)}) collective-permute-start(bf16[128,512]{1,0:T(8,128)(2,1)S(1)} %collective-permute-done.1.refs_2_), channel_id=1, source_target_pairs={{0,24},{4,28},{8,16},{12,20},{16,8},{20,12},{24,0},{28,4},{1,25},{... | collective-permute-start | bytes 393224 | tf_op jit(solution)/shard_map/ppermute | solution.py:40
  22.1 1.3 %collective-permute-done.3.refs_4_ = bf16[128,512]{1,0:T(8,128)(2,1)S(1)} collective-permute-done((bf16[128,512]{1,0:T(8,128)(2,1)S(1)}, bf16[128,512]{1,0:T(8,128)(2,1)S(1)}, u32[]{:S(2)}, u32[]{:S(2)}) %collective-permute-start.3) | collective-permute-done | bytes 131104 | tf_op jit(solution)/shard_map/ppermute | solution.py:30
  23.4 1.8 %collective-permute-start.6 = (bf16[128,512]{1,0:T(8,128)(2,1)S(1)}, bf16[128,512]{1,0:T(8,128)(2,1)S(1)}, u32[]{:S(2)}, u32[]{:S(2)}) collective-permute-start(bf16[128,512]{1,0:T(8,128)(2,1)S(1)} %collective-permute-done.1.refs_2_), channel_id=1, source_target_pairs={{0,8},{4,12},{8,0},{12,4},{1,9},{5,13},{9,1},{13,5},{2,10},{6,14},... | collective-permute-start | bytes 393224 | tf_op jit(solution)/shard_map/ppermute | solution.py:30
  25.2 1.7 %shard_map.109 = (bf16[256,2048]{1,0:T(8,128)(2,1)S(1)}, bf16[128,512]{1,0:T(8,128)(2,1)S(1)}, bf16[128,512]{1,0:T(8,128)(2,1)S(1)}) custom-call(bf16[256,2048]{1,0:T(8,128)(2,1)} %tok_hbm.1, f32[1,2048]{1,0:T(1,128)} %bitcast.5, bf16[128,512]{1,0:T(8,128)(2,1)} %down_hbm.1, bf16[128,512]{1,0:T(8,128)(2,1)} %up_hbm.1), custom_call_target="tpu_custom_call" | custom-call | flops 4194304 | bytes 2097152 | tf_op jit(solution)/shard_map/pallas_call | solution.py:48
  27.0 0.0 collective-permute-done.5.refs_0_
  27.0 0.1 collective-permute-start.4
  27.0 1.3 %collective-permute-done.6.refs_1_ = bf16[128,512]{1,0:T(8,128)(2,1)S(1)} collective-permute-done((bf16[128,512]{1,0:T(8,128)(2,1)S(1)}, bf16[128,512]{1,0:T(8,128)(2,1)S(1)}, u32[]{:S(2)}, u32[]{:S(2)}) %collective-permute-start.6) | collective-permute-done | bytes 131104 | tf_op jit(solution)/shard_map/ppermute | solution.py:30
  28.4 0.2 collective-permute-start.7
  28.6 4.7 %collective-permute-done.7.refs_2_ = bf16[128,512]{1,0:T(8,128)(2,1)S(1)} collective-permute-done((bf16[128,512]{1,0:T(8,128)(2,1)S(1)}, bf16[128,512]{1,0:T(8,128)(2,1)S(1)}, u32[]{:S(2)}, u32[]{:S(2)}) %collective-permute-start.7) | collective-permute-done | bytes 131104 | tf_op jit(solution)/shard_map/ppermute | solution.py:30
  33.3 1.3 %collective-permute-done.8.refs_3_ = bf16[128,512]{1,0:T(8,128)(2,1)S(1)} collective-permute-done((bf16[128,512]{1,0:T(8,128)(2,1)S(1)}, bf16[128,512]{1,0:T(8,128)(2,1)S(1)}, u32[]{:S(2)}, u32[]{:S(2)}) %collective-permute-start.8) | collective-permute-done | bytes 131104 | tf_op jit(solution)/shard_map/ppermute | solution.py:30
  34.7 0.1 collective-permute-start.9
  34.8 1.2 %collective-permute-done.9.refs_4_ = bf16[128,512]{1,0:T(8,128)(2,1)S(1)} collective-permute-done((bf16[128,512]{1,0:T(8,128)(2,1)S(1)}, bf16[128,512]{1,0:T(8,128)(2,1)S(1)}, u32[]{:S(2)}, u32[]{:S(2)}) %collective-permute-start.9) | collective-permute-done | bytes 131104 | tf_op jit(solution)/shard_map/ppermute | solution.py:30
  36.0 0.1 collective-permute-start.10
  36.2 0.1 shard_map.117.refs_1_
  36.3 1.1 %collective-permute-done.10.refs_5_ = bf16[128,512]{1,0:T(8,128)(2,1)S(1)} collective-permute-done((bf16[128,512]{1,0:T(8,128)(2,1)S(1)}, bf16[128,512]{1,0:T(8,128)(2,1)S(1)}, u32[]{:S(2)}, u32[]{:S(2)}) %collective-permute-start.10) | collective-permute-done | bytes 131104 | tf_op jit(solution)/shard_map/ppermute | solution.py:30
  37.4 4.0 %collective-permute-start.18 = (bf16[512,256]{1,0:T(8,128)(2,1)S(1)}, bf16[512,256]{1,0:T(8,128)(2,1)S(1)}, u32[]{:S(2)}, u32[]{:S(2)}) collective-permute-start(bf16[512,256]{1,0:T(8,128)(2,1)S(1)} %shard_map.117.refs_1_), channel_id=1, source_target_pairs={{0,2},{1,3},{2,0},{3,1},{16,19},{17,18},{18,17},{19,16},{4,6},{5,7... | collective-permute-start | bytes 786440 | tf_op jit(solution)/shard_map/ppermute | solution.py:40
  41.4 2.1 %shard_map.112 = (f32[16,256]{1,0:T(8,128)S(1)}, bf16[4,768,512]{2,1,0:T(8,128)(2,1)S(1)}) custom-call(bf16[256,2048]{1,0:T(8,128)(2,1)S(1)} %get-tuple-element.10.normed_ref, s32[1,4,4,4]{3,2,1,0:T(4,128)} %list_hbm.1, bf16[16,2048]{1,0:T(8,128)(2,1)} %bitcast.4, s32[8,256]{1,0:T(8,128)} %bitcast.6, s32[8,256]{1,0:T(8,128)} %bitcast.7, ...), custom_call_target="tpu_custom_call" | custom-call | flops 33554432 | bytes 2097152 | tf_op jit(solution)/shard_map/pallas_call | solution.py:48
  43.6 0.0 copy-start
  43.6 0.6 shard_map.111.sum_ref
  44.2 0.4 shard_map.113.pay_ref
  44.6 6.5 %collective-permute-done.17.refs_2_ = bf16[512,256]{1,0:T(8,128)(2,1)S(1)} collective-permute-done((bf16[512,256]{1,0:T(8,128)(2,1)S(1)}, bf16[512,256]{1,0:T(8,128)(2,1)S(1)}, u32[]{:S(2)}, u32[]{:S(2)}) %collective-permute-start.17) | collective-permute-done | bytes 262176 | tf_op jit(solution)/shard_map/ppermute | solution.py:30
  51.1 1.8 %collective-permute-start.14 = (bf16[272,512]{1,0:T(8,128)(2,1)S(1)}, bf16[272,512]{1,0:T(8,128)(2,1)S(1)}, u32[]{:S(2)}, u32[]{:S(2)}) collective-permute-start(bf16[272,512]{1,0:T(8,128)(2,1)S(1)} %shard_map.113.pay_ref), channel_id=1, source_target_pairs={{0,8},{4,12},{8,0},{12,4},{1,9},{5,13},{9,1},{13,5},{2,10},{6,14},... | collective-permute-start | bytes 835592 | tf_op jit(solution)/shard_map/ppermute | solution.py:30
  53.0 0.4 collective-permute-done.18.refs_3_
  53.4 1.8 %collective-permute-start.19 = (bf16[512,256]{1,0:T(8,128)(2,1)S(1)}, bf16[512,256]{1,0:T(8,128)(2,1)S(1)}, u32[]{:S(2)}, u32[]{:S(2)}) collective-permute-start(bf16[512,256]{1,0:T(8,128)(2,1)S(1)} %collective-permute-done.18.refs_3_), channel_id=1, source_target_pairs={{0,16},{16,0},{1,17},{17,1},{2,18},{18,2},{3,19},{19,3},{4,20},{20... | collective-permute-start | bytes 786440 | tf_op jit(solution)/shard_map/ppermute | solution.py:30
  55.2 6.0 %collective-permute-done.19.refs_4_ = bf16[512,256]{1,0:T(8,128)(2,1)S(1)} collective-permute-done((bf16[512,256]{1,0:T(8,128)(2,1)S(1)}, bf16[512,256]{1,0:T(8,128)(2,1)S(1)}, u32[]{:S(2)}, u32[]{:S(2)}) %collective-permute-start.19) | collective-permute-done | bytes 262176 | tf_op jit(solution)/shard_map/ppermute | solution.py:30
  61.2 0.5 collective-permute-start.22
  61.7 0.1 collective-permute-start.21
  61.8 0.4 collective-permute-start.23
  62.2 4.1 %shard_map.115.sum_ref = f32[256,512]{1,0:T(8,128)S(1)} custom-call(bf16[272,512]{1,0:T(8,128)(2,1)S(1)} %collective-permute-done.14.pay_ref, bf16[4,512,768]{2,1,0:T(8,128)(2,1)S(1)} %copy-done, bf16[4,512,768]{2,1,0:T(8,128)(2,1)S(1)} %copy-done.1, bf16[4,768,512]{2,1,0:T(8,128)(2,1)S(1)} %get-tuple-element.13.refs_2_, ...), custom_call_target="tpu_custom_call" | custom-call | flops 3623878656 | bytes 14155776 | tf_op jit(solution)/shard_map/pallas_call | solution.py:48
  66.4 1.0 %shard_map.116 = bf16[128,512]{1,0:T(8,128)(2,1)S(1)} custom-call(bf16[272,512]{1,0:T(8,128)(2,1)S(1)} %collective-permute-done.14.pay_ref, f32[256,512]{1,0:T(8,128)S(1)} %shard_map.115.sum_ref, bf16[4,512,768]{2,1,0:T(8,128)(2,1)S(1)} %copy-done, bf16[4,512,768]{2,1,0:T(8,128)(2,1)S(1)} %copy-done.1, bf16[4,768,512]{2,1,0:T(8,128)(2,1)S(1)} %get-tuple-element.13.refs_2_, ...), custom_call_target="tpu_custom_call" | custom-call | flops 603979776 | bytes 4718592 | tf_op jit(solution)/shard_map/pallas_call | solution.py:48
  67.4 1.6 %collective-permute-start.15 = (bf16[128,512]{1,0:T(8,128)(2,1)S(1)}, bf16[128,512]{1,0:T(8,128)(2,1)S(1)}, u32[]{:S(2)}, u32[]{:S(2)}) collective-permute-start(bf16[128,512]{1,0:T(8,128)(2,1)S(1)} %shard_map.116), channel_id=1, source_target_pairs={{0,8},{4,12},{8,0},{12,4},{1,9},{5,13},{9,1},{13,5},{2,10},{6,14},... | collective-permute-start | bytes 393224 | tf_op jit(solution)/shard_map/ppermute | solution.py:30
  68.9 1.0 %shard_map.118 = bf16[128,512]{1,0:T(8,128)(2,1)S(1)} custom-call(bf16[272,512]{1,0:T(8,128)(2,1)S(1)} %collective-permute-done.14.pay_ref, f32[256,512]{1,0:T(8,128)S(1)} %shard_map.115.sum_ref, bf16[4,512,768]{2,1,0:T(8,128)(2,1)S(1)} %copy-done, bf16[4,512,768]{2,1,0:T(8,128)(2,1)S(1)} %copy-done.1, bf16[4,768,512]{2,1,0:T(8,128)(2,1)S(1)} %get-tuple-element.13.refs_2_, ...), custom_call_target="tpu_custom_call" | custom-call | flops 603979776 | bytes 4718592 | tf_op jit(solution)/shard_map/pallas_call | solution.py:48
  69.9 0.6 collective-permute-start.24
  70.5 5.4 %shard_map.114.near_ref = f32[256,512]{1,0:T(8,128)S(1)} custom-call(bf16[272,512]{1,0:T(8,128)(2,1)S(1)} %shard_map.113.pay_ref, bf16[4,512,768]{2,1,0:T(8,128)(2,1)S(1)} %copy-done, bf16[4,512,768]{2,1,0:T(8,128)(2,1)S(1)} %copy-done.1, bf16[4,768,512]{2,1,0:T(8,128)(2,1)S(1)} %get-tuple-element.13.refs_2_, ...), custom_call_target="tpu_custom_call" | custom-call | flops 4831838208 | bytes 18874368 | tf_op jit(solution)/shard_map/pallas_call | solution.py:48
  76.0 1.3 %shard_map.119.refs_9_ = bf16[256,2048]{1,0:T(8,128)(2,1)} custom-call(f32[256,512]{1,0:T(8,128)S(1)} %shard_map.114.near_ref, bf16[128,512]{1,0:T(8,128)(2,1)S(1)} %collective-permute-done.24.refs_0_, bf16[512,256]{1,0:T(8,128)(2,1)S(1)} %shard_map.117.refs_1_, bf16[512,256]{1,0:T(8,128)(2,1)S(1)} %collective-permute-done.17.refs_2_, ...), custom_call_target="tpu_custom_call" | custom-call | flops 268435456 | bytes 2097152 | tf_op jit(solution)/shard_map/pallas_call | solution.py:48
  77.3 1.3 %shard_map.120 = bf16[256,2048]{1,0:T(8,128)(2,1)} custom-call(f32[256,512]{1,0:T(8,128)S(1)} %shard_map.114.near_ref, bf16[128,512]{1,0:T(8,128)(2,1)S(1)} %collective-permute-done.15.refs_0_, bf16[512,256]{1,0:T(8,128)(2,1)S(1)} %shard_map.117.refs_1_, bf16[512,256]{1,0:T(8,128)(2,1)S(1)} %collective-permute-done.17.refs_2_, ...), custom_call_target="tpu_custom_call", output_to_operand_aliasing={{}: (10, {})} | custom-call | flops 268435456 | bytes 2097152 | tf_op jit(solution)/shard_map/pallas_call | solution.py:48
  (18 shorter events, 0.1 us)
Async XLA Ops:
  0.0 61.7 %collective-permute-start.11 = (bf16[4,512,768]{2,1,0:T(8,128)(2,1)}, bf16[4,512,768]{2,1,0:T(8,128)(2,1)S(1)}, u32[]{:S(2)}, u32[]{:S(2)}) collective-permute-start(bf16[4,512,768]{2,1,0:T(8,128)(2,1)} %refs_0_.7), channel_id=1, source_target_pairs={{0,4},{4,0},{8,12},{12,8},{1,5},{5,1},{9,13},{13,9},{2,6},{6,2},{1... | collective-permute-start | bytes 9437192 | tf_op jit(solution)/shard_map/ppermute | solution.py:30
  0.5 61.3 %collective-permute-start.12 = (bf16[4,512,768]{2,1,0:T(8,128)(2,1)}, bf16[4,512,768]{2,1,0:T(8,128)(2,1)S(1)}, u32[]{:S(2)}, u32[]{:S(2)}) collective-permute-start(bf16[4,512,768]{2,1,0:T(8,128)(2,1)} %refs_1_.7), channel_id=1, source_target_pairs={{0,4},{4,0},{8,12},{12,8},{1,5},{5,1},{9,13},{13,9},{2,6},{6,2},{1... | collective-permute-start | bytes 9437192 | tf_op jit(solution)/shard_map/ppermute | solution.py:30
  0.5 61.7 %collective-permute-start.13 = (bf16[4,768,512]{2,1,0:T(8,128)(2,1)}, bf16[4,768,512]{2,1,0:T(8,128)(2,1)S(1)}, u32[]{:S(2)}, u32[]{:S(2)}) collective-permute-start(bf16[4,768,512]{2,1,0:T(8,128)(2,1)} %last_hbm.1), channel_id=1, source_target_pairs={{0,4},{4,0},{8,12},{12,8},{1,5},{5,1},{9,13},{13,9},{2,6},{6,2},{1... | collective-permute-start | bytes 9437192 | tf_op jit(solution)/shard_map/ppermute | solution.py:30
  1.0 9.4 %collective-permute-start = (bf16[128,512]{1,0:T(8,128)(2,1)}, bf16[128,512]{1,0:T(8,128)(2,1)S(1)}, u32[]{:S(2)}, u32[]{:S(2)}) collective-permute-start(bf16[128,512]{1,0:T(8,128)(2,1)} %down_hbm.1), channel_id=1, source_target_pairs={{0,1},{1,0},{2,3},{3,2},{4,5},{5,4},{6,7},{7,6},{8,9},{9,8},{10,11... | collective-permute-start | bytes 393224 | tf_op jit(solution)/shard_map/ppermute | solution.py:30
  3.6 9.6 %collective-permute-start.1 = (bf16[128,512]{1,0:T(8,128)(2,1)}, bf16[128,512]{1,0:T(8,128)(2,1)S(1)}, u32[]{:S(2)}, u32[]{:S(2)}) collective-permute-start(bf16[128,512]{1,0:T(8,128)(2,1)} %down_hbm.1), channel_id=1, source_target_pairs={{0,2},{1,3},{2,0},{3,1},{16,19},{17,18},{18,17},{19,16},{4,6},{5,7... | collective-permute-start | bytes 393224 | tf_op jit(solution)/shard_map/ppermute | solution.py:40
  10.4 6.6 %collective-permute-start.2 = (bf16[128,512]{1,0:T(8,128)(2,1)}, bf16[128,512]{1,0:T(8,128)(2,1)S(1)}, u32[]{:S(2)}, u32[]{:S(2)}) collective-permute-start(bf16[128,512]{1,0:T(8,128)(2,1)} %down_hbm.1), channel_id=1, source_target_pairs={{0,8},{4,12},{8,0},{12,4},{1,9},{5,13},{9,1},{13,5},{2,10},{6,14},... | collective-permute-start | bytes 393224 | tf_op jit(solution)/shard_map/ppermute | solution.py:30
  13.2 6.7 %collective-permute-start.16 = (bf16[128,512]{1,0:T(8,128)(2,1)}, bf16[128,512]{1,0:T(8,128)(2,1)S(1)}, u32[]{:S(2)}, u32[]{:S(2)}) collective-permute-start(bf16[128,512]{1,0:T(8,128)(2,1)} %up_hbm.1), channel_id=1, source_target_pairs={{0,8},{4,12},{8,0},{12,4},{1,9},{5,13},{9,1},{13,5},{2,10},{6,14},... | collective-permute-start | bytes 393224 | tf_op jit(solution)/shard_map/ppermute | solution.py:30
  17.0 6.4 %collective-permute-start.3 = (bf16[128,512]{1,0:T(8,128)(2,1)S(1)}, bf16[128,512]{1,0:T(8,128)(2,1)S(1)}, u32[]{:S(2)}, u32[]{:S(2)}) collective-permute-start(bf16[128,512]{1,0:T(8,128)(2,1)S(1)} %collective-permute-done.refs_1_), channel_id=1, source_target_pairs={{0,8},{4,12},{8,0},{12,4},{1,9},{5,13},{9,1},{13,5},{2,10},{6,14},... | collective-permute-start | bytes 393224 | tf_op jit(solution)/shard_map/ppermute | solution.py:30
  19.8 7.1 %collective-permute-start.5 = (bf16[128,512]{1,0:T(8,128)(2,1)S(1)}, bf16[128,512]{1,0:T(8,128)(2,1)S(1)}, u32[]{:S(2)}, u32[]{:S(2)}) collective-permute-start(bf16[128,512]{1,0:T(8,128)(2,1)S(1)} %collective-permute-done.1.refs_2_), channel_id=1, source_target_pairs={{0,24},{4,28},{8,16},{12,20},{16,8},{20,12},{24,0},{28,4},{1,25},{... | collective-permute-start | bytes 393224 | tf_op jit(solution)/shard_map/ppermute | solution.py:40
  23.4 5.0 %collective-permute-start.6 = (bf16[128,512]{1,0:T(8,128)(2,1)S(1)}, bf16[128,512]{1,0:T(8,128)(2,1)S(1)}, u32[]{:S(2)}, u32[]{:S(2)}) collective-permute-start(bf16[128,512]{1,0:T(8,128)(2,1)S(1)} %collective-permute-done.1.refs_2_), channel_id=1, source_target_pairs={{0,8},{4,12},{8,0},{12,4},{1,9},{5,13},{9,1},{13,5},{2,10},{6,14},... | collective-permute-start | bytes 393224 | tf_op jit(solution)/shard_map/ppermute | solution.py:30
  27.0 10.4 %collective-permute-start.4 = (bf16[640,512]{1,0:T(8,128)(2,1)S(1)}, bf16[640,512]{1,0:T(8,128)(2,1)S(1)}, u32[]{:S(2)}, u32[]{:S(2)}) collective-permute-start(bf16[640,512]{1,0:T(8,128)(2,1)S(1)} %shard_map.110.w0_ref), channel_id=1, source_target_pairs={{0,4},{4,0},{8,12},{12,8},{1,5},{5,1},{9,13},{13,9},{2,6},{6,2},{1... | collective-permute-start | bytes 1966088 | tf_op jit(solution)/shard_map/ppermute | solution.py:30
  28.4 5.0 %collective-permute-start.7 = (bf16[128,512]{1,0:T(8,128)(2,1)S(1)}, bf16[128,512]{1,0:T(8,128)(2,1)S(1)}, u32[]{:S(2)}, u32[]{:S(2)}) collective-permute-start(bf16[128,512]{1,0:T(8,128)(2,1)S(1)} %collective-permute-done.1.refs_2_), channel_id=1, source_target_pairs={{0,16},{16,0},{1,17},{17,1},{2,18},{18,2},{3,19},{19,3},{4,20},{20... | collective-permute-start | bytes 393224 | tf_op jit(solution)/shard_map/ppermute | solution.py:30
  33.3 1.3 %collective-permute-start.8 = (bf16[128,512]{1,0:T(8,128)(2,1)S(1)}, bf16[128,512]{1,0:T(8,128)(2,1)S(1)}, u32[]{:S(2)}, u32[]{:S(2)}) collective-permute-start(bf16[128,512]{1,0:T(8,128)(2,1)S(1)} %collective-permute-done.5.refs_0_), channel_id=1, source_target_pairs={{0,4},{4,0},{8,12},{12,8},{1,5},{5,1},{9,13},{13,9},{2,6},{6,2},{1... | collective-permute-start | bytes 393224 | tf_op jit(solution)/shard_map/ppermute | solution.py:30
  34.7 1.3 %collective-permute-start.9 = (bf16[128,512]{1,0:T(8,128)(2,1)S(1)}, bf16[128,512]{1,0:T(8,128)(2,1)S(1)}, u32[]{:S(2)}, u32[]{:S(2)}) collective-permute-start(bf16[128,512]{1,0:T(8,128)(2,1)S(1)} %collective-permute-done.6.refs_1_), channel_id=1, source_target_pairs={{0,4},{4,0},{8,12},{12,8},{1,5},{5,1},{9,13},{13,9},{2,6},{6,2},{1... | collective-permute-start | bytes 393224 | tf_op jit(solution)/shard_map/ppermute | solution.py:30
  36.0 1.3 %collective-permute-start.10 = (bf16[128,512]{1,0:T(8,128)(2,1)S(1)}, bf16[128,512]{1,0:T(8,128)(2,1)S(1)}, u32[]{:S(2)}, u32[]{:S(2)}) collective-permute-start(bf16[128,512]{1,0:T(8,128)(2,1)S(1)} %collective-permute-done.7.refs_2_), channel_id=1, source_target_pairs={{0,4},{4,0},{8,12},{12,8},{1,5},{5,1},{9,13},{13,9},{2,6},{6,2},{1... | collective-permute-start | bytes 393224 | tf_op jit(solution)/shard_map/ppermute | solution.py:30
  37.4 13.7 %collective-permute-start.17 = (bf16[512,256]{1,0:T(8,128)(2,1)S(1)}, bf16[512,256]{1,0:T(8,128)(2,1)S(1)}, u32[]{:S(2)}, u32[]{:S(2)}) collective-permute-start(bf16[512,256]{1,0:T(8,128)(2,1)S(1)} %shard_map.117.refs_1_), channel_id=1, source_target_pairs={{0,1},{1,0},{2,3},{3,2},{4,5},{5,4},{6,7},{7,6},{8,9},{9,8},{10,11... | collective-permute-start | bytes 786440 | tf_op jit(solution)/shard_map/ppermute | solution.py:30
  37.4 16.0 %collective-permute-start.18 = (bf16[512,256]{1,0:T(8,128)(2,1)S(1)}, bf16[512,256]{1,0:T(8,128)(2,1)S(1)}, u32[]{:S(2)}, u32[]{:S(2)}) collective-permute-start(bf16[512,256]{1,0:T(8,128)(2,1)S(1)} %shard_map.117.refs_1_), channel_id=1, source_target_pairs={{0,2},{1,3},{2,0},{3,1},{16,19},{17,18},{18,17},{19,16},{4,6},{5,7... | collective-permute-start | bytes 786440 | tf_op jit(solution)/shard_map/ppermute | solution.py:40
  41.4 20.8 %copy-start.1 = (bf16[4,512,768]{2,1,0:T(8,128)(2,1)S(1)}, bf16[4,512,768]{2,1,0:T(8,128)(2,1)}, u32[]{:S(2)}) copy-start(bf16[4,512,768]{2,1,0:T(8,128)(2,1)} %refs_1_.7) | copy-start | bytes 9437188
  43.6 18.7 %copy-start = (bf16[4,512,768]{2,1,0:T(8,128)(2,1)S(1)}, bf16[4,512,768]{2,1,0:T(8,128)(2,1)}, u32[]{:S(2)}) copy-start(bf16[4,512,768]{2,1,0:T(8,128)(2,1)} %refs_0_.7) | copy-start | bytes 9437188
  51.1 10.1 %collective-permute-start.14 = (bf16[272,512]{1,0:T(8,128)(2,1)S(1)}, bf16[272,512]{1,0:T(8,128)(2,1)S(1)}, u32[]{:S(2)}, u32[]{:S(2)}) collective-permute-start(bf16[272,512]{1,0:T(8,128)(2,1)S(1)} %shard_map.113.pay_ref), channel_id=1, source_target_pairs={{0,8},{4,12},{8,0},{12,4},{1,9},{5,13},{9,1},{13,5},{2,10},{6,14},... | collective-permute-start | bytes 835592 | tf_op jit(solution)/shard_map/ppermute | solution.py:30
  53.4 7.8 %collective-permute-start.19 = (bf16[512,256]{1,0:T(8,128)(2,1)S(1)}, bf16[512,256]{1,0:T(8,128)(2,1)S(1)}, u32[]{:S(2)}, u32[]{:S(2)}) collective-permute-start(bf16[512,256]{1,0:T(8,128)(2,1)S(1)} %collective-permute-done.18.refs_3_), channel_id=1, source_target_pairs={{0,16},{16,0},{1,17},{17,1},{2,18},{18,2},{3,19},{19,3},{4,20},{20... | collective-permute-start | bytes 786440 | tf_op jit(solution)/shard_map/ppermute | solution.py:30
  61.2 8.7 %collective-permute-start.20 = (bf16[512,256]{1,0:T(8,128)(2,1)S(1)}, bf16[512,256]{1,0:T(8,128)(2,1)S(1)}, u32[]{:S(2)}, u32[]{:S(2)}) collective-permute-start(bf16[512,256]{1,0:T(8,128)(2,1)S(1)} %shard_map.117.refs_1_), channel_id=1, source_target_pairs={{0,4},{4,0},{8,12},{12,8},{1,5},{5,1},{9,13},{13,9},{2,6},{6,2},{1... | collective-permute-start | bytes 786440 | tf_op jit(solution)/shard_map/ppermute | solution.py:30
  61.2 14.8 %collective-permute-start.22 = (bf16[512,256]{1,0:T(8,128)(2,1)S(1)}, bf16[512,256]{1,0:T(8,128)(2,1)S(1)}, u32[]{:S(2)}, u32[]{:S(2)}) collective-permute-start(bf16[512,256]{1,0:T(8,128)(2,1)S(1)} %collective-permute-done.18.refs_3_), channel_id=1, source_target_pairs={{0,4},{4,0},{8,12},{12,8},{1,5},{5,1},{9,13},{13,9},{2,6},{6,2},{1... | collective-permute-start | bytes 786440 | tf_op jit(solution)/shard_map/ppermute | solution.py:30
  61.7 14.3 %collective-permute-start.21 = (bf16[512,256]{1,0:T(8,128)(2,1)S(1)}, bf16[512,256]{1,0:T(8,128)(2,1)S(1)}, u32[]{:S(2)}, u32[]{:S(2)}) collective-permute-start(bf16[512,256]{1,0:T(8,128)(2,1)S(1)} %collective-permute-done.17.refs_2_), channel_id=1, source_target_pairs={{0,4},{4,0},{8,12},{12,8},{1,5},{5,1},{9,13},{13,9},{2,6},{6,2},{1... | collective-permute-start | bytes 786440 | tf_op jit(solution)/shard_map/ppermute | solution.py:30
  61.8 14.2 %collective-permute-start.23 = (bf16[512,256]{1,0:T(8,128)(2,1)S(1)}, bf16[512,256]{1,0:T(8,128)(2,1)S(1)}, u32[]{:S(2)}, u32[]{:S(2)}) collective-permute-start(bf16[512,256]{1,0:T(8,128)(2,1)S(1)} %collective-permute-done.19.refs_4_), channel_id=1, source_target_pairs={{0,4},{4,0},{8,12},{12,8},{1,5},{5,1},{9,13},{13,9},{2,6},{6,2},{1... | collective-permute-start | bytes 786440 | tf_op jit(solution)/shard_map/ppermute | solution.py:30
  67.4 9.9 %collective-permute-start.15 = (bf16[128,512]{1,0:T(8,128)(2,1)S(1)}, bf16[128,512]{1,0:T(8,128)(2,1)S(1)}, u32[]{:S(2)}, u32[]{:S(2)}) collective-permute-start(bf16[128,512]{1,0:T(8,128)(2,1)S(1)} %shard_map.116), channel_id=1, source_target_pairs={{0,8},{4,12},{8,0},{12,4},{1,9},{5,13},{9,1},{13,5},{2,10},{6,14},... | collective-permute-start | bytes 393224 | tf_op jit(solution)/shard_map/ppermute | solution.py:30
  69.9 6.1 %collective-permute-start.24 = (bf16[128,512]{1,0:T(8,128)(2,1)S(1)}, bf16[128,512]{1,0:T(8,128)(2,1)S(1)}, u32[]{:S(2)}, u32[]{:S(2)}) collective-permute-start(bf16[128,512]{1,0:T(8,128)(2,1)S(1)} %shard_map.118), channel_id=1, source_target_pairs={{0,8},{4,12},{8,0},{12,4},{1,9},{5,13},{9,1},{13,5},{2,10},{6,14},... | collective-permute-start | bytes 393224 | tf_op jit(solution)/shard_map/ppermute | solution.py:30

commit v6 on v5

--- a/solution.py
+++ b/solution.py
@@ -57,8 +57,10 @@
     )(*operands)
 
 
-def norm_kernel(tok_hbm, gain_hbm, down_hbm, up_hbm, normed_ref, down_ref, up_ref, tok_ref, gain_ref, sem):
-    pairs = ((tok_hbm, tok_ref), (gain_hbm, gain_ref), (down_hbm, down_ref), (up_hbm, up_ref))
+def norm_kernel(tok_hbm, gain_hbm, down_hbm, up_hbm, last_hbm, normed_ref, down_ref, up_ref, last_ref,
+                tok_ref, gain_ref, sem):
+    pairs = ((tok_hbm, tok_ref), (gain_hbm, gain_ref), (down_hbm, down_ref), (up_hbm, up_ref),
+             (last_hbm, last_ref))
     copies = [pltpu.make_async_copy(src, dst, sem.at[i]) for i, (src, dst) in enumerate(pairs)]
     for copy in copies:
         copy.start()
@@ -71,14 +73,12 @@
         copy.wait()
 
 
-def gate_kernel(top, normed_ref, list_hbm, router_hbm, ids_hbm, slot_hbm, last_hbm, wt_ref, last_ref,
-                list_ref, router_ref, ids_ref, slot_ref, sem):
-    pairs = ((router_hbm, router_ref), (ids_hbm, ids_ref), (slot_hbm, slot_ref), (list_hbm, list_ref),
-             (last_hbm, last_ref))
+def gate_kernel(top, normed_ref, list_hbm, router_hbm, ids_hbm, slot_hbm, wt_ref, list_ref, router_ref, ids_ref, slot_ref, sem):
+    pairs = ((router_hbm, router_ref), (ids_hbm, ids_ref), (slot_hbm, slot_ref), (list_hbm, list_ref))
     copies = [pltpu.make_async_copy(src, dst, sem.at[i]) for i, (src, dst) in enumerate(pairs)]
     for copy in copies:
         copy.start()
-    for copy in copies[:4]:
+    for copy in copies:
         copy.wait()
     logits = lax.dot_general(router_ref[...], normed_ref[...], (((1,), (1,)), ((), ())),
                              preferred_element_type=F32)
@@ -105,8 +105,6 @@
     served = lax.fori_loop(0, shards * copies_n, listed, served)
     denom = jnp.sum(total * sig, axis=0, keepdims=True)
     wt_ref[...] = jnp.where(served > 0.0, sig / denom, 0.0)
-    for copy in copies[4:]:
-        copy.wait()
 
 
 def pile_kernel(*refs):
@@ -172,7 +170,7 @@
     cols = columns(lax.axis_index("expert"), local, pay_ref, at, size)
     x = pay_ref[at:at + size, :]
     for j in span:
-        refs = w_refs[:3] if j < local else w_refs[3:]
+        refs = w_refs[:3] if j < local else w_refs[-3:]
         part = expert(x, cols[:, j:j + 1], *(ref[j % local] for ref in refs))
         if j == span[0]:
             out_ref[...] = part if start_ref is None else start_ref[at:at + size, :] + part
@@ -181,7 +179,11 @@
 
 
 def near_kernel(span, pay_ref, *refs):
-    run_experts(span, 0, refs[-1].shape[0], pay_ref, refs[:6], refs[-1])
+    run_experts(span, 0, refs[-1].shape[0], pay_ref, refs[:-1], refs[-1])
+
+
+def more_kernel(span, pay_ref, sum_ref, *refs):
+    run_experts(span, 0, refs[-1].shape[0], pay_ref, refs[:-1], refs[-1], sum_ref)
 
 
 def far_kernel(span, at, pay_ref, sum_ref, *refs):
@@ -261,19 +263,19 @@
                 down[(a, b)] = swap(down[(0, b)], "expert", 2 * a)
         ups_x = [swap(up_proj, "expert", 2 * a) for a in range(1, chips)]
 
-    normed, own_down, own_up = kernel(
-        norm_kernel, (shape((rows, width)), shape(down_proj.shape), shape(up_proj.shape)),
-        tuple(map(in_hbm, (tokens, norm_gain.reshape(1, width), down_proj, up_proj))),
-        [AN] * 4, 16, 8 * rows * width, 4 * rows * width,
-        [pltpu.VMEM((rows, width), BF16), pltpu.VMEM((1, width), F32), pltpu.SemaphoreType.DMA((4,))])
-    wt, last = kernel(
-        functools.partial(gate_kernel, top),
-        (shape((experts, rows), F32), shape(expert_down.shape)),
-        (normed, *map(in_hbm, (overflow_list, router.T, expert_ids.T, slot_pos.T, expert_down))),
-        [VM] + [AN] * 5, 14, 4 * rows * width * experts, 4 * rows * width,
+    normed, own_down, own_up, last = kernel(
+        norm_kernel, tuple(map(shape, ((rows, width), down_proj.shape, up_proj.shape,
+                                       expert_down.shape))),
+        tuple(map(in_hbm, (tokens, norm_gain.reshape(1, width), down_proj, up_proj, expert_down))),
+        [AN] * 5, 18, 8 * rows * width, 4 * rows * width,
+        [pltpu.VMEM((rows, width), BF16), pltpu.VMEM((1, width), F32), pltpu.SemaphoreType.DMA((5,))])
+    wt = kernel(
+        functools.partial(gate_kernel, top), shape((experts, rows), F32),
+        (normed, *map(in_hbm, (overflow_list, router.T, expert_ids.T, slot_pos.T))),
+        [VM] + [AN] * 4, 10, 4 * rows * width * experts, 2 * rows * width,
         [pltpu.SMEM(overflow_list.shape, jnp.int32), pltpu.VMEM((experts, width), BF16),
          pltpu.VMEM((top, rows), jnp.int32), pltpu.VMEM((top, rows), jnp.int32),
-         pltpu.SemaphoreType.DMA((5,))])
+         pltpu.SemaphoreType.DMA((4,))])
     down[(0, 0)] = own_down
     weights = (expert_gate, expert_up, last, *[
         swap(w, "expert", 1) for w in (expert_gate, expert_up, expert_down)])
@@ -302,17 +304,19 @@
     cut = count - local // 2
     far = [swap(own, "expert", 2 * a) for a in range(1, chips)]
 
-    def run(payload, span):
+    def run(body, operands, span):
         return kernel(
-            functools.partial(near_kernel, span), shape((rows, latent), F32), (payload, *weights),
-            [VM] * 7, 16, len(span) * work, len(span) * load)
-
-    near = run(own, range(count))
+            functools.partial(body, span), shape((rows, latent), F32), operands, [VM] * len(operands),
+            16, len(span) * work, len(span) * load)
+
+    near = run(near_kernel, (own, *weights[:3]), range(local))
+    near = run(more_kernel, (own, near, *weights), range(local, cut))
+    near = run(more_kernel, (own, near, *weights), range(cut, count))
     parts = 2
     size = rows // parts
     back = [[] for _ in range(parts)]
     for a in range(1, chips):
-        opened = run(far[a - 1], range(cut))
+        opened = run(near_kernel, (far[a - 1], *weights), range(cut))
         for h in range(parts):
             s = kernel(
                 functools.partial(far_kernel, range(cut, count), h * size),

time: 78.8 us -> 78.1 us (level)
  Pallas kernels: 19.1 us -> 20 us
  waiting for transfers between devices: 32.5 us -> 31.6 us
    ppermute x22, waiting for transfers between devices: 31.1 us -> 30 us  [swap(): return lax.ppermute(x, axis, [(i, i ^ bits) for i in range(size)])]
    pallas_call x12 -> x14, Pallas kernels: 19.1 us -> 20 us  [kernel(): pl.pallas_call(body, out_shape=out_shape, in_specs=specs, out_specs=out_s...]
  transfers between devices with their start and end apart: 25 -> 25, of which waited for: 13 -> 14; matrix products, arithmetic and copies ran while one was open for 0% -> 0% of each run, Pallas kernels for 23% -> 24%
where the time goes in v6:
time: 78.1 us; the launch traced here: 77.9 us
  waiting for transfers between devices  31.6 us (40%)
  starting transfers between devices  26.2 us (34%)
  Pallas kernels  20 us (26%)
    ppermute x22, waiting for transfers between devices, swap(): return lax.ppermute(x, axis, [(i, i ^ bits) for i in range(size)])  30 us
    pallas_call x14, Pallas kernels, kernel(): pl.pallas_call(body, out_shape=out_shape, in_specs=specs, out_specs=out_s...  20 us
    ppermute x22, starting transfers between devices, swap(): return lax.ppermute(x, axis, [(i, i ^ bits) for i in range(size)])  17.4 us
    ppermute x3, starting transfers between devices, swap_pair(): return lax.ppermute(x, axes, pairs)  8.79 us
    ppermute x3, waiting for transfers between devices, swap_pair(): return lax.ppermute(x, axes, pairs)  1.58 us
  transfers between devices with their start and end apart: 25, of which 14 were waited for; matrix products, arithmetic and copies ran while one was open for 0% of the time, Pallas kernels for 24%

profile of v6, /device:TPU:0, one launch (start us, length us, event | category | flops | bytes accessed | tf_op | source)
XLA Modules:
  0.0 77.9 jit_solution(13907462448823864299)
XLA Ops:
  0.0 0.5 collective-permute-start.11
  0.5 0.5 collective-permute-start.13
  1.0 2.6 %collective-permute-start = (bf16[128,512]{1,0:T(8,128)(2,1)}, bf16[128,512]{1,0:T(8,128)(2,1)S(1)}, u32[]{:S(2)}, u32[]{:S(2)}) collective-permute-start(bf16[128,512]{1,0:T(8,128)(2,1)} %down_hbm.1), channel_id=1, source_target_pairs={{0,1},{1,0},{2,3},{3,2},{4,5},{5,4},{6,7},{7,6},{8,9},{9,8},{10,11... | collective-permute-start | bytes 393224 | tf_op jit(solution)/shard_map/ppermute | solution.py:30
  3.6 2.6 %collective-permute-start.1 = (bf16[128,512]{1,0:T(8,128)(2,1)}, bf16[128,512]{1,0:T(8,128)(2,1)S(1)}, u32[]{:S(2)}, u32[]{:S(2)}) collective-permute-start(bf16[128,512]{1,0:T(8,128)(2,1)} %down_hbm.1), channel_id=1, source_target_pairs={{0,2},{1,3},{2,0},{3,1},{16,19},{17,18},{18,17},{19,16},{4,6},{5,7... | collective-permute-start | bytes 393224 | tf_op jit(solution)/shard_map/ppermute | solution.py:40
  6.2 4.3 %collective-permute-done.refs_1_ = bf16[128,512]{1,0:T(8,128)(2,1)S(1)} collective-permute-done((bf16[128,512]{1,0:T(8,128)(2,1)}, bf16[128,512]{1,0:T(8,128)(2,1)S(1)}, u32[]{:S(2)}, u32[]{:S(2)}) %collective-permute-start) | collective-permute-done | bytes 131104 | tf_op jit(solution)/shard_map/ppermute | solution.py:30
  10.4 1.8 %collective-permute-start.2 = (bf16[128,512]{1,0:T(8,128)(2,1)}, bf16[128,512]{1,0:T(8,128)(2,1)S(1)}, u32[]{:S(2)}, u32[]{:S(2)}) collective-permute-start(bf16[128,512]{1,0:T(8,128)(2,1)} %down_hbm.1), channel_id=1, source_target_pairs={{0,8},{4,12},{8,0},{12,4},{1,9},{5,13},{9,1},{13,5},{2,10},{6,14},... | collective-permute-start | bytes 393224 | tf_op jit(solution)/shard_map/ppermute | solution.py:30
  12.3 0.9 %collective-permute-done.1.refs_2_ = bf16[128,512]{1,0:T(8,128)(2,1)S(1)} collective-permute-done((bf16[128,512]{1,0:T(8,128)(2,1)}, bf16[128,512]{1,0:T(8,128)(2,1)S(1)}, u32[]{:S(2)}, u32[]{:S(2)}) %collective-permute-start.1) | collective-permute-done | bytes 131104 | tf_op jit(solution)/shard_map/ppermute | solution.py:40
  13.2 1.5 %collective-permute-start.16 = (bf16[128,512]{1,0:T(8,128)(2,1)}, bf16[128,512]{1,0:T(8,128)(2,1)S(1)}, u32[]{:S(2)}, u32[]{:S(2)}) collective-permute-start(bf16[128,512]{1,0:T(8,128)(2,1)} %up_hbm.1), channel_id=1, source_target_pairs={{0,8},{4,12},{8,0},{12,4},{1,9},{5,13},{9,1},{13,5},{2,10},{6,14},... | collective-permute-start | bytes 393224 | tf_op jit(solution)/shard_map/ppermute | solution.py:30
  14.7 2.3 %collective-permute-done.2.refs_3_ = bf16[128,512]{1,0:T(8,128)(2,1)S(1)} collective-permute-done((bf16[128,512]{1,0:T(8,128)(2,1)}, bf16[128,512]{1,0:T(8,128)(2,1)S(1)}, u32[]{:S(2)}, u32[]{:S(2)}) %collective-permute-start.2) | collective-permute-done | bytes 131104 | tf_op jit(solution)/shard_map/ppermute | solution.py:30
  17.0 1.8 %collective-permute-start.3 = (bf16[128,512]{1,0:T(8,128)(2,1)S(1)}, bf16[128,512]{1,0:T(8,128)(2,1)S(1)}, u32[]{:S(2)}, u32[]{:S(2)}) collective-permute-start(bf16[128,512]{1,0:T(8,128)(2,1)S(1)} %collective-permute-done.refs_1_), channel_id=1, source_target_pairs={{0,8},{4,12},{8,0},{12,4},{1,9},{5,13},{9,1},{13,5},{2,10},{6,14},... | collective-permute-start | bytes 393224 | tf_op jit(solution)/shard_map/ppermute | solution.py:30
  18.9 1.0 %collective-permute-done.16.refs_1_ = bf16[128,512]{1,0:T(8,128)(2,1)S(1)} collective-permute-done((bf16[128,512]{1,0:T(8,128)(2,1)}, bf16[128,512]{1,0:T(8,128)(2,1)S(1)}, u32[]{:S(2)}, u32[]{:S(2)}) %collective-permute-start.16) | collective-permute-done | bytes 131104 | tf_op jit(solution)/shard_map/ppermute | solution.py:30
  19.8 2.2 %collective-permute-start.5 = (bf16[128,512]{1,0:T(8,128)(2,1)S(1)}, bf16[128,512]{1,0:T(8,128)(2,1)S(1)}, u32[]{:S(2)}, u32[]{:S(2)}) collective-permute-start(bf16[128,512]{1,0:T(8,128)(2,1)S(1)} %collective-permute-done.1.refs_2_), channel_id=1, source_target_pairs={{0,24},{4,28},{8,16},{12,20},{16,8},{20,12},{24,0},{28,4},{1,25},{... | collective-permute-start | bytes 393224 | tf_op jit(solution)/shard_map/ppermute | solution.py:40
  22.1 1.3 %collective-permute-done.3.refs_4_ = bf16[128,512]{1,0:T(8,128)(2,1)S(1)} collective-permute-done((bf16[128,512]{1,0:T(8,128)(2,1)S(1)}, bf16[128,512]{1,0:T(8,128)(2,1)S(1)}, u32[]{:S(2)}, u32[]{:S(2)}) %collective-permute-start.3) | collective-permute-done | bytes 131104 | tf_op jit(solution)/shard_map/ppermute | solution.py:30
  23.4 1.8 %collective-permute-start.6 = (bf16[128,512]{1,0:T(8,128)(2,1)S(1)}, bf16[128,512]{1,0:T(8,128)(2,1)S(1)}, u32[]{:S(2)}, u32[]{:S(2)}) collective-permute-start(bf16[128,512]{1,0:T(8,128)(2,1)S(1)} %collective-permute-done.1.refs_2_), channel_id=1, source_target_pairs={{0,8},{4,12},{8,0},{12,4},{1,9},{5,13},{9,1},{13,5},{2,10},{6,14},... | collective-permute-start | bytes 393224 | tf_op jit(solution)/shard_map/ppermute | solution.py:30
  25.2 2.4 %shard_map.109 = (bf16[256,2048]{1,0:T(8,128)(2,1)S(1)}, bf16[128,512]{1,0:T(8,128)(2,1)S(1)}, bf16[128,512]{1,0:T(8,128)(2,1)S(1)}, bf16[4,768,512]{2,1,0:T(8,128)(2,1)S(1)}) custom-call(bf16[256,2048]{1,0:T(8,128)(2,1)} %tok_hbm.1, f32[1,2048]{1,0:T(1,128)} %bitcast.5, bf16[128,512]{1,0:T(8,128)(2,1)} %down_hbm.1, bf16[128,512]{1,0:T(8,128)(2,1)} %up_hbm.1, ...), custom_call_target="tpu_custom_call" | custom-call | flops 4194304 | bytes 2097152 | tf_op jit(solution)/shard_map/pallas_call | solution.py:48
  27.6 0.1 collective-permute-start.4
  27.7 0.6 collective-permute-done.6.refs_1_
  28.4 0.2 collective-permute-start.7
  28.6 5.0 %collective-permute-done.7.refs_2_ = bf16[128,512]{1,0:T(8,128)(2,1)S(1)} collective-permute-done((bf16[128,512]{1,0:T(8,128)(2,1)S(1)}, bf16[128,512]{1,0:T(8,128)(2,1)S(1)}, u32[]{:S(2)}, u32[]{:S(2)}) %collective-permute-start.7) | collective-permute-done | bytes 131104 | tf_op jit(solution)/shard_map/ppermute | solution.py:30
  33.6 1.3 %collective-permute-done.8.refs_3_ = bf16[128,512]{1,0:T(8,128)(2,1)S(1)} collective-permute-done((bf16[128,512]{1,0:T(8,128)(2,1)S(1)}, bf16[128,512]{1,0:T(8,128)(2,1)S(1)}, u32[]{:S(2)}, u32[]{:S(2)}) %collective-permute-start.8) | collective-permute-done | bytes 131104 | tf_op jit(solution)/shard_map/ppermute | solution.py:30
  35.0 0.1 collective-permute-start.9
  35.1 1.2 %collective-permute-done.9.refs_4_ = bf16[128,512]{1,0:T(8,128)(2,1)S(1)} collective-permute-done((bf16[128,512]{1,0:T(8,128)(2,1)S(1)}, bf16[128,512]{1,0:T(8,128)(2,1)S(1)}, u32[]{:S(2)}, u32[]{:S(2)}) %collective-permute-start.9) | collective-permute-done | bytes 131104 | tf_op jit(solution)/shard_map/ppermute | solution.py:30
  36.3 0.1 collective-permute-start.10
  36.5 0.1 shard_map.119.refs_1_
  36.6 1.1 %collective-permute-done.10.refs_5_ = bf16[128,512]{1,0:T(8,128)(2,1)S(1)} collective-permute-done((bf16[128,512]{1,0:T(8,128)(2,1)S(1)}, bf16[128,512]{1,0:T(8,128)(2,1)S(1)}, u32[]{:S(2)}, u32[]{:S(2)}) %collective-permute-start.10) | collective-permute-done | bytes 131104 | tf_op jit(solution)/shard_map/ppermute | solution.py:30
  37.7 4.0 %collective-permute-start.18 = (bf16[512,256]{1,0:T(8,128)(2,1)S(1)}, bf16[512,256]{1,0:T(8,128)(2,1)S(1)}, u32[]{:S(2)}, u32[]{:S(2)}) collective-permute-start(bf16[512,256]{1,0:T(8,128)(2,1)S(1)} %shard_map.119.refs_1_), channel_id=1, source_target_pairs={{0,2},{1,3},{2,0},{3,1},{16,19},{17,18},{18,17},{19,16},{4,6},{5,7... | collective-permute-start | bytes 786440 | tf_op jit(solution)/shard_map/ppermute | solution.py:40
  41.6 2.0 %shard_map.112.wt_ref = f32[16,256]{1,0:T(8,128)S(1)} custom-call(bf16[256,2048]{1,0:T(8,128)(2,1)S(1)} %get-tuple-element.9.normed_ref, s32[1,4,4,4]{3,2,1,0:T(4,128)} %list_hbm.1, bf16[16,2048]{1,0:T(8,128)(2,1)} %bitcast.4, s32[8,256]{1,0:T(8,128)} %bitcast.6, s32[8,256]{1,0:T(8,128)} %bitcast.7), custom_call_target="tpu_custom_call" | custom-call | flops 33554432 | bytes 1048576 | tf_op jit(solution)/shard_map/pallas_call | solution.py:48
  43.7 0.6 shard_map.111.sum_ref
  44.3 0.4 shard_map.113.pay_ref
  44.7 6.7 %collective-permute-done.17.refs_2_ = bf16[512,256]{1,0:T(8,128)(2,1)S(1)} collective-permute-done((bf16[512,256]{1,0:T(8,128)(2,1)S(1)}, bf16[512,256]{1,0:T(8,128)(2,1)S(1)}, u32[]{:S(2)}, u32[]{:S(2)}) %collective-permute-start.17) | collective-permute-done | bytes 262176 | tf_op jit(solution)/shard_map/ppermute | solution.py:30
  51.4 1.5 %collective-permute-start.14 = (bf16[272,512]{1,0:T(8,128)(2,1)S(1)}, bf16[272,512]{1,0:T(8,128)(2,1)S(1)}, u32[]{:S(2)}, u32[]{:S(2)}) collective-permute-start(bf16[272,512]{1,0:T(8,128)(2,1)S(1)} %shard_map.113.pay_ref), channel_id=1, source_target_pairs={{0,8},{4,12},{8,0},{12,4},{1,9},{5,13},{9,1},{13,5},{2,10},{6,14},... | collective-permute-start | bytes 835592 | tf_op jit(solution)/shard_map/ppermute | solution.py:30
  53.0 0.7 collective-permute-done.18.refs_3_
  53.6 1.6 %collective-permute-start.19 = (bf16[512,256]{1,0:T(8,128)(2,1)S(1)}, bf16[512,256]{1,0:T(8,128)(2,1)S(1)}, u32[]{:S(2)}, u32[]{:S(2)}) collective-permute-start(bf16[512,256]{1,0:T(8,128)(2,1)S(1)} %collective-permute-done.18.refs_3_), channel_id=1, source_target_pairs={{0,16},{16,0},{1,17},{17,1},{2,18},{18,2},{3,19},{19,3},{4,20},{20... | collective-permute-start | bytes 786440 | tf_op jit(solution)/shard_map/ppermute | solution.py:30
  55.2 2.8 %shard_map.114.sum_ref = f32[256,512]{1,0:T(8,128)S(1)} custom-call(bf16[272,512]{1,0:T(8,128)(2,1)S(1)} %shard_map.113.pay_ref, bf16[4,512,768]{2,1,0:T(8,128)(2,1)S(1)} %copy-done, bf16[4,512,768]{2,1,0:T(8,128)(2,1)S(1)} %copy-done.1, bf16[4,768,512]{2,1,0:T(8,128)(2,1)S(1)} %get-tuple-element.11.refs_2_), custom_call_target="tpu_custom_call" | custom-call | flops 2415919104 | bytes 9437184 | tf_op jit(solution)/shard_map/pallas_call | solution.py:48
  58.0 3.2 %collective-permute-done.19.refs_4_ = bf16[512,256]{1,0:T(8,128)(2,1)S(1)} collective-permute-done((bf16[512,256]{1,0:T(8,128)(2,1)S(1)}, bf16[512,256]{1,0:T(8,128)(2,1)S(1)}, u32[]{:S(2)}, u32[]{:S(2)}) %collective-permute-start.19) | collective-permute-done | bytes 262176 | tf_op jit(solution)/shard_map/ppermute | solution.py:30
  61.2 0.5 collective-permute-start.22
  61.7 0.1 collective-permute-start.21
  61.8 0.4 collective-permute-start.23
  62.2 4.1 %shard_map.117.sum_ref = f32[256,512]{1,0:T(8,128)S(1)} custom-call(bf16[272,512]{1,0:T(8,128)(2,1)S(1)} %collective-permute-done.14.pay_ref, bf16[4,512,768]{2,1,0:T(8,128)(2,1)S(1)} %copy-done, bf16[4,512,768]{2,1,0:T(8,128)(2,1)S(1)} %copy-done.1, bf16[4,768,512]{2,1,0:T(8,128)(2,1)S(1)} %get-tuple-element.11.refs_2_, ...), custom_call_target="tpu_custom_call" | custom-call | flops 3623878656 | bytes 14155776 | tf_op jit(solution)/shard_map/pallas_call | solution.py:48
  66.4 1.0 %shard_map.120 = bf16[128,512]{1,0:T(8,128)(2,1)S(1)} custom-call(bf16[272,512]{1,0:T(8,128)(2,1)S(1)} %collective-permute-done.14.pay_ref, f32[256,512]{1,0:T(8,128)S(1)} %shard_map.117.sum_ref, bf16[4,512,768]{2,1,0:T(8,128)(2,1)S(1)} %copy-done, bf16[4,512,768]{2,1,0:T(8,128)(2,1)S(1)} %copy-done.1, bf16[4,768,512]{2,1,0:T(8,128)(2,1)S(1)} %get-tuple-element.11.refs_2_, ...), custom_call_target="tpu_custom_call" | custom-call | flops 603979776 | bytes 4718592 | tf_op jit(solution)/shard_map/pallas_call | solution.py:48
  67.3 1.6 %collective-permute-start.24 = (bf16[128,512]{1,0:T(8,128)(2,1)S(1)}, bf16[128,512]{1,0:T(8,128)(2,1)S(1)}, u32[]{:S(2)}, u32[]{:S(2)}) collective-permute-start(bf16[128,512]{1,0:T(8,128)(2,1)S(1)} %shard_map.120), channel_id=1, source_target_pairs={{0,8},{4,12},{8,0},{12,4},{1,9},{5,13},{9,1},{13,5},{2,10},{6,14},... | collective-permute-start | bytes 393224 | tf_op jit(solution)/shard_map/ppermute | solution.py:30
  68.9 1.5 %shard_map.115.sum_ref = f32[256,512]{1,0:T(8,128)S(1)} custom-call(bf16[272,512]{1,0:T(8,128)(2,1)S(1)} %shard_map.113.pay_ref, f32[256,512]{1,0:T(8,128)S(1)} %shard_map.114.sum_ref, bf16[4,512,768]{2,1,0:T(8,128)(2,1)S(1)} %copy-done, bf16[4,512,768]{2,1,0:T(8,128)(2,1)S(1)} %copy-done.1, bf16[4,768,512]{2,1,0:T(8,128)(2,1)S(1)} %get-tuple-element.11.refs_2_, ...), custom_call_target="tpu_custom_call" | custom-call | flops 1207959552 | bytes 4718592 | tf_op jit(solution)/shard_map/pallas_call | solution.py:48
  70.4 1.0 %shard_map.118 = bf16[128,512]{1,0:T(8,128)(2,1)S(1)} custom-call(bf16[272,512]{1,0:T(8,128)(2,1)S(1)} %collective-permute-done.14.pay_ref, f32[256,512]{1,0:T(8,128)S(1)} %shard_map.117.sum_ref, bf16[4,512,768]{2,1,0:T(8,128)(2,1)S(1)} %copy-done, bf16[4,512,768]{2,1,0:T(8,128)(2,1)S(1)} %copy-done.1, bf16[4,768,512]{2,1,0:T(8,128)(2,1)S(1)} %get-tuple-element.11.refs_2_, ...), custom_call_target="tpu_custom_call" | custom-call | flops 603979776 | bytes 4718592 | tf_op jit(solution)/shard_map/pallas_call | solution.py:48
  71.4 0.6 collective-permute-start.15
  72.0 1.5 %shard_map.116.near_ref = f32[256,512]{1,0:T(8,128)S(1)} custom-call(bf16[272,512]{1,0:T(8,128)(2,1)S(1)} %shard_map.113.pay_ref, f32[256,512]{1,0:T(8,128)S(1)} %shard_map.115.sum_ref, bf16[4,512,768]{2,1,0:T(8,128)(2,1)S(1)} %copy-done, bf16[4,512,768]{2,1,0:T(8,128)(2,1)S(1)} %copy-done.1, bf16[4,768,512]{2,1,0:T(8,128)(2,1)S(1)} %get-tuple-element.11.refs_2_, ...), custom_call_target="tpu_custom_call" | custom-call | flops 1207959552 | bytes 4718592 | tf_op jit(solution)/shard_map/pallas_call | solution.py:48
  73.5 1.3 %shard_map.121.refs_9_ = bf16[256,2048]{1,0:T(8,128)(2,1)} custom-call(f32[256,512]{1,0:T(8,128)S(1)} %shard_map.116.near_ref, bf16[128,512]{1,0:T(8,128)(2,1)S(1)} %collective-permute-done.24.refs_0_, bf16[512,256]{1,0:T(8,128)(2,1)S(1)} %shard_map.119.refs_1_, bf16[512,256]{1,0:T(8,128)(2,1)S(1)} %collective-permute-done.17.refs_2_, ...), custom_call_target="tpu_custom_call" | custom-call | flops 268435456 | bytes 2097152 | tf_op jit(solution)/shard_map/pallas_call | solution.py:48
  74.8 1.8 %collective-permute-done.15.refs_0_ = bf16[128,512]{1,0:T(8,128)(2,1)S(1)} collective-permute-done((bf16[128,512]{1,0:T(8,128)(2,1)S(1)}, bf16[128,512]{1,0:T(8,128)(2,1)S(1)}, u32[]{:S(2)}, u32[]{:S(2)}) %collective-permute-start.15) | collective-permute-done | bytes 131104 | tf_op jit(solution)/shard_map/ppermute | solution.py:30
  76.6 1.3 %shard_map.122 = bf16[256,2048]{1,0:T(8,128)(2,1)} custom-call(f32[256,512]{1,0:T(8,128)S(1)} %shard_map.116.near_ref, bf16[128,512]{1,0:T(8,128)(2,1)S(1)} %collective-permute-done.15.refs_0_, bf16[512,256]{1,0:T(8,128)(2,1)S(1)} %shard_map.119.refs_1_, bf16[512,256]{1,0:T(8,128)(2,1)S(1)} %collective-permute-done.17.refs_2_, ...), custom_call_target="tpu_custom_call", output_to_operand_aliasing={{}: (10, {})} | custom-call | flops 268435456 | bytes 2097152 | tf_op jit(solution)/shard_map/pallas_call | solution.py:48
  (20 shorter events, 0.1 us)
Async XLA Ops:
  0.0 61.7 %collective-permute-start.11 = (bf16[4,512,768]{2,1,0:T(8,128)(2,1)}, bf16[4,512,768]{2,1,0:T(8,128)(2,1)S(1)}, u32[]{:S(2)}, u32[]{:S(2)}) collective-permute-start(bf16[4,512,768]{2,1,0:T(8,128)(2,1)} %refs_0_.11), channel_id=1, source_target_pairs={{0,4},{4,0},{8,12},{12,8},{1,5},{5,1},{9,13},{13,9},{2,6},{6,2},{1... | collective-permute-start | bytes 9437192 | tf_op jit(solution)/shard_map/ppermute | solution.py:30
  0.5 61.3 %collective-permute-start.12 = (bf16[4,512,768]{2,1,0:T(8,128)(2,1)}, bf16[4,512,768]{2,1,0:T(8,128)(2,1)S(1)}, u32[]{:S(2)}, u32[]{:S(2)}) collective-permute-start(bf16[4,512,768]{2,1,0:T(8,128)(2,1)} %refs_1_.11), channel_id=1, source_target_pairs={{0,4},{4,0},{8,12},{12,8},{1,5},{5,1},{9,13},{13,9},{2,6},{6,2},{1... | collective-permute-start | bytes 9437192 | tf_op jit(solution)/shard_map/ppermute | solution.py:30
  0.5 61.7 %collective-permute-start.13 = (bf16[4,768,512]{2,1,0:T(8,128)(2,1)}, bf16[4,768,512]{2,1,0:T(8,128)(2,1)S(1)}, u32[]{:S(2)}, u32[]{:S(2)}) collective-permute-start(bf16[4,768,512]{2,1,0:T(8,128)(2,1)} %last_hbm.1), channel_id=1, source_target_pairs={{0,4},{4,0},{8,12},{12,8},{1,5},{5,1},{9,13},{13,9},{2,6},{6,2},{1... | collective-permute-start | bytes 9437192 | tf_op jit(solution)/shard_map/ppermute | solution.py:30
  1.0 9.4 %collective-permute-start = (bf16[128,512]{1,0:T(8,128)(2,1)}, bf16[128,512]{1,0:T(8,128)(2,1)S(1)}, u32[]{:S(2)}, u32[]{:S(2)}) collective-permute-start(bf16[128,512]{1,0:T(8,128)(2,1)} %down_hbm.1), channel_id=1, source_target_pairs={{0,1},{1,0},{2,3},{3,2},{4,5},{5,4},{6,7},{7,6},{8,9},{9,8},{10,11... | collective-permute-start | bytes 393224 | tf_op jit(solution)/shard_map/ppermute | solution.py:30
  3.6 9.6 %collective-permute-start.1 = (bf16[128,512]{1,0:T(8,128)(2,1)}, bf16[128,512]{1,0:T(8,128)(2,1)S(1)}, u32[]{:S(2)}, u32[]{:S(2)}) collective-permute-start(bf16[128,512]{1,0:T(8,128)(2,1)} %down_hbm.1), channel_id=1, source_target_pairs={{0,2},{1,3},{2,0},{3,1},{16,19},{17,18},{18,17},{19,16},{4,6},{5,7... | collective-permute-start | bytes 393224 | tf_op jit(solution)/shard_map/ppermute | solution.py:40
  10.4 6.6 %collective-permute-start.2 = (bf16[128,512]{1,0:T(8,128)(2,1)}, bf16[128,512]{1,0:T(8,128)(2,1)S(1)}, u32[]{:S(2)}, u32[]{:S(2)}) collective-permute-start(bf16[128,512]{1,0:T(8,128)(2,1)} %down_hbm.1), channel_id=1, source_target_pairs={{0,8},{4,12},{8,0},{12,4},{1,9},{5,13},{9,1},{13,5},{2,10},{6,14},... | collective-permute-start | bytes 393224 | tf_op jit(solution)/shard_map/ppermute | solution.py:30
  13.2 6.7 %collective-permute-start.16 = (bf16[128,512]{1,0:T(8,128)(2,1)}, bf16[128,512]{1,0:T(8,128)(2,1)S(1)}, u32[]{:S(2)}, u32[]{:S(2)}) collective-permute-start(bf16[128,512]{1,0:T(8,128)(2,1)} %up_hbm.1), channel_id=1, source_target_pairs={{0,8},{4,12},{8,0},{12,4},{1,9},{5,13},{9,1},{13,5},{2,10},{6,14},... | collective-permute-start | bytes 393224 | tf_op jit(solution)/shard_map/ppermute | solution.py:30
  17.0 6.4 %collective-permute-start.3 = (bf16[128,512]{1,0:T(8,128)(2,1)S(1)}, bf16[128,512]{1,0:T(8,128)(2,1)S(1)}, u32[]{:S(2)}, u32[]{:S(2)}) collective-permute-start(bf16[128,512]{1,0:T(8,128)(2,1)S(1)} %collective-permute-done.refs_1_), channel_id=1, source_target_pairs={{0,8},{4,12},{8,0},{12,4},{1,9},{5,13},{9,1},{13,5},{2,10},{6,14},... | collective-permute-start | bytes 393224 | tf_op jit(solution)/shard_map/ppermute | solution.py:30
  19.8 7.8 %collective-permute-start.5 = (bf16[128,512]{1,0:T(8,128)(2,1)S(1)}, bf16[128,512]{1,0:T(8,128)(2,1)S(1)}, u32[]{:S(2)}, u32[]{:S(2)}) collective-permute-start(bf16[128,512]{1,0:T(8,128)(2,1)S(1)} %collective-permute-done.1.refs_2_), channel_id=1, source_target_pairs={{0,24},{4,28},{8,16},{12,20},{16,8},{20,12},{24,0},{28,4},{1,25},{... | collective-permute-start | bytes 393224 | tf_op jit(solution)/shard_map/ppermute | solution.py:40
  23.4 5.0 %collective-permute-start.6 = (bf16[128,512]{1,0:T(8,128)(2,1)S(1)}, bf16[128,512]{1,0:T(8,128)(2,1)S(1)}, u32[]{:S(2)}, u32[]{:S(2)}) collective-permute-start(bf16[128,512]{1,0:T(8,128)(2,1)S(1)} %collective-permute-done.1.refs_2_), channel_id=1, source_target_pairs={{0,8},{4,12},{8,0},{12,4},{1,9},{5,13},{9,1},{13,5},{2,10},{6,14},... | collective-permute-start | bytes 393224 | tf_op jit(solution)/shard_map/ppermute | solution.py:30
  27.6 10.0 %collective-permute-start.4 = (bf16[640,512]{1,0:T(8,128)(2,1)S(1)}, bf16[640,512]{1,0:T(8,128)(2,1)S(1)}, u32[]{:S(2)}, u32[]{:S(2)}) collective-permute-start(bf16[640,512]{1,0:T(8,128)(2,1)S(1)} %shard_map.110.w0_ref), channel_id=1, source_target_pairs={{0,4},{4,0},{8,12},{12,8},{1,5},{5,1},{9,13},{13,9},{2,6},{6,2},{1... | collective-permute-start | bytes 1966088 | tf_op jit(solution)/shard_map/ppermute | solution.py:30
  28.4 5.3 %collective-permute-start.7 = (bf16[128,512]{1,0:T(8,128)(2,1)S(1)}, bf16[128,512]{1,0:T(8,128)(2,1)S(1)}, u32[]{:S(2)}, u32[]{:S(2)}) collective-permute-start(bf16[128,512]{1,0:T(8,128)(2,1)S(1)} %collective-permute-done.1.refs_2_), channel_id=1, source_target_pairs={{0,16},{16,0},{1,17},{17,1},{2,18},{18,2},{3,19},{19,3},{4,20},{20... | collective-permute-start | bytes 393224 | tf_op jit(solution)/shard_map/ppermute | solution.py:30
  33.6 1.3 %collective-permute-start.8 = (bf16[128,512]{1,0:T(8,128)(2,1)S(1)}, bf16[128,512]{1,0:T(8,128)(2,1)S(1)}, u32[]{:S(2)}, u32[]{:S(2)}) collective-permute-start(bf16[128,512]{1,0:T(8,128)(2,1)S(1)} %collective-permute-done.5.refs_0_), channel_id=1, source_target_pairs={{0,4},{4,0},{8,12},{12,8},{1,5},{5,1},{9,13},{13,9},{2,6},{6,2},{1... | collective-permute-start | bytes 393224 | tf_op jit(solution)/shard_map/ppermute | solution.py:30
  35.0 1.3 %collective-permute-start.9 = (bf16[128,512]{1,0:T(8,128)(2,1)S(1)}, bf16[128,512]{1,0:T(8,128)(2,1)S(1)}, u32[]{:S(2)}, u32[]{:S(2)}) collective-permute-start(bf16[128,512]{1,0:T(8,128)(2,1)S(1)} %collective-permute-done.6.refs_1_), channel_id=1, source_target_pairs={{0,4},{4,0},{8,12},{12,8},{1,5},{5,1},{9,13},{13,9},{2,6},{6,2},{1... | collective-permute-start | bytes 393224 | tf_op jit(solution)/shard_map/ppermute | solution.py:30
  36.3 1.3 %collective-permute-start.10 = (bf16[128,512]{1,0:T(8,128)(2,1)S(1)}, bf16[128,512]{1,0:T(8,128)(2,1)S(1)}, u32[]{:S(2)}, u32[]{:S(2)}) collective-permute-start(bf16[128,512]{1,0:T(8,128)(2,1)S(1)} %collective-permute-done.7.refs_2_), channel_id=1, source_target_pairs={{0,4},{4,0},{8,12},{12,8},{1,5},{5,1},{9,13},{13,9},{2,6},{6,2},{1... | collective-permute-start | bytes 393224 | tf_op jit(solution)/shard_map/ppermute | solution.py:30
  37.7 13.7 %collective-permute-start.17 = (bf16[512,256]{1,0:T(8,128)(2,1)S(1)}, bf16[512,256]{1,0:T(8,128)(2,1)S(1)}, u32[]{:S(2)}, u32[]{:S(2)}) collective-permute-start(bf16[512,256]{1,0:T(8,128)(2,1)S(1)} %shard_map.119.refs_1_), channel_id=1, source_target_pairs={{0,1},{1,0},{2,3},{3,2},{4,5},{5,4},{6,7},{7,6},{8,9},{9,8},{10,11... | collective-permute-start | bytes 786440 | tf_op jit(solution)/shard_map/ppermute | solution.py:30
  37.7 16.0 %collective-permute-start.18 = (bf16[512,256]{1,0:T(8,128)(2,1)S(1)}, bf16[512,256]{1,0:T(8,128)(2,1)S(1)}, u32[]{:S(2)}, u32[]{:S(2)}) collective-permute-start(bf16[512,256]{1,0:T(8,128)(2,1)S(1)} %shard_map.119.refs_1_), channel_id=1, source_target_pairs={{0,2},{1,3},{2,0},{3,1},{16,19},{17,18},{18,17},{19,16},{4,6},{5,7... | collective-permute-start | bytes 786440 | tf_op jit(solution)/shard_map/ppermute | solution.py:40
  41.6 13.6 %copy-start = (bf16[4,512,768]{2,1,0:T(8,128)(2,1)S(1)}, bf16[4,512,768]{2,1,0:T(8,128)(2,1)}, u32[]{:S(2)}) copy-start(bf16[4,512,768]{2,1,0:T(8,128)(2,1)} %refs_0_.11) | copy-start | bytes 9437188
  41.6 13.6 %copy-start.1 = (bf16[4,512,768]{2,1,0:T(8,128)(2,1)S(1)}, bf16[4,512,768]{2,1,0:T(8,128)(2,1)}, u32[]{:S(2)}) copy-start(bf16[4,512,768]{2,1,0:T(8,128)(2,1)} %refs_1_.11) | copy-start | bytes 9437188
  51.4 9.8 %collective-permute-start.14 = (bf16[272,512]{1,0:T(8,128)(2,1)S(1)}, bf16[272,512]{1,0:T(8,128)(2,1)S(1)}, u32[]{:S(2)}, u32[]{:S(2)}) collective-permute-start(bf16[272,512]{1,0:T(8,128)(2,1)S(1)} %shard_map.113.pay_ref), channel_id=1, source_target_pairs={{0,8},{4,12},{8,0},{12,4},{1,9},{5,13},{9,1},{13,5},{2,10},{6,14},... | collective-permute-start | bytes 835592 | tf_op jit(solution)/shard_map/ppermute | solution.py:30
  53.6 7.5 %collective-permute-start.19 = (bf16[512,256]{1,0:T(8,128)(2,1)S(1)}, bf16[512,256]{1,0:T(8,128)(2,1)S(1)}, u32[]{:S(2)}, u32[]{:S(2)}) collective-permute-start(bf16[512,256]{1,0:T(8,128)(2,1)S(1)} %collective-permute-done.18.refs_3_), channel_id=1, source_target_pairs={{0,16},{16,0},{1,17},{17,1},{2,18},{18,2},{3,19},{19,3},{4,20},{20... | collective-permute-start | bytes 786440 | tf_op jit(solution)/shard_map/ppermute | solution.py:30
  61.2 10.2 %collective-permute-start.20 = (bf16[512,256]{1,0:T(8,128)(2,1)S(1)}, bf16[512,256]{1,0:T(8,128)(2,1)S(1)}, u32[]{:S(2)}, u32[]{:S(2)}) collective-permute-start(bf16[512,256]{1,0:T(8,128)(2,1)S(1)} %shard_map.119.refs_1_), channel_id=1, source_target_pairs={{0,4},{4,0},{8,12},{12,8},{1,5},{5,1},{9,13},{13,9},{2,6},{6,2},{1... | collective-permute-start | bytes 786440 | tf_op jit(solution)/shard_map/ppermute | solution.py:30
  61.2 12.3 %collective-permute-start.22 = (bf16[512,256]{1,0:T(8,128)(2,1)S(1)}, bf16[512,256]{1,0:T(8,128)(2,1)S(1)}, u32[]{:S(2)}, u32[]{:S(2)}) collective-permute-start(bf16[512,256]{1,0:T(8,128)(2,1)S(1)} %collective-permute-done.18.refs_3_), channel_id=1, source_target_pairs={{0,4},{4,0},{8,12},{12,8},{1,5},{5,1},{9,13},{13,9},{2,6},{6,2},{1... | collective-permute-start | bytes 786440 | tf_op jit(solution)/shard_map/ppermute | solution.py:30
  61.7 11.8 %collective-permute-start.21 = (bf16[512,256]{1,0:T(8,128)(2,1)S(1)}, bf16[512,256]{1,0:T(8,128)(2,1)S(1)}, u32[]{:S(2)}, u32[]{:S(2)}) collective-permute-start(bf16[512,256]{1,0:T(8,128)(2,1)S(1)} %collective-permute-done.17.refs_2_), channel_id=1, source_target_pairs={{0,4},{4,0},{8,12},{12,8},{1,5},{5,1},{9,13},{13,9},{2,6},{6,2},{1... | collective-permute-start | bytes 786440 | tf_op jit(solution)/shard_map/ppermute | solution.py:30
  61.8 11.7 %collective-permute-start.23 = (bf16[512,256]{1,0:T(8,128)(2,1)S(1)}, bf16[512,256]{1,0:T(8,128)(2,1)S(1)}, u32[]{:S(2)}, u32[]{:S(2)}) collective-permute-start(bf16[512,256]{1,0:T(8,128)(2,1)S(1)} %collective-permute-done.19.refs_4_), channel_id=1, source_target_pairs={{0,4},{4,0},{8,12},{12,8},{1,5},{5,1},{9,13},{13,9},{2,6},{6,2},{1... | collective-permute-start | bytes 786440 | tf_op jit(solution)/shard_map/ppermute | solution.py:30
  67.3 6.2 %collective-permute-start.24 = (bf16[128,512]{1,0:T(8,128)(2,1)S(1)}, bf16[128,512]{1,0:T(8,128)(2,1)S(1)}, u32[]{:S(2)}, u32[]{:S(2)}) collective-permute-start(bf16[128,512]{1,0:T(8,128)(2,1)S(1)} %shard_map.120), channel_id=1, source_target_pairs={{0,8},{4,12},{8,0},{12,4},{1,9},{5,13},{9,1},{13,5},{2,10},{6,14},... | collective-permute-start | bytes 393224 | tf_op jit(solution)/shard_map/ppermute | solution.py:30
  71.4 5.2 %collective-permute-start.15 = (bf16[128,512]{1,0:T(8,128)(2,1)S(1)}, bf16[128,512]{1,0:T(8,128)(2,1)S(1)}, u32[]{:S(2)}, u32[]{:S(2)}) collective-permute-start(bf16[128,512]{1,0:T(8,128)(2,1)S(1)} %shard_map.118), channel_id=1, source_target_pairs={{0,8},{4,12},{8,0},{12,4},{1,9},{5,13},{9,1},{13,5},{2,10},{6,14},... | collective-permute-start | bytes 393224 | tf_op jit(solution)/shard_map/ppermute | solution.py:30

commit v7 on v6

--- a/solution.py
+++ b/solution.py
@@ -57,10 +57,10 @@
     )(*operands)
 
 
-def norm_kernel(tok_hbm, gain_hbm, down_hbm, up_hbm, last_hbm, normed_ref, down_ref, up_ref, last_ref,
-                tok_ref, gain_ref, sem):
-    pairs = ((tok_hbm, tok_ref), (gain_hbm, gain_ref), (down_hbm, down_ref), (up_hbm, up_ref),
-             (last_hbm, last_ref))
+def norm_kernel(tok_hbm, gain_hbm, *refs):
+    n = (len(refs) - 4) // 2
+    normed_ref, (tok_ref, gain_ref, sem) = refs[n], refs[-3:]
+    pairs = ((tok_hbm, tok_ref), (gain_hbm, gain_ref), *zip(refs[:n], refs[n + 1:-3]))
     copies = [pltpu.make_async_copy(src, dst, sem.at[i]) for i, (src, dst) in enumerate(pairs)]
     for copy in copies:
         copy.start()
@@ -73,13 +73,9 @@
         copy.wait()
 
 
-def gate_kernel(top, normed_ref, list_hbm, router_hbm, ids_hbm, slot_hbm, wt_ref, list_ref, router_ref, ids_ref, slot_ref, sem):
-    pairs = ((router_hbm, router_ref), (ids_hbm, ids_ref), (slot_hbm, slot_ref), (list_hbm, list_ref))
-    copies = [pltpu.make_async_copy(src, dst, sem.at[i]) for i, (src, dst) in enumerate(pairs)]
-    for copy in copies:
-        copy.start()
-    for copy in copies:
-        copy.wait()
+def gate_kernel(top, normed_ref, router_ref, ids_ref, slot_ref, list_hbm, wt_ref, list_ref, sem):
+    load = pltpu.make_async_copy(list_hbm, list_ref, sem)
+    load.start()
     logits = lax.dot_general(router_ref[...], normed_ref[...], (((1,), (1,)), ((), ())),
                              preferred_element_type=F32)
     sig = jax.nn.sigmoid(logits)
@@ -92,6 +88,7 @@
         hit = sub == ids_ref[k:k + 1, :]
         total = total + jnp.where(hit, 1.0, 0.0)
         served = served + jnp.where(hit & (slot_ref[k:k + 1, :] >= 0), 1.0, 0.0)
+    load.wait()
     _, shards, copies_n, local = list_ref.shape
 
     def listed(i, served):
@@ -263,19 +260,17 @@
                 down[(a, b)] = swap(down[(0, b)], "expert", 2 * a)
         ups_x = [swap(up_proj, "expert", 2 * a) for a in range(1, chips)]
 
-    normed, own_down, own_up, last = kernel(
-        norm_kernel, tuple(map(shape, ((rows, width), down_proj.shape, up_proj.shape,
-                                       expert_down.shape))),
-        tuple(map(in_hbm, (tokens, norm_gain.reshape(1, width), down_proj, up_proj, expert_down))),
-        [AN] * 5, 18, 8 * rows * width, 4 * rows * width,
-        [pltpu.VMEM((rows, width), BF16), pltpu.VMEM((1, width), F32), pltpu.SemaphoreType.DMA((5,))])
+    moved = (down_proj, up_proj, expert_down, router.T, expert_ids.T, slot_pos.T)
+    normed, own_down, own_up, last, *routing = kernel(
+        norm_kernel, (shape((rows, width)), *[shape(x.shape, x.dtype) for x in moved]),
+        tuple(map(in_hbm, (tokens, norm_gain.reshape(1, width), *moved))), [AN] * (2 + len(moved)), 18,
+        8 * rows * width, 4 * rows * width,
+        [pltpu.VMEM((rows, width), BF16), pltpu.VMEM((1, width), F32),
+         pltpu.SemaphoreType.DMA((2 + len(moved),))])
     wt = kernel(
         functools.partial(gate_kernel, top), shape((experts, rows), F32),
-        (normed, *map(in_hbm, (overflow_list, router.T, expert_ids.T, slot_pos.T))),
-        [VM] + [AN] * 4, 10, 4 * rows * width * experts, 2 * rows * width,
-        [pltpu.SMEM(overflow_list.shape, jnp.int32), pltpu.VMEM((experts, width), BF16),
-         pltpu.VMEM((top, rows), jnp.int32), pltpu.VMEM((top, rows), jnp.int32),
-         pltpu.SemaphoreType.DMA((4,))])
+        (normed, *routing, in_hbm(overflow_list)), [VM] * 4 + [AN], 10, 4 * rows * width * experts,
+        2 * rows * width, [pltpu.SMEM(overflow_list.shape, jnp.int32), pltpu.SemaphoreType.DMA])
     down[(0, 0)] = own_down
     weights = (expert_gate, expert_up, last, *[
         swap(w, "expert", 1) for w in (expert_gate, expert_up, expert_down)])
@@ -316,7 +311,8 @@
     size = rows // parts
     back = [[] for _ in range(parts)]
     for a in range(1, chips):
-        opened = run(near_kernel, (far[a - 1], *weights), range(cut))
+        opened = run(near_kernel, (far[a - 1], *weights[:3]), range(local))
+        opened = run(more_kernel, (far[a - 1], opened, *weights), range(local, cut))
         for h in range(parts):
             s = kernel(
                 functools.partial(far_kernel, range(cut, count), h * size),

time: 78.1 us -> 77.2 us (0.988)
  starting transfers between devices: 26.2 us -> 16.5 us
  waiting for transfers between devices: 31.6 us -> 40.6 us
    ppermute x3, waiting for transfers between devices: 1.58 us -> 17.6 us  [swap_pair(): return lax.ppermute(x, axes, pairs)]
    ppermute x22, waiting for transfers between devices: 30 us -> 23 us  [swap(): return lax.ppermute(x, axis, [(i, i ^ bits) for i in range(size)])]
    ppermute x3, starting transfers between devices: 8.79 us -> 3.34 us  [swap_pair(): return lax.ppermute(x, axes, pairs)]
    ppermute x22, starting transfers between devices: 17.4 us -> 13.1 us  [swap(): return lax.ppermute(x, axis, [(i, i ^ bits) for i in range(size)])]
    pallas_call x14 -> x15, Pallas kernels: 20 us -> 19.7 us  [kernel(): pl.pallas_call(body, out_shape=out_shape, in_specs=specs, out_specs=out_s...]
  transfers between devices with their start and end apart: 25 -> 25, of which waited for: 14 -> 13; matrix products, arithmetic and copies ran while one was open for 0% -> 0% of each run, Pallas kernels for 24% -> 24%
where the time goes in v7:
time: 77.2 us; the launch traced here: 77 us
  waiting for transfers between devices  40.6 us (53%)
  Pallas kernels  19.7 us (26%)
  starting transfers between devices  16.5 us (21%)
    ppermute x22, waiting for transfers between devices, swap(): return lax.ppermute(x, axis, [(i, i ^ bits) for i in range(size)])  23 us
    pallas_call x15, Pallas kernels, kernel(): pl.pallas_call(body, out_shape=out_shape, in_specs=specs, out_specs=out_s...  19.7 us
    ppermute x3, waiting for transfers between devices, swap_pair(): return lax.ppermute(x, axes, pairs)  17.6 us
    ppermute x22, starting transfers between devices, swap(): return lax.ppermute(x, axis, [(i, i ^ bits) for i in range(size)])  13.1 us
    ppermute x3, starting transfers between devices, swap_pair(): return lax.ppermute(x, axes, pairs)  3.34 us
  transfers between devices with their start and end apart: 25, of which 13 were waited for; matrix products, arithmetic and copies ran while one was open for 0% of the time, Pallas kernels for 24%

profile of v7, /device:TPU:0, one launch (start us, length us, event | category | flops | bytes accessed | tf_op | source)
XLA Modules:
  0.0 77.0 jit_solution(5995233915835394578)
XLA Ops:
  0.0 0.5 collective-permute-start.11
  0.5 0.1 collective-permute-start.12
  0.6 0.4 collective-permute-start.13
  1.0 2.6 %collective-permute-start = (bf16[128,512]{1,0:T(8,128)(2,1)}, bf16[128,512]{1,0:T(8,128)(2,1)S(1)}, u32[]{:S(2)}, u32[]{:S(2)}) collective-permute-start(bf16[128,512]{1,0:T(8,128)(2,1)} %refs_0_.8), channel_id=1, source_target_pairs={{0,1},{1,0},{2,3},{3,2},{4,5},{5,4},{6,7},{7,6},{8,9},{9,8},{10,11... | collective-permute-start | bytes 393224 | tf_op jit(solution)/shard_map/ppermute | solution.py:30
  3.6 2.6 %collective-permute-start.1 = (bf16[128,512]{1,0:T(8,128)(2,1)}, bf16[128,512]{1,0:T(8,128)(2,1)S(1)}, u32[]{:S(2)}, u32[]{:S(2)}) collective-permute-start(bf16[128,512]{1,0:T(8,128)(2,1)} %refs_0_.8), channel_id=1, source_target_pairs={{0,2},{1,3},{2,0},{3,1},{16,19},{17,18},{18,17},{19,16},{4,6},{5,7... | collective-permute-start | bytes 393224 | tf_op jit(solution)/shard_map/ppermute | solution.py:40
  6.2 4.2 %collective-permute-done.refs_1_ = bf16[128,512]{1,0:T(8,128)(2,1)S(1)} collective-permute-done((bf16[128,512]{1,0:T(8,128)(2,1)}, bf16[128,512]{1,0:T(8,128)(2,1)S(1)}, u32[]{:S(2)}, u32[]{:S(2)}) %collective-permute-start) | collective-permute-done | bytes 131104 | tf_op jit(solution)/shard_map/ppermute | solution.py:30
  10.4 1.9 %collective-permute-start.2 = (bf16[128,512]{1,0:T(8,128)(2,1)}, bf16[128,512]{1,0:T(8,128)(2,1)S(1)}, u32[]{:S(2)}, u32[]{:S(2)}) collective-permute-start(bf16[128,512]{1,0:T(8,128)(2,1)} %refs_0_.8), channel_id=1, source_target_pairs={{0,8},{4,12},{8,0},{12,4},{1,9},{5,13},{9,1},{13,5},{2,10},{6,14},... | collective-permute-start | bytes 393224 | tf_op jit(solution)/shard_map/ppermute | solution.py:30
  12.3 0.9 %collective-permute-done.1.refs_2_ = bf16[128,512]{1,0:T(8,128)(2,1)S(1)} collective-permute-done((bf16[128,512]{1,0:T(8,128)(2,1)}, bf16[128,512]{1,0:T(8,128)(2,1)S(1)}, u32[]{:S(2)}, u32[]{:S(2)}) %collective-permute-start.1) | collective-permute-done | bytes 131104 | tf_op jit(solution)/shard_map/ppermute | solution.py:40
  13.2 1.5 %collective-permute-start.3 = (bf16[128,512]{1,0:T(8,128)(2,1)S(1)}, bf16[128,512]{1,0:T(8,128)(2,1)S(1)}, u32[]{:S(2)}, u32[]{:S(2)}) collective-permute-start(bf16[128,512]{1,0:T(8,128)(2,1)S(1)} %collective-permute-done.refs_1_), channel_id=1, source_target_pairs={{0,8},{4,12},{8,0},{12,4},{1,9},{5,13},{9,1},{13,5},{2,10},{6,14},... | collective-permute-start | bytes 393224 | tf_op jit(solution)/shard_map/ppermute | solution.py:30
  14.7 2.3 %collective-permute-done.2.refs_3_ = bf16[128,512]{1,0:T(8,128)(2,1)S(1)} collective-permute-done((bf16[128,512]{1,0:T(8,128)(2,1)}, bf16[128,512]{1,0:T(8,128)(2,1)S(1)}, u32[]{:S(2)}, u32[]{:S(2)}) %collective-permute-start.2) | collective-permute-done | bytes 131104 | tf_op jit(solution)/shard_map/ppermute | solution.py:30
  17.0 2.4 %shard_map.109 = (bf16[256,2048]{1,0:T(8,128)(2,1)S(1)}, bf16[128,512]{1,0:T(8,128)(2,1)S(1)}, bf16[128,512]{1,0:T(8,128)(2,1)S(1)}, bf16[4,768,512]{2,1,0:T(8,1...) custom-call(bf16[256,2048]{1,0:T(8,128)(2,1)} %tok_hbm.1, ...), custom_call_target="tpu_custom_call" | custom-call | flops 4194304 | bytes 2097152 | tf_op jit(solution)/shard_map/pallas_call | solution.py:48
  19.4 0.1 collective-permute-done.3.refs_4_
  19.5 0.1 collective-permute-start.4
  19.6 3.2 %collective-permute-done.5.refs_0_ = bf16[128,512]{1,0:T(8,128)(2,1)S(1)} collective-permute-done((bf16[128,512]{1,0:T(8,128)(2,1)S(1)}, bf16[128,512]{1,0:T(8,128)(2,1)S(1)}, u32[]{:S(2)}, u32[]{:S(2)}) %collective-permute-start.5) | collective-permute-done | bytes 131104 | tf_op jit(solution)/shard_map/ppermute | solution.py:40
  22.8 0.5 collective-permute-start.6
  23.3 4.5 %collective-permute-done.6.refs_1_ = bf16[128,512]{1,0:T(8,128)(2,1)S(1)} collective-permute-done((bf16[128,512]{1,0:T(8,128)(2,1)S(1)}, bf16[128,512]{1,0:T(8,128)(2,1)S(1)}, u32[]{:S(2)}, u32[]{:S(2)}) %collective-permute-start.6) | collective-permute-done | bytes 131104 | tf_op jit(solution)/shard_map/ppermute | solution.py:30
  27.8 5.0 %collective-permute-done.7.refs_2_ = bf16[128,512]{1,0:T(8,128)(2,1)S(1)} collective-permute-done((bf16[128,512]{1,0:T(8,128)(2,1)S(1)}, bf16[128,512]{1,0:T(8,128)(2,1)S(1)}, u32[]{:S(2)}, u32[]{:S(2)}) %collective-permute-start.7) | collective-permute-done | bytes 131104 | tf_op jit(solution)/shard_map/ppermute | solution.py:30
  32.8 1.3 %collective-permute-done.8.refs_3_ = bf16[128,512]{1,0:T(8,128)(2,1)S(1)} collective-permute-done((bf16[128,512]{1,0:T(8,128)(2,1)S(1)}, bf16[128,512]{1,0:T(8,128)(2,1)S(1)}, u32[]{:S(2)}, u32[]{:S(2)}) %collective-permute-start.8) | collective-permute-done | bytes 131104 | tf_op jit(solution)/shard_map/ppermute | solution.py:30
  34.1 0.1 collective-permute-start.9
  34.3 1.2 %collective-permute-done.9.refs_4_ = bf16[128,512]{1,0:T(8,128)(2,1)S(1)} collective-permute-done((bf16[128,512]{1,0:T(8,128)(2,1)S(1)}, bf16[128,512]{1,0:T(8,128)(2,1)S(1)}, u32[]{:S(2)}, u32[]{:S(2)}) %collective-permute-start.9) | collective-permute-done | bytes 131104 | tf_op jit(solution)/shard_map/ppermute | solution.py:30
  35.5 0.1 collective-permute-start.10
  35.6 0.5 collective-permute-start.16
  36.1 1.5 %shard_map.112.wt_ref = f32[16,256]{1,0:T(8,128)S(1)} custom-call(bf16[256,2048]{1,0:T(8,128)(2,1)S(1)} %get-tuple-element.12.normed_ref, bf16[16,2048]{1,0:T(8,128)(2,1)S(1)} %get-tuple-element.14.router_ref, s32[8,256]{1,0:T(8,128)S(1)} %get-tuple-element.15.ids_ref, s32[8,256]{1,0:T(8,128)S(1)} %get-tuple-element.16.slot_ref, s32[1,4,4,4]{3,2,1,0:T(4,128)} %list_hbm.1), custom_call_target="tpu_custom_call" | custom-call | flops 33554432 | bytes 1048576 | tf_op jit(solution)/shard_map/pallas_call | solution.py:48
  37.6 0.0 copy-start
  37.7 0.6 shard_map.111.sum_ref
  38.3 0.4 shard_map.113.pay_ref
  38.7 1.6 %collective-permute-start.14 = (bf16[272,512]{1,0:T(8,128)(2,1)S(1)}, bf16[272,512]{1,0:T(8,128)(2,1)S(1)}, u32[]{:S(2)}, u32[]{:S(2)}) collective-permute-start(bf16[272,512]{1,0:T(8,128)(2,1)S(1)} %shard_map.113.pay_ref), channel_id=1, source_target_pairs={{0,8},{4,12},{8,0},{12,4},{1,9},{5,13},{9,1},{13,5},{2,10},{6,14},... | collective-permute-start | bytes 835592 | tf_op jit(solution)/shard_map/ppermute | solution.py:30
  40.3 1.1 %collective-permute-done.16.refs_1_ = bf16[128,512]{1,0:T(8,128)(2,1)S(1)} collective-permute-done((bf16[128,512]{1,0:T(8,128)(2,1)S(1)}, bf16[128,512]{1,0:T(8,128)(2,1)S(1)}, u32[]{:S(2)}, u32[]{:S(2)}) %collective-permute-start.16) | collective-permute-done | bytes 131104 | tf_op jit(solution)/shard_map/ppermute | solution.py:30
  41.4 0.1 shard_map.120.refs_1_
  41.5 0.8 collective-permute-start.18
  42.3 13.5 %collective-permute-done.18.refs_3_ = bf16[512,256]{1,0:T(8,128)(2,1)S(1)} collective-permute-done((bf16[512,256]{1,0:T(8,128)(2,1)S(1)}, bf16[512,256]{1,0:T(8,128)(2,1)S(1)}, u32[]{:S(2)}, u32[]{:S(2)}) %collective-permute-start.18) | collective-permute-done | bytes 262176 | tf_op jit(solution)/shard_map/ppermute | solution.py:40
  55.8 2.8 %shard_map.114.sum_ref = f32[256,512]{1,0:T(8,128)S(1)} custom-call(bf16[272,512]{1,0:T(8,128)(2,1)S(1)} %shard_map.113.pay_ref, bf16[4,512,768]{2,1,0:T(8,128)(2,1)S(1)} %copy-done, bf16[4,512,768]{2,1,0:T(8,128)(2,1)S(1)} %copy-done.1, bf16[4,768,512]{2,1,0:T(8,128)(2,1)S(1)} %get-tuple-element.17.refs_2_), custom_call_target="tpu_custom_call" | custom-call | flops 2415919104 | bytes 9437184 | tf_op jit(solution)/shard_map/pallas_call | solution.py:48
  58.7 2.8 %shard_map.117.sum_ref = f32[256,512]{1,0:T(8,128)S(1)} custom-call(bf16[272,512]{1,0:T(8,128)(2,1)S(1)} %collective-permute-done.14.pay_ref, bf16[4,512,768]{2,1,0:T(8,128)(2,1)S(1)} %copy-done, bf16[4,512,768]{2,1,0:T(8,128)(2,1)S(1)} %copy-done.1, bf16[4,768,512]{2,1,0:T(8,128)(2,1)S(1)} %get-tuple-element.17.refs_2_), custom_call_target="tpu_custom_call" | custom-call | flops 2415919104 | bytes 9437184 | tf_op jit(solution)/shard_map/pallas_call | solution.py:48
  61.5 2.4 %collective-permute-done.17.refs_2_ = bf16[512,256]{1,0:T(8,128)(2,1)S(1)} collective-permute-done((bf16[512,256]{1,0:T(8,128)(2,1)S(1)}, bf16[512,256]{1,0:T(8,128)(2,1)S(1)}, u32[]{:S(2)}, u32[]{:S(2)}) %collective-permute-start.17) | collective-permute-done | bytes 262176 | tf_op jit(solution)/shard_map/ppermute | solution.py:30
  63.9 0.0 collective-permute-done.19.refs_4_
  63.9 0.5 collective-permute-start.22
  64.4 0.1 collective-permute-start.21
  64.5 0.4 collective-permute-start.23
  64.9 1.5 %shard_map.118.sum_ref = f32[256,512]{1,0:T(8,128)S(1)} custom-call(bf16[272,512]{1,0:T(8,128)(2,1)S(1)} %collective-permute-done.14.pay_ref, f32[256,512]{1,0:T(8,128)S(1)} %shard_map.117.sum_ref, bf16[4,512,768]{2,1,0:T(8,128)(2,1)S(1)} %copy-done, bf16[4,512,768]{2,1,0:T(8,128)(2,1)S(1)} %copy-done.1, bf16[4,768,512]{2,1,0:T(8,128)(2,1)S(1)} %get-tuple-element.17.refs_2_, ...), custom_call_target="tpu_custom_call" | custom-call | flops 1207959552 | bytes 4718592 | tf_op jit(solution)/shard_map/pallas_call | solution.py:48
  66.4 1.0 %shard_map.121 = bf16[128,512]{1,0:T(8,128)(2,1)S(1)} custom-call(bf16[272,512]{1,0:T(8,128)(2,1)S(1)} %collective-permute-done.14.pay_ref, f32[256,512]{1,0:T(8,128)S(1)} %shard_map.118.sum_ref, bf16[4,512,768]{2,1,0:T(8,128)(2,1)S(1)} %copy-done, bf16[4,512,768]{2,1,0:T(8,128)(2,1)S(1)} %copy-done.1, bf16[4,768,512]{2,1,0:T(8,128)(2,1)S(1)} %get-tuple-element.17.refs_2_, ...), custom_call_target="tpu_custom_call" | custom-call | flops 603979776 | bytes 4718592 | tf_op jit(solution)/shard_map/pallas_call | solution.py:48
  67.4 0.1 collective-permute-start.24
  67.5 1.5 %shard_map.115.sum_ref = f32[256,512]{1,0:T(8,128)S(1)} custom-call(bf16[272,512]{1,0:T(8,128)(2,1)S(1)} %shard_map.113.pay_ref, f32[256,512]{1,0:T(8,128)S(1)} %shard_map.114.sum_ref, bf16[4,512,768]{2,1,0:T(8,128)(2,1)S(1)} %copy-done, bf16[4,512,768]{2,1,0:T(8,128)(2,1)S(1)} %copy-done.1, bf16[4,768,512]{2,1,0:T(8,128)(2,1)S(1)} %get-tuple-element.17.refs_2_, ...), custom_call_target="tpu_custom_call" | custom-call | flops 1207959552 | bytes 4718592 | tf_op jit(solution)/shard_map/pallas_call | solution.py:48
  69.0 1.0 %shard_map.119 = bf16[128,512]{1,0:T(8,128)(2,1)S(1)} custom-call(bf16[272,512]{1,0:T(8,128)(2,1)S(1)} %collective-permute-done.14.pay_ref, f32[256,512]{1,0:T(8,128)S(1)} %shard_map.118.sum_ref, bf16[4,512,768]{2,1,0:T(8,128)(2,1)S(1)} %copy-done, bf16[4,512,768]{2,1,0:T(8,128)(2,1)S(1)} %copy-done.1, bf16[4,768,512]{2,1,0:T(8,128)(2,1)S(1)} %get-tuple-element.17.refs_2_, ...), custom_call_target="tpu_custom_call" | custom-call | flops 603979776 | bytes 4718592 | tf_op jit(solution)/shard_map/pallas_call | solution.py:48
  70.0 2.1 %collective-permute-start.15 = (bf16[128,512]{1,0:T(8,128)(2,1)S(1)}, bf16[128,512]{1,0:T(8,128)(2,1)S(1)}, u32[]{:S(2)}, u32[]{:S(2)}) collective-permute-start(bf16[128,512]{1,0:T(8,128)(2,1)S(1)} %shard_map.119), channel_id=1, source_target_pairs={{0,8},{4,12},{8,0},{12,4},{1,9},{5,13},{9,1},{13,5},{2,10},{6,14},... | collective-permute-start | bytes 393224 | tf_op jit(solution)/shard_map/ppermute | solution.py:30
  72.1 1.5 %shard_map.116.near_ref = f32[256,512]{1,0:T(8,128)S(1)} custom-call(bf16[272,512]{1,0:T(8,128)(2,1)S(1)} %shard_map.113.pay_ref, f32[256,512]{1,0:T(8,128)S(1)} %shard_map.115.sum_ref, bf16[4,512,768]{2,1,0:T(8,128)(2,1)S(1)} %copy-done, bf16[4,512,768]{2,1,0:T(8,128)(2,1)S(1)} %copy-done.1, bf16[4,768,512]{2,1,0:T(8,128)(2,1)S(1)} %get-tuple-element.17.refs_2_, ...), custom_call_target="tpu_custom_call" | custom-call | flops 1207959552 | bytes 4718592 | tf_op jit(solution)/shard_map/pallas_call | solution.py:48
  73.6 1.3 %shard_map.122.refs_9_ = bf16[256,2048]{1,0:T(8,128)(2,1)} custom-call(f32[256,512]{1,0:T(8,128)S(1)} %shard_map.116.near_ref, bf16[128,512]{1,0:T(8,128)(2,1)S(1)} %collective-permute-done.24.refs_0_, bf16[512,256]{1,0:T(8,128)(2,1)S(1)} %shard_map.120.refs_1_, bf16[512,256]{1,0:T(8,128)(2,1)S(1)} %collective-permute-done.17.refs_2_, ...), custom_call_target="tpu_custom_call" | custom-call | flops 268435456 | bytes 2097152 | tf_op jit(solution)/shard_map/pallas_call | solution.py:48
  74.9 0.8 %collective-permute-done.15.refs_0_ = bf16[128,512]{1,0:T(8,128)(2,1)S(1)} collective-permute-done((bf16[128,512]{1,0:T(8,128)(2,1)S(1)}, bf16[128,512]{1,0:T(8,128)(2,1)S(1)}, u32[]{:S(2)}, u32[]{:S(2)}) %collective-permute-start.15) | collective-permute-done | bytes 131104 | tf_op jit(solution)/shard_map/ppermute | solution.py:30
  75.7 1.3 %shard_map.123 = bf16[256,2048]{1,0:T(8,128)(2,1)} custom-call(f32[256,512]{1,0:T(8,128)S(1)} %shard_map.116.near_ref, bf16[128,512]{1,0:T(8,128)(2,1)S(1)} %collective-permute-done.15.refs_0_, bf16[512,256]{1,0:T(8,128)(2,1)S(1)} %shard_map.120.refs_1_, bf16[512,256]{1,0:T(8,128)(2,1)S(1)} %collective-permute-done.17.refs_2_, ...), custom_call_target="tpu_custom_call", output_to_operand_aliasing={{}: (10, {})} | custom-call | flops 268435456 | bytes 2097152 | tf_op jit(solution)/shard_map/pallas_call | solution.py:48
  (23 shorter events, 0.1 us)
Async XLA Ops:
  0.0 35.6 %copy-start.2 = (bf16[128,512]{1,0:T(8,128)(2,1)S(1)}, bf16[128,512]{1,0:T(8,128)(2,1)}, u32[]{:S(2)}) copy-start(bf16[128,512]{1,0:T(8,128)(2,1)} %refs_1_.8) | copy-start | bytes 393220
  0.0 64.4 %collective-permute-start.11 = (bf16[4,512,768]{2,1,0:T(8,128)(2,1)}, bf16[4,512,768]{2,1,0:T(8,128)(2,1)S(1)}, u32[]{:S(2)}, u32[]{:S(2)}) collective-permute-start(bf16[4,512,768]{2,1,0:T(8,128)(2,1)} %refs_0_.15), channel_id=1, source_target_pairs={{0,4},{4,0},{8,12},{12,8},{1,5},{5,1},{9,13},{13,9},{2,6},{6,2},{1... | collective-permute-start | bytes 9437192 | tf_op jit(solution)/shard_map/ppermute | solution.py:30
  0.5 64.0 %collective-permute-start.12 = (bf16[4,512,768]{2,1,0:T(8,128)(2,1)}, bf16[4,512,768]{2,1,0:T(8,128)(2,1)S(1)}, u32[]{:S(2)}, u32[]{:S(2)}) collective-permute-start(bf16[4,512,768]{2,1,0:T(8,128)(2,1)} %refs_1_.15), channel_id=1, source_target_pairs={{0,4},{4,0},{8,12},{12,8},{1,5},{5,1},{9,13},{13,9},{2,6},{6,2},{1... | collective-permute-start | bytes 9437192 | tf_op jit(solution)/shard_map/ppermute | solution.py:30
  0.6 64.4 %collective-permute-start.13 = (bf16[4,768,512]{2,1,0:T(8,128)(2,1)}, bf16[4,768,512]{2,1,0:T(8,128)(2,1)S(1)}, u32[]{:S(2)}, u32[]{:S(2)}) collective-permute-start(bf16[4,768,512]{2,1,0:T(8,128)(2,1)} %refs_2_.1), channel_id=1, source_target_pairs={{0,4},{4,0},{8,12},{12,8},{1,5},{5,1},{9,13},{13,9},{2,6},{6,2},{1... | collective-permute-start | bytes 9437192 | tf_op jit(solution)/shard_map/ppermute | solution.py:30
  1.0 9.4 %collective-permute-start = (bf16[128,512]{1,0:T(8,128)(2,1)}, bf16[128,512]{1,0:T(8,128)(2,1)S(1)}, u32[]{:S(2)}, u32[]{:S(2)}) collective-permute-start(bf16[128,512]{1,0:T(8,128)(2,1)} %refs_0_.8), channel_id=1, source_target_pairs={{0,1},{1,0},{2,3},{3,2},{4,5},{5,4},{6,7},{7,6},{8,9},{9,8},{10,11... | collective-permute-start | bytes 393224 | tf_op jit(solution)/shard_map/ppermute | solution.py:30
  3.6 9.5 %collective-permute-start.1 = (bf16[128,512]{1,0:T(8,128)(2,1)}, bf16[128,512]{1,0:T(8,128)(2,1)S(1)}, u32[]{:S(2)}, u32[]{:S(2)}) collective-permute-start(bf16[128,512]{1,0:T(8,128)(2,1)} %refs_0_.8), channel_id=1, source_target_pairs={{0,2},{1,3},{2,0},{3,1},{16,19},{17,18},{18,17},{19,16},{4,6},{5,7... | collective-permute-start | bytes 393224 | tf_op jit(solution)/shard_map/ppermute | solution.py:40
  10.4 6.6 %collective-permute-start.2 = (bf16[128,512]{1,0:T(8,128)(2,1)}, bf16[128,512]{1,0:T(8,128)(2,1)S(1)}, u32[]{:S(2)}, u32[]{:S(2)}) collective-permute-start(bf16[128,512]{1,0:T(8,128)(2,1)} %refs_0_.8), channel_id=1, source_target_pairs={{0,8},{4,12},{8,0},{12,4},{1,9},{5,13},{9,1},{13,5},{2,10},{6,14},... | collective-permute-start | bytes 393224 | tf_op jit(solution)/shard_map/ppermute | solution.py:30
  13.2 6.3 %collective-permute-start.3 = (bf16[128,512]{1,0:T(8,128)(2,1)S(1)}, bf16[128,512]{1,0:T(8,128)(2,1)S(1)}, u32[]{:S(2)}, u32[]{:S(2)}) collective-permute-start(bf16[128,512]{1,0:T(8,128)(2,1)S(1)} %collective-permute-done.refs_1_), channel_id=1, source_target_pairs={{0,8},{4,12},{8,0},{12,4},{1,9},{5,13},{9,1},{13,5},{2,10},{6,14},... | collective-permute-start | bytes 393224 | tf_op jit(solution)/shard_map/ppermute | solution.py:30
  17.0 5.9 %collective-permute-start.5 = (bf16[128,512]{1,0:T(8,128)(2,1)S(1)}, bf16[128,512]{1,0:T(8,128)(2,1)S(1)}, u32[]{:S(2)}, u32[]{:S(2)}) collective-permute-start(bf16[128,512]{1,0:T(8,128)(2,1)S(1)} %collective-permute-done.1.refs_2_), channel_id=1, source_target_pairs={{0,24},{4,28},{8,16},{12,20},{16,8},{20,12},{24,0},{28,4},{1,25},{... | collective-permute-start | bytes 393224 | tf_op jit(solution)/shard_map/ppermute | solution.py:40
  19.5 16.1 %collective-permute-start.4 = (bf16[640,512]{1,0:T(8,128)(2,1)S(1)}, bf16[640,512]{1,0:T(8,128)(2,1)S(1)}, u32[]{:S(2)}, u32[]{:S(2)}) collective-permute-start(bf16[640,512]{1,0:T(8,128)(2,1)S(1)} %shard_map.110.w0_ref), channel_id=1, source_target_pairs={{0,4},{4,0},{8,12},{12,8},{1,5},{5,1},{9,13},{13,9},{2,6},{6,2},{1... | collective-permute-start | bytes 1966088 | tf_op jit(solution)/shard_map/ppermute | solution.py:30
  22.8 5.0 %collective-permute-start.6 = (bf16[128,512]{1,0:T(8,128)(2,1)S(1)}, bf16[128,512]{1,0:T(8,128)(2,1)S(1)}, u32[]{:S(2)}, u32[]{:S(2)}) collective-permute-start(bf16[128,512]{1,0:T(8,128)(2,1)S(1)} %collective-permute-done.1.refs_2_), channel_id=1, source_target_pairs={{0,8},{4,12},{8,0},{12,4},{1,9},{5,13},{9,1},{13,5},{2,10},{6,14},... | collective-permute-start | bytes 393224 | tf_op jit(solution)/shard_map/ppermute | solution.py:30
  27.8 5.0 %collective-permute-start.7 = (bf16[128,512]{1,0:T(8,128)(2,1)S(1)}, bf16[128,512]{1,0:T(8,128)(2,1)S(1)}, u32[]{:S(2)}, u32[]{:S(2)}) collective-permute-start(bf16[128,512]{1,0:T(8,128)(2,1)S(1)} %collective-permute-done.1.refs_2_), channel_id=1, source_target_pairs={{0,16},{16,0},{1,17},{17,1},{2,18},{18,2},{3,19},{19,3},{4,20},{20... | collective-permute-start | bytes 393224 | tf_op jit(solution)/shard_map/ppermute | solution.py:30
  32.8 1.3 %collective-permute-start.8 = (bf16[128,512]{1,0:T(8,128)(2,1)S(1)}, bf16[128,512]{1,0:T(8,128)(2,1)S(1)}, u32[]{:S(2)}, u32[]{:S(2)}) collective-permute-start(bf16[128,512]{1,0:T(8,128)(2,1)S(1)} %collective-permute-done.5.refs_0_), channel_id=1, source_target_pairs={{0,4},{4,0},{8,12},{12,8},{1,5},{5,1},{9,13},{13,9},{2,6},{6,2},{1... | collective-permute-start | bytes 393224 | tf_op jit(solution)/shard_map/ppermute | solution.py:30
  34.1 1.3 %collective-permute-start.9 = (bf16[128,512]{1,0:T(8,128)(2,1)S(1)}, bf16[128,512]{1,0:T(8,128)(2,1)S(1)}, u32[]{:S(2)}, u32[]{:S(2)}) collective-permute-start(bf16[128,512]{1,0:T(8,128)(2,1)S(1)} %collective-permute-done.6.refs_1_), channel_id=1, source_target_pairs={{0,4},{4,0},{8,12},{12,8},{1,5},{5,1},{9,13},{13,9},{2,6},{6,2},{1... | collective-permute-start | bytes 393224 | tf_op jit(solution)/shard_map/ppermute | solution.py:30
  35.5 2.8 %collective-permute-start.10 = (bf16[128,512]{1,0:T(8,128)(2,1)S(1)}, bf16[128,512]{1,0:T(8,128)(2,1)S(1)}, u32[]{:S(2)}, u32[]{:S(2)}) collective-permute-start(bf16[128,512]{1,0:T(8,128)(2,1)S(1)} %collective-permute-done.7.refs_2_), channel_id=1, source_target_pairs={{0,4},{4,0},{8,12},{12,8},{1,5},{5,1},{9,13},{13,9},{2,6},{6,2},{1... | collective-permute-start | bytes 393224 | tf_op jit(solution)/shard_map/ppermute | solution.py:30
  35.6 5.8 %collective-permute-start.16 = (bf16[128,512]{1,0:T(8,128)(2,1)S(1)}, bf16[128,512]{1,0:T(8,128)(2,1)S(1)}, u32[]{:S(2)}, u32[]{:S(2)}) collective-permute-start(bf16[128,512]{1,0:T(8,128)(2,1)S(1)} %copy-done.2), channel_id=1, source_target_pairs={{0,8},{4,12},{8,0},{12,4},{1,9},{5,13},{9,1},{13,5},{2,10},{6,14},... | collective-permute-start | bytes 393224 | tf_op jit(solution)/shard_map/ppermute | solution.py:30
  36.1 19.7 %copy-start.1 = (bf16[4,512,768]{2,1,0:T(8,128)(2,1)S(1)}, bf16[4,512,768]{2,1,0:T(8,128)(2,1)}, u32[]{:S(2)}) copy-start(bf16[4,512,768]{2,1,0:T(8,128)(2,1)} %refs_1_.15) | copy-start | bytes 9437188
  37.6 18.2 %copy-start = (bf16[4,512,768]{2,1,0:T(8,128)(2,1)S(1)}, bf16[4,512,768]{2,1,0:T(8,128)(2,1)}, u32[]{:S(2)}) copy-start(bf16[4,512,768]{2,1,0:T(8,128)(2,1)} %refs_0_.15) | copy-start | bytes 9437188
  38.7 17.1 %collective-permute-start.14 = (bf16[272,512]{1,0:T(8,128)(2,1)S(1)}, bf16[272,512]{1,0:T(8,128)(2,1)S(1)}, u32[]{:S(2)}, u32[]{:S(2)}) collective-permute-start(bf16[272,512]{1,0:T(8,128)(2,1)S(1)} %shard_map.113.pay_ref), channel_id=1, source_target_pairs={{0,8},{4,12},{8,0},{12,4},{1,9},{5,13},{9,1},{13,5},{2,10},{6,14},... | collective-permute-start | bytes 835592 | tf_op jit(solution)/shard_map/ppermute | solution.py:30
  41.5 14.3 %collective-permute-start.18 = (bf16[512,256]{1,0:T(8,128)(2,1)S(1)}, bf16[512,256]{1,0:T(8,128)(2,1)S(1)}, u32[]{:S(2)}, u32[]{:S(2)}) collective-permute-start(bf16[512,256]{1,0:T(8,128)(2,1)S(1)} %shard_map.120.refs_1_), channel_id=1, source_target_pairs={{0,2},{1,3},{2,0},{3,1},{16,19},{17,18},{18,17},{19,16},{4,6},{5,7... | collective-permute-start | bytes 786440 | tf_op jit(solution)/shard_map/ppermute | solution.py:40
  55.8 8.1 %collective-permute-start.17 = (bf16[512,256]{1,0:T(8,128)(2,1)S(1)}, bf16[512,256]{1,0:T(8,128)(2,1)S(1)}, u32[]{:S(2)}, u32[]{:S(2)}) collective-permute-start(bf16[512,256]{1,0:T(8,128)(2,1)S(1)} %shard_map.120.refs_1_), channel_id=1, source_target_pairs={{0,1},{1,0},{2,3},{3,2},{4,5},{5,4},{6,7},{7,6},{8,9},{9,8},{10,11... | collective-permute-start | bytes 786440 | tf_op jit(solution)/shard_map/ppermute | solution.py:30
  55.8 8.1 %collective-permute-start.19 = (bf16[512,256]{1,0:T(8,128)(2,1)S(1)}, bf16[512,256]{1,0:T(8,128)(2,1)S(1)}, u32[]{:S(2)}, u32[]{:S(2)}) collective-permute-start(bf16[512,256]{1,0:T(8,128)(2,1)S(1)} %collective-permute-done.18.refs_3_), channel_id=1, source_target_pairs={{0,16},{16,0},{1,17},{17,1},{2,18},{18,2},{3,19},{19,3},{4,20},{20... | collective-permute-start | bytes 786440 | tf_op jit(solution)/shard_map/ppermute | solution.py:30
  63.9 6.1 %collective-permute-start.20 = (bf16[512,256]{1,0:T(8,128)(2,1)S(1)}, bf16[512,256]{1,0:T(8,128)(2,1)S(1)}, u32[]{:S(2)}, u32[]{:S(2)}) collective-permute-start(bf16[512,256]{1,0:T(8,128)(2,1)S(1)} %shard_map.120.refs_1_), channel_id=1, source_target_pairs={{0,4},{4,0},{8,12},{12,8},{1,5},{5,1},{9,13},{13,9},{2,6},{6,2},{1... | collective-permute-start | bytes 786440 | tf_op jit(solution)/shard_map/ppermute | solution.py:30
  63.9 9.7 %collective-permute-start.22 = (bf16[512,256]{1,0:T(8,128)(2,1)S(1)}, bf16[512,256]{1,0:T(8,128)(2,1)S(1)}, u32[]{:S(2)}, u32[]{:S(2)}) collective-permute-start(bf16[512,256]{1,0:T(8,128)(2,1)S(1)} %collective-permute-done.18.refs_3_), channel_id=1, source_target_pairs={{0,4},{4,0},{8,12},{12,8},{1,5},{5,1},{9,13},{13,9},{2,6},{6,2},{1... | collective-permute-start | bytes 786440 | tf_op jit(solution)/shard_map/ppermute | solution.py:30
  64.4 9.2 %collective-permute-start.21 = (bf16[512,256]{1,0:T(8,128)(2,1)S(1)}, bf16[512,256]{1,0:T(8,128)(2,1)S(1)}, u32[]{:S(2)}, u32[]{:S(2)}) collective-permute-start(bf16[512,256]{1,0:T(8,128)(2,1)S(1)} %collective-permute-done.17.refs_2_), channel_id=1, source_target_pairs={{0,4},{4,0},{8,12},{12,8},{1,5},{5,1},{9,13},{13,9},{2,6},{6,2},{1... | collective-permute-start | bytes 786440 | tf_op jit(solution)/shard_map/ppermute | solution.py:30
  64.5 9.1 %collective-permute-start.23 = (bf16[512,256]{1,0:T(8,128)(2,1)S(1)}, bf16[512,256]{1,0:T(8,128)(2,1)S(1)}, u32[]{:S(2)}, u32[]{:S(2)}) collective-permute-start(bf16[512,256]{1,0:T(8,128)(2,1)S(1)} %collective-permute-done.19.refs_4_), channel_id=1, source_target_pairs={{0,4},{4,0},{8,12},{12,8},{1,5},{5,1},{9,13},{13,9},{2,6},{6,2},{1... | collective-permute-start | bytes 786440 | tf_op jit(solution)/shard_map/ppermute | solution.py:30
  67.4 6.2 %collective-permute-start.24 = (bf16[128,512]{1,0:T(8,128)(2,1)S(1)}, bf16[128,512]{1,0:T(8,128)(2,1)S(1)}, u32[]{:S(2)}, u32[]{:S(2)}) collective-permute-start(bf16[128,512]{1,0:T(8,128)(2,1)S(1)} %shard_map.121), channel_id=1, source_target_pairs={{0,8},{4,12},{8,0},{12,4},{1,9},{5,13},{9,1},{13,5},{2,10},{6,14},... | collective-permute-start | bytes 393224 | tf_op jit(solution)/shard_map/ppermute | solution.py:30
  70.0 5.8 %collective-permute-start.15 = (bf16[128,512]{1,0:T(8,128)(2,1)S(1)}, bf16[128,512]{1,0:T(8,128)(2,1)S(1)}, u32[]{:S(2)}, u32[]{:S(2)}) collective-permute-start(bf16[128,512]{1,0:T(8,128)(2,1)S(1)} %shard_map.119), channel_id=1, source_target_pairs={{0,8},{4,12},{8,0},{12,4},{1,9},{5,13},{9,1},{13,5},{2,10},{6,14},... | collective-permute-start | bytes 393224 | tf_op jit(solution)/shard_map/ppermute | solution.py:30

commit v8 on v7

--- a/solution.py
+++ b/solution.py
@@ -312,12 +312,11 @@
     back = [[] for _ in range(parts)]
     for a in range(1, chips):
         opened = run(near_kernel, (far[a - 1], *weights[:3]), range(local))
-        opened = run(more_kernel, (far[a - 1], opened, *weights), range(local, cut))
         for h in range(parts):
             s = kernel(
-                functools.partial(far_kernel, range(cut, count), h * size),
+                functools.partial(far_kernel, range(local, count), h * size),
                 shape((size, latent)), (far[a - 1], opened, *weights), [VM] * 8, 14,
-                (count - cut) * work // parts, (count - cut) * load, [pltpu.VMEM((size, latent), F32)])
+                local * work // parts, local * load, [pltpu.VMEM((size, latent), F32)])
             back[h].append(swap(s, "expert", 2 * a))
 
     pair = kernel(join_kernel, shape((latent, chips * depth)), (own_up, *ups_x),

time: 77.2 us -> 77.2 us (level)
    pallas_call x15 -> x14, Pallas kernels: 19.7 us -> 19.9 us  [kernel(): pl.pallas_call(body, out_shape=out_shape, in_specs=specs, out_specs=out_s...]
where the time goes in v8:
time: 77.2 us; the launch traced here: 77 us
  waiting for transfers between devices  40.4 us (52%)
  Pallas kernels  19.9 us (26%)
  starting transfers between devices  16.5 us (21%)
    ppermute x22, waiting for transfers between devices, swap(): return lax.ppermute(x, axis, [(i, i ^ bits) for i in range(size)])  22.8 us
    pallas_call x14, Pallas kernels, kernel(): pl.pallas_call(body, out_shape=out_shape, in_specs=specs, out_specs=out_s...  19.9 us
    ppermute x3, waiting for transfers between devices, swap_pair(): return lax.ppermute(x, axes, pairs)  17.6 us
    ppermute x22, starting transfers between devices, swap(): return lax.ppermute(x, axis, [(i, i ^ bits) for i in range(size)])  13.1 us
    ppermute x3, starting transfers between devices, swap_pair(): return lax.ppermute(x, axes, pairs)  3.34 us
  transfers between devices with their start and end apart: 25, of which 13 were waited for; matrix products, arithmetic and copies ran while one was open for 0% of the time, Pallas kernels for 24%

profile of v8, /device:TPU:0, one launch (start us, length us, event | category | flops | bytes accessed | tf_op | source)
XLA Modules:
  0.0 77.0 jit_solution(16931747086878096391)
XLA Ops:
  0.0 0.5 collective-permute-start.11
  0.5 0.1 collective-permute-start.12
  0.6 0.4 collective-permute-start.13
  1.0 2.6 %collective-permute-start = (bf16[128,512]{1,0:T(8,128)(2,1)}, bf16[128,512]{1,0:T(8,128)(2,1)S(1)}, u32[]{:S(2)}, u32[]{:S(2)}) collective-permute-start(bf16[128,512]{1,0:T(8,128)(2,1)} %refs_0_.7), channel_id=1, source_target_pairs={{0,1},{1,0},{2,3},{3,2},{4,5},{5,4},{6,7},{7,6},{8,9},{9,8},{10,11... | collective-permute-start | bytes 393224 | tf_op jit(solution)/shard_map/ppermute | solution.py:30
  3.6 2.6 %collective-permute-start.1 = (bf16[128,512]{1,0:T(8,128)(2,1)}, bf16[128,512]{1,0:T(8,128)(2,1)S(1)}, u32[]{:S(2)}, u32[]{:S(2)}) collective-permute-start(bf16[128,512]{1,0:T(8,128)(2,1)} %refs_0_.7), channel_id=1, source_target_pairs={{0,2},{1,3},{2,0},{3,1},{16,19},{17,18},{18,17},{19,16},{4,6},{5,7... | collective-permute-start | bytes 393224 | tf_op jit(solution)/shard_map/ppermute | solution.py:40
  6.2 4.2 %collective-permute-done.refs_1_ = bf16[128,512]{1,0:T(8,128)(2,1)S(1)} collective-permute-done((bf16[128,512]{1,0:T(8,128)(2,1)}, bf16[128,512]{1,0:T(8,128)(2,1)S(1)}, u32[]{:S(2)}, u32[]{:S(2)}) %collective-permute-start) | collective-permute-done | bytes 131104 | tf_op jit(solution)/shard_map/ppermute | solution.py:30
  10.4 1.9 %collective-permute-start.2 = (bf16[128,512]{1,0:T(8,128)(2,1)}, bf16[128,512]{1,0:T(8,128)(2,1)S(1)}, u32[]{:S(2)}, u32[]{:S(2)}) collective-permute-start(bf16[128,512]{1,0:T(8,128)(2,1)} %refs_0_.7), channel_id=1, source_target_pairs={{0,8},{4,12},{8,0},{12,4},{1,9},{5,13},{9,1},{13,5},{2,10},{6,14},... | collective-permute-start | bytes 393224 | tf_op jit(solution)/shard_map/ppermute | solution.py:30
  12.3 0.9 %collective-permute-done.1.refs_2_ = bf16[128,512]{1,0:T(8,128)(2,1)S(1)} collective-permute-done((bf16[128,512]{1,0:T(8,128)(2,1)}, bf16[128,512]{1,0:T(8,128)(2,1)S(1)}, u32[]{:S(2)}, u32[]{:S(2)}) %collective-permute-start.1) | collective-permute-done | bytes 131104 | tf_op jit(solution)/shard_map/ppermute | solution.py:40
  13.2 1.5 %collective-permute-start.3 = (bf16[128,512]{1,0:T(8,128)(2,1)S(1)}, bf16[128,512]{1,0:T(8,128)(2,1)S(1)}, u32[]{:S(2)}, u32[]{:S(2)}) collective-permute-start(bf16[128,512]{1,0:T(8,128)(2,1)S(1)} %collective-permute-done.refs_1_), channel_id=1, source_target_pairs={{0,8},{4,12},{8,0},{12,4},{1,9},{5,13},{9,1},{13,5},{2,10},{6,14},... | collective-permute-start | bytes 393224 | tf_op jit(solution)/shard_map/ppermute | solution.py:30
  14.7 2.3 %collective-permute-done.2.refs_3_ = bf16[128,512]{1,0:T(8,128)(2,1)S(1)} collective-permute-done((bf16[128,512]{1,0:T(8,128)(2,1)}, bf16[128,512]{1,0:T(8,128)(2,1)S(1)}, u32[]{:S(2)}, u32[]{:S(2)}) %collective-permute-start.2) | collective-permute-done | bytes 131104 | tf_op jit(solution)/shard_map/ppermute | solution.py:30
  17.0 2.4 %shard_map.109 = (bf16[256,2048]{1,0:T(8,128)(2,1)S(1)}, bf16[128,512]{1,0:T(8,128)(2,1)S(1)}, bf16[128,512]{1,0:T(8,128)(2,1)S(1)}, bf16[4,768,512]{2,1,0:T(8,1...) custom-call(bf16[256,2048]{1,0:T(8,128)(2,1)} %tok_hbm.1, ...), custom_call_target="tpu_custom_call" | custom-call | flops 4194304 | bytes 2097152 | tf_op jit(solution)/shard_map/pallas_call | solution.py:48
  19.4 0.1 collective-permute-done.3.refs_4_
  19.5 0.1 collective-permute-start.4
  19.6 3.2 %collective-permute-done.5.refs_0_ = bf16[128,512]{1,0:T(8,128)(2,1)S(1)} collective-permute-done((bf16[128,512]{1,0:T(8,128)(2,1)S(1)}, bf16[128,512]{1,0:T(8,128)(2,1)S(1)}, u32[]{:S(2)}, u32[]{:S(2)}) %collective-permute-start.5) | collective-permute-done | bytes 131104 | tf_op jit(solution)/shard_map/ppermute | solution.py:40
  22.8 0.5 collective-permute-start.6
  23.3 4.5 %collective-permute-done.6.refs_1_ = bf16[128,512]{1,0:T(8,128)(2,1)S(1)} collective-permute-done((bf16[128,512]{1,0:T(8,128)(2,1)S(1)}, bf16[128,512]{1,0:T(8,128)(2,1)S(1)}, u32[]{:S(2)}, u32[]{:S(2)}) %collective-permute-start.6) | collective-permute-done | bytes 131104 | tf_op jit(solution)/shard_map/ppermute | solution.py:30
  27.8 0.0 collective-permute-start.7
  27.8 5.0 %collective-permute-done.7.refs_2_ = bf16[128,512]{1,0:T(8,128)(2,1)S(1)} collective-permute-done((bf16[128,512]{1,0:T(8,128)(2,1)S(1)}, bf16[128,512]{1,0:T(8,128)(2,1)S(1)}, u32[]{:S(2)}, u32[]{:S(2)}) %collective-permute-start.7) | collective-permute-done | bytes 131104 | tf_op jit(solution)/shard_map/ppermute | solution.py:30
  32.8 1.3 %collective-permute-done.8.refs_3_ = bf16[128,512]{1,0:T(8,128)(2,1)S(1)} collective-permute-done((bf16[128,512]{1,0:T(8,128)(2,1)S(1)}, bf16[128,512]{1,0:T(8,128)(2,1)S(1)}, u32[]{:S(2)}, u32[]{:S(2)}) %collective-permute-start.8) | collective-permute-done | bytes 131104 | tf_op jit(solution)/shard_map/ppermute | solution.py:30
  34.1 0.1 collective-permute-start.9
  34.3 1.2 %collective-permute-done.9.refs_4_ = bf16[128,512]{1,0:T(8,128)(2,1)S(1)} collective-permute-done((bf16[128,512]{1,0:T(8,128)(2,1)S(1)}, bf16[128,512]{1,0:T(8,128)(2,1)S(1)}, u32[]{:S(2)}, u32[]{:S(2)}) %collective-permute-start.9) | collective-permute-done | bytes 131104 | tf_op jit(solution)/shard_map/ppermute | solution.py:30
  35.5 0.1 collective-permute-start.10
  35.6 0.5 collective-permute-start.16
  36.1 1.5 %shard_map.112.wt_ref = f32[16,256]{1,0:T(8,128)S(1)} custom-call(bf16[256,2048]{1,0:T(8,128)(2,1)S(1)} %get-tuple-element.12.normed_ref, bf16[16,2048]{1,0:T(8,128)(2,1)S(1)} %get-tuple-element.14.router_ref, s32[8,256]{1,0:T(8,128)S(1)} %get-tuple-element.15.ids_ref, s32[8,256]{1,0:T(8,128)S(1)} %get-tuple-element.16.slot_ref, s32[1,4,4,4]{3,2,1,0:T(4,128)} %list_hbm.1), custom_call_target="tpu_custom_call" | custom-call | flops 33554432 | bytes 1048576 | tf_op jit(solution)/shard_map/pallas_call | solution.py:48
  37.6 0.0 copy-start
  37.7 0.6 shard_map.111.sum_ref
  38.3 0.4 shard_map.113.pay_ref
  38.7 1.6 %collective-permute-start.14 = (bf16[272,512]{1,0:T(8,128)(2,1)S(1)}, bf16[272,512]{1,0:T(8,128)(2,1)S(1)}, u32[]{:S(2)}, u32[]{:S(2)}) collective-permute-start(bf16[272,512]{1,0:T(8,128)(2,1)S(1)} %shard_map.113.pay_ref), channel_id=1, source_target_pairs={{0,8},{4,12},{8,0},{12,4},{1,9},{5,13},{9,1},{13,5},{2,10},{6,14},... | collective-permute-start | bytes 835592 | tf_op jit(solution)/shard_map/ppermute | solution.py:30
  40.3 1.1 %collective-permute-done.16.refs_1_ = bf16[128,512]{1,0:T(8,128)(2,1)S(1)} collective-permute-done((bf16[128,512]{1,0:T(8,128)(2,1)S(1)}, bf16[128,512]{1,0:T(8,128)(2,1)S(1)}, u32[]{:S(2)}, u32[]{:S(2)}) %collective-permute-start.16) | collective-permute-done | bytes 131104 | tf_op jit(solution)/shard_map/ppermute | solution.py:30
  41.4 0.1 shard_map.119.refs_1_
  41.5 0.8 collective-permute-start.18
  42.3 13.5 %collective-permute-done.18.refs_3_ = bf16[512,256]{1,0:T(8,128)(2,1)S(1)} collective-permute-done((bf16[512,256]{1,0:T(8,128)(2,1)S(1)}, bf16[512,256]{1,0:T(8,128)(2,1)S(1)}, u32[]{:S(2)}, u32[]{:S(2)}) %collective-permute-start.18) | collective-permute-done | bytes 262176 | tf_op jit(solution)/shard_map/ppermute | solution.py:40
  55.8 2.8 %shard_map.114.sum_ref = f32[256,512]{1,0:T(8,128)S(1)} custom-call(bf16[272,512]{1,0:T(8,128)(2,1)S(1)} %shard_map.113.pay_ref, bf16[4,512,768]{2,1,0:T(8,128)(2,1)S(1)} %copy-done, bf16[4,512,768]{2,1,0:T(8,128)(2,1)S(1)} %copy-done.1, bf16[4,768,512]{2,1,0:T(8,128)(2,1)S(1)} %get-tuple-element.17.refs_2_), custom_call_target="tpu_custom_call" | custom-call | flops 2415919104 | bytes 9437184 | tf_op jit(solution)/shard_map/pallas_call | solution.py:48
  58.7 2.8 %shard_map.117.sum_ref = f32[256,512]{1,0:T(8,128)S(1)} custom-call(bf16[272,512]{1,0:T(8,128)(2,1)S(1)} %collective-permute-done.14.pay_ref, bf16[4,512,768]{2,1,0:T(8,128)(2,1)S(1)} %copy-done, bf16[4,512,768]{2,1,0:T(8,128)(2,1)S(1)} %copy-done.1, bf16[4,768,512]{2,1,0:T(8,128)(2,1)S(1)} %get-tuple-element.17.refs_2_), custom_call_target="tpu_custom_call" | custom-call | flops 2415919104 | bytes 9437184 | tf_op jit(solution)/shard_map/pallas_call | solution.py:48
  61.5 2.4 %collective-permute-done.17.refs_2_ = bf16[512,256]{1,0:T(8,128)(2,1)S(1)} collective-permute-done((bf16[512,256]{1,0:T(8,128)(2,1)S(1)}, bf16[512,256]{1,0:T(8,128)(2,1)S(1)}, u32[]{:S(2)}, u32[]{:S(2)}) %collective-permute-start.17) | collective-permute-done | bytes 262176 | tf_op jit(solution)/shard_map/ppermute | solution.py:30
  63.9 0.0 collective-permute-done.19.refs_4_
  63.9 0.5 collective-permute-start.22
  64.4 0.1 collective-permute-start.21
  64.5 0.4 collective-permute-start.23
  64.9 1.8 %shard_map.120 = bf16[128,512]{1,0:T(8,128)(2,1)S(1)} custom-call(bf16[272,512]{1,0:T(8,128)(2,1)S(1)} %collective-permute-done.14.pay_ref, f32[256,512]{1,0:T(8,128)S(1)} %shard_map.117.sum_ref, bf16[4,512,768]{2,1,0:T(8,128)(2,1)S(1)} %copy-done, bf16[4,512,768]{2,1,0:T(8,128)(2,1)S(1)} %copy-done.1, bf16[4,768,512]{2,1,0:T(8,128)(2,1)S(1)} %get-tuple-element.17.refs_2_, ...), custom_call_target="tpu_custom_call" | custom-call | flops 1207959552 | bytes 9437184 | tf_op jit(solution)/shard_map/pallas_call | solution.py:48
  66.7 0.1 collective-permute-start.24
  66.8 1.8 %shard_map.118 = bf16[128,512]{1,0:T(8,128)(2,1)S(1)} custom-call(bf16[272,512]{1,0:T(8,128)(2,1)S(1)} %collective-permute-done.14.pay_ref, f32[256,512]{1,0:T(8,128)S(1)} %shard_map.117.sum_ref, bf16[4,512,768]{2,1,0:T(8,128)(2,1)S(1)} %copy-done, bf16[4,512,768]{2,1,0:T(8,128)(2,1)S(1)} %copy-done.1, bf16[4,768,512]{2,1,0:T(8,128)(2,1)S(1)} %get-tuple-element.17.refs_2_, ...), custom_call_target="tpu_custom_call" | custom-call | flops 1207959552 | bytes 9437184 | tf_op jit(solution)/shard_map/pallas_call | solution.py:48
  68.6 1.5 %shard_map.115.sum_ref = f32[256,512]{1,0:T(8,128)S(1)} custom-call(bf16[272,512]{1,0:T(8,128)(2,1)S(1)} %shard_map.113.pay_ref, f32[256,512]{1,0:T(8,128)S(1)} %shard_map.114.sum_ref, bf16[4,512,768]{2,1,0:T(8,128)(2,1)S(1)} %copy-done, bf16[4,512,768]{2,1,0:T(8,128)(2,1)S(1)} %copy-done.1, bf16[4,768,512]{2,1,0:T(8,128)(2,1)S(1)} %get-tuple-element.17.refs_2_, ...), custom_call_target="tpu_custom_call" | custom-call | flops 1207959552 | bytes 4718592 | tf_op jit(solution)/shard_map/pallas_call | solution.py:48
  70.1 2.1 %collective-permute-start.15 = (bf16[128,512]{1,0:T(8,128)(2,1)S(1)}, bf16[128,512]{1,0:T(8,128)(2,1)S(1)}, u32[]{:S(2)}, u32[]{:S(2)}) collective-permute-start(bf16[128,512]{1,0:T(8,128)(2,1)S(1)} %shard_map.118), channel_id=1, source_target_pairs={{0,8},{4,12},{8,0},{12,4},{1,9},{5,13},{9,1},{13,5},{2,10},{6,14},... | collective-permute-start | bytes 393224 | tf_op jit(solution)/shard_map/ppermute | solution.py:30
  72.2 1.5 %shard_map.116.near_ref = f32[256,512]{1,0:T(8,128)S(1)} custom-call(bf16[272,512]{1,0:T(8,128)(2,1)S(1)} %shard_map.113.pay_ref, f32[256,512]{1,0:T(8,128)S(1)} %shard_map.115.sum_ref, bf16[4,512,768]{2,1,0:T(8,128)(2,1)S(1)} %copy-done, bf16[4,512,768]{2,1,0:T(8,128)(2,1)S(1)} %copy-done.1, bf16[4,768,512]{2,1,0:T(8,128)(2,1)S(1)} %get-tuple-element.17.refs_2_, ...), custom_call_target="tpu_custom_call" | custom-call | flops 1207959552 | bytes 4718592 | tf_op jit(solution)/shard_map/pallas_call | solution.py:48
  73.7 1.3 %shard_map.121.refs_9_ = bf16[256,2048]{1,0:T(8,128)(2,1)} custom-call(f32[256,512]{1,0:T(8,128)S(1)} %shard_map.116.near_ref, bf16[128,512]{1,0:T(8,128)(2,1)S(1)} %collective-permute-done.24.refs_0_, bf16[512,256]{1,0:T(8,128)(2,1)S(1)} %shard_map.119.refs_1_, bf16[512,256]{1,0:T(8,128)(2,1)S(1)} %collective-permute-done.17.refs_2_, ...), custom_call_target="tpu_custom_call" | custom-call | flops 268435456 | bytes 2097152 | tf_op jit(solution)/shard_map/pallas_call | solution.py:48
  75.0 0.7 collective-permute-done.15.refs_0_
  75.7 1.3 %shard_map.122 = bf16[256,2048]{1,0:T(8,128)(2,1)} custom-call(f32[256,512]{1,0:T(8,128)S(1)} %shard_map.116.near_ref, bf16[128,512]{1,0:T(8,128)(2,1)S(1)} %collective-permute-done.15.refs_0_, bf16[512,256]{1,0:T(8,128)(2,1)S(1)} %shard_map.119.refs_1_, bf16[512,256]{1,0:T(8,128)(2,1)S(1)} %collective-permute-done.17.refs_2_, ...), custom_call_target="tpu_custom_call", output_to_operand_aliasing={{}: (10, {})} | custom-call | flops 268435456 | bytes 2097152 | tf_op jit(solution)/shard_map/pallas_call | solution.py:48
  (22 shorter events, 0.1 us)
Async XLA Ops:
  0.0 35.6 %copy-start.2 = (bf16[128,512]{1,0:T(8,128)(2,1)S(1)}, bf16[128,512]{1,0:T(8,128)(2,1)}, u32[]{:S(2)}) copy-start(bf16[128,512]{1,0:T(8,128)(2,1)} %refs_1_.7) | copy-start | bytes 393220
  0.0 64.4 %collective-permute-start.11 = (bf16[4,512,768]{2,1,0:T(8,128)(2,1)}, bf16[4,512,768]{2,1,0:T(8,128)(2,1)S(1)}, u32[]{:S(2)}, u32[]{:S(2)}) collective-permute-start(bf16[4,512,768]{2,1,0:T(8,128)(2,1)} %refs_0_.13), channel_id=1, source_target_pairs={{0,4},{4,0},{8,12},{12,8},{1,5},{5,1},{9,13},{13,9},{2,6},{6,2},{1... | collective-permute-start | bytes 9437192 | tf_op jit(solution)/shard_map/ppermute | solution.py:30
  0.5 64.0 %collective-permute-start.12 = (bf16[4,512,768]{2,1,0:T(8,128)(2,1)}, bf16[4,512,768]{2,1,0:T(8,128)(2,1)S(1)}, u32[]{:S(2)}, u32[]{:S(2)}) collective-permute-start(bf16[4,512,768]{2,1,0:T(8,128)(2,1)} %refs_1_.13), channel_id=1, source_target_pairs={{0,4},{4,0},{8,12},{12,8},{1,5},{5,1},{9,13},{13,9},{2,6},{6,2},{1... | collective-permute-start | bytes 9437192 | tf_op jit(solution)/shard_map/ppermute | solution.py:30
  0.6 64.4 %collective-permute-start.13 = (bf16[4,768,512]{2,1,0:T(8,128)(2,1)}, bf16[4,768,512]{2,1,0:T(8,128)(2,1)S(1)}, u32[]{:S(2)}, u32[]{:S(2)}) collective-permute-start(bf16[4,768,512]{2,1,0:T(8,128)(2,1)} %refs_2_.1), channel_id=1, source_target_pairs={{0,4},{4,0},{8,12},{12,8},{1,5},{5,1},{9,13},{13,9},{2,6},{6,2},{1... | collective-permute-start | bytes 9437192 | tf_op jit(solution)/shard_map/ppermute | solution.py:30
  1.0 9.4 %collective-permute-start = (bf16[128,512]{1,0:T(8,128)(2,1)}, bf16[128,512]{1,0:T(8,128)(2,1)S(1)}, u32[]{:S(2)}, u32[]{:S(2)}) collective-permute-start(bf16[128,512]{1,0:T(8,128)(2,1)} %refs_0_.7), channel_id=1, source_target_pairs={{0,1},{1,0},{2,3},{3,2},{4,5},{5,4},{6,7},{7,6},{8,9},{9,8},{10,11... | collective-permute-start | bytes 393224 | tf_op jit(solution)/shard_map/ppermute | solution.py:30
  3.6 9.5 %collective-permute-start.1 = (bf16[128,512]{1,0:T(8,128)(2,1)}, bf16[128,512]{1,0:T(8,128)(2,1)S(1)}, u32[]{:S(2)}, u32[]{:S(2)}) collective-permute-start(bf16[128,512]{1,0:T(8,128)(2,1)} %refs_0_.7), channel_id=1, source_target_pairs={{0,2},{1,3},{2,0},{3,1},{16,19},{17,18},{18,17},{19,16},{4,6},{5,7... | collective-permute-start | bytes 393224 | tf_op jit(solution)/shard_map/ppermute | solution.py:40
  10.4 6.6 %collective-permute-start.2 = (bf16[128,512]{1,0:T(8,128)(2,1)}, bf16[128,512]{1,0:T(8,128)(2,1)S(1)}, u32[]{:S(2)}, u32[]{:S(2)}) collective-permute-start(bf16[128,512]{1,0:T(8,128)(2,1)} %refs_0_.7), channel_id=1, source_target_pairs={{0,8},{4,12},{8,0},{12,4},{1,9},{5,13},{9,1},{13,5},{2,10},{6,14},... | collective-permute-start | bytes 393224 | tf_op jit(solution)/shard_map/ppermute | solution.py:30
  13.2 6.3 %collective-permute-start.3 = (bf16[128,512]{1,0:T(8,128)(2,1)S(1)}, bf16[128,512]{1,0:T(8,128)(2,1)S(1)}, u32[]{:S(2)}, u32[]{:S(2)}) collective-permute-start(bf16[128,512]{1,0:T(8,128)(2,1)S(1)} %collective-permute-done.refs_1_), channel_id=1, source_target_pairs={{0,8},{4,12},{8,0},{12,4},{1,9},{5,13},{9,1},{13,5},{2,10},{6,14},... | collective-permute-start | bytes 393224 | tf_op jit(solution)/shard_map/ppermute | solution.py:30
  17.0 5.9 %collective-permute-start.5 = (bf16[128,512]{1,0:T(8,128)(2,1)S(1)}, bf16[128,512]{1,0:T(8,128)(2,1)S(1)}, u32[]{:S(2)}, u32[]{:S(2)}) collective-permute-start(bf16[128,512]{1,0:T(8,128)(2,1)S(1)} %collective-permute-done.1.refs_2_), channel_id=1, source_target_pairs={{0,24},{4,28},{8,16},{12,20},{16,8},{20,12},{24,0},{28,4},{1,25},{... | collective-permute-start | bytes 393224 | tf_op jit(solution)/shard_map/ppermute | solution.py:40
  19.5 16.1 %collective-permute-start.4 = (bf16[640,512]{1,0:T(8,128)(2,1)S(1)}, bf16[640,512]{1,0:T(8,128)(2,1)S(1)}, u32[]{:S(2)}, u32[]{:S(2)}) collective-permute-start(bf16[640,512]{1,0:T(8,128)(2,1)S(1)} %shard_map.110.w0_ref), channel_id=1, source_target_pairs={{0,4},{4,0},{8,12},{12,8},{1,5},{5,1},{9,13},{13,9},{2,6},{6,2},{1... | collective-permute-start | bytes 1966088 | tf_op jit(solution)/shard_map/ppermute | solution.py:30
  22.8 5.0 %collective-permute-start.6 = (bf16[128,512]{1,0:T(8,128)(2,1)S(1)}, bf16[128,512]{1,0:T(8,128)(2,1)S(1)}, u32[]{:S(2)}, u32[]{:S(2)}) collective-permute-start(bf16[128,512]{1,0:T(8,128)(2,1)S(1)} %collective-permute-done.1.refs_2_), channel_id=1, source_target_pairs={{0,8},{4,12},{8,0},{12,4},{1,9},{5,13},{9,1},{13,5},{2,10},{6,14},... | collective-permute-start | bytes 393224 | tf_op jit(solution)/shard_map/ppermute | solution.py:30
  27.8 5.0 %collective-permute-start.7 = (bf16[128,512]{1,0:T(8,128)(2,1)S(1)}, bf16[128,512]{1,0:T(8,128)(2,1)S(1)}, u32[]{:S(2)}, u32[]{:S(2)}) collective-permute-start(bf16[128,512]{1,0:T(8,128)(2,1)S(1)} %collective-permute-done.1.refs_2_), channel_id=1, source_target_pairs={{0,16},{16,0},{1,17},{17,1},{2,18},{18,2},{3,19},{19,3},{4,20},{20... | collective-permute-start | bytes 393224 | tf_op jit(solution)/shard_map/ppermute | solution.py:30
  32.8 1.3 %collective-permute-start.8 = (bf16[128,512]{1,0:T(8,128)(2,1)S(1)}, bf16[128,512]{1,0:T(8,128)(2,1)S(1)}, u32[]{:S(2)}, u32[]{:S(2)}) collective-permute-start(bf16[128,512]{1,0:T(8,128)(2,1)S(1)} %collective-permute-done.5.refs_0_), channel_id=1, source_target_pairs={{0,4},{4,0},{8,12},{12,8},{1,5},{5,1},{9,13},{13,9},{2,6},{6,2},{1... | collective-permute-start | bytes 393224 | tf_op jit(solution)/shard_map/ppermute | solution.py:30
  34.1 1.3 %collective-permute-start.9 = (bf16[128,512]{1,0:T(8,128)(2,1)S(1)}, bf16[128,512]{1,0:T(8,128)(2,1)S(1)}, u32[]{:S(2)}, u32[]{:S(2)}) collective-permute-start(bf16[128,512]{1,0:T(8,128)(2,1)S(1)} %collective-permute-done.6.refs_1_), channel_id=1, source_target_pairs={{0,4},{4,0},{8,12},{12,8},{1,5},{5,1},{9,13},{13,9},{2,6},{6,2},{1... | collective-permute-start | bytes 393224 | tf_op jit(solution)/shard_map/ppermute | solution.py:30
  35.5 2.8 %collective-permute-start.10 = (bf16[128,512]{1,0:T(8,128)(2,1)S(1)}, bf16[128,512]{1,0:T(8,128)(2,1)S(1)}, u32[]{:S(2)}, u32[]{:S(2)}) collective-permute-start(bf16[128,512]{1,0:T(8,128)(2,1)S(1)} %collective-permute-done.7.refs_2_), channel_id=1, source_target_pairs={{0,4},{4,0},{8,12},{12,8},{1,5},{5,1},{9,13},{13,9},{2,6},{6,2},{1... | collective-permute-start | bytes 393224 | tf_op jit(solution)/shard_map/ppermute | solution.py:30
  35.6 5.8 %collective-permute-start.16 = (bf16[128,512]{1,0:T(8,128)(2,1)S(1)}, bf16[128,512]{1,0:T(8,128)(2,1)S(1)}, u32[]{:S(2)}, u32[]{:S(2)}) collective-permute-start(bf16[128,512]{1,0:T(8,128)(2,1)S(1)} %copy-done.2), channel_id=1, source_target_pairs={{0,8},{4,12},{8,0},{12,4},{1,9},{5,13},{9,1},{13,5},{2,10},{6,14},... | collective-permute-start | bytes 393224 | tf_op jit(solution)/shard_map/ppermute | solution.py:30
  36.1 19.7 %copy-start.1 = (bf16[4,512,768]{2,1,0:T(8,128)(2,1)S(1)}, bf16[4,512,768]{2,1,0:T(8,128)(2,1)}, u32[]{:S(2)}) copy-start(bf16[4,512,768]{2,1,0:T(8,128)(2,1)} %refs_1_.13) | copy-start | bytes 9437188
  37.6 18.2 %copy-start = (bf16[4,512,768]{2,1,0:T(8,128)(2,1)S(1)}, bf16[4,512,768]{2,1,0:T(8,128)(2,1)}, u32[]{:S(2)}) copy-start(bf16[4,512,768]{2,1,0:T(8,128)(2,1)} %refs_0_.13) | copy-start | bytes 9437188
  38.7 17.1 %collective-permute-start.14 = (bf16[272,512]{1,0:T(8,128)(2,1)S(1)}, bf16[272,512]{1,0:T(8,128)(2,1)S(1)}, u32[]{:S(2)}, u32[]{:S(2)}) collective-permute-start(bf16[272,512]{1,0:T(8,128)(2,1)S(1)} %shard_map.113.pay_ref), channel_id=1, source_target_pairs={{0,8},{4,12},{8,0},{12,4},{1,9},{5,13},{9,1},{13,5},{2,10},{6,14},... | collective-permute-start | bytes 835592 | tf_op jit(solution)/shard_map/ppermute | solution.py:30
  41.5 14.3 %collective-permute-start.18 = (bf16[512,256]{1,0:T(8,128)(2,1)S(1)}, bf16[512,256]{1,0:T(8,128)(2,1)S(1)}, u32[]{:S(2)}, u32[]{:S(2)}) collective-permute-start(bf16[512,256]{1,0:T(8,128)(2,1)S(1)} %shard_map.119.refs_1_), channel_id=1, source_target_pairs={{0,2},{1,3},{2,0},{3,1},{16,19},{17,18},{18,17},{19,16},{4,6},{5,7... | collective-permute-start | bytes 786440 | tf_op jit(solution)/shard_map/ppermute | solution.py:40
  55.8 8.1 %collective-permute-start.17 = (bf16[512,256]{1,0:T(8,128)(2,1)S(1)}, bf16[512,256]{1,0:T(8,128)(2,1)S(1)}, u32[]{:S(2)}, u32[]{:S(2)}) collective-permute-start(bf16[512,256]{1,0:T(8,128)(2,1)S(1)} %shard_map.119.refs_1_), channel_id=1, source_target_pairs={{0,1},{1,0},{2,3},{3,2},{4,5},{5,4},{6,7},{7,6},{8,9},{9,8},{10,11... | collective-permute-start | bytes 786440 | tf_op jit(solution)/shard_map/ppermute | solution.py:30
  55.8 8.1 %collective-permute-start.19 = (bf16[512,256]{1,0:T(8,128)(2,1)S(1)}, bf16[512,256]{1,0:T(8,128)(2,1)S(1)}, u32[]{:S(2)}, u32[]{:S(2)}) collective-permute-start(bf16[512,256]{1,0:T(8,128)(2,1)S(1)} %collective-permute-done.18.refs_3_), channel_id=1, source_target_pairs={{0,16},{16,0},{1,17},{17,1},{2,18},{18,2},{3,19},{19,3},{4,20},{20... | collective-permute-start | bytes 786440 | tf_op jit(solution)/shard_map/ppermute | solution.py:30
  63.9 6.2 %collective-permute-start.20 = (bf16[512,256]{1,0:T(8,128)(2,1)S(1)}, bf16[512,256]{1,0:T(8,128)(2,1)S(1)}, u32[]{:S(2)}, u32[]{:S(2)}) collective-permute-start(bf16[512,256]{1,0:T(8,128)(2,1)S(1)} %shard_map.119.refs_1_), channel_id=1, source_target_pairs={{0,4},{4,0},{8,12},{12,8},{1,5},{5,1},{9,13},{13,9},{2,6},{6,2},{1... | collective-permute-start | bytes 786440 | tf_op jit(solution)/shard_map/ppermute | solution.py:30
  63.9 9.8 %collective-permute-start.22 = (bf16[512,256]{1,0:T(8,128)(2,1)S(1)}, bf16[512,256]{1,0:T(8,128)(2,1)S(1)}, u32[]{:S(2)}, u32[]{:S(2)}) collective-permute-start(bf16[512,256]{1,0:T(8,128)(2,1)S(1)} %collective-permute-done.18.refs_3_), channel_id=1, source_target_pairs={{0,4},{4,0},{8,12},{12,8},{1,5},{5,1},{9,13},{13,9},{2,6},{6,2},{1... | collective-permute-start | bytes 786440 | tf_op jit(solution)/shard_map/ppermute | solution.py:30
  64.4 9.3 %collective-permute-start.21 = (bf16[512,256]{1,0:T(8,128)(2,1)S(1)}, bf16[512,256]{1,0:T(8,128)(2,1)S(1)}, u32[]{:S(2)}, u32[]{:S(2)}) collective-permute-start(bf16[512,256]{1,0:T(8,128)(2,1)S(1)} %collective-permute-done.17.refs_2_), channel_id=1, source_target_pairs={{0,4},{4,0},{8,12},{12,8},{1,5},{5,1},{9,13},{13,9},{2,6},{6,2},{1... | collective-permute-start | bytes 786440 | tf_op jit(solution)/shard_map/ppermute | solution.py:30
  64.5 9.2 %collective-permute-start.23 = (bf16[512,256]{1,0:T(8,128)(2,1)S(1)}, bf16[512,256]{1,0:T(8,128)(2,1)S(1)}, u32[]{:S(2)}, u32[]{:S(2)}) collective-permute-start(bf16[512,256]{1,0:T(8,128)(2,1)S(1)} %collective-permute-done.19.refs_4_), channel_id=1, source_target_pairs={{0,4},{4,0},{8,12},{12,8},{1,5},{5,1},{9,13},{13,9},{2,6},{6,2},{1... | collective-permute-start | bytes 786440 | tf_op jit(solution)/shard_map/ppermute | solution.py:30
  66.7 7.0 %collective-permute-start.24 = (bf16[128,512]{1,0:T(8,128)(2,1)S(1)}, bf16[128,512]{1,0:T(8,128)(2,1)S(1)}, u32[]{:S(2)}, u32[]{:S(2)}) collective-permute-start(bf16[128,512]{1,0:T(8,128)(2,1)S(1)} %shard_map.120), channel_id=1, source_target_pairs={{0,8},{4,12},{8,0},{12,4},{1,9},{5,13},{9,1},{13,5},{2,10},{6,14},... | collective-permute-start | bytes 393224 | tf_op jit(solution)/shard_map/ppermute | solution.py:30
  70.1 5.6 %collective-permute-start.15 = (bf16[128,512]{1,0:T(8,128)(2,1)S(1)}, bf16[128,512]{1,0:T(8,128)(2,1)S(1)}, u32[]{:S(2)}, u32[]{:S(2)}) collective-permute-start(bf16[128,512]{1,0:T(8,128)(2,1)S(1)} %shard_map.118), channel_id=1, source_target_pairs={{0,8},{4,12},{8,0},{12,4},{1,9},{5,13},{9,1},{13,5},{2,10},{6,14},... | collective-permute-start | bytes 393224 | tf_op jit(solution)/shard_map/ppermute | solution.py:30

commit v9 on v8

--- a/solution.py
+++ b/solution.py
@@ -91,15 +91,20 @@
     load.wait()
     _, shards, copies_n, local = list_ref.shape
 
-    def listed(i, served):
-        shard, copy = i // copies_n, i % copies_n
-        for m in range(local):
-            entry = list_ref[0, shard, copy, m]
-            owner = jnp.where(entry >= 0, entry, -top) // top
-            served = served + jnp.where((lane == owner) & (sub == shard * local + m), 1.0, 0.0)
-        return served
-
-    served = lax.fori_loop(0, shards * copies_n, listed, served)
+    width = 128
+    column = lax.broadcasted_iota(jnp.int32, (experts, width), 0)
+
+    def listed(copy, served):
+        owner = jnp.full((experts, width), -1, jnp.int32)
+        for shard in range(shards):
+            for m in range(local):
+                entry = list_ref[0, shard, copy, m]
+                row = jnp.where(entry >= 0, entry, -top) // top
+                owner = jnp.where(column == shard * local + m, row, owner)
+        hits = [jnp.where(lane[:, i:i + width] == owner, 1.0, 0.0) for i in range(0, rows, width)]
+        return served + jnp.concatenate(hits, axis=1)
+
+    served = lax.fori_loop(0, copies_n, listed, served)
     denom = jnp.sum(total * sig, axis=0, keepdims=True)
     wt_ref[...] = jnp.where(served > 0.0, sig / denom, 0.0)
 
@@ -247,7 +252,7 @@
             down[(a, 0)] = swap(down_proj, "expert", 2 * a)
         ups_x = [swap(up_proj, "expert", 2 * a) for a in range(1, chips)]
         for a in range(1, chips):
-            down[(a, 1)] = swap(near_z, "expert", 2 * a)
+            down[(a, 1)] = swap(down[(a, 0)], "replica", 1)
             down[(a, "B")] = swap_pair(far_z, ("groups", "expert"),
                                        lambda i, j: (i ^ 1, j ^ (2 * a)))
             down[(a, "A")] = swap(far_z, "expert", 2 * a)
@@ -260,8 +265,8 @@
                 down[(a, b)] = swap(down[(0, b)], "expert", 2 * a)
         ups_x = [swap(up_proj, "expert", 2 * a) for a in range(1, chips)]
 
-    moved = (down_proj, up_proj, expert_down, router.T, expert_ids.T, slot_pos.T)
-    normed, own_down, own_up, last, *routing = kernel(
+    moved = (down_proj, up_proj, router.T, expert_ids.T, slot_pos.T)
+    normed, own_down, own_up, *routing = kernel(
         norm_kernel, (shape((rows, width)), *[shape(x.shape, x.dtype) for x in moved]),
         tuple(map(in_hbm, (tokens, norm_gain.reshape(1, width), *moved))), [AN] * (2 + len(moved)), 18,
         8 * rows * width, 4 * rows * width,
@@ -272,7 +277,7 @@
         (normed, *routing, in_hbm(overflow_list)), [VM] * 4 + [AN], 10, 4 * rows * width * experts,
         2 * rows * width, [pltpu.SMEM(overflow_list.shape, jnp.int32), pltpu.SemaphoreType.DMA])
     down[(0, 0)] = own_down
-    weights = (expert_gate, expert_up, last, *[
+    weights = (expert_gate, expert_up, expert_down, *[
         swap(w, "expert", 1) for w in (expert_gate, expert_up, expert_down)])
 
     late = [k for k in down if (k[1] == "A" and k[0]) or k[1] == "B"] or list(down)[-1:]

time: 77.2 us -> 77.7 us (level)
  starting transfers between devices: 16.5 us -> 20.8 us
  waiting for transfers between devices: 40.4 us -> 37.4 us
  Pallas kernels: 19.9 us -> 19.1 us
    ppermute x22, waiting for transfers between devices: 22.8 us -> 16.8 us  [swap(): return lax.ppermute(x, axis, [(i, i ^ bits) for i in range(size)])]
    ppermute x3, waiting for transfers between devices: 17.6 us -> 20.6 us  [swap_pair(): return lax.ppermute(x, axes, pairs)]
    ppermute x22, starting transfers between devices: 13.1 us -> 15.4 us  [swap(): return lax.ppermute(x, axis, [(i, i ^ bits) for i in range(size)])]
    ppermute x3, starting transfers between devices: 3.34 us -> 5.35 us  [swap_pair(): return lax.ppermute(x, axes, pairs)]
  transfers between devices with their start and end apart: 25 -> 25, of which waited for: 13 -> 11; matrix products, arithmetic and copies ran while one was open for 0% -> 0% of each run, Pallas kernels for 24% -> 23%
where the time goes in v9:
time: 77.7 us; the launch traced here: 77.5 us
  waiting for transfers between devices  37.4 us (48%)
  starting transfers between devices  20.8 us (27%)
  Pallas kernels  19.1 us (25%)
    ppermute x3, waiting for transfers between devices, swap_pair(): return lax.ppermute(x, axes, pairs)  20.6 us
    pallas_call x14, Pallas kernels, kernel(): pl.pallas_call(body, out_shape=out_shape, in_specs=specs, out_specs=out_s...  19.1 us
    ppermute x22, waiting for transfers between devices, swap(): return lax.ppermute(x, axis, [(i, i ^ bits) for i in range(size)])  16.8 us
    ppermute x22, starting transfers between devices, swap(): return lax.ppermute(x, axis, [(i, i ^ bits) for i in range(size)])  15.4 us
    ppermute x3, starting transfers between devices, swap_pair(): return lax.ppermute(x, axes, pairs)  5.35 us
  transfers between devices with their start and end apart: 25, of which 11 were waited for; matrix products, arithmetic and copies ran while one was open for 0% of the time, Pallas kernels for 23%

profile of v9, /device:TPU:0, one launch (start us, length us, event | category | flops | bytes accessed | tf_op | source)
XLA Modules:
  0.0 77.5 jit_solution(6932691301342552197)
XLA Ops:
  0.0 0.5 collective-permute-start.11
  0.5 0.0 collective-permute-start.12
  0.5 0.5 collective-permute-start.13
  1.0 2.6 %collective-permute-start = (bf16[128,512]{1,0:T(8,128)(2,1)}, bf16[128,512]{1,0:T(8,128)(2,1)S(1)}, u32[]{:S(2)}, u32[]{:S(2)}) collective-permute-start(bf16[128,512]{1,0:T(8,128)(2,1)} %refs_0_.7), channel_id=1, source_target_pairs={{0,1},{1,0},{2,3},{3,2},{4,5},{5,4},{6,7},{7,6},{8,9},{9,8},{10,11... | collective-permute-start | bytes 393224 | tf_op jit(solution)/shard_map/ppermute | solution.py:30
  3.6 1.5 %collective-permute-start.2 = (bf16[128,512]{1,0:T(8,128)(2,1)}, bf16[128,512]{1,0:T(8,128)(2,1)S(1)}, u32[]{:S(2)}, u32[]{:S(2)}) collective-permute-start(bf16[128,512]{1,0:T(8,128)(2,1)} %refs_0_.7), channel_id=1, source_target_pairs={{0,8},{4,12},{8,0},{12,4},{1,9},{5,13},{9,1},{13,5},{2,10},{6,14},... | collective-permute-start | bytes 393224 | tf_op jit(solution)/shard_map/ppermute | solution.py:30
  5.1 2.9 %collective-permute-done.refs_1_ = bf16[128,512]{1,0:T(8,128)(2,1)S(1)} collective-permute-done((bf16[128,512]{1,0:T(8,128)(2,1)}, bf16[128,512]{1,0:T(8,128)(2,1)S(1)}, u32[]{:S(2)}, u32[]{:S(2)}) %collective-permute-start) | collective-permute-done | bytes 131104 | tf_op jit(solution)/shard_map/ppermute | solution.py:30
  7.9 2.8 %collective-permute-start.1 = (bf16[128,512]{1,0:T(8,128)(2,1)}, bf16[128,512]{1,0:T(8,128)(2,1)S(1)}, u32[]{:S(2)}, u32[]{:S(2)}) collective-permute-start(bf16[128,512]{1,0:T(8,128)(2,1)} %refs_0_.7), channel_id=1, source_target_pairs={{0,2},{1,3},{2,0},{3,1},{16,19},{17,18},{18,17},{19,16},{4,6},{5,7... | collective-permute-start | bytes 393224 | tf_op jit(solution)/shard_map/ppermute | solution.py:40
  10.7 1.6 %collective-permute-start.3 = (bf16[128,512]{1,0:T(8,128)(2,1)S(1)}, bf16[128,512]{1,0:T(8,128)(2,1)S(1)}, u32[]{:S(2)}, u32[]{:S(2)}) collective-permute-start(bf16[128,512]{1,0:T(8,128)(2,1)S(1)} %collective-permute-done.2.refs_3_), channel_id=1, source_target_pairs={{0,1},{1,0},{2,3},{3,2},{4,5},{5,4},{6,7},{7,6},{8,9},{9,8},{10,11... | collective-permute-start | bytes 393224 | tf_op jit(solution)/shard_map/ppermute | solution.py:30
  12.3 5.0 %collective-permute-done.1.refs_2_ = bf16[128,512]{1,0:T(8,128)(2,1)S(1)} collective-permute-done((bf16[128,512]{1,0:T(8,128)(2,1)}, bf16[128,512]{1,0:T(8,128)(2,1)S(1)}, u32[]{:S(2)}, u32[]{:S(2)}) %collective-permute-start.1) | collective-permute-done | bytes 131104 | tf_op jit(solution)/shard_map/ppermute | solution.py:40
  17.3 1.6 %collective-permute-start.5 = (bf16[128,512]{1,0:T(8,128)(2,1)S(1)}, bf16[128,512]{1,0:T(8,128)(2,1)S(1)}, u32[]{:S(2)}, u32[]{:S(2)}) collective-permute-start(bf16[128,512]{1,0:T(8,128)(2,1)S(1)} %collective-permute-done.1.refs_2_), channel_id=1, source_target_pairs={{0,24},{4,28},{8,16},{12,20},{16,8},{20,12},{24,0},{28,4},{1,25},{... | collective-permute-start | bytes 393224 | tf_op jit(solution)/shard_map/ppermute | solution.py:40
  18.9 1.8 %shard_map.109 = (bf16[256,2048]{1,0:T(8,128)(2,1)S(1)}, bf16[128,512]{1,0:T(8,128)(2,1)S(1)}, bf16[128,512]{1,0:T(8,128)(2,1)S(1)}, bf16[16,2048]{1,0:T(8,128)(...) custom-call(bf16[256,2048]{1,0:T(8,128)(2,1)} %tok_hbm.1, f32[1,2048]{1,0:T(1,128)} %bitcast.5, ...), custom_call_target="tpu_custom_call" | custom-call | flops 4194304 | bytes 2097152 | tf_op jit(solution)/shard_map/pallas_call | solution.py:48
  20.9 0.1 collective-permute-start.4
  20.9 2.2 %collective-permute-done.5.refs_0_ = bf16[128,512]{1,0:T(8,128)(2,1)S(1)} collective-permute-done((bf16[128,512]{1,0:T(8,128)(2,1)S(1)}, bf16[128,512]{1,0:T(8,128)(2,1)S(1)}, u32[]{:S(2)}, u32[]{:S(2)}) %collective-permute-start.5) | collective-permute-done | bytes 131104 | tf_op jit(solution)/shard_map/ppermute | solution.py:40
  23.2 1.4 %collective-permute-start.6 = (bf16[128,512]{1,0:T(8,128)(2,1)S(1)}, bf16[128,512]{1,0:T(8,128)(2,1)S(1)}, u32[]{:S(2)}, u32[]{:S(2)}) collective-permute-start(bf16[128,512]{1,0:T(8,128)(2,1)S(1)} %collective-permute-done.1.refs_2_), channel_id=1, source_target_pairs={{0,8},{4,12},{8,0},{12,4},{1,9},{5,13},{9,1},{13,5},{2,10},{6,14},... | collective-permute-start | bytes 393224 | tf_op jit(solution)/shard_map/ppermute | solution.py:30
  24.5 3.6 %collective-permute-done.6.refs_1_ = bf16[128,512]{1,0:T(8,128)(2,1)S(1)} collective-permute-done((bf16[128,512]{1,0:T(8,128)(2,1)S(1)}, bf16[128,512]{1,0:T(8,128)(2,1)S(1)}, u32[]{:S(2)}, u32[]{:S(2)}) %collective-permute-start.6) | collective-permute-done | bytes 131104 | tf_op jit(solution)/shard_map/ppermute | solution.py:30
  28.1 0.7 collective-permute-start.7
  28.8 4.2 %collective-permute-done.7.refs_2_ = bf16[128,512]{1,0:T(8,128)(2,1)S(1)} collective-permute-done((bf16[128,512]{1,0:T(8,128)(2,1)S(1)}, bf16[128,512]{1,0:T(8,128)(2,1)S(1)}, u32[]{:S(2)}, u32[]{:S(2)}) %collective-permute-start.7) | collective-permute-done | bytes 131104 | tf_op jit(solution)/shard_map/ppermute | solution.py:30
  33.1 1.3 %collective-permute-done.8.refs_3_ = bf16[128,512]{1,0:T(8,128)(2,1)S(1)} collective-permute-done((bf16[128,512]{1,0:T(8,128)(2,1)S(1)}, bf16[128,512]{1,0:T(8,128)(2,1)S(1)}, u32[]{:S(2)}, u32[]{:S(2)}) %collective-permute-start.8) | collective-permute-done | bytes 131104 | tf_op jit(solution)/shard_map/ppermute | solution.py:30
  34.4 0.1 collective-permute-start.9
  34.6 1.2 %collective-permute-done.9.refs_4_ = bf16[128,512]{1,0:T(8,128)(2,1)S(1)} collective-permute-done((bf16[128,512]{1,0:T(8,128)(2,1)S(1)}, bf16[128,512]{1,0:T(8,128)(2,1)S(1)}, u32[]{:S(2)}, u32[]{:S(2)}) %collective-permute-start.9) | collective-permute-done | bytes 131104 | tf_op jit(solution)/shard_map/ppermute | solution.py:30
  35.8 0.1 collective-permute-start.10
  35.9 1.4 %collective-permute-start.16 = (bf16[128,512]{1,0:T(8,128)(2,1)}, bf16[128,512]{1,0:T(8,128)(2,1)S(1)}, u32[]{:S(2)}, u32[]{:S(2)}) collective-permute-start(bf16[128,512]{1,0:T(8,128)(2,1)} %refs_1_.7), channel_id=1, source_target_pairs={{0,8},{4,12},{8,0},{12,4},{1,9},{5,13},{9,1},{13,5},{2,10},{6,14},... | collective-permute-start | bytes 393224 | tf_op jit(solution)/shard_map/ppermute | solution.py:30
  37.3 1.3 %shard_map.112.wt_ref = f32[16,256]{1,0:T(8,128)S(1)} custom-call(bf16[256,2048]{1,0:T(8,128)(2,1)S(1)} %get-tuple-element.11.normed_ref, bf16[16,2048]{1,0:T(8,128)(2,1)S(1)} %get-tuple-element.13.router_ref, s32[8,256]{1,0:T(8,128)S(1)} %get-tuple-element.14.ids_ref, s32[8,256]{1,0:T(8,128)S(1)} %get-tuple-element.15.slot_ref, s32[1,4,4,4]{3,2,1,0:T(4,128)} %list_hbm.1), custom_call_target="tpu_custom_call" | custom-call | flops 33554432 | bytes 1048576 | tf_op jit(solution)/shard_map/pallas_call | solution.py:48
  38.6 0.0 copy-start
  38.6 0.6 shard_map.111.sum_ref
  39.3 0.4 shard_map.113.pay_ref
  39.7 0.7 collective-permute-start.14
  40.4 1.5 %collective-permute-done.16.refs_1_ = bf16[128,512]{1,0:T(8,128)(2,1)S(1)} collective-permute-done((bf16[128,512]{1,0:T(8,128)(2,1)}, bf16[128,512]{1,0:T(8,128)(2,1)S(1)}, u32[]{:S(2)}, u32[]{:S(2)}) %collective-permute-start.16) | collective-permute-done | bytes 131104 | tf_op jit(solution)/shard_map/ppermute | solution.py:30
  41.9 0.1 shard_map.119.refs_1_
  42.0 0.9 %collective-permute-start.18 = (bf16[512,256]{1,0:T(8,128)(2,1)S(1)}, bf16[512,256]{1,0:T(8,128)(2,1)S(1)}, u32[]{:S(2)}, u32[]{:S(2)}) collective-permute-start(bf16[512,256]{1,0:T(8,128)(2,1)S(1)} %shard_map.119.refs_1_), channel_id=1, source_target_pairs={{0,2},{1,3},{2,0},{3,1},{16,19},{17,18},{18,17},{19,16},{4,6},{5,7... | collective-permute-start | bytes 786440 | tf_op jit(solution)/shard_map/ppermute | solution.py:40
  43.0 13.3 %collective-permute-done.18.refs_3_ = bf16[512,256]{1,0:T(8,128)(2,1)S(1)} collective-permute-done((bf16[512,256]{1,0:T(8,128)(2,1)S(1)}, bf16[512,256]{1,0:T(8,128)(2,1)S(1)}, u32[]{:S(2)}, u32[]{:S(2)}) %collective-permute-start.18) | collective-permute-done | bytes 262176 | tf_op jit(solution)/shard_map/ppermute | solution.py:40
  56.4 1.1 %collective-permute-start.19 = (bf16[512,256]{1,0:T(8,128)(2,1)S(1)}, bf16[512,256]{1,0:T(8,128)(2,1)S(1)}, u32[]{:S(2)}, u32[]{:S(2)}) collective-permute-start(bf16[512,256]{1,0:T(8,128)(2,1)S(1)} %collective-permute-done.18.refs_3_), channel_id=1, source_target_pairs={{0,16},{16,0},{1,17},{17,1},{2,18},{18,2},{3,19},{19,3},{4,20},{20... | collective-permute-start | bytes 786440 | tf_op jit(solution)/shard_map/ppermute | solution.py:30
  57.4 2.8 %shard_map.114.sum_ref = f32[256,512]{1,0:T(8,128)S(1)} custom-call(bf16[272,512]{1,0:T(8,128)(2,1)S(1)} %shard_map.113.pay_ref, bf16[4,512,768]{2,1,0:T(8,128)(2,1)S(1)} %copy-done, bf16[4,512,768]{2,1,0:T(8,128)(2,1)S(1)} %copy-done.1, bf16[4,768,512]{2,1,0:T(8,128)(2,1)S(1)} %copy-done.2), custom_call_target="tpu_custom_call" | custom-call | flops 2415919104 | bytes 9437184 | tf_op jit(solution)/shard_map/pallas_call | solution.py:48
  60.3 2.8 %shard_map.117.sum_ref = f32[256,512]{1,0:T(8,128)S(1)} custom-call(bf16[272,512]{1,0:T(8,128)(2,1)S(1)} %collective-permute-done.14.pay_ref, bf16[4,512,768]{2,1,0:T(8,128)(2,1)S(1)} %copy-done, bf16[4,512,768]{2,1,0:T(8,128)(2,1)S(1)} %copy-done.1, bf16[4,768,512]{2,1,0:T(8,128)(2,1)S(1)} %copy-done.2), custom_call_target="tpu_custom_call" | custom-call | flops 2415919104 | bytes 9437184 | tf_op jit(solution)/shard_map/pallas_call | solution.py:48
  63.1 0.4 collective-permute-done.17.refs_2_
  63.5 0.0 collective-permute-done.19.refs_4_
  63.5 0.5 collective-permute-start.22
  64.0 0.1 collective-permute-start.21
  64.1 0.4 collective-permute-start.23
  64.5 1.8 %shard_map.120 = bf16[128,512]{1,0:T(8,128)(2,1)S(1)} custom-call(bf16[272,512]{1,0:T(8,128)(2,1)S(1)} %collective-permute-done.14.pay_ref, f32[256,512]{1,0:T(8,128)S(1)} %shard_map.117.sum_ref, bf16[4,512,768]{2,1,0:T(8,128)(2,1)S(1)} %copy-done, bf16[4,512,768]{2,1,0:T(8,128)(2,1)S(1)} %copy-done.1, bf16[4,768,512]{2,1,0:T(8,128)(2,1)S(1)} %copy-done.2, ...), custom_call_target="tpu_custom_call" | custom-call | flops 1207959552 | bytes 9437184 | tf_op jit(solution)/shard_map/pallas_call | solution.py:48
  66.3 1.3 %collective-permute-start.24 = (bf16[128,512]{1,0:T(8,128)(2,1)S(1)}, bf16[128,512]{1,0:T(8,128)(2,1)S(1)}, u32[]{:S(2)}, u32[]{:S(2)}) collective-permute-start(bf16[128,512]{1,0:T(8,128)(2,1)S(1)} %shard_map.120), channel_id=1, source_target_pairs={{0,8},{4,12},{8,0},{12,4},{1,9},{5,13},{9,1},{13,5},{2,10},{6,14},... | collective-permute-start | bytes 393224 | tf_op jit(solution)/shard_map/ppermute | solution.py:30
  67.7 1.8 %shard_map.118 = bf16[128,512]{1,0:T(8,128)(2,1)S(1)} custom-call(bf16[272,512]{1,0:T(8,128)(2,1)S(1)} %collective-permute-done.14.pay_ref, f32[256,512]{1,0:T(8,128)S(1)} %shard_map.117.sum_ref, bf16[4,512,768]{2,1,0:T(8,128)(2,1)S(1)} %copy-done, bf16[4,512,768]{2,1,0:T(8,128)(2,1)S(1)} %copy-done.1, bf16[4,768,512]{2,1,0:T(8,128)(2,1)S(1)} %copy-done.2, ...), custom_call_target="tpu_custom_call" | custom-call | flops 1207959552 | bytes 9437184 | tf_op jit(solution)/shard_map/pallas_call | solution.py:48
  69.5 1.5 %shard_map.115.sum_ref = f32[256,512]{1,0:T(8,128)S(1)} custom-call(bf16[272,512]{1,0:T(8,128)(2,1)S(1)} %shard_map.113.pay_ref, f32[256,512]{1,0:T(8,128)S(1)} %shard_map.114.sum_ref, bf16[4,512,768]{2,1,0:T(8,128)(2,1)S(1)} %copy-done, bf16[4,512,768]{2,1,0:T(8,128)(2,1)S(1)} %copy-done.1, bf16[4,768,512]{2,1,0:T(8,128)(2,1)S(1)} %copy-done.2, ...), custom_call_target="tpu_custom_call" | custom-call | flops 1207959552 | bytes 4718592 | tf_op jit(solution)/shard_map/pallas_call | solution.py:48
  71.0 0.8 %collective-permute-start.15 = (bf16[128,512]{1,0:T(8,128)(2,1)S(1)}, bf16[128,512]{1,0:T(8,128)(2,1)S(1)}, u32[]{:S(2)}, u32[]{:S(2)}) collective-permute-start(bf16[128,512]{1,0:T(8,128)(2,1)S(1)} %shard_map.118), channel_id=1, source_target_pairs={{0,8},{4,12},{8,0},{12,4},{1,9},{5,13},{9,1},{13,5},{2,10},{6,14},... | collective-permute-start | bytes 393224 | tf_op jit(solution)/shard_map/ppermute | solution.py:30
  71.8 1.5 %shard_map.116.near_ref = f32[256,512]{1,0:T(8,128)S(1)} custom-call(bf16[272,512]{1,0:T(8,128)(2,1)S(1)} %shard_map.113.pay_ref, f32[256,512]{1,0:T(8,128)S(1)} %shard_map.115.sum_ref, bf16[4,512,768]{2,1,0:T(8,128)(2,1)S(1)} %copy-done, bf16[4,512,768]{2,1,0:T(8,128)(2,1)S(1)} %copy-done.1, bf16[4,768,512]{2,1,0:T(8,128)(2,1)S(1)} %copy-done.2, ...), custom_call_target="tpu_custom_call" | custom-call | flops 1207959552 | bytes 4718592 | tf_op jit(solution)/shard_map/pallas_call | solution.py:48
  73.3 1.3 %shard_map.121.refs_9_ = bf16[256,2048]{1,0:T(8,128)(2,1)} custom-call(f32[256,512]{1,0:T(8,128)S(1)} %shard_map.116.near_ref, bf16[128,512]{1,0:T(8,128)(2,1)S(1)} %collective-permute-done.24.refs_0_, bf16[512,256]{1,0:T(8,128)(2,1)S(1)} %shard_map.119.refs_1_, bf16[512,256]{1,0:T(8,128)(2,1)S(1)} %collective-permute-done.17.refs_2_, ...), custom_call_target="tpu_custom_call" | custom-call | flops 268435456 | bytes 2097152 | tf_op jit(solution)/shard_map/pallas_call | solution.py:48
  74.6 1.6 %collective-permute-done.15.refs_0_ = bf16[128,512]{1,0:T(8,128)(2,1)S(1)} collective-permute-done((bf16[128,512]{1,0:T(8,128)(2,1)S(1)}, bf16[128,512]{1,0:T(8,128)(2,1)S(1)}, u32[]{:S(2)}, u32[]{:S(2)}) %collective-permute-start.15) | collective-permute-done | bytes 131104 | tf_op jit(solution)/shard_map/ppermute | solution.py:30
  76.2 1.3 %shard_map.122 = bf16[256,2048]{1,0:T(8,128)(2,1)} custom-call(f32[256,512]{1,0:T(8,128)S(1)} %shard_map.116.near_ref, bf16[128,512]{1,0:T(8,128)(2,1)S(1)} %collective-permute-done.15.refs_0_, bf16[512,256]{1,0:T(8,128)(2,1)S(1)} %shard_map.119.refs_1_, bf16[512,256]{1,0:T(8,128)(2,1)S(1)} %collective-permute-done.17.refs_2_, ...), custom_call_target="tpu_custom_call", output_to_operand_aliasing={{}: (10, {})} | custom-call | flops 268435456 | bytes 2097152 | tf_op jit(solution)/shard_map/pallas_call | solution.py:48
  (22 shorter events, 0.1 us)
Async XLA Ops:
  0.0 64.0 %collective-permute-start.11 = (bf16[4,512,768]{2,1,0:T(8,128)(2,1)}, bf16[4,512,768]{2,1,0:T(8,128)(2,1)S(1)}, u32[]{:S(2)}, u32[]{:S(2)}) collective-permute-start(bf16[4,512,768]{2,1,0:T(8,128)(2,1)} %refs_0_.13), channel_id=1, source_target_pairs={{0,4},{4,0},{8,12},{12,8},{1,5},{5,1},{9,13},{13,9},{2,6},{6,2},{1... | collective-permute-start | bytes 9437192 | tf_op jit(solution)/shard_map/ppermute | solution.py:30
  0.5 63.6 %collective-permute-start.12 = (bf16[4,512,768]{2,1,0:T(8,128)(2,1)}, bf16[4,512,768]{2,1,0:T(8,128)(2,1)S(1)}, u32[]{:S(2)}, u32[]{:S(2)}) collective-permute-start(bf16[4,512,768]{2,1,0:T(8,128)(2,1)} %refs_1_.13), channel_id=1, source_target_pairs={{0,4},{4,0},{8,12},{12,8},{1,5},{5,1},{9,13},{13,9},{2,6},{6,2},{1... | collective-permute-start | bytes 9437192 | tf_op jit(solution)/shard_map/ppermute | solution.py:30
  0.5 64.0 %collective-permute-start.13 = (bf16[4,768,512]{2,1,0:T(8,128)(2,1)}, bf16[4,768,512]{2,1,0:T(8,128)(2,1)S(1)}, u32[]{:S(2)}, u32[]{:S(2)}) collective-permute-start(bf16[4,768,512]{2,1,0:T(8,128)(2,1)} %refs_2_.11), channel_id=1, source_target_pairs={{0,4},{4,0},{8,12},{12,8},{1,5},{5,1},{9,13},{13,9},{2,6},{6,2},{1... | collective-permute-start | bytes 9437192 | tf_op jit(solution)/shard_map/ppermute | solution.py:30
  1.0 6.9 %collective-permute-start = (bf16[128,512]{1,0:T(8,128)(2,1)}, bf16[128,512]{1,0:T(8,128)(2,1)S(1)}, u32[]{:S(2)}, u32[]{:S(2)}) collective-permute-start(bf16[128,512]{1,0:T(8,128)(2,1)} %refs_0_.7), channel_id=1, source_target_pairs={{0,1},{1,0},{2,3},{3,2},{4,5},{5,4},{6,7},{7,6},{8,9},{9,8},{10,11... | collective-permute-start | bytes 393224 | tf_op jit(solution)/shard_map/ppermute | solution.py:30
  3.6 7.1 %collective-permute-start.2 = (bf16[128,512]{1,0:T(8,128)(2,1)}, bf16[128,512]{1,0:T(8,128)(2,1)S(1)}, u32[]{:S(2)}, u32[]{:S(2)}) collective-permute-start(bf16[128,512]{1,0:T(8,128)(2,1)} %refs_0_.7), channel_id=1, source_target_pairs={{0,8},{4,12},{8,0},{12,4},{1,9},{5,13},{9,1},{13,5},{2,10},{6,14},... | collective-permute-start | bytes 393224 | tf_op jit(solution)/shard_map/ppermute | solution.py:30
  7.9 9.3 %collective-permute-start.1 = (bf16[128,512]{1,0:T(8,128)(2,1)}, bf16[128,512]{1,0:T(8,128)(2,1)S(1)}, u32[]{:S(2)}, u32[]{:S(2)}) collective-permute-start(bf16[128,512]{1,0:T(8,128)(2,1)} %refs_0_.7), channel_id=1, source_target_pairs={{0,2},{1,3},{2,0},{3,1},{16,19},{17,18},{18,17},{19,16},{4,6},{5,7... | collective-permute-start | bytes 393224 | tf_op jit(solution)/shard_map/ppermute | solution.py:40
  10.7 10.1 %collective-permute-start.3 = (bf16[128,512]{1,0:T(8,128)(2,1)S(1)}, bf16[128,512]{1,0:T(8,128)(2,1)S(1)}, u32[]{:S(2)}, u32[]{:S(2)}) collective-permute-start(bf16[128,512]{1,0:T(8,128)(2,1)S(1)} %collective-permute-done.2.refs_3_), channel_id=1, source_target_pairs={{0,1},{1,0},{2,3},{3,2},{4,5},{5,4},{6,7},{7,6},{8,9},{9,8},{10,11... | collective-permute-start | bytes 393224 | tf_op jit(solution)/shard_map/ppermute | solution.py:30
  17.3 5.9 %collective-permute-start.5 = (bf16[128,512]{1,0:T(8,128)(2,1)S(1)}, bf16[128,512]{1,0:T(8,128)(2,1)S(1)}, u32[]{:S(2)}, u32[]{:S(2)}) collective-permute-start(bf16[128,512]{1,0:T(8,128)(2,1)S(1)} %collective-permute-done.1.refs_2_), channel_id=1, source_target_pairs={{0,24},{4,28},{8,16},{12,20},{16,8},{20,12},{24,0},{28,4},{1,25},{... | collective-permute-start | bytes 393224 | tf_op jit(solution)/shard_map/ppermute | solution.py:40
  18.9 38.5 %copy-start.2 = (bf16[4,768,512]{2,1,0:T(8,128)(2,1)S(1)}, bf16[4,768,512]{2,1,0:T(8,128)(2,1)}, u32[]{:S(2)}) copy-start(bf16[4,768,512]{2,1,0:T(8,128)(2,1)} %refs_2_.11) | copy-start | bytes 9437188
  20.9 15.1 %collective-permute-start.4 = (bf16[640,512]{1,0:T(8,128)(2,1)S(1)}, bf16[640,512]{1,0:T(8,128)(2,1)S(1)}, u32[]{:S(2)}, u32[]{:S(2)}) collective-permute-start(bf16[640,512]{1,0:T(8,128)(2,1)S(1)} %shard_map.110.w0_ref), channel_id=1, source_target_pairs={{0,4},{4,0},{8,12},{12,8},{1,5},{5,1},{9,13},{13,9},{2,6},{6,2},{1... | collective-permute-start | bytes 1966088 | tf_op jit(solution)/shard_map/ppermute | solution.py:30
  23.2 5.0 %collective-permute-start.6 = (bf16[128,512]{1,0:T(8,128)(2,1)S(1)}, bf16[128,512]{1,0:T(8,128)(2,1)S(1)}, u32[]{:S(2)}, u32[]{:S(2)}) collective-permute-start(bf16[128,512]{1,0:T(8,128)(2,1)S(1)} %collective-permute-done.1.refs_2_), channel_id=1, source_target_pairs={{0,8},{4,12},{8,0},{12,4},{1,9},{5,13},{9,1},{13,5},{2,10},{6,14},... | collective-permute-start | bytes 393224 | tf_op jit(solution)/shard_map/ppermute | solution.py:30
  28.1 5.0 %collective-permute-start.7 = (bf16[128,512]{1,0:T(8,128)(2,1)S(1)}, bf16[128,512]{1,0:T(8,128)(2,1)S(1)}, u32[]{:S(2)}, u32[]{:S(2)}) collective-permute-start(bf16[128,512]{1,0:T(8,128)(2,1)S(1)} %collective-permute-done.1.refs_2_), channel_id=1, source_target_pairs={{0,16},{16,0},{1,17},{17,1},{2,18},{18,2},{3,19},{19,3},{4,20},{20... | collective-permute-start | bytes 393224 | tf_op jit(solution)/shard_map/ppermute | solution.py:30
  33.1 1.3 %collective-permute-start.8 = (bf16[128,512]{1,0:T(8,128)(2,1)S(1)}, bf16[128,512]{1,0:T(8,128)(2,1)S(1)}, u32[]{:S(2)}, u32[]{:S(2)}) collective-permute-start(bf16[128,512]{1,0:T(8,128)(2,1)S(1)} %collective-permute-done.5.refs_0_), channel_id=1, source_target_pairs={{0,4},{4,0},{8,12},{12,8},{1,5},{5,1},{9,13},{13,9},{2,6},{6,2},{1... | collective-permute-start | bytes 393224 | tf_op jit(solution)/shard_map/ppermute | solution.py:30
  34.4 1.3 %collective-permute-start.9 = (bf16[128,512]{1,0:T(8,128)(2,1)S(1)}, bf16[128,512]{1,0:T(8,128)(2,1)S(1)}, u32[]{:S(2)}, u32[]{:S(2)}) collective-permute-start(bf16[128,512]{1,0:T(8,128)(2,1)S(1)} %collective-permute-done.6.refs_1_), channel_id=1, source_target_pairs={{0,4},{4,0},{8,12},{12,8},{1,5},{5,1},{9,13},{13,9},{2,6},{6,2},{1... | collective-permute-start | bytes 393224 | tf_op jit(solution)/shard_map/ppermute | solution.py:30
  35.8 3.5 %collective-permute-start.10 = (bf16[128,512]{1,0:T(8,128)(2,1)S(1)}, bf16[128,512]{1,0:T(8,128)(2,1)S(1)}, u32[]{:S(2)}, u32[]{:S(2)}) collective-permute-start(bf16[128,512]{1,0:T(8,128)(2,1)S(1)} %collective-permute-done.7.refs_2_), channel_id=1, source_target_pairs={{0,4},{4,0},{8,12},{12,8},{1,5},{5,1},{9,13},{13,9},{2,6},{6,2},{1... | collective-permute-start | bytes 393224 | tf_op jit(solution)/shard_map/ppermute | solution.py:30
  35.9 6.0 %collective-permute-start.16 = (bf16[128,512]{1,0:T(8,128)(2,1)}, bf16[128,512]{1,0:T(8,128)(2,1)S(1)}, u32[]{:S(2)}, u32[]{:S(2)}) collective-permute-start(bf16[128,512]{1,0:T(8,128)(2,1)} %refs_1_.7), channel_id=1, source_target_pairs={{0,8},{4,12},{8,0},{12,4},{1,9},{5,13},{9,1},{13,5},{2,10},{6,14},... | collective-permute-start | bytes 393224 | tf_op jit(solution)/shard_map/ppermute | solution.py:30
  37.3 20.1 %copy-start.1 = (bf16[4,512,768]{2,1,0:T(8,128)(2,1)S(1)}, bf16[4,512,768]{2,1,0:T(8,128)(2,1)}, u32[]{:S(2)}) copy-start(bf16[4,512,768]{2,1,0:T(8,128)(2,1)} %refs_1_.13) | copy-start | bytes 9437188
  38.6 18.8 %copy-start = (bf16[4,512,768]{2,1,0:T(8,128)(2,1)S(1)}, bf16[4,512,768]{2,1,0:T(8,128)(2,1)}, u32[]{:S(2)}) copy-start(bf16[4,512,768]{2,1,0:T(8,128)(2,1)} %refs_0_.13) | copy-start | bytes 9437188
  39.7 16.7 %collective-permute-start.14 = (bf16[272,512]{1,0:T(8,128)(2,1)S(1)}, bf16[272,512]{1,0:T(8,128)(2,1)S(1)}, u32[]{:S(2)}, u32[]{:S(2)}) collective-permute-start(bf16[272,512]{1,0:T(8,128)(2,1)S(1)} %shard_map.113.pay_ref), channel_id=1, source_target_pairs={{0,8},{4,12},{8,0},{12,4},{1,9},{5,13},{9,1},{13,5},{2,10},{6,14},... | collective-permute-start | bytes 835592 | tf_op jit(solution)/shard_map/ppermute | solution.py:30
  42.0 14.3 %collective-permute-start.18 = (bf16[512,256]{1,0:T(8,128)(2,1)S(1)}, bf16[512,256]{1,0:T(8,128)(2,1)S(1)}, u32[]{:S(2)}, u32[]{:S(2)}) collective-permute-start(bf16[512,256]{1,0:T(8,128)(2,1)S(1)} %shard_map.119.refs_1_), channel_id=1, source_target_pairs={{0,2},{1,3},{2,0},{3,1},{16,19},{17,18},{18,17},{19,16},{4,6},{5,7... | collective-permute-start | bytes 786440 | tf_op jit(solution)/shard_map/ppermute | solution.py:40
  56.3 7.1 %collective-permute-start.17 = (bf16[512,256]{1,0:T(8,128)(2,1)S(1)}, bf16[512,256]{1,0:T(8,128)(2,1)S(1)}, u32[]{:S(2)}, u32[]{:S(2)}) collective-permute-start(bf16[512,256]{1,0:T(8,128)(2,1)S(1)} %shard_map.119.refs_1_), channel_id=1, source_target_pairs={{0,1},{1,0},{2,3},{3,2},{4,5},{5,4},{6,7},{7,6},{8,9},{9,8},{10,11... | collective-permute-start | bytes 786440 | tf_op jit(solution)/shard_map/ppermute | solution.py:30
  56.4 7.1 %collective-permute-start.19 = (bf16[512,256]{1,0:T(8,128)(2,1)S(1)}, bf16[512,256]{1,0:T(8,128)(2,1)S(1)}, u32[]{:S(2)}, u32[]{:S(2)}) collective-permute-start(bf16[512,256]{1,0:T(8,128)(2,1)S(1)} %collective-permute-done.18.refs_3_), channel_id=1, source_target_pairs={{0,16},{16,0},{1,17},{17,1},{2,18},{18,2},{3,19},{19,3},{4,20},{20... | collective-permute-start | bytes 786440 | tf_op jit(solution)/shard_map/ppermute | solution.py:30
  63.5 7.5 %collective-permute-start.20 = (bf16[512,256]{1,0:T(8,128)(2,1)S(1)}, bf16[512,256]{1,0:T(8,128)(2,1)S(1)}, u32[]{:S(2)}, u32[]{:S(2)}) collective-permute-start(bf16[512,256]{1,0:T(8,128)(2,1)S(1)} %shard_map.119.refs_1_), channel_id=1, source_target_pairs={{0,4},{4,0},{8,12},{12,8},{1,5},{5,1},{9,13},{13,9},{2,6},{6,2},{1... | collective-permute-start | bytes 786440 | tf_op jit(solution)/shard_map/ppermute | solution.py:30
  63.5 9.8 %collective-permute-start.22 = (bf16[512,256]{1,0:T(8,128)(2,1)S(1)}, bf16[512,256]{1,0:T(8,128)(2,1)S(1)}, u32[]{:S(2)}, u32[]{:S(2)}) collective-permute-start(bf16[512,256]{1,0:T(8,128)(2,1)S(1)} %collective-permute-done.18.refs_3_), channel_id=1, source_target_pairs={{0,4},{4,0},{8,12},{12,8},{1,5},{5,1},{9,13},{13,9},{2,6},{6,2},{1... | collective-permute-start | bytes 786440 | tf_op jit(solution)/shard_map/ppermute | solution.py:30
  64.0 9.3 %collective-permute-start.21 = (bf16[512,256]{1,0:T(8,128)(2,1)S(1)}, bf16[512,256]{1,0:T(8,128)(2,1)S(1)}, u32[]{:S(2)}, u32[]{:S(2)}) collective-permute-start(bf16[512,256]{1,0:T(8,128)(2,1)S(1)} %collective-permute-done.17.refs_2_), channel_id=1, source_target_pairs={{0,4},{4,0},{8,12},{12,8},{1,5},{5,1},{9,13},{13,9},{2,6},{6,2},{1... | collective-permute-start | bytes 786440 | tf_op jit(solution)/shard_map/ppermute | solution.py:30
  64.1 9.2 %collective-permute-start.23 = (bf16[512,256]{1,0:T(8,128)(2,1)S(1)}, bf16[512,256]{1,0:T(8,128)(2,1)S(1)}, u32[]{:S(2)}, u32[]{:S(2)}) collective-permute-start(bf16[512,256]{1,0:T(8,128)(2,1)S(1)} %collective-permute-done.19.refs_4_), channel_id=1, source_target_pairs={{0,4},{4,0},{8,12},{12,8},{1,5},{5,1},{9,13},{13,9},{2,6},{6,2},{1... | collective-permute-start | bytes 786440 | tf_op jit(solution)/shard_map/ppermute | solution.py:30
  66.3 7.0 %collective-permute-start.24 = (bf16[128,512]{1,0:T(8,128)(2,1)S(1)}, bf16[128,512]{1,0:T(8,128)(2,1)S(1)}, u32[]{:S(2)}, u32[]{:S(2)}) collective-permute-start(bf16[128,512]{1,0:T(8,128)(2,1)S(1)} %shard_map.120), channel_id=1, source_target_pairs={{0,8},{4,12},{8,0},{12,4},{1,9},{5,13},{9,1},{13,5},{2,10},{6,14},... | collective-permute-start | bytes 393224 | tf_op jit(solution)/shard_map/ppermute | solution.py:30
  71.0 5.3 %collective-permute-start.15 = (bf16[128,512]{1,0:T(8,128)(2,1)S(1)}, bf16[128,512]{1,0:T(8,128)(2,1)S(1)}, u32[]{:S(2)}, u32[]{:S(2)}) collective-permute-start(bf16[128,512]{1,0:T(8,128)(2,1)S(1)} %shard_map.118), channel_id=1, source_target_pairs={{0,8},{4,12},{8,0},{12,4},{1,9},{5,13},{9,1},{13,5},{2,10},{6,14},... | collective-permute-start | bytes 393224 | tf_op jit(solution)/shard_map/ppermute | solution.py:30
